TPU v7x, 32 devices: a whole 2x2x4 slice. The times are simulated.
32 devices in a mesh: groups: 2 (over x), ctx: 16 (over z, y, core).
Axes of the slice: x: 2, y: 2, z: 4, core: 2. Of those that a mesh axis runs over, the one named last changes fastest.
Arguments:
- hidden_in: bfloat16 [32, 8192], P('groups', 'ctx'), parts along dimension 0, may hold values from -6 to 6
- attn_gain: float32 [8192], replicated, may hold values from 0.1 to 1.9
- w_query: bfloat16 [8192, 4096], P(None, 'ctx'), may hold values from -0.0625 to 0.0625
- w_key: bfloat16 [8192, 512], P(None, 'ctx'), may hold values from -0.375 to 0.375
- w_value: bfloat16 [8192, 512], P(None, 'ctx'), may hold values from -0.0625 to 0.0625
- rotated_prefix_keys: bfloat16 [32768, 4, 128], P(('groups', 'ctx')), parts along dimension 0, may hold values from -70 to 70
- cache_values: bfloat16 [32768, 4, 128], P(('groups', 'ctx')), parts along dimension 0, may hold values from -6 to 6
- w_out: bfloat16 [4096, 8192], P(None, 'ctx'), may hold values from -0.09375 to 0.09375
- ffn_gain: float32 [8192], replicated, may hold values from 0.1 to 1.9
- w_gate: bfloat16 [8192, 14336], P(None, 'ctx'), may hold values from -0.0625 to 0.0625
- w_up: bfloat16 [8192, 14336], P(None, 'ctx'), may hold values from -0.0625 to 0.0625
- w_down: bfloat16 [14336, 8192], P(None, 'ctx'), may hold values from -0.046875 to 0.046875
- doc_offsets: int32 [32], P('groups'), parts along dimension 0, may hold values from 8192 to 16384
- slot_request: int32 [32], P('groups'), parts along dimension 0, may hold values from 0 to 15, each once
Outputs:
- layer_out: bfloat16 [32, 8192], P('groups', 'ctx'), parts along dimension 0
There are 2 independent parts, one for each index of `groups`. A program takes and returns all parts, laid end to end along the dimension named above; an argument that names none is the same for every part. Nothing has to cross between parts.
Inputs may be any that keep to these rules, and one draw needn't show every extreme that they name: `slot_request`: each slot holds a different request.
All inputs are finite; a program needn't handle non-finite values.
Results may differ from a plain program's by a relative error of at most 0.011.
Values may be sent and summed in bfloat16 or wider, within the bound.
No kernel may reach another device: no remote copies, remote signals or barrier semaphores. Data moves between devices by JAX's collectives and lax.ppermute only.
A program may use at most 128 MiB of HBM per device.

v0:
```python
import math

import jax
import jax.numpy as jnp
from jax import lax
from jax.sharding import PartitionSpec as P

NORM_EPSILON = 1e-05
ROPE_BASE = 500000.0
MASKED = -1e30


def joined(part, axis, combine):
    gathered = jax.tree.map(lambda a: lax.all_gather(a, axis), part)

    def take(source):
        return jax.tree.map(lambda a: lax.dynamic_index_in_dim(a, source, 0, False), gathered)

    return lax.fori_loop(
        1, lax.axis_size(axis), lambda source, state: combine(state, take(source)), take(0)
    )


def rms_norm(values, gain_row):
    wide_rows = values.astype(jnp.float32)
    factor = lax.rsqrt(jnp.mean(wide_rows * wide_rows, axis=1, keepdims=True) + NORM_EPSILON)
    return (wide_rows * factor * gain_row[None, :]).astype(jnp.bfloat16)


def rotate(columns, first_col, positions, head_dim):
    col_count = columns.shape[1]
    pair_cols = first_col + jnp.arange(col_count // 2, dtype=jnp.int32) * 2
    in_head = (pair_cols % head_dim).astype(jnp.float32)
    frequency = jnp.exp(-(in_head / head_dim) * jnp.log(jnp.float32(ROPE_BASE)))
    angles = positions.astype(jnp.float32)[:, None] * frequency[None, :]
    paired = columns.reshape(columns.shape[0], col_count // 2, 2)
    even_part = paired[..., 0]
    odd_part = paired[..., 1]
    cosine = jnp.cos(angles)
    sine = jnp.sin(angles)
    turned = jnp.stack(
        [even_part * cosine - odd_part * sine, even_part * sine + odd_part * cosine], axis=-1
    )
    return turned.reshape(columns.shape)


def combine_parts(first_part, second_part):
    top_first, total_first, accum_first = first_part
    top_second, total_second, accum_second = second_part
    peak_score = jnp.maximum(top_first, top_second)
    share_first = jnp.exp(top_first - peak_score)
    share_second = jnp.exp(top_second - peak_score)
    merged_total = total_first * share_first + total_second * share_second
    merged_accum = accum_first * share_first[..., None] + accum_second * share_second[..., None]
    return (peak_score, merged_total, merged_accum)


def shards(
    hidden_in,
    attn_gain,
    w_query,
    w_key,
    w_value,
    rotated_prefix_keys,
    cache_values,
    w_out,
    ffn_gain,
    w_gate,
    w_up,
    w_down,
    doc_offsets,
    slot_request,
):
    devices = lax.axis_size("ctx")
    device = lax.axis_index("ctx")
    batch_rows = hidden_in.shape[0]
    block_span, value_heads, head_dim = rotated_prefix_keys.shape
    query_width = w_query.shape[1]
    key_width = w_key.shape[1]
    head_count = query_width * devices // head_dim
    group_size = head_count // value_heads
    logit_scale_factor = 1.0 / math.sqrt(head_dim)
    slot_index = jnp.arange(batch_rows, dtype=jnp.int32)
    positions = jnp.sum(
        jnp.where(slot_request[:, None] == slot_index[None, :], doc_offsets[None, :], 0), axis=1
    )
    full_rows = lax.all_gather(hidden_in, "ctx", axis=1, tiled=True)
    normed = rms_norm(full_rows, attn_gain)
    query_part = rotate(
        jnp.dot(normed, w_query, preferred_element_type=jnp.float32),
        device * query_width,
        positions,
        head_dim,
    ).astype(jnp.bfloat16)
    key_part = rotate(
        jnp.dot(normed, w_key, preferred_element_type=jnp.float32),
        device * key_width,
        positions,
        head_dim,
    ).astype(jnp.bfloat16)
    value_part = jnp.dot(normed, w_value, preferred_element_type=jnp.float32).astype(jnp.bfloat16)
    queries, key_new, value_new = (
        lax.all_gather(query_part, "ctx", axis=1, tiled=True),
        lax.all_gather(key_part, "ctx", axis=1, tiled=True),
        lax.all_gather(value_part, "ctx", axis=1, tiled=True),
    )
    query_groups = queries.reshape(batch_rows, value_heads, group_size, head_dim)
    attention_logits = (
        jnp.einsum(
            "owqa,zwa->owqz", query_groups, rotated_prefix_keys, preferred_element_type=jnp.float32
        )
        * logit_scale_factor
    )
    places = device * block_span + jnp.arange(block_span, dtype=jnp.int32)
    visible = (places[None, :] < positions[:, None])[:, None, None, :]
    masked = jnp.where(visible, attention_logits, MASKED)
    block_top = jnp.max(masked, axis=3)
    weights = jnp.where(visible, jnp.exp(masked - block_top[..., None]), 0.0)
    block_total = jnp.sum(weights, axis=3)
    block_value_sum = jnp.einsum(
        "nelw,weh->nelh",
        weights.astype(jnp.bfloat16),
        cache_values,
        preferred_element_type=jnp.float32,
    )
    own_score = (
        jnp.einsum(
            "rkgd,rkd->rkg",
            query_groups,
            key_new.reshape(batch_rows, value_heads, head_dim),
            preferred_element_type=jnp.float32,
        )
        * logit_scale_factor
    ).reshape(batch_rows, head_count)
    spread_value = jnp.broadcast_to(
        value_new.reshape(batch_rows, value_heads, 1, head_dim),
        (batch_rows, value_heads, group_size, head_dim),
    ).reshape(batch_rows, head_count * head_dim)
    global_top, global_total, prefix_accum = joined(
        (block_top, block_total, block_value_sum), "ctx", combine_parts
    )
    finish_global_top = global_top
    finish_global_total = global_total
    finish_global_top = finish_global_top.reshape(batch_rows, head_count)
    finish_global_total = finish_global_total.reshape(batch_rows, head_count)
    peak_score = jnp.maximum(finish_global_top, own_score)
    kept_share = jnp.exp(finish_global_top - peak_score)
    fresh_share = jnp.exp(own_score - peak_score)
    denominator = finish_global_total * kept_share + fresh_share

    def columns(per_head):
        return jnp.repeat(per_head, head_dim, axis=1)

    value_cols = spread_value.astype(jnp.float32)
    attn_all = (
        (
            prefix_accum.reshape(batch_rows, head_count * head_dim) * columns(kept_share)
            + columns(fresh_share) * value_cols
        )
        / columns(denominator)
    ).astype(jnp.bfloat16)
    attn_part = jnp.dot(attn_all, w_out, preferred_element_type=jnp.float32)
    mid_part = (hidden_in.astype(jnp.float32) + attn_part).astype(jnp.bfloat16)
    mid_full = lax.all_gather(mid_part, "ctx", axis=1, tiled=True)
    normed_mid = rms_norm(mid_full, ffn_gain)
    gate_act = jnp.dot(normed_mid, w_gate, preferred_element_type=jnp.float32)
    up_act = jnp.dot(normed_mid, w_up, preferred_element_type=jnp.float32)
    hidden = (jax.nn.silu(gate_act) * up_act).astype(jnp.bfloat16)
    down_part = jnp.dot(
        lax.all_gather(hidden, "ctx", axis=1, tiled=True),
        w_down,
        preferred_element_type=jnp.float32,
    )
    return (mid_part.astype(jnp.float32) + down_part).astype(jnp.bfloat16)


def solution(mesh):
    return jax.shard_map(
        shards,
        mesh=mesh,
        in_specs=(
            P("groups", "ctx"),
            P(),
            P(None, "ctx"),
            P(None, "ctx"),
            P(None, "ctx"),
            P(("groups", "ctx"), None, None),
            P(("groups", "ctx"), None, None),
            P(None, "ctx"),
            P(),
            P(None, "ctx"),
            P(None, "ctx"),
            P(None, "ctx"),
            P("groups"),
            P("groups"),
        ),
        out_specs=P("groups", "ctx"),
        check_vma=False,
    )
```

profile of v0, /device:TPU:0, one launch (start us, length us, event | category | flops | bytes accessed | tf_op | source)
XLA Modules:
  0.0 229.2 jit_solution(7356914629997899854)
XLA Ops:
  6.6 0.9 select_reduce_fusion
  7.5 0.1 broadcast_compare_fusion
  7.6 24.1 %all_gather.36 = bf16[16,8192]{1,0:T(8,128)(2,1)S(1)} all-gather(bf16[16,512]{1,0:T(8,128)(2,1)} %param.16), channel_id=1, replica_groups=mesh['groups'=2,'ctx'=16] {'ctx'}, dimensions={1}, use_global_device_ids=true | all-gather | bytes 278528 | tf_op jit(solution)/shard_map/all_gather | solution.py:87
  31.7 0.2 fusion.22
  31.9 4.0 %fusion.71 = f32[16,256]{0,1:T(8,128)S(1)} fusion(bf16[8192,256]{1,0:T(8,128)(2,1)} %param.18, bf16[16,8192]{1,0:T(8,128)(2,1)S(1)} %all_gather.36, f32[8192]{0:T(1024)} %param.17, f32[16]{0:T(128)S(1)} %add_rsqrt_fusion.1), kind=kOutput, calls=%fused_computation.108 | convolution fusion | flops 67633152 | bytes 4505664 | tf_op jit(solution)/shard_map/dot_general | solution.py:90
  35.9 0.1 fusion.76
  36.1 0.1 fusion.50
  36.2 0.1 copy.106
  36.4 20.5 %all_gather.37 = bf16[16,4096]{0,1:T(8,128)(2,1)S(1)} all-gather(bf16[16,256]{0,1:T(8,128)(2,1)S(1)} %bitcast.138), channel_id=1, replica_groups=mesh['groups'=2,'ctx'=16] {'ctx'}, dimensions={1}, use_global_device_ids=true | all-gather | bytes 139264 | tf_op jit(solution)/shard_map/all_gather | solution.py:103
  56.9 0.3 copy.108
  57.2 0.7 bitcast_reduce_fusion
  57.9 1.3 copy-done.2
  59.3 1.7 convolution_bitcast_fusion
  61.0 0.4 copy.137
  61.5 1.5 fusion.69
  63.2 0.1 fusion.46
  63.4 0.1 copy.124
  63.5 0.1 copy.125
  63.5 19.9 %all-gather.3 = bf16[16,32,16]{1,2,0:T(8,128)(2,1)S(1)} all-gather(bf16[1,32,16]{1,2,0:T(8,128)(2,1)S(1)} %copy.125), channel_id=1, replica_groups=mesh['groups'=2,'ctx'=16] {'ctx'}, dimensions={0}, use_global_device_ids=true | all-gather | bytes 17408 | tf_op jit(solution)/shard_map/all_gather | solution.py:104
  83.5 0.1 reshape.338
  83.6 0.3 fusion.11
  83.9 18.2 %all-gather.4 = bf16[16,32,16]{1,2,0:T(8,128)(2,1)S(1)} all-gather(bf16[1,32,16]{1,2,0:T(8,128)(2,1)S(1)} %fusion.11), channel_id=1, replica_groups=mesh['groups'=2,'ctx'=16] {'ctx'}, dimensions={0}, use_global_device_ids=true | all-gather | bytes 17408 | tf_op jit(solution)/shard_map/all_gather | solution.py:105
  102.2 0.1 reshape.341
  102.3 0.2 fusion.78
  102.5 0.1 copy.136
  102.6 0.8 fusion.7
  103.4 20.9 %all-gather.1 = f32[256,4,8]{2,1,0:T(4,128)S(1)} all-gather(f32[16,4,8]{2,1,0:T(4,128)S(1)} %copy.111), channel_id=3, replica_groups=mesh['groups'=2,'ctx'=16] {'ctx'}, dimensions={0}, use_global_device_ids=true | all-gather | bytes 34816 | tf_op jit(solution)/shard_map/all_gather | solution.py:14
  124.4 0.2 copy.119
  124.6 18.9 %all-gather = f32[256,4,8]{2,1,0:T(4,128)S(1)} all-gather(f32[16,4,8]{2,1,0:T(4,128)S(1)} %copy.110), channel_id=2, replica_groups=mesh['groups'=2,'ctx'=16] {'ctx'}, dimensions={0}, use_global_device_ids=true | all-gather | bytes 34816 | tf_op jit(solution)/shard_map/all_gather | solution.py:14
  143.6 0.2 copy.118
  143.8 1.0 slice.26
  144.8 21.4 %while.19 = (s32[]{:T(128)}, f32[16,4,8]{0,2,1:T(8,128)S(1)}, f32[16,4,8]{0,2,1:T(8,128)S(1)}, f32[16,4,8,128]{3,2,1,0:T(8,128)S(1)}, f32[16,16,4,8]{1,3,2,0:T(8...) while((s32[]{:T(128)}, f32[16,4,8]{0,2,1:T(8,128)S(1)}, ...), condition=%wide.region_5.6_spmd, body=%wide.region_4.5_spmd.sunk | while | flops 199685 | bytes 815247 | solution.py:19
  145.0 1.2 fusion.93
  146.4 1.2 fusion.93
  147.9 1.2 fusion.93
  149.3 1.2 fusion.93
  150.6 0.1 copy.182
  150.7 1.2 fusion.93
  152.0 0.1 copy.182
  152.2 1.2 fusion.93
  153.4 0.1 copy.182
  153.6 1.2 fusion.93
  154.9 0.1 copy.182
  155.0 1.2 fusion.93
  156.3 0.1 copy.182
  156.4 1.2 fusion.93
  157.9 1.2 fusion.93
  159.3 1.2 fusion.93
  160.7 1.2 fusion.93
  162.2 1.2 fusion.93
  163.6 1.2 fusion.93
  165.0 1.2 fusion.93
  166.5 0.1 broadcast_in_dim.74
  166.6 0.1 broadcast_in_dim.73
  166.8 0.1 broadcast_in_dim.76
  166.9 3.8 %fusion.10 = bf16[16,512]{1,0:T(8,128)(2,1)S(1)} fusion(bf16[4096,512]{1,0:T(8,128)(2,1)} %param.23, f32[2,8,32,128]{3,2,1,0:T(8,128)S(1)} %bitcast.135, f32[2,8,32,128]{3,2,1,0:T(8,128)S(1)} %bitcast.132, f32[2,8,32,128]{3,2,1,0:T(8,128)S(1)} %bitcast.133, f32[2,8,32,128]{3,2,1,0:T(8,128)S(1)} %bitcast.134, f32[2,8,32,128]{3,2,1,0:T(8,128)S(1)} %bitcast.127, ...), kind=kOutput, calls=%fused_computation.23 | convolution fusion | flops 67461120 | bytes 5537792 | tf_op jit(solution)/shard_map/dot_general | solution.py:162
  170.7 19.6 %all_gather.46 = bf16[16,8192]{1,0:T(8,128)(2,1)S(1)} all-gather(bf16[16,512]{1,0:T(8,128)(2,1)S(1)} %fusion.10), channel_id=1, replica_groups=mesh['groups'=2,'ctx'=16] {'ctx'}, dimensions={1}, use_global_device_ids=true | all-gather | bytes 278528 | tf_op jit(solution)/shard_map/all_gather | solution.py:164
  190.3 0.2 fusion.25
  190.6 7.4 %fusion.32 = f32[16,896]{1,0:T(8,128)S(1)} fusion(bf16[8192,896]{1,0:T(8,128)(2,1)} %param.25, bf16[16,8192]{1,0:T(8,128)(2,1)S(1)} %all_gather.46, f32[8192]{0:T(1024)S(1)} %copy-done.4, f32[16]{0:T(128)S(1)} %add_rsqrt_fusion), kind=kOutput, calls=%fused_computation.50 | convolution fusion | flops 235405312 | bytes 15032384 | tf_op jit(solution)/shard_map/dot_general | solution.py:166
  198.0 0.2 slice-done.2
  198.2 0.6 slice-done.3
  198.8 2.0 fusion.8
  200.8 18.8 %all_gather.47 = bf16[16,14336]{1,0:T(8,128)(2,1)S(1)} all-gather(bf16[16,896]{1,0:T(8,128)(2,1)S(1)} %fusion.8), channel_id=1, replica_groups=mesh['groups'=2,'ctx'=16] {'ctx'}, dimensions={1}, use_global_device_ids=true | all-gather | bytes 487424 | tf_op jit(solution)/shard_map/all_gather | solution.py:170
  219.7 2.6 %fusion.9 = bf16[16,512]{1,0:T(8,128)(2,1)} fusion(bf16[16,14336]{1,0:T(8,128)(2,1)S(1)} %all_gather.47, bf16[14336,512]{1,0:T(8,128)(2,1)S(1)} %bitcast.126, bf16[16,512]{1,0:T(8,128)(2,1)S(1)} %fusion.10), kind=kOutput, calls=%fused_computation.22 | convolution fusion | flops 234905600 | bytes 15171584 | tf_op jit(solution)/shard_map/dot_general | solution.py:169
  (105 shorter events, 3.3 us)
Async XLA Ops:
  6.5 50.7 %copy-start = (bf16[1024,4,128]{2,1,0:T(4,128)(2,1)S(1)}, bf16[1024,4,128]{2,1,0:T(4,128)(2,1)}, u32[]{:S(2)}) copy-start(bf16[1024,4,128]{2,1,0:T(4,128)(2,1)} %param.21) | copy-start | bytes 3145732
  6.5 137.3 %all-gather.7.cloned.1.call-start = ((), (), s32[]{:S(2)}) async-start(), calls=%async_computation | async-start | bytes 4456448 | tf_op jit(solution)/shard_map/all_gather | solution.py:14
  57.2 2.0 copy-start.8
  57.9 1.4 copy-start.2
  59.3 2.2 copy-start.6
  61.0 22.6 %copy-start.5 = (bf16[8192,32]{0,1:T(8,128)(2,1)S(1)}, bf16[8192,32]{0,1:T(8,128)(2,1)}, u32[]{:S(2)}) copy-start(bf16[8192,32]{0,1:T(8,128)(2,1)} %param.20) | copy-start | bytes 1572868
  61.5 41.1 %copy-start.3 = (f32[4,16,8,1024]{3,2,1,0:T(8,128)S(1)}, f32[4,16,8,1024]{3,2,1,0:T(8,128)}, u32[]{:S(2)}) copy-start(f32[4,16,8,1024]{3,2,1,0:T(8,128)} %copy-done.2) | copy-start | bytes 6291460
  144.8 22.1 %copy-start.7 = (bf16[16,512]{1,0:T(8,128)(2,1)S(1)}, bf16[16,512]{1,0:T(8,128)(2,1)}, u32[]{:S(2)}) copy-start(bf16[16,512]{1,0:T(8,128)(2,1)} %param.16) | copy-start | bytes 49156
  166.9 23.6 %copy-start.4 = (f32[8192]{0:T(1024)S(1)}, f32[8192]{0:T(1024)}, u32[]{:S(2)}) copy-start(f32[8192]{0:T(1024)} %param.24) | copy-start | bytes 98308
  166.9 31.0 %slice-start = ((s8[14680064]{0:T(1024)(128)(4,1)}), s8[4194304]{0:T(1024)(128)(4,1)S(1)}, s32[]{:S(2)}) async-start(s8[14680064]{0:T(1024)(128)(4,1)} %bitcast.123), calls=%async_computation.1 | async-start | bytes 8388608
  190.6 7.4 %slice-start.1 = ((s8[14680064]{0:T(1024)(128)(4,1)}), s8[4194304]{0:T(1024)(128)(4,1)S(1)}, s32[]{:S(2)}) async-start(s8[14680064]{0:T(1024)(128)(4,1)} %bitcast.123), calls=%async_computation.2 | async-start | bytes 8388608
  190.6 7.6 %slice-start.2 = ((s8[14680064]{0:T(1024)(128)(4,1)}), s8[4194304]{0:T(1024)(128)(4,1)S(1)}, s32[]{:S(2)}) async-start(s8[14680064]{0:T(1024)(128)(4,1)} %bitcast.123), calls=%async_computation.3 | async-start | bytes 8388608
  190.6 8.2 %slice-start.3 = ((s8[14680064]{0:T(1024)(128)(4,1)}), s8[2097152]{0:T(1024)(128)(4,1)S(1)}, s32[]{:S(2)}) async-start(s8[14680064]{0:T(1024)(128)(4,1)} %bitcast.123), calls=%async_computation.4 | async-start | bytes 4194304
  190.6 29.1 %slice-start.4 = ((s8[14680064]{0:T(1024)(128)(4,1)}), s8[4194304]{0:T(1024)(128)(4,1)S(1)}, s32[]{:S(2)}) async-start(s8[14680064]{0:T(1024)(128)(4,1)} %bitcast.125), calls=%async_computation.5 | async-start | bytes 8388608
  190.6 29.1 %slice-start.5 = ((s8[14680064]{0:T(1024)(128)(4,1)}), s8[4194304]{0:T(1024)(128)(4,1)S(1)}, s32[]{:S(2)}) async-start(s8[14680064]{0:T(1024)(128)(4,1)} %bitcast.125), calls=%async_computation.6 | async-start | bytes 8388608
  198.8 20.9 %slice-start.6 = ((s8[14680064]{0:T(1024)(128)(4,1)}), s8[4194304]{0:T(1024)(128)(4,1)S(1)}, s32[]{:S(2)}) async-start(s8[14680064]{0:T(1024)(128)(4,1)} %bitcast.125), calls=%async_computation.7 | async-start | bytes 8388608
  198.8 20.9 %slice-start.7 = ((s8[14680064]{0:T(1024)(128)(4,1)}), s8[2097152]{0:T(1024)(128)(4,1)S(1)}, s32[]{:S(2)}) async-start(s8[14680064]{0:T(1024)(128)(4,1)} %bitcast.125), calls=%async_computation.8 | async-start | bytes 4194304
  219.7 2.6 %copy-start.1 = (bf16[1024,4,128]{2,1,0:T(4,128)(2,1)S(1)}, bf16[1024,4,128]{2,1,0:T(4,128)(2,1)}, u32[]{:S(2)}) copy-start(bf16[1024,4,128]{2,1,0:T(4,128)(2,1)} %param.21) | copy-start | bytes 3145732
Sparse Core Ops, SparseCore 0:
  61.2 51.4 all-gather.6
where the time goes:
time: 230 us; the launch traced here: 229 us
  blocking collectives  161 us (70%)
  matrix products  24.2 us (11%)
  other arithmetic  21.2 us (9%)
  between operations  13.7 us (6%)
  local copies, waits for them, and re-layouts  8.55 us (4%)
    all_gather x2, blocking collectives, joined(): gathered = jax.tree.map(lambda a: lax.all_gather(a, axis), part)  39.8 us
    all_gather x1, blocking collectives, shards(): full_rows = lax.all_gather(hidden_in, 'ctx', axis=1, tiled=True)  24.1 us
    all_gather x1, blocking collectives, shards(): lax.all_gather(query_part, 'ctx', axis=1, tiled=True)  20.5 us
    all_gather x1, blocking collectives, shards(): lax.all_gather(key_part, 'ctx', axis=1, tiled=True)  19.9 us
    all_gather x1, blocking collectives, shards(): mid_full = lax.all_gather(mid_part, 'ctx', axis=1, tiled=True)  19.6 us
    all_gather x1, blocking collectives, shards(): lax.all_gather(hidden, 'ctx', axis=1, tiled=True)  18.8 us
    all_gather x1, blocking collectives, shards(): lax.all_gather(value_part, 'ctx', axis=1, tiled=True)  18.2 us
    add x15, other arithmetic, combine_parts(): accum_first * share_first[..., None]  18.2 us
  transfers between devices with their start and end apart: 1, of which 0 were waited for; matrix products, arithmetic and copies ran while one was open for 2% of the time, Pallas kernels for 0%

commit v1 on v0

v1 whole, which is shorter than its diff:
```python
import math

import jax
import jax.numpy as jnp
from jax import lax
from jax.experimental import pallas as pl
from jax.experimental.pallas import tpu as pltpu
from jax.sharding import PartitionSpec as P

NORM_EPSILON = 1e-05
ROPE_BASE = 500000.0
MASKED = -1e30


LANES = 128
VMEM = pl.BlockSpec(memory_space=pltpu.VMEM)


def exchange(blocks):
    return lax.all_to_all(blocks, "ctx", 0, 0)


def call(body, name, out_shape, args, scratch=(), flops=0):
    moved = sum(a.size * a.dtype.itemsize for a in args)
    return pl.pallas_call(
        body,
        out_shape=out_shape,
        in_specs=[VMEM] * len(args),
        out_specs=jax.tree.map(lambda _: VMEM, out_shape),
        scratch_shapes=list(scratch),
        compiler_params=pltpu.CompilerParams(vmem_limit_bytes=6 << 20),
        cost_estimate=pl.CostEstimate(flops=flops, bytes_accessed=moved, transcendentals=0),
        name=name,
    )(*args)


def norm_factor(blocks_ref):
    devices, rows, width = blocks_ref.shape

    def add(index, total):
        wide = blocks_ref[index].astype(jnp.float32)
        return total + wide * wide

    total = lax.fori_loop(0, devices, add, jnp.zeros((rows, width), jnp.float32), unroll=4)
    mean = jnp.sum(total, axis=1, keepdims=True) / (devices * width)
    return lax.rsqrt(mean + NORM_EPSILON)


def normed_block(blocks_ref, gain_ref, factor, index):
    wide = blocks_ref[index].astype(jnp.float32)
    return (wide * factor * gain_ref[index]).astype(jnp.bfloat16)


def products(devices, depth, block_of, weight_refs, total_refs):
    for total_ref in total_refs:
        total_ref[...] = jnp.zeros_like(total_ref)

    def step(index, carry):
        block = block_of(index)
        span = pl.ds(pl.multiple_of(index * depth, depth), depth)
        for weight_ref, total_ref in zip(weight_refs, total_refs):
            total_ref[...] += jnp.dot(
                block, weight_ref[span, :], preferred_element_type=jnp.float32
            )
        return carry

    lax.fori_loop(0, devices, step, 0, unroll=4)


def project_kernel(
    blocks_ref, gain_ref, query_ref, key_ref, value_ref, cos_ref, sin_ref, out_ref,
    query_total, key_total, value_total, joined,
):
    devices, _, depth = blocks_ref.shape
    factor = norm_factor(blocks_ref)
    products(
        devices, depth,
        lambda index: normed_block(blocks_ref, gain_ref, factor, index),
        (query_ref, key_ref, value_ref),
        (query_total, key_total, value_total),
    )
    query_width = query_total.shape[1]
    key_width = key_total.shape[1]
    used = query_width + 2 * key_width
    joined[...] = jnp.zeros_like(joined)
    joined[:, :query_width] = query_total[...]
    joined[:, query_width : query_width + key_width] = key_total[...]
    joined[:, query_width + key_width : used] = value_total[...]
    columns = joined[...]
    width = columns.shape[1]
    lane = lax.broadcasted_iota(jnp.int32, columns.shape, 1)
    partner = jnp.where(
        lane % 2 == 1, pltpu.roll(columns, 1, 1), -pltpu.roll(columns, width - 1, 1)
    )
    turned = columns * cos_ref[...] + partner * sin_ref[...]
    sent = turned.astype(jnp.bfloat16)[:, :used]

    def put(index, carry):
        out_ref[index] = sent
        return carry

    lax.fori_loop(0, devices, put, 0, unroll=4)


def attend_kernel(scale, query_ref, key_ref, value_ref, limit_ref, out_ref):
    heads, rows, head_dim = query_ref.shape
    span = key_ref.shape[0]
    value_heads = key_ref.shape[1] // head_dim
    group = heads // value_heads
    devices = out_ref.shape[0]
    pairs = heads * rows // devices
    place = lax.broadcasted_iota(jnp.int32, (rows, span), 1)
    visible = (place < limit_ref[...])[None]
    for g in range(value_heads):
        lanes = pl.ds(g * head_dim, head_dim)
        queries = query_ref[g * group : (g + 1) * group].reshape(group * rows, head_dim)
        logits = lax.dot_general(
            queries, key_ref[:, lanes], (((1,), (1,)), ((), ())),
            preferred_element_type=jnp.float32,
        ) * scale
        masked = jnp.where(visible, logits.reshape(group, rows, span), MASKED)
        top = jnp.max(masked, axis=2, keepdims=True)
        weights = jnp.where(visible, jnp.exp(masked - top), 0.0)
        total = jnp.sum(weights, axis=2, keepdims=True).reshape(group * rows, 1)
        top = top.reshape(group * rows, 1)
        summed = jnp.dot(
            weights.astype(jnp.bfloat16).reshape(group * rows, span), value_ref[:, lanes],
            preferred_element_type=jnp.float32,
        )
        seen = total > 0.0
        safe = jnp.where(seen, total, 1.0)
        means = (summed / safe).astype(jnp.bfloat16)
        level = jnp.where(seen, top + jnp.log(safe), MASKED)
        across = jnp.transpose(jnp.broadcast_to(level, (group * rows, LANES)))[:8]
        for first in range(0, group * rows, LANES):
            line = across[:, first : first + LANES]
            high = line.astype(jnp.bfloat16)
            rest = line - high.astype(jnp.float32)
            middle = rest.astype(jnp.bfloat16)
            low = (rest - middle.astype(jnp.float32)).astype(jnp.bfloat16)
            row = lax.broadcasted_iota(jnp.int32, line.shape, 0)
            terms = jnp.where(
                row == 0,
                high.astype(jnp.float32),
                jnp.where(row == 1, middle.astype(jnp.float32), low.astype(jnp.float32)),
            ).astype(jnp.bfloat16)
            for begin in range(0, LANES, pairs):
                index = (g * group * rows + first + begin) // pairs
                out_ref[index, :pairs] = means[first + begin : first + begin + pairs]
                out_ref[index, pairs:] = terms


def output_kernel(blocks_ref, weight_ref, residual_ref, mid_ref, out_ref, total):
    heads, rows, head_dim = blocks_ref.shape
    devices = out_ref.shape[0]

    def block_of(index):
        return jnp.concatenate([blocks_ref[2 * index], blocks_ref[2 * index + 1]], axis=1)

    products(heads // 2, 2 * head_dim, block_of, (weight_ref,), (total,))
    mid = (residual_ref[...].astype(jnp.float32) + total[...]).astype(jnp.bfloat16)
    mid_ref[...] = mid

    def put(index, carry):
        out_ref[index] = mid
        return carry

    lax.fori_loop(0, devices, put, 0, unroll=4)


def gated_kernel(blocks_ref, gain_ref, gate_ref, up_ref, out_ref, gate_total, up_total):
    devices, _, depth = blocks_ref.shape
    factor = norm_factor(blocks_ref)
    products(
        devices, depth,
        lambda index: normed_block(blocks_ref, gain_ref, factor, index),
        (gate_ref, up_ref),
        (gate_total, up_total),
    )
    gate = gate_total[...]
    hidden = (gate / (1.0 + jnp.exp(-gate)) * up_total[...]).astype(jnp.bfloat16)

    def put(index, carry):
        out_ref[index] = hidden
        return carry

    lax.fori_loop(0, devices, put, 0, unroll=4)


def down_kernel(blocks_ref, weight_ref, residual_ref, out_ref, total):
    devices, _, depth = blocks_ref.shape
    products(devices, depth, lambda index: blocks_ref[index], (weight_ref,), (total,))
    out_ref[...] = (residual_ref[...].astype(jnp.float32) + total[...]).astype(jnp.bfloat16)


def rotation(first_col, width, positions, head_dim):
    col = jnp.arange(width, dtype=jnp.int32)
    in_head = ((first_col + col - col % 2) % head_dim).astype(jnp.float32)
    frequency = jnp.exp(-(in_head / head_dim) * jnp.log(jnp.float32(ROPE_BASE)))
    angles = positions.astype(jnp.float32)[:, None] * frequency[None, :]
    return jnp.cos(angles), jnp.sin(angles)


def shards(
    hidden_in,
    attn_gain,
    w_query,
    w_key,
    w_value,
    rotated_prefix_keys,
    cache_values,
    w_out,
    ffn_gain,
    w_gate,
    w_up,
    w_down,
    doc_offsets,
    slot_request,
):
    devices = lax.axis_size("ctx")
    device = lax.axis_index("ctx")
    rows, width = hidden_in.shape
    span, value_heads, head_dim = rotated_prefix_keys.shape
    query_width = w_query.shape[1]
    key_width = w_key.shape[1]
    heads = query_width * devices // head_dim
    group = heads // value_heads
    scale = 1.0 / math.sqrt(head_dim)
    slot_index = jnp.arange(rows, dtype=jnp.int32)
    positions = jnp.sum(
        jnp.where(slot_request[:, None] == slot_index[None, :], doc_offsets[None, :], 0), axis=1
    )

    def buffer(*shape, dtype=jnp.bfloat16):
        return jax.ShapeDtypeStruct(shape, dtype)

    def totals(*widths):
        return [pltpu.VMEM((rows, w), jnp.float32) for w in widths]

    used = query_width + 2 * key_width
    padded = -(-used // LANES) * LANES
    query_cos, query_sin = rotation(device * query_width, query_width, positions, head_dim)
    key_cos, key_sin = rotation(device * key_width, key_width, positions, head_dim)
    still = jnp.ones((rows, padded - query_width - key_width), jnp.float32)
    cosine = jnp.concatenate([query_cos, key_cos, still], axis=1)
    sine = jnp.concatenate([query_sin, key_sin, still * 0.0], axis=1)
    full = exchange(jnp.broadcast_to(hidden_in[None], (devices, rows, width)))
    packed = exchange(
        call(
            project_kernel, "project", buffer(devices, rows, used),
            (full, attn_gain.reshape(devices, 1, width), w_query, w_key, w_value, cosine, sine),
            totals(query_width, key_width, key_width, padded),
            2 * rows * devices * width * used,
        )
    )

    def unpacked(first, part_width):
        part = packed[:, :, first : first + part_width]
        if part_width >= head_dim:
            split = part.reshape(devices, rows, part_width // head_dim, head_dim)
            return split.transpose(0, 2, 1, 3).reshape(-1, rows, head_dim)
        run = head_dim // part_width
        return part.reshape(-1, run, rows, part_width).transpose(0, 2, 1, 3).reshape(
            -1, rows, head_dim
        )

    queries = unpacked(0, query_width)
    key_new = unpacked(query_width, key_width)
    value_new = unpacked(query_width + key_width, key_width)
    pairs = heads * rows // devices
    limit = (positions - device * span)[:, None]
    sent = call(
        lambda *refs: attend_kernel(scale, *refs), "attend", buffer(devices, pairs + 8, LANES),
        (
            queries,
            rotated_prefix_keys.reshape(span, value_heads * head_dim),
            cache_values.reshape(span, value_heads * head_dim),
            limit,
        ),
        (),
        4 * heads * rows * span * head_dim,
    )
    got = exchange(sent)
    first_pair = device * pairs
    means = got[:, :pairs].astype(jnp.float32)
    terms = lax.dynamic_slice_in_dim(
        got[:, pairs : pairs + 3].astype(jnp.float32), first_pair % LANES, pairs, 2
    )
    levels = terms[:, 0] + terms[:, 1] + terms[:, 2]

    def mine(every):
        return lax.dynamic_slice_in_dim(
            every.reshape(heads * rows, head_dim), first_pair, pairs, 0
        ).astype(jnp.float32)

    def spread(new):
        return jnp.broadcast_to(new[:, None], (value_heads, group, rows, head_dim))

    own_score = jnp.sum(mine(queries) * mine(spread(key_new)), axis=1) * scale
    own_value = mine(spread(value_new))
    peak = jnp.maximum(jnp.max(levels, axis=0), own_score)
    shares = jnp.exp(levels - peak[None, :])
    own_share = jnp.exp(own_score - peak)
    numerator = jnp.sum(shares[..., None] * means, axis=0) + own_share[:, None] * own_value
    denominator = jnp.sum(shares, axis=0) + own_share
    attn_part = (numerator / denominator[:, None]).astype(jnp.bfloat16)
    attn_all = exchange(jnp.broadcast_to(attn_part[None], (devices, pairs, head_dim)))
    mid_part, mid_sent = call(
        output_kernel, "output", (buffer(rows, width), buffer(devices, rows, width)),
        (attn_all.reshape(heads, rows, head_dim), w_out, hidden_in),
        totals(width),
        2 * rows * heads * head_dim * width,
    )
    hidden_width = w_gate.shape[1]
    hidden_sent = call(
        gated_kernel, "gated", buffer(devices, rows, hidden_width),
        (exchange(mid_sent), ffn_gain.reshape(devices, 1, width), w_gate, w_up),
        totals(hidden_width, hidden_width),
        4 * rows * devices * width * hidden_width,
    )
    return call(
        down_kernel, "down", buffer(rows, width),
        (exchange(hidden_sent), w_down, mid_part),
        totals(width),
        2 * rows * devices * hidden_width * width,
    )


def solution(mesh):
    return jax.shard_map(
        shards,
        mesh=mesh,
        in_specs=(
            P("groups", "ctx"),
            P(),
            P(None, "ctx"),
            P(None, "ctx"),
            P(None, "ctx"),
            P(("groups", "ctx"), None, None),
            P(("groups", "ctx"), None, None),
            P(None, "ctx"),
            P(),
            P(None, "ctx"),
            P(None, "ctx"),
            P(None, "ctx"),
            P("groups"),
            P("groups"),
        ),
        out_specs=P("groups", "ctx"),
        check_vma=False,
    )
```

time: 230 us -> 113 us (0.49)
  blocking collectives: 161 us -> 39 us
  matrix products: 24.2 us -> 0 us
  other arithmetic: 21.2 us -> 1.68 us
  waiting for transfers between devices: 0.03 us -> 18.8 us
  local copies, waits for them, and re-layouts: 8.55 us -> 25 us
  starting transfers between devices: 0.01 us -> 14.5 us
  between operations: 13.7 us -> 0.23 us
  Pallas kernels: 0 us -> 13.4 us
    all_gather x8 -> x0, blocking collectives: 161 us -> none  [the longest x2 39.8 us: joined(): gathered = jax.tree.map(lambda a: lax.all_gather(a, axis), part)]
    all_to_all x0 -> x3, blocking collectives: none -> 39 us  [exchange(): return lax.all_to_all(blocks, 'ctx', 0, 0)]
    dot_general x10 -> x0, matrix products: 24.2 us -> none  [the longest x1 7.36 us: shards(): gate_act = jnp.dot(normed_mid, w_gate, preferred_element_type=jnp.float32)]
    all_to_all x0 -> x3, waiting for transfers between devices: none -> 18.8 us  [exchange(): return lax.all_to_all(blocks, 'ctx', 0, 0)]
    add x32 -> x1, other arithmetic: 18.6 us -> 0.01 us  [shards(): denominator = jnp.sum(shares, axis=0) + own_share]
    unnamed x40 -> x26, local copies, waits for them, and re-layouts: 2.69 us -> 20.9 us
    all_to_all x0 -> x3, starting transfers between devices: none -> 14.5 us  [exchange(): return lax.all_to_all(blocks, 'ctx', 0, 0)]
    pallas_call x0 -> x5, Pallas kernels: none -> 13.4 us  [call(): pl.pallas_call(body, out_shape=out_shape, in_specs=[VMEM] * len(args), ou...]
  transfers between devices with their start and end apart: 1 -> 3, of which waited for: 0 -> 3; matrix products, arithmetic and copies ran while one was open for 2% -> 7% of each run, Pallas kernels for 0% -> 0%
where the time goes in v1:
time: 113 us
  blocking collectives  39 us (35%)
  local copies, waits for them, and re-layouts  25 us (22%)
  waiting for transfers between devices  18.8 us (17%)
  starting transfers between devices  14.5 us (13%)
  Pallas kernels  13.4 us (12%)
  other arithmetic  1.68 us (1%)
    all_to_all x3, blocking collectives, exchange(): return lax.all_to_all(blocks, 'ctx', 0, 0)  39 us
    unnamed x26, local copies, waits for them, and re-layouts  20.9 us
    all_to_all x3, waiting for transfers between devices, exchange(): return lax.all_to_all(blocks, 'ctx', 0, 0)  18.8 us
    all_to_all x3, starting transfers between devices, exchange(): return lax.all_to_all(blocks, 'ctx', 0, 0)  14.5 us
    pallas_call x5, Pallas kernels, call(): pl.pallas_call(body, out_shape=out_shape, in_specs=[VMEM] * len(args), ou...  13.4 us
  transfers between devices with their start and end apart: 3, of which 3 were waited for; matrix products, arithmetic and copies ran while one was open for 7% of the time, Pallas kernels for 0%

profile of v1, /device:TPU:0, one launch (start us, length us, event | category | flops | bytes accessed | tf_op | source)
XLA Modules:
  0.0 112.6 jit_solution(14072220286838936345)
XLA Ops:
  0.0 0.0 copy-start.6
  0.0 1.5 %broadcast_in_dim.26 = bf16[16,16,512]{2,1,0:T(8,128)(2,1)} broadcast(bf16[16,512]{1,0:T(8,128)(2,1)} %residual_ref.1), dimensions={1,2} | broadcast | bytes 278528 | tf_op jit(solution)/shard_map/broadcast_in_dim | solution.py:247
  1.5 7.4 %all-to-all-start = ((bf16[16,16,512]{2,1,0:T(8,128)(2,1)}), bf16[16,16,512]{2,1,0:T(8,128)(2,1)S(1)}, u32[]{:S(2)}, u32[]{:S(2)}) async-start(bf16[16,16,512]{2,1,0:T(8,128)(2,1)} %broadcast_in_dim.26), calls=%async_computation | async-start | bytes 524288 | tf_op jit(solution)/shard_map/all_to_all | solution.py:20
  8.9 0.9 select_reduce_fusion
  9.8 0.1 multiply_sine_fusion.1
  9.9 1.9 %copy.25.key_ref = bf16[8192,32]{1,0:T(8,128)(2,1)S(1)} copy(bf16[8192,32]{0,1:T(8,128)(2,1)} %param.17) | data formatting | bytes 1048576 | tf_op args[3]
  11.9 2.7 %copy.26.value_ref = bf16[8192,32]{1,0:T(8,128)(2,1)} copy(bf16[8192,32]{0,1:T(8,128)(2,1)} %param.18) | data formatting | bytes 1048576 | tf_op args[4]
  14.5 0.1 pad.5.clone
  14.6 0.1 pad.2.clone
  14.7 0.1 copy.28.refs_3_
  14.8 0.1 multiply_sine_fusion
  14.9 4.0 %all-to-all-done.blocks_ref = bf16[16,16,512]{2,1,0:T(8,128)(2,1)S(1)} async-done(((bf16[16,16,512]{2,1,0:T(8,128)(2,1)}), bf16[16,16,512]{2,1,0:T(8,128)(2,1)S(1)}, u32[]{:S(2)}, u32[]{:S(2)}) %all-to-all-start) | async-done | bytes 262176 | tf_op jit(solution)/shard_map/all_to_all | solution.py:20
  18.9 0.0 copy-done.6
  18.9 0.0 copy-start.2
  18.9 1.6 %copy-done.2 = bf16[8192,32]{1,0:T(8,128)(2,1)S(1)} copy-done((bf16[8192,32]{1,0:T(8,128)(2,1)S(1)}, bf16[8192,32]{1,0:T(8,128)(2,1)}, u32[]{:S(2)}) %copy-start.2) | copy-done | bytes 524312
  20.5 0.0 copy-start.3
  20.5 2.2 %copy-done.3 = bf16[8192,256]{1,0:T(8,128)(2,1)S(1)} copy-done((bf16[8192,256]{1,0:T(8,128)(2,1)S(1)}, bf16[8192,256]{1,0:T(8,128)(2,1)}, u32[]{:S(2)}) %copy-start.3) | copy-done | bytes 4194328
  22.7 2.6 %project.1 = bf16[16,16,320]{2,1,0:T(8,128)(2,1)} custom-call(bf16[16,16,512]{2,1,0:T(8,128)(2,1)S(1)} %all-to-all-done.blocks_ref, f32[16,1,512]{2,1,0:T(1,128)S(1)} %bitcast.37, bf16[8192,256]{1,0:T(8,128)(2,1)S(1)} %copy-done.3, bf16[8192,32]{1,0:T(8,128)(2,1)S(1)} %copy.25.key_ref, bf16[8192,32]{1,0:T(8,128)(2,1)S(1)} %copy-done.2, ...), custom_call_target="tpu_custom_call" | custom-call | flops 83886080 | bytes 5586944 | tf_op jit(solution)/shard_map/project/pallas_call | solution.py:25
  25.3 3.5 %all-to-all-start.1 = ((bf16[16,16,320]{2,1,0:T(8,128)(2,1)}), bf16[16,16,320]{2,1,0:T(8,128)(2,1)S(1)}, u32[]{:S(2)}, u32[]{:S(2)}) async-start(bf16[16,16,320]{2,1,0:T(8,128)(2,1)} %project.1), calls=%async_computation.1 | async-start | bytes 393216 | tf_op jit(solution)/shard_map/all_to_all | solution.py:20
  28.8 0.0 copy-start.5
  28.8 1.9 %copy_bitcast_fusion = (bf16[1024,512]{1,0:T(8,128)(2,1)S(1)}, bf16[1024,512]{1,0:T(8,128)(2,1)S(1)}) fusion(bf16[128,8,4,128]{3,2,1,0:T(4,128)(2,1)} %bitcast.39, bf16[128,8,4,128]{3,2,1,0:T(4,128)(2,1)} %bitcast.40), kind=kLoop, calls=%fused_computation | loop fusion | bytes 4194304 | tf_op jit(solution)/shard_map/reshape | solution.py:277
  30.7 7.0 %all-to-all-done.1 = bf16[16,16,320]{2,1,0:T(8,128)(2,1)S(1)} async-done(((bf16[16,16,320]{2,1,0:T(8,128)(2,1)}), bf16[16,16,320]{2,1,0:T(8,128)(2,1)S(1)}, u32[]{:S(2)}, u32[]{:S(2)}) %all-to-all-start.1) | async-done | bytes 163872 | tf_op jit(solution)/shard_map/all_to_all | solution.py:20
  37.7 0.0 copy-start.7
  37.7 2.3 %attend.1 = bf16[16,40,128]{2,1,0:T(8,128)(2,1)} custom-call(bf16[32,16,128]{2,1,0:T(8,128)(2,1)S(1)} %bitcast.34, bf16[1024,512]{1,0:T(8,128)(2,1)S(1)} %get-tuple-element.26.refs_1_, bf16[1024,512]{1,0:T(8,128)(2,1)S(1)} %get-tuple-element.25.refs_2_, s32[16,1]{1,0:T(8,128)S(1)} %copy.28.refs_3_), custom_call_target="tpu_custom_call" | custom-call | flops 268435456 | bytes 2228288 | tf_op jit(solution)/shard_map/attend/pallas_call | solution.py:25
  40.0 3.5 %all-to-all-start.2 = ((bf16[16,40,128]{2,1,0:T(8,128)(2,1)}), bf16[16,40,128]{2,1,0:T(8,128)(2,1)S(1)}, u32[]{:S(2)}, u32[]{:S(2)}) async-start(bf16[16,40,128]{2,1,0:T(8,128)(2,1)} %attend.1), calls=%async_computation.2 | async-start | bytes 327680 | tf_op jit(solution)/shard_map/all_to_all | solution.py:20
  43.6 0.1 fusion.17
  43.7 0.0 slice-start
  43.7 0.1 broadcast_in_dim.30
  43.9 0.1 broadcast_in_dim.32
  44.0 0.1 multiply_reduce_fusion.1
  44.1 7.8 %all-to-all-done.2 = bf16[16,40,128]{2,1,0:T(8,128)(2,1)S(1)} async-done(((bf16[16,40,128]{2,1,0:T(8,128)(2,1)}), bf16[16,40,128]{2,1,0:T(8,128)(2,1)S(1)}, u32[]{:S(2)}, u32[]{:S(2)}) %all-to-all-start.2) | async-done | bytes 163872 | tf_op jit(solution)/shard_map/all_to_all | solution.py:20
  52.0 0.1 dynamic-slice_convert_fusion
  52.1 0.1 multiply_reduce_fusion
  52.3 0.1 divide_convert_fusion
  52.4 10.5 %all_to_all.30 = bf16[16,32,128]{2,1,0:T(8,128)(2,1)S(1)} all-to-all(bf16[16,32,128]{2,1,0:T(8,128)(2,1)S(1)} %broadcast_in_dim.34), channel_id=1, replica_groups=mesh['groups'=2,'ctx'=16] {'ctx'}, dimensions={0} | all-to-all | bytes 262144 | tf_op jit(solution)/shard_map/all_to_all | solution.py:20
  62.9 0.0 copy-done.5
  62.9 0.0 copy-start.4
  62.9 2.2 %copy-done.4 = bf16[4096,512]{1,0:T(8,128)(2,1)S(1)} copy-done((bf16[4096,512]{1,0:T(8,128)(2,1)S(1)}, bf16[4096,512]{1,0:T(8,128)(2,1)}, u32[]{:S(2)}) %copy-start.4) | copy-done | bytes 4194328
  65.1 1.0 output.1
  66.2 12.6 %all_to_all.31.blocks_ref = bf16[16,16,512]{2,1,0:T(8,128)(2,1)S(1)} all-to-all(bf16[16,16,512]{2,1,0:T(8,128)(2,1)S(1)} %get-tuple-element.7), channel_id=1, replica_groups=mesh['groups'=2,'ctx'=16] {'ctx'}, dimensions={0} | all-to-all | bytes 524288 | tf_op jit(solution)/shard_map/all_to_all | solution.py:20
  78.8 0.0 copy-done.7
  78.8 0.0 copy-start
  78.8 5.2 %copy-done = bf16[8192,896]{1,0:T(8,128)(2,1)S(1)} copy-done((bf16[8192,896]{1,0:T(8,128)(2,1)S(1)}, bf16[8192,896]{1,0:T(8,128)(2,1)}, u32[]{:S(2)}) %copy-start) | copy-done | bytes 14680088
  84.0 0.0 copy-start.1
  84.0 5.2 %copy-done.1 = bf16[8192,896]{1,0:T(8,128)(2,1)S(1)} copy-done((bf16[8192,896]{1,0:T(8,128)(2,1)S(1)}, bf16[8192,896]{1,0:T(8,128)(2,1)}, u32[]{:S(2)}) %copy-start.1) | copy-done | bytes 14680088
  89.1 0.0 slice-start.1
  89.1 0.0 slice-start.2
  89.1 0.0 slice-start.3
  89.1 4.5 %gated.1 = bf16[16,16,896]{2,1,0:T(8,128)(2,1)S(1)} custom-call(bf16[16,16,512]{2,1,0:T(8,128)(2,1)S(1)} %all_to_all.31.blocks_ref, f32[16,1,512]{2,1,0:T(1,128)S(1)} %bitcast.38, bf16[8192,896]{1,0:T(8,128)(2,1)S(1)} %copy-done, bf16[8192,896]{1,0:T(8,128)(2,1)S(1)} %copy-done.1), custom_call_target="tpu_custom_call" | custom-call | flops 469762048 | bytes 29655040 | tf_op jit(solution)/shard_map/gated/pallas_call | solution.py:25
  93.6 15.9 %all_to_all.32.blocks_ref = bf16[16,16,896]{2,1,0:T(8,128)(2,1)S(1)} all-to-all(bf16[16,16,896]{2,1,0:T(8,128)(2,1)S(1)} %gated.1), channel_id=1, replica_groups=mesh['groups'=2,'ctx'=16] {'ctx'}, dimensions={0} | all-to-all | bytes 917504 | tf_op jit(solution)/shard_map/all_to_all | solution.py:20
  109.5 0.0 slice-done
  109.5 0.0 slice-done.1
  109.6 0.0 slice-done.2
  109.6 0.0 slice-done.3
  109.6 3.0 %down.1 = bf16[16,512]{1,0:T(8,128)(2,1)} custom-call(bf16[16,16,896]{2,1,0:T(8,128)(2,1)S(1)} %all_to_all.32.blocks_ref, bf16[14336,512]{1,0:T(8,128)(2,1)S(1)} %bitcast.33, bf16[16,512]{1,0:T(8,128)(2,1)S(1)} %get-tuple-element.8.residual_ref), custom_call_target="tpu_custom_call" | custom-call | flops 234881024 | bytes 15155200 | tf_op jit(solution)/shard_map/down/pallas_call | solution.py:25
  (18 shorter events, 0.3 us)
Async XLA Ops:
  0.0 18.9 %copy-start.6 = (f32[8192]{0:T(1024)S(1)}, f32[8192]{0:T(1024)}, u32[]{:S(2)}) copy-start(f32[8192]{0:T(1024)} %param.15) | copy-start | bytes 98308
  1.5 17.4 %all-to-all-start = ((bf16[16,16,512]{2,1,0:T(8,128)(2,1)}), bf16[16,16,512]{2,1,0:T(8,128)(2,1)S(1)}, u32[]{:S(2)}, u32[]{:S(2)}) async-start(bf16[16,16,512]{2,1,0:T(8,128)(2,1)} %broadcast_in_dim.26), calls=%async_computation | async-start | bytes 524288 | tf_op jit(solution)/shard_map/all_to_all | solution.py:20
  18.9 1.6 %copy-start.2 = (bf16[8192,32]{1,0:T(8,128)(2,1)S(1)}, bf16[8192,32]{1,0:T(8,128)(2,1)}, u32[]{:S(2)}) copy-start(bf16[8192,32]{1,0:T(8,128)(2,1)} %copy.26.value_ref) | copy-start | bytes 1572868
  20.5 2.2 %copy-start.3 = (bf16[8192,256]{1,0:T(8,128)(2,1)S(1)}, bf16[8192,256]{1,0:T(8,128)(2,1)}, u32[]{:S(2)}) copy-start(bf16[8192,256]{1,0:T(8,128)(2,1)} %query_ref.1) | copy-start | bytes 12582916
  25.3 12.5 %all-to-all-start.1 = ((bf16[16,16,320]{2,1,0:T(8,128)(2,1)}), bf16[16,16,320]{2,1,0:T(8,128)(2,1)S(1)}, u32[]{:S(2)}, u32[]{:S(2)}) async-start(bf16[16,16,320]{2,1,0:T(8,128)(2,1)} %project.1), calls=%async_computation.1 | async-start | bytes 393216 | tf_op jit(solution)/shard_map/all_to_all | solution.py:20
  28.8 34.1 %copy-start.5 = (bf16[16,512]{1,0:T(8,128)(2,1)S(1)}, bf16[16,512]{1,0:T(8,128)(2,1)}, u32[]{:S(2)}) copy-start(bf16[16,512]{1,0:T(8,128)(2,1)} %residual_ref.1) | copy-start | bytes 49156
  37.7 41.0 %copy-start.7 = (f32[8192]{0:T(1024)S(1)}, f32[8192]{0:T(1024)}, u32[]{:S(2)}) copy-start(f32[8192]{0:T(1024)} %param.22) | copy-start | bytes 98308
  40.0 11.9 %all-to-all-start.2 = ((bf16[16,40,128]{2,1,0:T(8,128)(2,1)}), bf16[16,40,128]{2,1,0:T(8,128)(2,1)S(1)}, u32[]{:S(2)}, u32[]{:S(2)}) async-start(bf16[16,40,128]{2,1,0:T(8,128)(2,1)} %attend.1), calls=%async_computation.2 | async-start | bytes 327680 | tf_op jit(solution)/shard_map/all_to_all | solution.py:20
  43.7 65.8 %slice-start = ((s8[14680064]{0:T(1024)(128)(4,1)}), s8[2097152]{0:T(1024)(128)(4,1)S(1)}, s32[]{:S(2)}) async-start(s8[14680064]{0:T(1024)(128)(4,1)} %bitcast.32), calls=%async_computation.6 | async-start | bytes 4194304
  62.9 2.2 %copy-start.4 = (bf16[4096,512]{1,0:T(8,128)(2,1)S(1)}, bf16[4096,512]{1,0:T(8,128)(2,1)}, u32[]{:S(2)}) copy-start(bf16[4096,512]{1,0:T(8,128)(2,1)} %weight_ref.2) | copy-start | bytes 12582916
  78.8 5.2 %copy-start = (bf16[8192,896]{1,0:T(8,128)(2,1)S(1)}, bf16[8192,896]{1,0:T(8,128)(2,1)}, u32[]{:S(2)}) copy-start(bf16[8192,896]{1,0:T(8,128)(2,1)} %gate_ref.1) | copy-start | bytes 44040196
  84.0 5.2 %copy-start.1 = (bf16[8192,896]{1,0:T(8,128)(2,1)S(1)}, bf16[8192,896]{1,0:T(8,128)(2,1)}, u32[]{:S(2)}) copy-start(bf16[8192,896]{1,0:T(8,128)(2,1)} %up_ref.1) | copy-start | bytes 44040196
  89.1 20.4 %slice-start.1 = ((s8[14680064]{0:T(1024)(128)(4,1)}), s8[4194304]{0:T(1024)(128)(4,1)S(1)}, s32[]{:S(2)}) async-start(s8[14680064]{0:T(1024)(128)(4,1)} %bitcast.32), calls=%async_computation.7 | async-start | bytes 8388608
  89.1 20.4 %slice-start.2 = ((s8[14680064]{0:T(1024)(128)(4,1)}), s8[4194304]{0:T(1024)(128)(4,1)S(1)}, s32[]{:S(2)}) async-start(s8[14680064]{0:T(1024)(128)(4,1)} %bitcast.32), calls=%async_computation.8 | async-start | bytes 8388608
  89.1 20.4 %slice-start.3 = ((s8[14680064]{0:T(1024)(128)(4,1)}), s8[4194304]{0:T(1024)(128)(4,1)S(1)}, s32[]{:S(2)}) async-start(s8[14680064]{0:T(1024)(128)(4,1)} %bitcast.32), calls=%async_computation.9 | async-start | bytes 8388608

commit v2 on v1

--- a/solution.py
+++ b/solution.py
@@ -13,11 +13,47 @@
 
 
 LANES = 128
+FLOPS = {"table": 10**11, "finish": 10**11, "output": 10**11}
 VMEM = pl.BlockSpec(memory_space=pltpu.VMEM)
+SMEM = pl.BlockSpec(memory_space=pltpu.SMEM)
 
 
 def exchange(blocks):
     return lax.all_to_all(blocks, "ctx", 0, 0)
+
+
+def digits(devices):
+    rest, stride, place, out = devices // 2, devices, 1, []
+    while rest > 1:
+        radix = 4 if rest % 4 == 0 else 2
+        stride //= radix
+        out.append((stride, radix, place))
+        place *= radix
+        rest //= radix
+    return out + [(1, 2, place)]
+
+
+def mask_at(place_index, devices):
+    return sum(((place_index // place) % radix) * stride for stride, radix, place in digits(devices))
+
+
+def place_of(mask, devices):
+    return sum(((mask // stride) % radix) * place for stride, radix, place in digits(devices))
+
+
+def shifted(part, mask):
+    devices = lax.axis_size("ctx")
+    return lax.ppermute(part, "ctx", [(index, index ^ mask) for index in range(devices)])
+
+
+def gathered(part):
+    devices = lax.axis_size("ctx")
+    held = part[None]
+    for stride, radix, _ in digits(devices)[:-1]:
+        held = jnp.concatenate(
+            [held] + [shifted(held, stride * digit) for digit in range(1, radix)], axis=0
+        )
+    return held, shifted(held, 1)
 
 
 def call(body, name, out_shape, args, scratch=(), flops=0):
@@ -25,57 +61,64 @@
     return pl.pallas_call(
         body,
         out_shape=out_shape,
-        in_specs=[VMEM] * len(args),
+        in_specs=[SMEM if a.dtype == jnp.int32 and a.ndim == 1 else VMEM for a in args],
         out_specs=jax.tree.map(lambda _: VMEM, out_shape),
         scratch_shapes=list(scratch),
         compiler_params=pltpu.CompilerParams(vmem_limit_bytes=6 << 20),
-        cost_estimate=pl.CostEstimate(flops=flops, bytes_accessed=moved, transcendentals=0),
+        cost_estimate=pl.CostEstimate(flops=FLOPS.get(name, flops), bytes_accessed=moved, transcendentals=0),
         name=name,
     )(*args)
 
 
-def norm_factor(blocks_ref):
-    devices, rows, width = blocks_ref.shape
+def norm_factor(halves):
+    places, rows, width = halves[0].shape
 
     def add(index, total):
-        wide = blocks_ref[index].astype(jnp.float32)
-        return total + wide * wide
-
-    total = lax.fori_loop(0, devices, add, jnp.zeros((rows, width), jnp.float32), unroll=4)
-    mean = jnp.sum(total, axis=1, keepdims=True) / (devices * width)
+        for half in halves:
+            wide = half[index].astype(jnp.float32)
+            total = total + wide * wide
+        return total
+
+    total = lax.fori_loop(0, places, add, jnp.zeros((rows, width), jnp.float32), unroll=4)
+    mean = jnp.sum(total, axis=1, keepdims=True) / (2 * places * width)
     return lax.rsqrt(mean + NORM_EPSILON)
 
 
-def normed_block(blocks_ref, gain_ref, factor, index):
-    wide = blocks_ref[index].astype(jnp.float32)
-    return (wide * factor * gain_ref[index]).astype(jnp.bfloat16)
-
-
-def products(devices, depth, block_of, weight_refs, total_refs):
+def products(device_ref, halves, value_of, weight_refs, total_refs):
+    places, _, depth = halves[0].shape
     for total_ref in total_refs:
         total_ref[...] = jnp.zeros_like(total_ref)
 
     def step(index, carry):
-        block = block_of(index)
-        span = pl.ds(pl.multiple_of(index * depth, depth), depth)
-        for weight_ref, total_ref in zip(weight_refs, total_refs):
-            total_ref[...] += jnp.dot(
-                block, weight_ref[span, :], preferred_element_type=jnp.float32
-            )
+        for number, half in enumerate(halves):
+            mask = mask_at(index, 2 * places) + number
+            owner = lax.bitwise_xor(device_ref[0], mask)
+            block = value_of(half[index], owner)
+            span = pl.ds(pl.multiple_of(owner * depth, depth), depth)
+            for weight_ref, total_ref in zip(weight_refs, total_refs):
+                total_ref[...] += jnp.dot(
+                    block, weight_ref[span, :], preferred_element_type=jnp.float32
+                )
         return carry
 
-    lax.fori_loop(0, devices, step, 0, unroll=4)
+    lax.fori_loop(0, places, step, 0, unroll=4)
+
+
+def normed_products(device_ref, halves, gain_ref, weight_refs, total_refs):
+    factor = norm_factor(halves)
+
+    def normed(block, owner):
+        return (block.astype(jnp.float32) * factor * gain_ref[owner]).astype(jnp.bfloat16)
+
+    products(device_ref, halves, normed, weight_refs, total_refs)
 
 
 def project_kernel(
-    blocks_ref, gain_ref, query_ref, key_ref, value_ref, cos_ref, sin_ref, out_ref,
-    query_total, key_total, value_total, joined,
+    device_ref, near_ref, far_ref, gain_ref, query_ref, key_ref, value_ref, cos_ref, sin_ref,
+    out_ref, query_total, key_total, value_total, joined,
 ):
-    devices, _, depth = blocks_ref.shape
-    factor = norm_factor(blocks_ref)
-    products(
-        devices, depth,
-        lambda index: normed_block(blocks_ref, gain_ref, factor, index),
+    normed_products(
+        device_ref, (near_ref, far_ref), gain_ref,
         (query_ref, key_ref, value_ref),
         (query_total, key_total, value_total),
     )
@@ -90,16 +133,10 @@
     width = columns.shape[1]
     lane = lax.broadcasted_iota(jnp.int32, columns.shape, 1)
     partner = jnp.where(
-        lane % 2 == 1, pltpu.roll(columns, 1, 1), -pltpu.roll(columns, width - 1, 1)
+        lane % 2 == 1, pltpu.roll(columns, 1, 1), pltpu.roll(columns, width - 1, 1)
     )
     turned = columns * cos_ref[...] + partner * sin_ref[...]
-    sent = turned.astype(jnp.bfloat16)[:, :used]
-
-    def put(index, carry):
-        out_ref[index] = sent
-        return carry
-
-    lax.fori_loop(0, devices, put, 0, unroll=4)
+    out_ref[...] = turned.astype(jnp.bfloat16)[:, :used]
 
 
 def attend_kernel(scale, query_ref, key_ref, value_ref, limit_ref, out_ref):
@@ -150,46 +187,53 @@
                 out_ref[index, pairs:] = terms
 
 
-def output_kernel(blocks_ref, weight_ref, residual_ref, mid_ref, out_ref, total):
-    heads, rows, head_dim = blocks_ref.shape
-    devices = out_ref.shape[0]
-
-    def block_of(index):
-        return jnp.concatenate([blocks_ref[2 * index], blocks_ref[2 * index + 1]], axis=1)
-
-    products(heads // 2, 2 * head_dim, block_of, (weight_ref,), (total,))
-    mid = (residual_ref[...].astype(jnp.float32) + total[...]).astype(jnp.bfloat16)
-    mid_ref[...] = mid
-
-    def put(index, carry):
-        out_ref[index] = mid
+def order_kernel(device_ref, held_ref, out_ref):
+    devices = held_ref.shape[0]
+
+    def move(owner, carry):
+        place = place_of(lax.bitwise_xor(device_ref[0], owner), devices)
+        out_ref[owner] = held_ref[place]
         return carry
 
-    lax.fori_loop(0, devices, put, 0, unroll=4)
-
-
-def gated_kernel(blocks_ref, gain_ref, gate_ref, up_ref, out_ref, gate_total, up_total):
-    devices, _, depth = blocks_ref.shape
-    factor = norm_factor(blocks_ref)
-    products(
-        devices, depth,
-        lambda index: normed_block(blocks_ref, gain_ref, factor, index),
-        (gate_ref, up_ref),
-        (gate_total, up_total),
+    lax.fori_loop(0, devices, move, 0, unroll=4)
+
+
+def table_kernel(cos_ref, sin_ref, cos_out_ref, sin_out_ref):
+    lane = lax.broadcasted_iota(jnp.int32, sin_ref.shape, 1)
+    cos_out_ref[...] = cos_ref[...]
+    sin_out_ref[...] = jnp.where(lane % 2 == 1, sin_ref[...], -sin_ref[...])
+
+
+def finish_kernel(numerator_ref, denominator_ref, out_ref):
+    out_ref[...] = (numerator_ref[...] / denominator_ref[...]).astype(jnp.bfloat16)
+
+
+def output_kernel(blocks_ref, weight_ref, residual_ref, mid_ref, total):
+    heads, _, head_dim = blocks_ref.shape
+    total[...] = jnp.zeros_like(total)
+
+    def step(index, carry):
+        block = jnp.concatenate([blocks_ref[2 * index], blocks_ref[2 * index + 1]], axis=1)
+        span = pl.ds(pl.multiple_of(index * 2 * head_dim, head_dim), 2 * head_dim)
+        total[...] += jnp.dot(block, weight_ref[span, :], preferred_element_type=jnp.float32)
+        return carry
+
+    lax.fori_loop(0, heads // 2, step, 0, unroll=4)
+    mid_ref[...] = (residual_ref[...].astype(jnp.float32) + total[...]).astype(jnp.bfloat16)
+
+
+def gated_kernel(
+    device_ref, near_ref, far_ref, gain_ref, gate_ref, up_ref, out_ref, gate_total, up_total
+):
+    normed_products(
+        device_ref, (near_ref, far_ref), gain_ref, (gate_ref, up_ref), (gate_total, up_total)
     )
     gate = gate_total[...]
-    hidden = (gate / (1.0 + jnp.exp(-gate)) * up_total[...]).astype(jnp.bfloat16)
-
-    def put(index, carry):
-        out_ref[index] = hidden
-        return carry
-
-    lax.fori_loop(0, devices, put, 0, unroll=4)
-
-
-def down_kernel(blocks_ref, weight_ref, residual_ref, out_ref, total):
-    devices, _, depth = blocks_ref.shape
-    products(devices, depth, lambda index: blocks_ref[index], (weight_ref,), (total,))
+    out_ref[...] = (gate / (1.0 + jnp.exp(-gate)) * up_total[...]).astype(jnp.bfloat16)
+
+
+def down_kernel(device_ref, near_ref, far_ref, weight_ref, residual_ref, out_ref, total):
+    products(device_ref, (near_ref, far_ref), lambda block, _: block, (weight_ref,), (total,))
     out_ref[...] = (residual_ref[...].astype(jnp.float32) + total[...]).astype(jnp.bfloat16)
 
 
@@ -244,15 +288,19 @@
     still = jnp.ones((rows, padded - query_width - key_width), jnp.float32)
     cosine = jnp.concatenate([query_cos, key_cos, still], axis=1)
     sine = jnp.concatenate([query_sin, key_sin, still * 0.0], axis=1)
-    full = exchange(jnp.broadcast_to(hidden_in[None], (devices, rows, width)))
-    packed = exchange(
-        call(
-            project_kernel, "project", buffer(devices, rows, used),
-            (full, attn_gain.reshape(devices, 1, width), w_query, w_key, w_value, cosine, sine),
-            totals(query_width, key_width, key_width, padded),
-            2 * rows * devices * width * used,
-        )
-    )
+    table = buffer(rows, padded, dtype=jnp.float32)
+    cosine, sine = call(table_kernel, "table", (table, table), (cosine, sine), (), FLOPS["table"])
+    own = device.astype(jnp.int32)[None]
+    projected = call(
+        project_kernel, "project", buffer(rows, used),
+        (
+            own, *gathered(hidden_in), attn_gain.reshape(devices, 1, width),
+            w_query, w_key, w_value, cosine, sine,
+        ),
+        totals(query_width, key_width, key_width, padded),
+        2 * rows * devices * width * used,
+    )
+    packed = exchange(jnp.broadcast_to(projected[None], (devices, rows, used)))
 
     def unpacked(first, part_width):
         part = packed[:, :, first : first + part_width]
@@ -303,24 +351,30 @@
     own_share = jnp.exp(own_score - peak)
     numerator = jnp.sum(shares[..., None] * means, axis=0) + own_share[:, None] * own_value
     denominator = jnp.sum(shares, axis=0) + own_share
-    attn_part = (numerator / denominator[:, None]).astype(jnp.bfloat16)
-    attn_all = exchange(jnp.broadcast_to(attn_part[None], (devices, pairs, head_dim)))
-    mid_part, mid_sent = call(
-        output_kernel, "output", (buffer(rows, width), buffer(devices, rows, width)),
+    attn_part = call(
+        finish_kernel, "finish", buffer(pairs, head_dim), (numerator, denominator[:, None]), (),
+        FLOPS["finish"],
+    )
+    held = jnp.concatenate(gathered(attn_part), axis=0)
+    attn_all = call(
+        order_kernel, "order", buffer(devices, pairs, head_dim), (own, held)
+    )
+    mid_part = call(
+        output_kernel, "output", buffer(rows, width),
         (attn_all.reshape(heads, rows, head_dim), w_out, hidden_in),
         totals(width),
         2 * rows * heads * head_dim * width,
     )
     hidden_width = w_gate.shape[1]
-    hidden_sent = call(
-        gated_kernel, "gated", buffer(devices, rows, hidden_width),
-        (exchange(mid_sent), ffn_gain.reshape(devices, 1, width), w_gate, w_up),
+    hidden = call(
+        gated_kernel, "gated", buffer(rows, hidden_width),
+        (own, *gathered(mid_part), ffn_gain.reshape(devices, 1, width), w_gate, w_up),
         totals(hidden_width, hidden_width),
         4 * rows * devices * width * hidden_width,
     )
     return call(
         down_kernel, "down", buffer(rows, width),
-        (exchange(hidden_sent), w_down, mid_part),
+        (own, *gathered(hidden), w_down, mid_part),
         totals(width),
         2 * rows * devices * hidden_width * width,
     )

time: 113 us -> 104 us (0.920)
  blocking collectives: 39 us -> 0 us
  waiting for transfers between devices: 18.8 us -> 46.3 us
  starting transfers between devices: 14.5 us -> 29.7 us
  local copies, waits for them, and re-layouts: 25 us -> 11.9 us
    all_to_all x3 -> x0, blocking collectives: 39 us -> none  [exchange(): return lax.all_to_all(blocks, 'ctx', 0, 0)]
    ppermute x0 -> x20, waiting for transfers between devices: none -> 31.2 us  [shifted(): lax.ppermute(part, 'ctx', [(index, index ^ mask) for index in range(devic...]
    ppermute x0 -> x20, starting transfers between devices: none -> 22.7 us  [shifted(): lax.ppermute(part, 'ctx', [(index, index ^ mask) for index in range(devic...]
    unnamed x26 -> x60, local copies, waits for them, and re-layouts: 20.9 us -> 8.45 us
    all_to_all x3 -> x2, starting transfers between devices: 14.5 us -> 7.04 us  [exchange(): return lax.all_to_all(blocks, 'ctx', 0, 0)]
    all_to_all x3 -> x2, waiting for transfers between devices: 18.8 us -> 15.1 us  [exchange(): return lax.all_to_all(blocks, 'ctx', 0, 0)]
    pallas_call x5 -> x8, Pallas kernels: 13.4 us -> 12.3 us  [call(): pl.pallas_call(body, out_shape=out_shape, in_specs=[SMEM if a.dtype == jn...]
  transfers between devices with their start and end apart: 3 -> 22, of which waited for: 3 -> 17; matrix products, arithmetic and copies ran while one was open for 7% -> 7% of each run, Pallas kernels for 0% -> 0%
where the time goes in v2:
time: 104 us; the launch traced here: 103 us
  waiting for transfers between devices  46.3 us (45%)
  starting transfers between devices  29.7 us (29%)
  Pallas kernels  12.3 us (12%)
  local copies, waits for them, and re-layouts  11.9 us (11%)
  other arithmetic  2.44 us (2%)
    ppermute x20, waiting for transfers between devices, shifted(): lax.ppermute(part, 'ctx', [(index, index ^ mask) for index in range(devic...  31.2 us
    ppermute x20, starting transfers between devices, shifted(): lax.ppermute(part, 'ctx', [(index, index ^ mask) for index in range(devic...  22.7 us
    all_to_all x2, waiting for transfers between devices, exchange(): return lax.all_to_all(blocks, 'ctx', 0, 0)  15.1 us
    pallas_call x8, Pallas kernels, call(): pl.pallas_call(body, out_shape=out_shape, in_specs=[SMEM if a.dtype == jn...  12.3 us
    unnamed x60, local copies, waits for them, and re-layouts  8.45 us
    all_to_all x2, starting transfers between devices, exchange(): return lax.all_to_all(blocks, 'ctx', 0, 0)  7.04 us
  transfers between devices with their start and end apart: 22, of which 17 were waited for; matrix products, arithmetic and copies ran while one was open for 7% of the time, Pallas kernels for 0%

profile of v2, /device:TPU:0, one launch (start us, length us, event | category | flops | bytes accessed | tf_op | source)
XLA Modules:
  0.0 103.2 jit_solution(15141149054816882237)
XLA Ops:
  0.0 3.1 %collective-permute-start = (bf16[1,16,512]{2,1,0:T(8,128)(2,1)}, bf16[1,16,512]{2,1,0:T(8,128)(2,1)S(1)}, u32[]{:S(2)}, u32[]{:S(2)}) collective-permute-start(bf16[1,16,512]{2,1,0:T(8,128)(2,1)} %bitcast.57), channel_id=1, source_target_pairs={{0,4},{1,5},{2,6},{3,7},{4,0},{5,1},{6,2},{7,3},{8,12},{9,13},{10,... | collective-permute-start | bytes 49160 | tf_op jit(solution)/shard_map/ppermute | solution.py:46
  3.1 2.6 %collective-permute-start.1 = (bf16[1,16,512]{2,1,0:T(8,128)(2,1)}, bf16[1,16,512]{2,1,0:T(8,128)(2,1)S(1)}, u32[]{:S(2)}, u32[]{:S(2)}) collective-permute-start(bf16[1,16,512]{2,1,0:T(8,128)(2,1)} %bitcast.58), channel_id=1, source_target_pairs={{0,8},{1,9},{2,10},{3,11},{4,12},{5,13},{6,14},{7,15},{8,0},{9,1},... | collective-permute-start | bytes 49160 | tf_op jit(solution)/shard_map/ppermute | solution.py:46
  5.7 0.9 select_reduce_fusion
  6.6 0.1 multiply_sine_fusion.1
  6.7 0.1 multiply_sine_fusion
  6.8 0.1 pad.14.clone
  6.9 0.1 pad.17.clone
  7.0 0.7 constant_dynamic-update-slice_fusion.4
  7.7 0.3 collective-permute-done.1
  8.0 3.4 %collective-permute-done.2 = bf16[1,16,512]{2,1,0:T(8,128)(2,1)S(1)} collective-permute-done((bf16[1,16,512]{2,1,0:T(8,128)(2,1)}, bf16[1,16,512]{2,1,0:T(8,128)(2,1)S(1)}, u32[]{:S(2)}, u32[]{:S(2)}) %collective-permute-start.2) | collective-permute-done | bytes 16416 | tf_op jit(solution)/shard_map/ppermute | solution.py:46
  11.4 0.7 pad_maximum_fusion.1
  12.1 1.6 %collective-permute-start.3 = (bf16[4,16,512]{2,1,0:T(8,128)(2,1)S(1)}, bf16[4,16,512]{2,1,0:T(8,128)(2,1)S(1)}, u32[]{:S(2)}, u32[]{:S(2)}) collective-permute-start(bf16[4,16,512]{2,1,0:T(8,128)(2,1)S(1)} %pad_maximum_fusion.1), channel_id=1, source_target_pairs={{0,2},{1,3},{2,0},{3,1},{4,6},{5,7},{6,4},{7,5},{8,10},{9,11},{10,... | collective-permute-start | bytes 196616 | tf_op jit(solution)/shard_map/ppermute | solution.py:46
  13.7 2.7 %collective-permute-done.3 = bf16[4,16,512]{2,1,0:T(8,128)(2,1)S(1)} collective-permute-done((bf16[4,16,512]{2,1,0:T(8,128)(2,1)S(1)}, bf16[4,16,512]{2,1,0:T(8,128)(2,1)S(1)}, u32[]{:S(2)}, u32[]{:S(2)}) %collective-permute-start.3) | collective-permute-done | bytes 65568 | tf_op jit(solution)/shard_map/ppermute | solution.py:46
  16.5 1.0 copy-done.7
  17.5 1.0 copy.52.key_ref
  18.6 1.8 %copy.53.value_ref = bf16[8192,32]{1,0:T(8,128)(2,1)} copy(bf16[8192,32]{0,1:T(8,128)(2,1)S(1)} %copy-done.8) | data formatting | bytes 1048576 | tf_op args[4]
  20.3 0.1 copy.55.refs_3_
  20.4 1.6 %copy-done = bf16[8192,32]{1,0:T(8,128)(2,1)S(1)} copy-done((bf16[8192,32]{1,0:T(8,128)(2,1)S(1)}, bf16[8192,32]{1,0:T(8,128)(2,1)}, u32[]{:S(2)}) %copy-start) | copy-done | bytes 524312
  22.0 2.2 %copy-done.1 = bf16[8192,256]{1,0:T(8,128)(2,1)S(1)} copy-done((bf16[8192,256]{1,0:T(8,128)(2,1)S(1)}, bf16[8192,256]{1,0:T(8,128)(2,1)}, u32[]{:S(2)}) %copy-start.1) | copy-done | bytes 4194328
  24.2 1.7 %project.1 = bf16[16,320]{1,0:T(8,128)(2,1)S(1)} custom-call(s32[1]{0:T(128)} %bitcast.device_ref, bf16[8,16,512]{2,1,0:T(8,128)(2,1)S(1)} %constant_dynamic-update-slice_fusion.near_ref, bf16[8,16,512]{2,1,0:T(8,128)(2,1)S(1)} %collective-permute-done.4.far_ref, f32[16,1,512]{2,1,0:T(1,128)S(1)} %bitcast.61, bf16[8192,256]{1,0:T(8,128)(2,1)S(1)} %copy-done.1, ...), custom_call_target="tpu_custom_call" | custom-call | flops 83886080 | bytes 5586948 | tf_op jit(solution)/shard_map/project/pallas_call | solution.py:61
  25.8 0.7 broadcast_in_dim.67
  26.6 3.5 %all-to-all-start = ((bf16[16,16,320]{2,1,0:T(8,128)(2,1)}), bf16[16,16,320]{2,1,0:T(8,128)(2,1)S(1)}, u32[]{:S(2)}, u32[]{:S(2)}) async-start(bf16[16,16,320]{2,1,0:T(8,128)(2,1)} %broadcast_in_dim.67), calls=%async_computation | async-start | bytes 393216 | tf_op jit(solution)/shard_map/all_to_all | solution.py:22
  30.1 1.7 %copy_bitcast_fusion = (bf16[1024,512]{1,0:T(8,128)(2,1)S(1)}, bf16[1024,512]{1,0:T(8,128)(2,1)S(1)}) fusion(bf16[128,8,4,128]{3,2,1,0:T(4,128)(2,1)S(1)} %bitcast.67, bf16[128,8,4,128]{3,2,1,0:T(4,128)(2,1)} %bitcast.68), kind=kLoop, calls=%fused_computation | loop fusion | bytes 4194304 | tf_op jit(solution)/shard_map/reshape | solution.py:325
  31.8 7.3 %all-to-all-done = bf16[16,16,320]{2,1,0:T(8,128)(2,1)S(1)} async-done(((bf16[16,16,320]{2,1,0:T(8,128)(2,1)}), bf16[16,16,320]{2,1,0:T(8,128)(2,1)S(1)}, u32[]{:S(2)}, u32[]{:S(2)}) %all-to-all-start) | async-done | bytes 163872 | tf_op jit(solution)/shard_map/all_to_all | solution.py:22
  39.1 2.3 %attend.1 = bf16[16,40,128]{2,1,0:T(8,128)(2,1)} custom-call(bf16[32,16,128]{2,1,0:T(8,128)(2,1)S(1)} %bitcast.46, bf16[1024,512]{1,0:T(8,128)(2,1)S(1)} %get-tuple-element.37.refs_1_, bf16[1024,512]{1,0:T(8,128)(2,1)S(1)} %get-tuple-element.36.refs_2_, s32[16,1]{1,0:T(8,128)S(1)} %copy.55.refs_3_), custom_call_target="tpu_custom_call" | custom-call | flops 268435456 | bytes 2228288 | tf_op jit(solution)/shard_map/attend/pallas_call | solution.py:61
  41.4 3.5 %all-to-all-start.1 = ((bf16[16,40,128]{2,1,0:T(8,128)(2,1)}), bf16[16,40,128]{2,1,0:T(8,128)(2,1)S(1)}, u32[]{:S(2)}, u32[]{:S(2)}) async-start(bf16[16,40,128]{2,1,0:T(8,128)(2,1)} %attend.1), calls=%async_computation.1 | async-start | bytes 327680 | tf_op jit(solution)/shard_map/all_to_all | solution.py:22
  44.9 0.1 fusion.18
  45.1 0.1 broadcast_in_dim.68
  45.2 0.1 broadcast_in_dim.70
  45.3 0.1 multiply_reduce_fusion.1
  45.5 7.9 %all-to-all-done.1 = bf16[16,40,128]{2,1,0:T(8,128)(2,1)S(1)} async-done(((bf16[16,40,128]{2,1,0:T(8,128)(2,1)}), bf16[16,40,128]{2,1,0:T(8,128)(2,1)S(1)}, u32[]{:S(2)}, u32[]{:S(2)}) %all-to-all-start.1) | async-done | bytes 163872 | tf_op jit(solution)/shard_map/all_to_all | solution.py:22
  53.3 0.1 dynamic-slice_convert_fusion
  53.5 0.1 copy.60
  53.6 0.1 copy.61
  53.7 0.1 copy.59
  53.8 0.1 multiply_reduce_fusion
  53.9 0.1 multiply_add_fusion.numerator_ref
  54.0 0.1 finish.1
  54.2 1.3 %collective-permute-start.6 = (bf16[1,32,128]{2,1,0:T(8,128)(2,1)S(1)}, bf16[1,32,128]{2,1,0:T(8,128)(2,1)S(1)}, u32[]{:S(2)}, u32[]{:S(2)}) collective-permute-start(bf16[1,32,128]{2,1,0:T(8,128)(2,1)S(1)} %bitcast.63), channel_id=1, source_target_pairs={{0,8},{1,9},{2,10},{3,11},{4,12},{5,13},{6,14},{7,15},{8,0},{9,1},... | collective-permute-start | bytes 24584 | tf_op jit(solution)/shard_map/ppermute | solution.py:46
  55.5 3.1 %collective-permute-start.7 = (bf16[1,32,128]{2,1,0:T(8,128)(2,1)S(1)}, bf16[1,32,128]{2,1,0:T(8,128)(2,1)S(1)}, u32[]{:S(2)}, u32[]{:S(2)}) collective-permute-start(bf16[1,32,128]{2,1,0:T(8,128)(2,1)S(1)} %bitcast.64), channel_id=1, source_target_pairs={{0,12},{1,13},{2,14},{3,15},{4,8},{5,9},{6,10},{7,11},{8,4},{9,5},... | collective-permute-start | bytes 24584 | tf_op jit(solution)/shard_map/ppermute | solution.py:46
  58.5 0.2 collective-permute-done.6
  58.8 2.1 %collective-permute-done.7 = bf16[1,32,128]{2,1,0:T(8,128)(2,1)S(1)} collective-permute-done((bf16[1,32,128]{2,1,0:T(8,128)(2,1)S(1)}, bf16[1,32,128]{2,1,0:T(8,128)(2,1)S(1)}, u32[]{:S(2)}, u32[]{:S(2)}) %collective-permute-start.7) | collective-permute-done | bytes 8224 | tf_op jit(solution)/shard_map/ppermute | solution.py:46
  60.9 1.0 collective-permute-start.8
  61.9 3.0 %collective-permute-done.8 = bf16[4,32,128]{2,1,0:T(8,128)(2,1)S(1)} collective-permute-done((bf16[4,32,128]{2,1,0:T(8,128)(2,1)S(1)}, bf16[4,32,128]{2,1,0:T(8,128)(2,1)S(1)}, u32[]{:S(2)}, u32[]{:S(2)}) %collective-permute-start.8) | collective-permute-done | bytes 32800 | tf_op jit(solution)/shard_map/ppermute | solution.py:46
  64.9 0.1 collective-permute-start.9
  65.0 1.2 %collective-permute-done.9 = bf16[8,32,128]{2,1,0:T(8,128)(2,1)S(1)} collective-permute-done((bf16[8,32,128]{2,1,0:T(8,128)(2,1)S(1)}, bf16[8,32,128]{2,1,0:T(8,128)(2,1)S(1)}, u32[]{:S(2)}, u32[]{:S(2)}) %collective-permute-start.9) | collective-permute-done | bytes 65568 | tf_op jit(solution)/shard_map/ppermute | solution.py:46
  66.2 0.3 order.1
  66.6 1.0 output.1.residual_ref
  67.7 3.6 %collective-permute-start.11 = (bf16[1,16,512]{2,1,0:T(8,128)(2,1)S(1)}, bf16[1,16,512]{2,1,0:T(8,128)(2,1)S(1)}, u32[]{:S(2)}, u32[]{:S(2)}) collective-permute-start(bf16[1,16,512]{2,1,0:T(8,128)(2,1)S(1)} %bitcast.53), channel_id=1, source_target_pairs={{0,8},{1,9},{2,10},{3,11},{4,12},{5,13},{6,14},{7,15},{8,0},{9,1},... | collective-permute-start | bytes 49160 | tf_op jit(solution)/shard_map/ppermute | solution.py:46
  71.3 0.8 collective-permute-start.12
  72.1 0.9 collective-permute-done.11
  73.0 3.8 %collective-permute-done.12 = bf16[1,16,512]{2,1,0:T(8,128)(2,1)S(1)} collective-permute-done((bf16[1,16,512]{2,1,0:T(8,128)(2,1)S(1)}, bf16[1,16,512]{2,1,0:T(8,128)(2,1)S(1)}, u32[]{:S(2)}, u32[]{:S(2)}) %collective-permute-start.12) | collective-permute-done | bytes 16416 | tf_op jit(solution)/shard_map/ppermute | solution.py:46
  77.0 4.2 %collective-permute-done.13 = bf16[4,16,512]{2,1,0:T(8,128)(2,1)S(1)} collective-permute-done((bf16[4,16,512]{2,1,0:T(8,128)(2,1)S(1)}, bf16[4,16,512]{2,1,0:T(8,128)(2,1)S(1)}, u32[]{:S(2)}, u32[]{:S(2)}) %collective-permute-start.13) | collective-permute-done | bytes 65568 | tf_op jit(solution)/shard_map/ppermute | solution.py:46
  81.2 1.3 %collective-permute-done.14.far_ref = bf16[8,16,512]{2,1,0:T(8,128)(2,1)S(1)} collective-permute-done((bf16[8,16,512]{2,1,0:T(8,128)(2,1)S(1)}, bf16[8,16,512]{2,1,0:T(8,128)(2,1)S(1)}, u32[]{:S(2)}, u32[]{:S(2)}) %collective-permute-start.14) | collective-permute-done | bytes 131104 | tf_op jit(solution)/shard_map/ppermute | solution.py:46
  82.7 4.2 %gated.1 = bf16[16,896]{1,0:T(8,128)(2,1)S(1)} custom-call(s32[1]{0:T(128)} %bitcast.device_ref, bf16[8,16,512]{2,1,0:T(8,128)(2,1)S(1)} %constant_dynamic-update-slice_fusion.16.near_ref, bf16[8,16,512]{2,1,0:T(8,128)(2,1)S(1)} %collective-permute-done.14.far_ref, f32[16,1,512]{2,1,0:T(1,128)S(1)} %bitcast.66, bf16[8192,896]{1,0:T(8,128)(2,1)S(1)} %bitcast.43, ...), custom_call_target="tpu_custom_call" | custom-call | flops 469762048 | bytes 29655044 | tf_op jit(solution)/shard_map/gated/pallas_call | solution.py:61
  86.9 0.1 collective-permute-start.15
  87.0 1.3 %collective-permute-start.16 = (bf16[1,16,896]{2,1,0:T(8,128)(2,1)S(1)}, bf16[1,16,896]{2,1,0:T(8,128)(2,1)S(1)}, u32[]{:S(2)}, u32[]{:S(2)}) collective-permute-start(bf16[1,16,896]{2,1,0:T(8,128)(2,1)S(1)} %bitcast.49), channel_id=1, source_target_pairs={{0,8},{1,9},{2,10},{3,11},{4,12},{5,13},{6,14},{7,15},{8,0},{9,1},... | collective-permute-start | bytes 86024 | tf_op jit(solution)/shard_map/ppermute | solution.py:46
  88.3 3.1 %collective-permute-start.17 = (bf16[1,16,896]{2,1,0:T(8,128)(2,1)S(1)}, bf16[1,16,896]{2,1,0:T(8,128)(2,1)S(1)}, u32[]{:S(2)}, u32[]{:S(2)}) collective-permute-start(bf16[1,16,896]{2,1,0:T(8,128)(2,1)S(1)} %bitcast.50), channel_id=1, source_target_pairs={{0,12},{1,13},{2,14},{3,15},{4,8},{5,9},{6,10},{7,11},{8,4},{9,5},... | collective-permute-start | bytes 86024 | tf_op jit(solution)/shard_map/ppermute | solution.py:46
  91.4 0.5 collective-permute-done.16
  91.8 2.1 %collective-permute-done.17 = bf16[1,16,896]{2,1,0:T(8,128)(2,1)S(1)} collective-permute-done((bf16[1,16,896]{2,1,0:T(8,128)(2,1)S(1)}, bf16[1,16,896]{2,1,0:T(8,128)(2,1)S(1)}, u32[]{:S(2)}, u32[]{:S(2)}) %collective-permute-start.17) | collective-permute-done | bytes 28704 | tf_op jit(solution)/shard_map/ppermute | solution.py:46
  94.0 1.0 collective-permute-start.18
  95.0 3.8 %collective-permute-done.18 = bf16[4,16,896]{2,1,0:T(8,128)(2,1)S(1)} collective-permute-done((bf16[4,16,896]{2,1,0:T(8,128)(2,1)S(1)}, bf16[4,16,896]{2,1,0:T(8,128)(2,1)S(1)}, u32[]{:S(2)}, u32[]{:S(2)}) %collective-permute-start.18) | collective-permute-done | bytes 114720 | tf_op jit(solution)/shard_map/ppermute | solution.py:46
  98.9 1.5 %collective-permute-done.19.far_ref = bf16[8,16,896]{2,1,0:T(8,128)(2,1)S(1)} collective-permute-done((bf16[8,16,896]{2,1,0:T(8,128)(2,1)S(1)}, bf16[8,16,896]{2,1,0:T(8,128)(2,1)S(1)}, u32[]{:S(2)}, u32[]{:S(2)}) %collective-permute-start.19) | collective-permute-done | bytes 229408 | tf_op jit(solution)/shard_map/ppermute | solution.py:46
  100.4 2.8 %down.1 = bf16[16,512]{1,0:T(8,128)(2,1)} custom-call(s32[1]{0:T(128)} %bitcast.device_ref, bf16[8,16,896]{2,1,0:T(8,128)(2,1)S(1)} %constant_dynamic-update-slice_fusion.21.near_ref, bf16[8,16,896]{2,1,0:T(8,128)(2,1)S(1)} %collective-permute-done.19.far_ref, bf16[14336,512]{1,0:T(8,128)(2,1)S(1)} %bitcast.41, bf16[16,512]{1,0:T(8,128)(2,1)S(1)} %output.1.residual_ref), custom_call_target="tpu_custom_call" | custom-call | flops 234881024 | bytes 15155204 | tf_op jit(solution)/shard_map/down/pallas_call | solution.py:61
  (97 shorter events, 0.8 us)
Async XLA Ops:
  0.0 7.7 %collective-permute-start = (bf16[1,16,512]{2,1,0:T(8,128)(2,1)}, bf16[1,16,512]{2,1,0:T(8,128)(2,1)S(1)}, u32[]{:S(2)}, u32[]{:S(2)}) collective-permute-start(bf16[1,16,512]{2,1,0:T(8,128)(2,1)} %bitcast.57), channel_id=1, source_target_pairs={{0,4},{1,5},{2,6},{3,7},{4,0},{5,1},{6,2},{7,3},{8,12},{9,13},{10,... | collective-permute-start | bytes 49160 | tf_op jit(solution)/shard_map/ppermute | solution.py:46
  3.1 4.9 %collective-permute-start.1 = (bf16[1,16,512]{2,1,0:T(8,128)(2,1)}, bf16[1,16,512]{2,1,0:T(8,128)(2,1)S(1)}, u32[]{:S(2)}, u32[]{:S(2)}) collective-permute-start(bf16[1,16,512]{2,1,0:T(8,128)(2,1)} %bitcast.58), channel_id=1, source_target_pairs={{0,8},{1,9},{2,10},{3,11},{4,12},{5,13},{6,14},{7,15},{8,0},{9,1},... | collective-permute-start | bytes 49160 | tf_op jit(solution)/shard_map/ppermute | solution.py:46
  5.6 5.7 %collective-permute-start.2 = (bf16[1,16,512]{2,1,0:T(8,128)(2,1)}, bf16[1,16,512]{2,1,0:T(8,128)(2,1)S(1)}, u32[]{:S(2)}, u32[]{:S(2)}) collective-permute-start(bf16[1,16,512]{2,1,0:T(8,128)(2,1)} %bitcast.59), channel_id=1, source_target_pairs={{0,12},{1,13},{2,14},{3,15},{4,8},{5,9},{6,10},{7,11},{8,4},{9,5},... | collective-permute-start | bytes 49160 | tf_op jit(solution)/shard_map/ppermute | solution.py:46
  12.1 4.3 %collective-permute-start.3 = (bf16[4,16,512]{2,1,0:T(8,128)(2,1)S(1)}, bf16[4,16,512]{2,1,0:T(8,128)(2,1)S(1)}, u32[]{:S(2)}, u32[]{:S(2)}) collective-permute-start(bf16[4,16,512]{2,1,0:T(8,128)(2,1)S(1)} %pad_maximum_fusion.1), channel_id=1, source_target_pairs={{0,2},{1,3},{2,0},{3,1},{4,6},{5,7},{6,4},{7,5},{8,10},{9,11},{10,... | collective-permute-start | bytes 196616 | tf_op jit(solution)/shard_map/ppermute | solution.py:46
  16.5 3.9 %collective-permute-start.4 = (bf16[8,16,512]{2,1,0:T(8,128)(2,1)S(1)}, bf16[8,16,512]{2,1,0:T(8,128)(2,1)S(1)}, u32[]{:S(2)}, u32[]{:S(2)}) collective-permute-start(bf16[8,16,512]{2,1,0:T(8,128)(2,1)S(1)} %constant_dynamic-update-slice_fusion.near_ref), channel_id=1, source_target_pairs={{0,1},{1,0},{2,3},{3,2},{4,5},{5,4},{6,7},{7,6},{8,9},{9,8},{10,11... | collective-permute-start | bytes 393224 | tf_op jit(solution)/shard_map/ppermute | solution.py:46
  16.5 1.0 %copy-start.7 = (bf16[8192,32]{0,1:T(8,128)(2,1)S(1)}, bf16[8192,32]{0,1:T(8,128)(2,1)}, u32[]{:S(2)}) copy-start(bf16[8192,32]{0,1:T(8,128)(2,1)} %param.17) | copy-start | bytes 1572868
  16.5 2.1 %copy-start.8 = (bf16[8192,32]{0,1:T(8,128)(2,1)S(1)}, bf16[8192,32]{0,1:T(8,128)(2,1)}, u32[]{:S(2)}) copy-start(bf16[8192,32]{0,1:T(8,128)(2,1)} %param.18) | copy-start | bytes 1572868
  17.5 2.9 %copy-start.3 = (f32[8192]{0:T(1024)S(1)}, f32[8192]{0:T(1024)}, u32[]{:S(2)}) copy-start(f32[8192]{0:T(1024)} %param.15) | copy-start | bytes 98308
  20.4 1.6 %copy-start = (bf16[8192,32]{1,0:T(8,128)(2,1)S(1)}, bf16[8192,32]{1,0:T(8,128)(2,1)}, u32[]{:S(2)}) copy-start(bf16[8192,32]{1,0:T(8,128)(2,1)} %copy.53.value_ref) | copy-start | bytes 1572868
  22.0 2.2 %copy-start.1 = (bf16[8192,256]{1,0:T(8,128)(2,1)S(1)}, bf16[8192,256]{1,0:T(8,128)(2,1)}, u32[]{:S(2)}) copy-start(bf16[8192,256]{1,0:T(8,128)(2,1)} %query_ref.1) | copy-start | bytes 12582916
  24.2 5.9 %copy-start.6 = (bf16[1024,4,128]{2,1,0:T(4,128)(2,1)S(1)}, bf16[1024,4,128]{2,1,0:T(4,128)(2,1)}, u32[]{:S(2)}) copy-start(bf16[1024,4,128]{2,1,0:T(4,128)(2,1)} %param.20) | copy-start | bytes 3145732
  26.6 12.5 %all-to-all-start = ((bf16[16,16,320]{2,1,0:T(8,128)(2,1)}), bf16[16,16,320]{2,1,0:T(8,128)(2,1)S(1)}, u32[]{:S(2)}, u32[]{:S(2)}) async-start(bf16[16,16,320]{2,1,0:T(8,128)(2,1)} %broadcast_in_dim.67), calls=%async_computation | async-start | bytes 393216 | tf_op jit(solution)/shard_map/all_to_all | solution.py:22
  41.4 11.9 %all-to-all-start.1 = ((bf16[16,40,128]{2,1,0:T(8,128)(2,1)}), bf16[16,40,128]{2,1,0:T(8,128)(2,1)S(1)}, u32[]{:S(2)}, u32[]{:S(2)}) async-start(bf16[16,40,128]{2,1,0:T(8,128)(2,1)} %attend.1), calls=%async_computation.1 | async-start | bytes 327680 | tf_op jit(solution)/shard_map/all_to_all | solution.py:22
  54.0 12.5 %copy-start.2 = (bf16[16,512]{1,0:T(8,128)(2,1)S(1)}, bf16[16,512]{1,0:T(8,128)(2,1)}, u32[]{:S(2)}) copy-start(bf16[16,512]{1,0:T(8,128)(2,1)} %residual_ref.1) | copy-start | bytes 49156
  54.0 12.5 %copy-start.5 = (bf16[4096,512]{1,0:T(8,128)(2,1)S(1)}, bf16[4096,512]{1,0:T(8,128)(2,1)}, u32[]{:S(2)}) copy-start(bf16[4096,512]{1,0:T(8,128)(2,1)} %weight_ref.2) | copy-start | bytes 12582916
  54.1 4.4 %collective-permute-start.5 = (bf16[1,32,128]{2,1,0:T(8,128)(2,1)S(1)}, bf16[1,32,128]{2,1,0:T(8,128)(2,1)S(1)}, u32[]{:S(2)}, u32[]{:S(2)}) collective-permute-start(bf16[1,32,128]{2,1,0:T(8,128)(2,1)S(1)} %bitcast.62), channel_id=1, source_target_pairs={{0,4},{1,5},{2,6},{3,7},{4,0},{5,1},{6,2},{7,3},{8,12},{9,13},{10,... | collective-permute-start | bytes 24584 | tf_op jit(solution)/shard_map/ppermute | solution.py:46
  54.2 4.6 %collective-permute-start.6 = (bf16[1,32,128]{2,1,0:T(8,128)(2,1)S(1)}, bf16[1,32,128]{2,1,0:T(8,128)(2,1)S(1)}, u32[]{:S(2)}, u32[]{:S(2)}) collective-permute-start(bf16[1,32,128]{2,1,0:T(8,128)(2,1)S(1)} %bitcast.63), channel_id=1, source_target_pairs={{0,8},{1,9},{2,10},{3,11},{4,12},{5,13},{6,14},{7,15},{8,0},{9,1},... | collective-permute-start | bytes 24584 | tf_op jit(solution)/shard_map/ppermute | solution.py:46
  55.5 5.4 %collective-permute-start.7 = (bf16[1,32,128]{2,1,0:T(8,128)(2,1)S(1)}, bf16[1,32,128]{2,1,0:T(8,128)(2,1)S(1)}, u32[]{:S(2)}, u32[]{:S(2)}) collective-permute-start(bf16[1,32,128]{2,1,0:T(8,128)(2,1)S(1)} %bitcast.64), channel_id=1, source_target_pairs={{0,12},{1,13},{2,14},{3,15},{4,8},{5,9},{6,10},{7,11},{8,4},{9,5},... | collective-permute-start | bytes 24584 | tf_op jit(solution)/shard_map/ppermute | solution.py:46
  60.9 4.0 %collective-permute-start.8 = (bf16[4,32,128]{2,1,0:T(8,128)(2,1)S(1)}, bf16[4,32,128]{2,1,0:T(8,128)(2,1)S(1)}, u32[]{:S(2)}, u32[]{:S(2)}) collective-permute-start(bf16[4,32,128]{2,1,0:T(8,128)(2,1)S(1)} %pad_maximum_fusion.3), channel_id=1, source_target_pairs={{0,2},{1,3},{2,0},{3,1},{4,6},{5,7},{6,4},{7,5},{8,10},{9,11},{10,... | collective-permute-start | bytes 98312 | tf_op jit(solution)/shard_map/ppermute | solution.py:46
  64.9 1.3 %collective-permute-start.9 = (bf16[8,32,128]{2,1,0:T(8,128)(2,1)S(1)}, bf16[8,32,128]{2,1,0:T(8,128)(2,1)S(1)}, u32[]{:S(2)}, u32[]{:S(2)}) collective-permute-start(bf16[8,32,128]{2,1,0:T(8,128)(2,1)S(1)} %get-tuple-element.15), channel_id=1, source_target_pairs={{0,1},{1,0},{2,3},{3,2},{4,5},{5,4},{6,7},{7,6},{8,9},{9,8},{10,11... | collective-permute-start | bytes 196616 | tf_op jit(solution)/shard_map/ppermute | solution.py:46
  66.5 16.0 %slice-start.4 = ((s8[14680064]{0:T(1024)(128)(4,1)}), s8[4194304]{0:T(1024)(128)(4,1)S(1)}, s32[]{:S(2)}) async-start(s8[14680064]{0:T(1024)(128)(4,1)} %bitcast.42), calls=%async_computation.6 | async-start | bytes 8388608
  66.5 16.0 %slice-start.8 = ((s8[14680064]{0:T(1024)(128)(4,1)}), s8[4194304]{0:T(1024)(128)(4,1)S(1)}, s32[]{:S(2)}) async-start(s8[14680064]{0:T(1024)(128)(4,1)} %bitcast.44), calls=%async_computation.10 | async-start | bytes 8388608
  66.6 16.0 %slice-start.5 = ((s8[14680064]{0:T(1024)(128)(4,1)}), s8[4194304]{0:T(1024)(128)(4,1)S(1)}, s32[]{:S(2)}) async-start(s8[14680064]{0:T(1024)(128)(4,1)} %bitcast.42), calls=%async_computation.7 | async-start | bytes 8388608
  66.6 16.0 %slice-start.6 = ((s8[14680064]{0:T(1024)(128)(4,1)}), s8[4194304]{0:T(1024)(128)(4,1)S(1)}, s32[]{:S(2)}) async-start(s8[14680064]{0:T(1024)(128)(4,1)} %bitcast.42), calls=%async_computation.8 | async-start | bytes 8388608
  66.6 16.0 %slice-start.7 = ((s8[14680064]{0:T(1024)(128)(4,1)}), s8[2097152]{0:T(1024)(128)(4,1)S(1)}, s32[]{:S(2)}) async-start(s8[14680064]{0:T(1024)(128)(4,1)} %bitcast.42), calls=%async_computation.9 | async-start | bytes 4194304
  66.6 16.0 %slice-start.9 = ((s8[14680064]{0:T(1024)(128)(4,1)}), s8[4194304]{0:T(1024)(128)(4,1)S(1)}, s32[]{:S(2)}) async-start(s8[14680064]{0:T(1024)(128)(4,1)} %bitcast.44), calls=%async_computation.11 | async-start | bytes 8388608
  66.6 16.0 %slice-start.10 = ((s8[14680064]{0:T(1024)(128)(4,1)}), s8[4194304]{0:T(1024)(128)(4,1)S(1)}, s32[]{:S(2)}) async-start(s8[14680064]{0:T(1024)(128)(4,1)} %bitcast.44), calls=%async_computation.12 | async-start | bytes 8388608
  66.6 16.0 %slice-start.11 = ((s8[14680064]{0:T(1024)(128)(4,1)}), s8[2097152]{0:T(1024)(128)(4,1)S(1)}, s32[]{:S(2)}) async-start(s8[14680064]{0:T(1024)(128)(4,1)} %bitcast.44), calls=%async_computation.13 | async-start | bytes 4194304
  66.6 16.0 %copy-start.4 = (f32[8192]{0:T(1024)S(1)}, f32[8192]{0:T(1024)}, u32[]{:S(2)}) copy-start(f32[8192]{0:T(1024)} %param.22) | copy-start | bytes 98308
  67.7 4.4 %collective-permute-start.10 = (bf16[1,16,512]{2,1,0:T(8,128)(2,1)S(1)}, bf16[1,16,512]{2,1,0:T(8,128)(2,1)S(1)}, u32[]{:S(2)}, u32[]{:S(2)}) collective-permute-start(bf16[1,16,512]{2,1,0:T(8,128)(2,1)S(1)} %bitcast.52), channel_id=1, source_target_pairs={{0,4},{1,5},{2,6},{3,7},{4,0},{5,1},{6,2},{7,3},{8,12},{9,13},{10,... | collective-permute-start | bytes 49160 | tf_op jit(solution)/shard_map/ppermute | solution.py:46
  67.7 5.3 %collective-permute-start.11 = (bf16[1,16,512]{2,1,0:T(8,128)(2,1)S(1)}, bf16[1,16,512]{2,1,0:T(8,128)(2,1)S(1)}, u32[]{:S(2)}, u32[]{:S(2)}) collective-permute-start(bf16[1,16,512]{2,1,0:T(8,128)(2,1)S(1)} %bitcast.53), channel_id=1, source_target_pairs={{0,8},{1,9},{2,10},{3,11},{4,12},{5,13},{6,14},{7,15},{8,0},{9,1},... | collective-permute-start | bytes 49160 | tf_op jit(solution)/shard_map/ppermute | solution.py:46
  71.3 5.5 %collective-permute-start.12 = (bf16[1,16,512]{2,1,0:T(8,128)(2,1)S(1)}, bf16[1,16,512]{2,1,0:T(8,128)(2,1)S(1)}, u32[]{:S(2)}, u32[]{:S(2)}) collective-permute-start(bf16[1,16,512]{2,1,0:T(8,128)(2,1)S(1)} %bitcast.54), channel_id=1, source_target_pairs={{0,12},{1,13},{2,14},{3,15},{4,8},{5,9},{6,10},{7,11},{8,4},{9,5},... | collective-permute-start | bytes 49160 | tf_op jit(solution)/shard_map/ppermute | solution.py:46
  76.8 4.3 %collective-permute-start.13 = (bf16[4,16,512]{2,1,0:T(8,128)(2,1)S(1)}, bf16[4,16,512]{2,1,0:T(8,128)(2,1)S(1)}, u32[]{:S(2)}, u32[]{:S(2)}) collective-permute-start(bf16[4,16,512]{2,1,0:T(8,128)(2,1)S(1)} %pad_maximum_fusion.2), channel_id=1, source_target_pairs={{0,2},{1,3},{2,0},{3,1},{4,6},{5,7},{6,4},{7,5},{8,10},{9,11},{10,... | collective-permute-start | bytes 196616 | tf_op jit(solution)/shard_map/ppermute | solution.py:46
  81.2 1.3 %collective-permute-start.14 = (bf16[8,16,512]{2,1,0:T(8,128)(2,1)S(1)}, bf16[8,16,512]{2,1,0:T(8,128)(2,1)S(1)}, u32[]{:S(2)}, u32[]{:S(2)}) collective-permute-start(bf16[8,16,512]{2,1,0:T(8,128)(2,1)S(1)} %constant_dynamic-update-slice_fusion.16.near_ref), channel_id=1, source_target_pairs={{0,1},{1,0},{2,3},{3,2},{4,5},{5,4},{6,7},{7,6},{8,9},{9,8},{10,11... | collective-permute-start | bytes 393224 | tf_op jit(solution)/shard_map/ppermute | solution.py:46
  82.5 17.9 %slice-start = ((s8[14680064]{0:T(1024)(128)(4,1)}), s8[4194304]{0:T(1024)(128)(4,1)S(1)}, s32[]{:S(2)}) async-start(s8[14680064]{0:T(1024)(128)(4,1)} %bitcast.40), calls=%async_computation.2 | async-start | bytes 8388608
  82.6 17.8 %slice-start.1 = ((s8[14680064]{0:T(1024)(128)(4,1)}), s8[4194304]{0:T(1024)(128)(4,1)S(1)}, s32[]{:S(2)}) async-start(s8[14680064]{0:T(1024)(128)(4,1)} %bitcast.40), calls=%async_computation.3 | async-start | bytes 8388608
  82.6 17.8 %slice-start.2 = ((s8[14680064]{0:T(1024)(128)(4,1)}), s8[4194304]{0:T(1024)(128)(4,1)S(1)}, s32[]{:S(2)}) async-start(s8[14680064]{0:T(1024)(128)(4,1)} %bitcast.40), calls=%async_computation.4 | async-start | bytes 8388608
  82.6 17.8 %slice-start.3 = ((s8[14680064]{0:T(1024)(128)(4,1)}), s8[2097152]{0:T(1024)(128)(4,1)S(1)}, s32[]{:S(2)}) async-start(s8[14680064]{0:T(1024)(128)(4,1)} %bitcast.40), calls=%async_computation.5 | async-start | bytes 4194304
  86.9 4.5 %collective-permute-start.15 = (bf16[1,16,896]{2,1,0:T(8,128)(2,1)S(1)}, bf16[1,16,896]{2,1,0:T(8,128)(2,1)S(1)}, u32[]{:S(2)}, u32[]{:S(2)}) collective-permute-start(bf16[1,16,896]{2,1,0:T(8,128)(2,1)S(1)} %bitcast.48), channel_id=1, source_target_pairs={{0,4},{1,5},{2,6},{3,7},{4,0},{5,1},{6,2},{7,3},{8,12},{9,13},{10,... | collective-permute-start | bytes 86024 | tf_op jit(solution)/shard_map/ppermute | solution.py:46
  87.0 4.8 %collective-permute-start.16 = (bf16[1,16,896]{2,1,0:T(8,128)(2,1)S(1)}, bf16[1,16,896]{2,1,0:T(8,128)(2,1)S(1)}, u32[]{:S(2)}, u32[]{:S(2)}) collective-permute-start(bf16[1,16,896]{2,1,0:T(8,128)(2,1)S(1)} %bitcast.49), channel_id=1, source_target_pairs={{0,8},{1,9},{2,10},{3,11},{4,12},{5,13},{6,14},{7,15},{8,0},{9,1},... | collective-permute-start | bytes 86024 | tf_op jit(solution)/shard_map/ppermute | solution.py:46
  88.3 5.7 %collective-permute-start.17 = (bf16[1,16,896]{2,1,0:T(8,128)(2,1)S(1)}, bf16[1,16,896]{2,1,0:T(8,128)(2,1)S(1)}, u32[]{:S(2)}, u32[]{:S(2)}) collective-permute-start(bf16[1,16,896]{2,1,0:T(8,128)(2,1)S(1)} %bitcast.50), channel_id=1, source_target_pairs={{0,12},{1,13},{2,14},{3,15},{4,8},{5,9},{6,10},{7,11},{8,4},{9,5},... | collective-permute-start | bytes 86024 | tf_op jit(solution)/shard_map/ppermute | solution.py:46
  94.0 4.9 %collective-permute-start.18 = (bf16[4,16,896]{2,1,0:T(8,128)(2,1)S(1)}, bf16[4,16,896]{2,1,0:T(8,128)(2,1)S(1)}, u32[]{:S(2)}, u32[]{:S(2)}) collective-permute-start(bf16[4,16,896]{2,1,0:T(8,128)(2,1)S(1)} %pad_maximum_fusion), channel_id=1, source_target_pairs={{0,2},{1,3},{2,0},{3,1},{4,6},{5,7},{6,4},{7,5},{8,10},{9,11},{10,... | collective-permute-start | bytes 344072 | tf_op jit(solution)/shard_map/ppermute | solution.py:46
  98.8 1.6 %collective-permute-start.19 = (bf16[8,16,896]{2,1,0:T(8,128)(2,1)S(1)}, bf16[8,16,896]{2,1,0:T(8,128)(2,1)S(1)}, u32[]{:S(2)}, u32[]{:S(2)}) collective-permute-start(bf16[8,16,896]{2,1,0:T(8,128)(2,1)S(1)} %constant_dynamic-update-slice_fusion.21.near_ref), channel_id=1, source_target_pairs={{0,1},{1,0},{2,3},{3,2},{4,5},{5,4},{6,7},{7,6},{8,9},{9,8},{10,11... | collective-permute-start | bytes 688136 | tf_op jit(solution)/shard_map/ppermute | solution.py:46

commit v3 on v2

--- a/solution.py
+++ b/solution.py
@@ -7,13 +7,14 @@
 from jax.experimental.pallas import tpu as pltpu
 from jax.sharding import PartitionSpec as P
 
+
 NORM_EPSILON = 1e-05
 ROPE_BASE = 500000.0
 MASKED = -1e30
 
 
 LANES = 128
-FLOPS = {"table": 10**11, "finish": 10**11, "output": 10**11}
+FLOPS = {"begin": 10**11, "table": 10**11, "finish": 10**11, "output": 10**11, "relay": 10**11}
 VMEM = pl.BlockSpec(memory_space=pltpu.VMEM)
 SMEM = pl.BlockSpec(memory_space=pltpu.SMEM)
 
@@ -49,11 +50,21 @@
 def gathered(part):
     devices = lax.axis_size("ctx")
     held = part[None]
-    for stride, radix, _ in digits(devices)[:-1]:
-        held = jnp.concatenate(
-            [held] + [shifted(held, stride * digit) for digit in range(1, radix)], axis=0
-        )
-    return held, shifted(held, 1)
+    *rounds, last, _ = digits(devices)
+
+    def arrive(stride, radix):
+        return [shifted(held, stride * digit) for digit in range(1, radix)]
+
+    for stride, radix, _ in rounds:
+        held = jnp.concatenate([held] + arrive(stride, radix), axis=0)
+    brought = arrive(*last[:2])
+    near = jnp.concatenate([held] + brought, axis=0)
+    return held, brought, shifted(near, 1)
+
+
+def together(pieces):
+    held, brought, far = pieces
+    return jnp.concatenate([held, *brought, far], axis=0)
 
 
 def call(body, name, out_shape, args, scratch=(), flops=0):
@@ -66,70 +77,103 @@
         scratch_shapes=list(scratch),
         compiler_params=pltpu.CompilerParams(vmem_limit_bytes=6 << 20),
         cost_estimate=pl.CostEstimate(flops=FLOPS.get(name, flops), bytes_accessed=moved, transcendentals=0),
-        name=name,
     )(*args)
 
 
-def norm_factor(halves):
-    places, rows, width = halves[0].shape
-
-    def add(index, total):
-        for half in halves:
-            wide = half[index].astype(jnp.float32)
-            total = total + wide * wide
-        return total
-
-    total = lax.fori_loop(0, places, add, jnp.zeros((rows, width), jnp.float32), unroll=4)
-    mean = jnp.sum(total, axis=1, keepdims=True) / (2 * places * width)
-    return lax.rsqrt(mean + NORM_EPSILON)
-
-
-def products(device_ref, halves, value_of, weight_refs, total_refs):
-    places, _, depth = halves[0].shape
-    for total_ref in total_refs:
-        total_ref[...] = jnp.zeros_like(total_ref)
-
-    def step(index, carry):
-        for number, half in enumerate(halves):
-            mask = mask_at(index, 2 * places) + number
-            owner = lax.bitwise_xor(device_ref[0], mask)
-            block = value_of(half[index], owner)
+def accumulate(device_ref, devices, pieces, gain_ref, weight_refs, total_refs, square_ref):
+    for first, piece_ref in pieces:
+        places, _, depth = piece_ref.shape
+
+        def step(index, carry):
+            owner = lax.bitwise_xor(device_ref[0], mask_at(first + index, devices))
+            block = piece_ref[index]
+            if gain_ref is not None:
+                wide = block.astype(jnp.float32)
+                block = (wide * gain_ref[owner]).astype(jnp.bfloat16)
+                square_ref[...] += sum(
+                    wide[:, lane : lane + LANES] * wide[:, lane : lane + LANES]
+                    for lane in range(0, depth, LANES)
+                ) if depth % LANES == 0 else jnp.broadcast_to(
+                    jnp.sum(wide * wide, axis=1, keepdims=True) / LANES, square_ref.shape
+                )
             span = pl.ds(pl.multiple_of(owner * depth, depth), depth)
             for weight_ref, total_ref in zip(weight_refs, total_refs):
-                total_ref[...] += jnp.dot(
-                    block, weight_ref[span, :], preferred_element_type=jnp.float32
-                )
-        return carry
-
-    lax.fori_loop(0, places, step, 0, unroll=4)
-
-
-def normed_products(device_ref, halves, gain_ref, weight_refs, total_refs):
-    factor = norm_factor(halves)
-
-    def normed(block, owner):
-        return (block.astype(jnp.float32) * factor * gain_ref[owner]).astype(jnp.bfloat16)
-
-    products(device_ref, halves, normed, weight_refs, total_refs)
-
-
-def project_kernel(
-    device_ref, near_ref, far_ref, gain_ref, query_ref, key_ref, value_ref, cos_ref, sin_ref,
-    out_ref, query_total, key_total, value_total, joined,
-):
-    normed_products(
-        device_ref, (near_ref, far_ref), gain_ref,
-        (query_ref, key_ref, value_ref),
-        (query_total, key_total, value_total),
-    )
-    query_width = query_total.shape[1]
-    key_width = key_total.shape[1]
+                if weight_ref.shape[1] == devices * depth:
+                    total_ref[...] += lax.dot_general(
+                        block, weight_ref[:, span], (((1,), (1,)), ((), ())),
+                        preferred_element_type=jnp.float32,
+                    )
+                else:
+                    total_ref[...] += jnp.dot(
+                        block, weight_ref[span, :], preferred_element_type=jnp.float32
+                    )
+            return carry
+
+        lax.fori_loop(0, places, step, 0, unroll=4)
+
+
+def contract(name, pieces, own, weights, widths, gain, finish, extras, out_shape):
+    held, brought, far = pieces
+    devices = lax.axis_size("ctx")
+    _, rows, depth = held.shape
+    normed = gain is not None
+    gains = [gain.reshape(devices, 1, depth)] if normed else []
+    totals_of = [jax.ShapeDtypeStruct((rows, w), jnp.float32) for w in widths]
+    if normed:
+        totals_of.append(jax.ShapeDtypeStruct((rows, LANES), jnp.float32))
+    scratch = [pltpu.VMEM(t.shape, t.dtype) for t in totals_of]
+
+    def stage(label, first, parts, before, last):
+        def kernel(device_ref, *refs):
+            refs = list(refs)
+            take = lambda count: [refs.pop(0) for _ in range(count)]
+            part_refs, gain_refs, weight_refs = take(len(parts)), take(len(gains)), take(len(weights))
+            before_refs = take(len(before))
+            extra_refs = take(len(extras)) if last else []
+            out_refs = take(1 if last else 0)
+            total_refs = refs
+            for index, total_ref in enumerate(total_refs):
+                if before:
+                    total_ref[...] = before_refs[index][...]
+                else:
+                    total_ref[...] = jnp.zeros_like(total_ref)
+            place, placed = first, []
+            for part_ref in part_refs:
+                placed.append((place, part_ref))
+                place += part_ref.shape[0]
+            accumulate(
+                device_ref, devices, placed, gain_refs[0] if normed else None,
+                weight_refs, total_refs[: len(weights)], total_refs[-1],
+            )
+            if last:
+                factor = None
+                if normed:
+                    mean = jnp.sum(total_refs[-1][...], axis=1, keepdims=True) / (devices * depth)
+                    factor = lax.rsqrt(mean + NORM_EPSILON)
+                finish(factor, [t[...] for t in total_refs[: len(weights)]], extra_refs, out_refs[0])
+
+        return call(
+            kernel, name + label, out_shape if last else tuple(totals_of),
+            (own, *parts, *gains, *weights, *before, *(extras if last else ())),
+            scratch if last else (),
+            2 * rows * sum(p.shape[0] for p in parts) * depth * sum(widths),
+        )
+
+    near = held.shape[0]
+    sums = stage("_a", 0, [held], (), False)
+    sums = stage("_b", near, brought, sums, False)
+    return stage("_c", devices // 2, [far], sums, True)
+
+
+def project_finish(factor, totals, extra_refs, out_ref):
+    cos_ref, sin_ref = extra_refs
+    query, key, value = (factor * total for total in totals)
+    query_width = query.shape[1]
+    key_width = key.shape[1]
     used = query_width + 2 * key_width
-    joined[...] = jnp.zeros_like(joined)
-    joined[:, :query_width] = query_total[...]
-    joined[:, query_width : query_width + key_width] = key_total[...]
-    joined[:, query_width + key_width : used] = value_total[...]
-    columns = joined[...]
+    columns = jnp.concatenate(
+        [query, key, value, jnp.zeros((query.shape[0], cos_ref.shape[1] - used), jnp.float32)], axis=1
+    )
     width = columns.shape[1]
     lane = lax.broadcasted_iota(jnp.int32, columns.shape, 1)
     partner = jnp.where(
@@ -137,6 +181,19 @@
     )
     turned = columns * cos_ref[...] + partner * sin_ref[...]
     out_ref[...] = turned.astype(jnp.bfloat16)[:, :used]
+
+
+def gated_finish(factor, totals, extra_refs, out_ref):
+    gate, up = (factor * total for total in totals)
+    out_ref[...] = (gate / (1.0 + jnp.exp(-gate)) * up).astype(jnp.bfloat16)
+
+
+def down_finish(factor, totals, extra_refs, out_ref):
+    out_ref[...] = (extra_refs[0][...].astype(jnp.float32) + totals[0]).astype(jnp.bfloat16)
+
+
+def begin_kernel(device_ref, in_ref, out_ref):
+    out_ref[...] = in_ref[...]
 
 
 def attend_kernel(scale, query_ref, key_ref, value_ref, limit_ref, out_ref):
@@ -147,7 +204,7 @@
     devices = out_ref.shape[0]
     pairs = heads * rows // devices
     place = lax.broadcasted_iota(jnp.int32, (rows, span), 1)
-    visible = (place < limit_ref[...])[None]
+    visible = (place < limit_ref[:, :1])[None]
     for g in range(value_heads):
         lanes = pl.ds(g * head_dim, head_dim)
         queries = query_ref[g * group : (g + 1) * group].reshape(group * rows, head_dim)
@@ -222,21 +279,6 @@
     mid_ref[...] = (residual_ref[...].astype(jnp.float32) + total[...]).astype(jnp.bfloat16)
 
 
-def gated_kernel(
-    device_ref, near_ref, far_ref, gain_ref, gate_ref, up_ref, out_ref, gate_total, up_total
-):
-    normed_products(
-        device_ref, (near_ref, far_ref), gain_ref, (gate_ref, up_ref), (gate_total, up_total)
-    )
-    gate = gate_total[...]
-    out_ref[...] = (gate / (1.0 + jnp.exp(-gate)) * up_total[...]).astype(jnp.bfloat16)
-
-
-def down_kernel(device_ref, near_ref, far_ref, weight_ref, residual_ref, out_ref, total):
-    products(device_ref, (near_ref, far_ref), lambda block, _: block, (weight_ref,), (total,))
-    out_ref[...] = (residual_ref[...].astype(jnp.float32) + total[...]).astype(jnp.bfloat16)
-
-
 def rotation(first_col, width, positions, head_dim):
     col = jnp.arange(width, dtype=jnp.int32)
     in_head = ((first_col + col - col % 2) % head_dim).astype(jnp.float32)
@@ -263,6 +305,7 @@
 ):
     devices = lax.axis_size("ctx")
     device = lax.axis_index("ctx")
+    own = lax.optimization_barrier(device.astype(jnp.int32)[None])
     rows, width = hidden_in.shape
     span, value_heads, head_dim = rotated_prefix_keys.shape
     query_width = w_query.shape[1]
@@ -283,22 +326,20 @@
 
     used = query_width + 2 * key_width
     padded = -(-used // LANES) * LANES
-    query_cos, query_sin = rotation(device * query_width, query_width, positions, head_dim)
-    key_cos, key_sin = rotation(device * key_width, key_width, positions, head_dim)
+    query_cos, query_sin = rotation(own * query_width, query_width, positions, head_dim)
+    key_cos, key_sin = rotation(own * key_width, key_width, positions, head_dim)
     still = jnp.ones((rows, padded - query_width - key_width), jnp.float32)
     cosine = jnp.concatenate([query_cos, key_cos, still], axis=1)
     sine = jnp.concatenate([query_sin, key_sin, still * 0.0], axis=1)
     table = buffer(rows, padded, dtype=jnp.float32)
     cosine, sine = call(table_kernel, "table", (table, table), (cosine, sine), (), FLOPS["table"])
-    own = device.astype(jnp.int32)[None]
-    projected = call(
-        project_kernel, "project", buffer(rows, used),
-        (
-            own, *gathered(hidden_in), attn_gain.reshape(devices, 1, width),
-            w_query, w_key, w_value, cosine, sine,
-        ),
-        totals(query_width, key_width, key_width, padded),
-        2 * rows * devices * width * used,
+    begun = call(begin_kernel, "begin", buffer(rows, width), (own, hidden_in))
+    sides = (w_key, w_value)
+    if width % LANES == 0:
+        sides = (w_key.T, w_value.T)
+    projected = contract(
+        "project", gathered(begun), own, (w_query, *sides), (query_width, key_width, key_width),
+        attn_gain, project_finish, (cosine, sine), buffer(rows, used),
     )
     packed = exchange(jnp.broadcast_to(projected[None], (devices, rows, used)))
 
@@ -316,7 +357,7 @@
     key_new = unpacked(query_width, key_width)
     value_new = unpacked(query_width + key_width, key_width)
     pairs = heads * rows // devices
-    limit = (positions - device * span)[:, None]
+    limit = jnp.broadcast_to((positions - own * span)[:, None], (rows, LANES))
     sent = call(
         lambda *refs: attend_kernel(scale, *refs), "attend", buffer(devices, pairs + 8, LANES),
         (
@@ -355,7 +396,7 @@
         finish_kernel, "finish", buffer(pairs, head_dim), (numerator, denominator[:, None]), (),
         FLOPS["finish"],
     )
-    held = jnp.concatenate(gathered(attn_part), axis=0)
+    held = together(gathered(attn_part))
     attn_all = call(
         order_kernel, "order", buffer(devices, pairs, head_dim), (own, held)
     )
@@ -366,17 +407,14 @@
         2 * rows * heads * head_dim * width,
     )
     hidden_width = w_gate.shape[1]
-    hidden = call(
-        gated_kernel, "gated", buffer(rows, hidden_width),
-        (own, *gathered(mid_part), ffn_gain.reshape(devices, 1, width), w_gate, w_up),
-        totals(hidden_width, hidden_width),
-        4 * rows * devices * width * hidden_width,
-    )
-    return call(
-        down_kernel, "down", buffer(rows, width),
-        (own, *gathered(hidden), w_down, mid_part),
-        totals(width),
-        2 * rows * devices * hidden_width * width,
+    hidden = contract(
+        "gated", gathered(mid_part), own, (w_gate, w_up), (hidden_width, hidden_width),
+        ffn_gain, gated_finish, (), buffer(rows, hidden_width),
+    )
+    hidden = call(begin_kernel, "relay", buffer(rows, hidden_width), (own, hidden))
+    return contract(
+        "down", gathered(hidden), own, (w_down,), (width,),
+        None, down_finish, (mid_part,), buffer(rows, width),
     )
 
 

time: 104 us -> 92.4 us (0.89)
  local copies, waits for them, and re-layouts: 11.9 us -> 6.55 us
  waiting for transfers between devices: 46.3 us -> 42 us
  other arithmetic: 2.44 us -> 1.04 us
    unnamed x60 -> x50, local copies, waits for them, and re-layouts: 8.45 us -> 3.27 us
    ppermute x20, waiting for transfers between devices: 31.2 us -> 26.8 us  [shifted(): lax.ppermute(part, 'ctx', [(index, index ^ mask) for index in range(devic...]
    ppermute x20, starting transfers between devices: 22.7 us -> 21.4 us  [shifted(): lax.ppermute(part, 'ctx', [(index, index ^ mask) for index in range(devic...]
    pallas_call x8 -> x16, Pallas kernels: 12.3 us -> 12.5 us  [call(): pl.pallas_call(body, out_shape=out_shape, in_specs=[SMEM if a.dtype == jn...]
  transfers between devices with their start and end apart: 22 -> 22, of which waited for: 17 -> 18; matrix products, arithmetic and copies ran while one was open for 7% -> 3% of each run, Pallas kernels for 0% -> 4%
where the time goes in v3:
time: 92.4 us; the launch traced here: 91.9 us
  waiting for transfers between devices  42 us (45%)
  starting transfers between devices  29.3 us (32%)
  Pallas kernels  12.5 us (14%)
  local copies, waits for them, and re-layouts  6.55 us (7%)
  other arithmetic  1.04 us (1%)
    ppermute x20, waiting for transfers between devices, shifted(): lax.ppermute(part, 'ctx', [(index, index ^ mask) for index in range(devic...  26.8 us
    ppermute x20, starting transfers between devices, shifted(): lax.ppermute(part, 'ctx', [(index, index ^ mask) for index in range(devic...  21.4 us
    all_to_all x2, waiting for transfers between devices, exchange(): return lax.all_to_all(blocks, 'ctx', 0, 0)  15.2 us
    pallas_call x16, Pallas kernels, call(): pl.pallas_call(body, out_shape=out_shape, in_specs=[SMEM if a.dtype == jn...  12.5 us
    all_to_all x2, starting transfers between devices, exchange(): return lax.all_to_all(blocks, 'ctx', 0, 0)  7.98 us
    unnamed x50, local copies, waits for them, and re-layouts  3.27 us
  transfers between devices with their start and end apart: 22, of which 18 were waited for; matrix products, arithmetic and copies ran while one was open for 3% of the time, Pallas kernels for 4%

profile of v3, /device:TPU:0, one launch (start us, length us, event | category | flops | bytes accessed | tf_op | source)
XLA Modules:
  0.0 91.9 jit_solution(14886930015273612863)
XLA Ops:
  0.0 0.7 copy-done.8
  0.7 5.1 %collective-permute-start.2 = (bf16[1,16,512]{2,1,0:T(8,128)(2,1)S(1)}, bf16[1,16,512]{2,1,0:T(8,128)(2,1)S(1)}, u32[]{:S(2)}, u32[]{:S(2)}) collective-permute-start(bf16[1,16,512]{2,1,0:T(8,128)(2,1)S(1)} %bitcast.68), channel_id=1, source_target_pairs={{0,12},{1,13},{2,14},{3,15},{4,8},{5,9},{6,10},{7,11},{8,4},{9,5},... | collective-permute-start | bytes 49160 | tf_op jit(solution)/shard_map/ppermute | solution.py:47
  5.8 0.6 collective-permute-start
  6.6 0.2 select_reduce_fusion
  6.8 0.1 multiply_sine_fusion.1
  7.0 0.1 multiply_sine_fusion
  7.1 0.4 collective-permute-done.2
  7.5 2.9 %collective-permute-done.1 = bf16[1,16,512]{2,1,0:T(8,128)(2,1)S(1)} collective-permute-done((bf16[1,16,512]{2,1,0:T(8,128)(2,1)S(1)}, bf16[1,16,512]{2,1,0:T(8,128)(2,1)S(1)}, u32[]{:S(2)}, u32[]{:S(2)}) %collective-permute-start.1) | collective-permute-done | bytes 16416 | tf_op jit(solution)/shard_map/ppermute | solution.py:47
  10.5 1.6 %collective-permute-start.3 = (bf16[4,16,512]{2,1,0:T(8,128)(2,1)S(1)}, bf16[4,16,512]{2,1,0:T(8,128)(2,1)S(1)}, u32[]{:S(2)}, u32[]{:S(2)}) collective-permute-start(bf16[4,16,512]{2,1,0:T(8,128)(2,1)S(1)} %pad_maximum_fusion.1.refs_0_), channel_id=1, source_target_pairs={{0,2},{1,3},{2,0},{3,1},{4,6},{5,7},{6,4},{7,5},{8,10},{9,11},{10,... | collective-permute-start | bytes 196616 | tf_op jit(solution)/shard_map/ppermute | solution.py:47
  12.1 2.7 %collective-permute-done.3.refs_0_ = bf16[4,16,512]{2,1,0:T(8,128)(2,1)S(1)} collective-permute-done((bf16[4,16,512]{2,1,0:T(8,128)(2,1)S(1)}, bf16[4,16,512]{2,1,0:T(8,128)(2,1)S(1)}, u32[]{:S(2)}, u32[]{:S(2)}) %collective-permute-start.3) | collective-permute-done | bytes 65568 | tf_op jit(solution)/shard_map/ppermute | solution.py:47
  14.9 2.1 %copy-done.2 = bf16[8192,256]{1,0:T(8,128)(2,1)S(1)} copy-done((bf16[8192,256]{1,0:T(8,128)(2,1)S(1)}, bf16[8192,256]{1,0:T(8,128)(2,1)}, u32[]{:S(2)}) %copy-start.2) | copy-done | bytes 4194328
  17.0 0.1 copy-done.3
  17.1 0.2 copy-done.4
  17.3 0.3 shard_map.137
  17.6 0.3 shard_map.138
  17.9 0.8 shard_map.140
  18.8 0.7 broadcast_in_dim.72
  19.5 4.5 %all-to-all-start = ((bf16[16,16,320]{2,1,0:T(8,128)(2,1)}), bf16[16,16,320]{2,1,0:T(8,128)(2,1)S(1)}, u32[]{:S(2)}, u32[]{:S(2)}) async-start(bf16[16,16,320]{2,1,0:T(8,128)(2,1)} %broadcast_in_dim.72), calls=%async_computation | async-start | bytes 393216 | tf_op jit(solution)/shard_map/all_to_all | solution.py:23
  24.0 1.6 %copy_bitcast_fusion = (bf16[1024,512]{1,0:T(8,128)(2,1)S(1)}, bf16[1024,512]{1,0:T(8,128)(2,1)S(1)}) fusion(bf16[128,8,4,128]{3,2,1,0:T(4,128)(2,1)S(1)} %bitcast.76, bf16[128,8,4,128]{3,2,1,0:T(4,128)(2,1)} %bitcast.77), kind=kLoop, calls=%fused_computation | loop fusion | bytes 4194304 | tf_op jit(solution)/shard_map/reshape | solution.py:366
  25.6 7.4 %all-to-all-done = bf16[16,16,320]{2,1,0:T(8,128)(2,1)S(1)} async-done(((bf16[16,16,320]{2,1,0:T(8,128)(2,1)}), bf16[16,16,320]{2,1,0:T(8,128)(2,1)S(1)}, u32[]{:S(2)}, u32[]{:S(2)}) %all-to-all-start) | async-done | bytes 163872 | tf_op jit(solution)/shard_map/all_to_all | solution.py:23
  33.1 2.3 %shard_map.141 = bf16[16,40,128]{2,1,0:T(8,128)(2,1)} custom-call(bf16[32,16,128]{2,1,0:T(8,128)(2,1)S(1)} %bitcast.51, bf16[1024,512]{1,0:T(8,128)(2,1)S(1)} %get-tuple-element.65.refs_1_, bf16[1024,512]{1,0:T(8,128)(2,1)S(1)} %get-tuple-element.64.refs_2_, s32[16,128]{1,0:T(8,128)S(1)} %broadcast_in_dim.73.refs_3_), custom_call_target="tpu_custom_call" | custom-call | flops 268435456 | bytes 2236416 | tf_op jit(solution)/shard_map/pallas_call | solution.py:72
  35.4 3.5 %all-to-all-start.1 = ((bf16[16,40,128]{2,1,0:T(8,128)(2,1)}), bf16[16,40,128]{2,1,0:T(8,128)(2,1)S(1)}, u32[]{:S(2)}, u32[]{:S(2)}) async-start(bf16[16,40,128]{2,1,0:T(8,128)(2,1)} %shard_map.141), calls=%async_computation.1 | async-start | bytes 327680 | tf_op jit(solution)/shard_map/all_to_all | solution.py:23
  38.9 0.1 fusion.18
  39.1 0.1 broadcast_in_dim.76
  39.2 0.1 broadcast_in_dim.74
  39.3 0.1 multiply_reduce_fusion.1
  39.5 7.9 %all-to-all-done.1 = bf16[16,40,128]{2,1,0:T(8,128)(2,1)S(1)} async-done(((bf16[16,40,128]{2,1,0:T(8,128)(2,1)}), bf16[16,40,128]{2,1,0:T(8,128)(2,1)S(1)}, u32[]{:S(2)}, u32[]{:S(2)}) %all-to-all-start.1) | async-done | bytes 163872 | tf_op jit(solution)/shard_map/all_to_all | solution.py:23
  47.3 0.1 dynamic-slice_convert_fusion
  47.5 0.1 copy.46
  47.6 0.1 copy.45
  47.7 0.1 copy.44
  47.8 0.1 multiply_reduce_fusion
  48.1 0.8 collective-permute-start.7
  48.9 3.6 %collective-permute-start.5 = (bf16[1,32,128]{2,1,0:T(8,128)(2,1)S(1)}, bf16[1,32,128]{2,1,0:T(8,128)(2,1)S(1)}, u32[]{:S(2)}, u32[]{:S(2)}) collective-permute-start(bf16[1,32,128]{2,1,0:T(8,128)(2,1)S(1)} %bitcast.74), channel_id=1, source_target_pairs={{0,4},{1,5},{2,6},{3,7},{4,0},{5,1},{6,2},{7,3},{8,12},{9,13},{10,... | collective-permute-start | bytes 24584 | tf_op jit(solution)/shard_map/ppermute | solution.py:47
  52.5 1.1 %collective-permute-done.7 = bf16[1,32,128]{2,1,0:T(8,128)(2,1)S(1)} collective-permute-done((bf16[1,32,128]{2,1,0:T(8,128)(2,1)S(1)}, bf16[1,32,128]{2,1,0:T(8,128)(2,1)S(1)}, u32[]{:S(2)}, u32[]{:S(2)}) %collective-permute-start.7) | collective-permute-done | bytes 8224 | tf_op jit(solution)/shard_map/ppermute | solution.py:47
  53.7 0.5 collective-permute-done.5
  54.2 0.3 collective-permute-start.8
  54.5 3.7 %collective-permute-done.8 = bf16[4,32,128]{2,1,0:T(8,128)(2,1)S(1)} collective-permute-done((bf16[4,32,128]{2,1,0:T(8,128)(2,1)S(1)}, bf16[4,32,128]{2,1,0:T(8,128)(2,1)S(1)}, u32[]{:S(2)}, u32[]{:S(2)}) %collective-permute-start.8) | collective-permute-done | bytes 32800 | tf_op jit(solution)/shard_map/ppermute | solution.py:47
  58.3 1.2 %collective-permute-done.9 = bf16[8,32,128]{2,1,0:T(8,128)(2,1)S(1)} collective-permute-done((bf16[8,32,128]{2,1,0:T(8,128)(2,1)S(1)}, bf16[8,32,128]{2,1,0:T(8,128)(2,1)S(1)}, u32[]{:S(2)}, u32[]{:S(2)}) %collective-permute-start.9) | collective-permute-done | bytes 65568 | tf_op jit(solution)/shard_map/ppermute | solution.py:47
  59.5 0.3 shard_map.143
  59.8 1.0 %shard_map.144.refs_3_ = bf16[16,512]{1,0:T(8,128)(2,1)S(1)} custom-call(bf16[32,16,128]{2,1,0:T(8,128)(2,1)S(1)} %bitcast.63, bf16[4096,512]{1,0:T(8,128)(2,1)S(1)} %copy-done.7, bf16[16,512]{1,0:T(8,128)(2,1)S(1)} %copy-done.9), custom_call_target="tpu_custom_call" | custom-call | flops 99999997952 | bytes 4341760 | tf_op jit(solution)/shard_map/pallas_call | solution.py:72
  60.8 2.4 %collective-permute-start.12 = (bf16[1,16,512]{2,1,0:T(8,128)(2,1)S(1)}, bf16[1,16,512]{2,1,0:T(8,128)(2,1)S(1)}, u32[]{:S(2)}, u32[]{:S(2)}) collective-permute-start(bf16[1,16,512]{2,1,0:T(8,128)(2,1)S(1)} %bitcast.59), channel_id=1, source_target_pairs={{0,12},{1,13},{2,14},{3,15},{4,8},{5,9},{6,10},{7,11},{8,4},{9,5},... | collective-permute-start | bytes 49160 | tf_op jit(solution)/shard_map/ppermute | solution.py:47
  63.2 1.1 %collective-permute-start.11 = (bf16[1,16,512]{2,1,0:T(8,128)(2,1)S(1)}, bf16[1,16,512]{2,1,0:T(8,128)(2,1)S(1)}, u32[]{:S(2)}, u32[]{:S(2)}) collective-permute-start(bf16[1,16,512]{2,1,0:T(8,128)(2,1)S(1)} %bitcast.60), channel_id=1, source_target_pairs={{0,8},{1,9},{2,10},{3,11},{4,12},{5,13},{6,14},{7,15},{8,0},{9,1},... | collective-permute-start | bytes 49160 | tf_op jit(solution)/shard_map/ppermute | solution.py:47
  64.3 0.9 collective-permute-start.10
  65.3 1.2 %collective-permute-done.12 = bf16[1,16,512]{2,1,0:T(8,128)(2,1)S(1)} collective-permute-done((bf16[1,16,512]{2,1,0:T(8,128)(2,1)S(1)}, bf16[1,16,512]{2,1,0:T(8,128)(2,1)S(1)}, u32[]{:S(2)}, u32[]{:S(2)}) %collective-permute-start.12) | collective-permute-done | bytes 16416 | tf_op jit(solution)/shard_map/ppermute | solution.py:47
  66.4 1.5 %collective-permute-done.11 = bf16[1,16,512]{2,1,0:T(8,128)(2,1)S(1)} collective-permute-done((bf16[1,16,512]{2,1,0:T(8,128)(2,1)S(1)}, bf16[1,16,512]{2,1,0:T(8,128)(2,1)S(1)}, u32[]{:S(2)}, u32[]{:S(2)}) %collective-permute-start.11) | collective-permute-done | bytes 16416 | tf_op jit(solution)/shard_map/ppermute | solution.py:47
  67.9 0.2 collective-permute-done.10
  68.1 0.1 collective-permute-start.13
  68.2 4.2 %collective-permute-done.13.refs_0_ = bf16[4,16,512]{2,1,0:T(8,128)(2,1)S(1)} collective-permute-done((bf16[4,16,512]{2,1,0:T(8,128)(2,1)S(1)}, bf16[4,16,512]{2,1,0:T(8,128)(2,1)S(1)}, u32[]{:S(2)}, u32[]{:S(2)}) %collective-permute-start.13) | collective-permute-done | bytes 65568 | tf_op jit(solution)/shard_map/ppermute | solution.py:47
  72.5 1.1 %shard_map.145 = (f32[16,896]{1,0:T(8,128)S(1)}, f32[16,896]{1,0:T(8,128)S(1)}, f32[16,128]{1,0:T(8,128)S(1)}) custom-call(s32[1]{0:T(128)} %bitcast.device_ref, bf16[4,16,512]{2,1,0:T(8,128)(2,1)S(1)} %pad_maximum_fusion.2.refs_0_, f32[16,1,512]{2,1,0:T(1,128)S(1)} %bitcast.56, bf16[8192,896]{1,0:T(8,128)(2,1)S(1)} %copy-done, bf16[8192,896]{1,0:T(8,128)(2,1)S(1)} %copy-done.1), custom_call_target="tpu_custom_call" | custom-call | flops 117440512 | bytes 29458436 | tf_op jit(solution)/shard_map/pallas_call | solution.py:72
  73.5 1.1 %shard_map.146 = (f32[16,896]{1,0:T(8,128)S(1)}, f32[16,896]{1,0:T(8,128)S(1)}, f32[16,128]{1,0:T(8,128)S(1)}) custom-call(s32[1]{0:T(128)} %bitcast.device_ref, bf16[4,16,512]{2,1,0:T(8,128)(2,1)S(1)} %collective-permute-done.13.refs_0_, f32[16,1,512]{2,1,0:T(1,128)S(1)} %bitcast.57, bf16[8192,896]{1,0:T(8,128)(2,1)S(1)} %copy-done, ...), custom_call_target="tpu_custom_call" | custom-call | flops 117440512 | bytes 29581316 | tf_op jit(solution)/shard_map/pallas_call | solution.py:72
  74.6 2.2 %shard_map.147.in_ref = bf16[16,896]{1,0:T(8,128)(2,1)S(1)} custom-call(s32[1]{0:T(128)} %bitcast.device_ref, bf16[8,16,512]{2,1,0:T(8,128)(2,1)S(1)} %collective-permute-done.14.refs_0_, f32[16,1,512]{2,1,0:T(1,128)S(1)} %bitcast.58, bf16[8192,896]{1,0:T(8,128)(2,1)S(1)} %copy-done, bf16[8192,896]{1,0:T(8,128)(2,1)S(1)} %copy-done.1, ...), custom_call_target="tpu_custom_call" | custom-call | flops 234881024 | bytes 29646852 | tf_op jit(solution)/shard_map/pallas_call | solution.py:72
  76.9 1.5 %collective-permute-start.17 = (bf16[1,16,896]{2,1,0:T(8,128)(2,1)S(1)}, bf16[1,16,896]{2,1,0:T(8,128)(2,1)S(1)}, u32[]{:S(2)}, u32[]{:S(2)}) collective-permute-start(bf16[1,16,896]{2,1,0:T(8,128)(2,1)S(1)} %bitcast.64), channel_id=1, source_target_pairs={{0,12},{1,13},{2,14},{3,15},{4,8},{5,9},{6,10},{7,11},{8,4},{9,5},... | collective-permute-start | bytes 86024 | tf_op jit(solution)/shard_map/ppermute | solution.py:47
  78.4 1.0 %collective-permute-start.16 = (bf16[1,16,896]{2,1,0:T(8,128)(2,1)S(1)}, bf16[1,16,896]{2,1,0:T(8,128)(2,1)S(1)}, u32[]{:S(2)}, u32[]{:S(2)}) collective-permute-start(bf16[1,16,896]{2,1,0:T(8,128)(2,1)S(1)} %bitcast.65), channel_id=1, source_target_pairs={{0,8},{1,9},{2,10},{3,11},{4,12},{5,13},{6,14},{7,15},{8,0},{9,1},... | collective-permute-start | bytes 86024 | tf_op jit(solution)/shard_map/ppermute | solution.py:47
  79.3 2.0 %collective-permute-start.15 = (bf16[1,16,896]{2,1,0:T(8,128)(2,1)S(1)}, bf16[1,16,896]{2,1,0:T(8,128)(2,1)S(1)}, u32[]{:S(2)}, u32[]{:S(2)}) collective-permute-start(bf16[1,16,896]{2,1,0:T(8,128)(2,1)S(1)} %bitcast.66), channel_id=1, source_target_pairs={{0,4},{1,5},{2,6},{3,7},{4,0},{5,1},{6,2},{7,3},{8,12},{9,13},{10,... | collective-permute-start | bytes 86024 | tf_op jit(solution)/shard_map/ppermute | solution.py:47
  81.4 1.4 %collective-permute-done.17 = bf16[1,16,896]{2,1,0:T(8,128)(2,1)S(1)} collective-permute-done((bf16[1,16,896]{2,1,0:T(8,128)(2,1)S(1)}, bf16[1,16,896]{2,1,0:T(8,128)(2,1)S(1)}, u32[]{:S(2)}, u32[]{:S(2)}) %collective-permute-start.17) | collective-permute-done | bytes 28704 | tf_op jit(solution)/shard_map/ppermute | solution.py:47
  82.8 0.7 collective-permute-done.16
  83.5 0.2 collective-permute-done.15
  83.7 0.3 collective-permute-start.18
  84.0 4.6 %collective-permute-done.18.refs_0_ = bf16[4,16,896]{2,1,0:T(8,128)(2,1)S(1)} collective-permute-done((bf16[4,16,896]{2,1,0:T(8,128)(2,1)S(1)}, bf16[4,16,896]{2,1,0:T(8,128)(2,1)S(1)}, u32[]{:S(2)}, u32[]{:S(2)}) %collective-permute-start.18) | collective-permute-done | bytes 114720 | tf_op jit(solution)/shard_map/ppermute | solution.py:47
  88.7 0.6 shard_map.149.refs_2_
  89.3 0.6 shard_map.150.refs_2_
  89.9 0.3 collective-permute-done.19.refs_0_
  90.1 1.8 %shard_map.151 = bf16[16,512]{1,0:T(8,128)(2,1)} custom-call(s32[1]{0:T(128)} %bitcast.device_ref, bf16[8,16,896]{2,1,0:T(8,128)(2,1)S(1)} %collective-permute-done.19.refs_0_, bf16[14336,512]{1,0:T(8,128)(2,1)S(1)} %bitcast.44, f32[16,512]{1,0:T(8,128)S(1)} %shard_map.150.refs_2_, bf16[16,512]{1,0:T(8,128)(2,1)S(1)} %shard_map.144.refs_3_), custom_call_target="tpu_custom_call" | custom-call | flops 117440512 | bytes 14958596 | tf_op jit(solution)/shard_map/pallas_call | solution.py:72
  (93 shorter events, 1.1 us)
Async XLA Ops:
  0.0 0.7 copy-start.8
  0.7 5.9 %copy-start.11 = (s32[16]{0:T(128)S(1)}, s32[16]{0:T(128)}, u32[]{:S(2)}) copy-start(s32[16]{0:T(128)} %param.26) | copy-start | bytes 196
  0.7 5.9 %copy-start.12 = (s32[16]{0:T(128)S(1)}, s32[16]{0:T(128)}, u32[]{:S(2)}) copy-start(s32[16]{0:T(128)} %param.27) | copy-start | bytes 196
  0.7 6.8 %collective-permute-start.2 = (bf16[1,16,512]{2,1,0:T(8,128)(2,1)S(1)}, bf16[1,16,512]{2,1,0:T(8,128)(2,1)S(1)}, u32[]{:S(2)}, u32[]{:S(2)}) collective-permute-start(bf16[1,16,512]{2,1,0:T(8,128)(2,1)S(1)} %bitcast.68), channel_id=1, source_target_pairs={{0,12},{1,13},{2,14},{3,15},{4,8},{5,9},{6,10},{7,11},{8,4},{9,5},... | collective-permute-start | bytes 49160 | tf_op jit(solution)/shard_map/ppermute | solution.py:47
  5.8 4.6 %collective-permute-start.1 = (bf16[1,16,512]{2,1,0:T(8,128)(2,1)S(1)}, bf16[1,16,512]{2,1,0:T(8,128)(2,1)S(1)}, u32[]{:S(2)}, u32[]{:S(2)}) collective-permute-start(bf16[1,16,512]{2,1,0:T(8,128)(2,1)S(1)} %bitcast.69), channel_id=1, source_target_pairs={{0,8},{1,9},{2,10},{3,11},{4,12},{5,13},{6,14},{7,15},{8,0},{9,1},... | collective-permute-start | bytes 49160 | tf_op jit(solution)/shard_map/ppermute | solution.py:47
  5.8 4.6 %collective-permute-start = (bf16[1,16,512]{2,1,0:T(8,128)(2,1)S(1)}, bf16[1,16,512]{2,1,0:T(8,128)(2,1)S(1)}, u32[]{:S(2)}, u32[]{:S(2)}) collective-permute-start(bf16[1,16,512]{2,1,0:T(8,128)(2,1)S(1)} %bitcast.70), channel_id=1, source_target_pairs={{0,4},{1,5},{2,6},{3,7},{4,0},{5,1},{6,2},{7,3},{8,12},{9,13},{10,... | collective-permute-start | bytes 49160 | tf_op jit(solution)/shard_map/ppermute | solution.py:47
  10.5 4.3 %collective-permute-start.3 = (bf16[4,16,512]{2,1,0:T(8,128)(2,1)S(1)}, bf16[4,16,512]{2,1,0:T(8,128)(2,1)S(1)}, u32[]{:S(2)}, u32[]{:S(2)}) collective-permute-start(bf16[4,16,512]{2,1,0:T(8,128)(2,1)S(1)} %pad_maximum_fusion.1.refs_0_), channel_id=1, source_target_pairs={{0,2},{1,3},{2,0},{3,1},{4,6},{5,7},{6,4},{7,5},{8,10},{9,11},{10,... | collective-permute-start | bytes 196616 | tf_op jit(solution)/shard_map/ppermute | solution.py:47
  14.8 3.1 %collective-permute-start.4 = (bf16[8,16,512]{2,1,0:T(8,128)(2,1)S(1)}, bf16[8,16,512]{2,1,0:T(8,128)(2,1)S(1)}, u32[]{:S(2)}, u32[]{:S(2)}) collective-permute-start(bf16[8,16,512]{2,1,0:T(8,128)(2,1)S(1)} %constant_dynamic-update-slice_fusion), channel_id=1, source_target_pairs={{0,1},{1,0},{2,3},{3,2},{4,5},{5,4},{6,7},{7,6},{8,9},{9,8},{10,11... | collective-permute-start | bytes 393224 | tf_op jit(solution)/shard_map/ppermute | solution.py:47
  14.8 2.2 %copy-start.2 = (bf16[8192,256]{1,0:T(8,128)(2,1)S(1)}, bf16[8192,256]{1,0:T(8,128)(2,1)}, u32[]{:S(2)}) copy-start(bf16[8192,256]{1,0:T(8,128)(2,1)} %refs_2_.8) | copy-start | bytes 12582916
  14.8 2.3 %copy-start.3 = (bf16[8192,32]{0,1:T(8,128)(2,1)S(1)}, bf16[8192,32]{0,1:T(8,128)(2,1)}, u32[]{:S(2)}) copy-start(bf16[8192,32]{0,1:T(8,128)(2,1)} %param.17) | copy-start | bytes 1572868
  14.8 2.4 %copy-start.4 = (bf16[8192,32]{0,1:T(8,128)(2,1)S(1)}, bf16[8192,32]{0,1:T(8,128)(2,1)}, u32[]{:S(2)}) copy-start(bf16[8192,32]{0,1:T(8,128)(2,1)} %param.18) | copy-start | bytes 1572868
  14.8 2.4 %copy-start.5 = (f32[8192]{0:T(1024)S(1)}, f32[8192]{0:T(1024)}, u32[]{:S(2)}) copy-start(f32[8192]{0:T(1024)} %param.15) | copy-start | bytes 98308
  14.9 9.1 %copy-start.10 = (bf16[1024,4,128]{2,1,0:T(4,128)(2,1)S(1)}, bf16[1024,4,128]{2,1,0:T(4,128)(2,1)}, u32[]{:S(2)}) copy-start(bf16[1024,4,128]{2,1,0:T(4,128)(2,1)} %param.20) | copy-start | bytes 3145732
  19.5 13.4 %all-to-all-start = ((bf16[16,16,320]{2,1,0:T(8,128)(2,1)}), bf16[16,16,320]{2,1,0:T(8,128)(2,1)S(1)}, u32[]{:S(2)}, u32[]{:S(2)}) async-start(bf16[16,16,320]{2,1,0:T(8,128)(2,1)} %broadcast_in_dim.72), calls=%async_computation | async-start | bytes 393216 | tf_op jit(solution)/shard_map/all_to_all | solution.py:23
  35.4 11.9 %all-to-all-start.1 = ((bf16[16,40,128]{2,1,0:T(8,128)(2,1)}), bf16[16,40,128]{2,1,0:T(8,128)(2,1)S(1)}, u32[]{:S(2)}, u32[]{:S(2)}) async-start(bf16[16,40,128]{2,1,0:T(8,128)(2,1)} %shard_map.141), calls=%async_computation.1 | async-start | bytes 327680 | tf_op jit(solution)/shard_map/all_to_all | solution.py:23
  48.0 11.8 %copy-start.7 = (bf16[4096,512]{1,0:T(8,128)(2,1)S(1)}, bf16[4096,512]{1,0:T(8,128)(2,1)}, u32[]{:S(2)}) copy-start(bf16[4096,512]{1,0:T(8,128)(2,1)} %weight_ref.1) | copy-start | bytes 12582916
  48.0 11.8 %copy-start.9 = (bf16[16,512]{1,0:T(8,128)(2,1)S(1)}, bf16[16,512]{1,0:T(8,128)(2,1)}, u32[]{:S(2)}) copy-start(bf16[16,512]{1,0:T(8,128)(2,1)} %residual_ref.1) | copy-start | bytes 49156
  48.1 5.6 %collective-permute-start.7 = (bf16[1,32,128]{2,1,0:T(8,128)(2,1)S(1)}, bf16[1,32,128]{2,1,0:T(8,128)(2,1)S(1)}, u32[]{:S(2)}, u32[]{:S(2)}) collective-permute-start(bf16[1,32,128]{2,1,0:T(8,128)(2,1)S(1)} %bitcast.72), channel_id=1, source_target_pairs={{0,12},{1,13},{2,14},{3,15},{4,8},{5,9},{6,10},{7,11},{8,4},{9,5},... | collective-permute-start | bytes 24584 | tf_op jit(solution)/shard_map/ppermute | solution.py:47
  48.9 4.8 %collective-permute-start.6 = (bf16[1,32,128]{2,1,0:T(8,128)(2,1)S(1)}, bf16[1,32,128]{2,1,0:T(8,128)(2,1)S(1)}, u32[]{:S(2)}, u32[]{:S(2)}) collective-permute-start(bf16[1,32,128]{2,1,0:T(8,128)(2,1)S(1)} %bitcast.73), channel_id=1, source_target_pairs={{0,8},{1,9},{2,10},{3,11},{4,12},{5,13},{6,14},{7,15},{8,0},{9,1},... | collective-permute-start | bytes 24584 | tf_op jit(solution)/shard_map/ppermute | solution.py:47
  48.9 5.3 %collective-permute-start.5 = (bf16[1,32,128]{2,1,0:T(8,128)(2,1)S(1)}, bf16[1,32,128]{2,1,0:T(8,128)(2,1)S(1)}, u32[]{:S(2)}, u32[]{:S(2)}) collective-permute-start(bf16[1,32,128]{2,1,0:T(8,128)(2,1)S(1)} %bitcast.74), channel_id=1, source_target_pairs={{0,4},{1,5},{2,6},{3,7},{4,0},{5,1},{6,2},{7,3},{8,12},{9,13},{10,... | collective-permute-start | bytes 24584 | tf_op jit(solution)/shard_map/ppermute | solution.py:47
  54.2 4.0 %collective-permute-start.8 = (bf16[4,32,128]{2,1,0:T(8,128)(2,1)S(1)}, bf16[4,32,128]{2,1,0:T(8,128)(2,1)S(1)}, u32[]{:S(2)}, u32[]{:S(2)}) collective-permute-start(bf16[4,32,128]{2,1,0:T(8,128)(2,1)S(1)} %pad_maximum_fusion.3), channel_id=1, source_target_pairs={{0,2},{1,3},{2,0},{3,1},{4,6},{5,7},{6,4},{7,5},{8,10},{9,11},{10,... | collective-permute-start | bytes 98312 | tf_op jit(solution)/shard_map/ppermute | solution.py:47
  58.2 1.3 %collective-permute-start.9 = (bf16[8,32,128]{2,1,0:T(8,128)(2,1)S(1)}, bf16[8,32,128]{2,1,0:T(8,128)(2,1)S(1)}, u32[]{:S(2)}, u32[]{:S(2)}) collective-permute-start(bf16[8,32,128]{2,1,0:T(8,128)(2,1)S(1)} %get-tuple-element.43), channel_id=1, source_target_pairs={{0,1},{1,0},{2,3},{3,2},{4,5},{5,4},{6,7},{7,6},{8,9},{9,8},{10,11... | collective-permute-start | bytes 196616 | tf_op jit(solution)/shard_map/ppermute | solution.py:47
  59.8 12.7 %copy-start = (bf16[8192,896]{1,0:T(8,128)(2,1)S(1)}, bf16[8192,896]{1,0:T(8,128)(2,1)}, u32[]{:S(2)}) copy-start(bf16[8192,896]{1,0:T(8,128)(2,1)} %refs_2_.11) | copy-start | bytes 44040196
  59.8 12.7 %copy-start.1 = (bf16[8192,896]{1,0:T(8,128)(2,1)S(1)}, bf16[8192,896]{1,0:T(8,128)(2,1)}, u32[]{:S(2)}) copy-start(bf16[8192,896]{1,0:T(8,128)(2,1)} %refs_3_.5) | copy-start | bytes 44040196
  59.8 12.7 %copy-start.6 = (f32[8192]{0:T(1024)S(1)}, f32[8192]{0:T(1024)}, u32[]{:S(2)}) copy-start(f32[8192]{0:T(1024)} %param.22) | copy-start | bytes 98308
  60.8 5.6 %collective-permute-start.12 = (bf16[1,16,512]{2,1,0:T(8,128)(2,1)S(1)}, bf16[1,16,512]{2,1,0:T(8,128)(2,1)S(1)}, u32[]{:S(2)}, u32[]{:S(2)}) collective-permute-start(bf16[1,16,512]{2,1,0:T(8,128)(2,1)S(1)} %bitcast.59), channel_id=1, source_target_pairs={{0,12},{1,13},{2,14},{3,15},{4,8},{5,9},{6,10},{7,11},{8,4},{9,5},... | collective-permute-start | bytes 49160 | tf_op jit(solution)/shard_map/ppermute | solution.py:47
  63.2 4.6 %collective-permute-start.11 = (bf16[1,16,512]{2,1,0:T(8,128)(2,1)S(1)}, bf16[1,16,512]{2,1,0:T(8,128)(2,1)S(1)}, u32[]{:S(2)}, u32[]{:S(2)}) collective-permute-start(bf16[1,16,512]{2,1,0:T(8,128)(2,1)S(1)} %bitcast.60), channel_id=1, source_target_pairs={{0,8},{1,9},{2,10},{3,11},{4,12},{5,13},{6,14},{7,15},{8,0},{9,1},... | collective-permute-start | bytes 49160 | tf_op jit(solution)/shard_map/ppermute | solution.py:47
  64.3 3.7 %collective-permute-start.10 = (bf16[1,16,512]{2,1,0:T(8,128)(2,1)S(1)}, bf16[1,16,512]{2,1,0:T(8,128)(2,1)S(1)}, u32[]{:S(2)}, u32[]{:S(2)}) collective-permute-start(bf16[1,16,512]{2,1,0:T(8,128)(2,1)S(1)} %bitcast.61), channel_id=1, source_target_pairs={{0,4},{1,5},{2,6},{3,7},{4,0},{5,1},{6,2},{7,3},{8,12},{9,13},{10,... | collective-permute-start | bytes 49160 | tf_op jit(solution)/shard_map/ppermute | solution.py:47
  68.1 4.3 %collective-permute-start.13 = (bf16[4,16,512]{2,1,0:T(8,128)(2,1)S(1)}, bf16[4,16,512]{2,1,0:T(8,128)(2,1)S(1)}, u32[]{:S(2)}, u32[]{:S(2)}) collective-permute-start(bf16[4,16,512]{2,1,0:T(8,128)(2,1)S(1)} %pad_maximum_fusion.2.refs_0_), channel_id=1, source_target_pairs={{0,2},{1,3},{2,0},{3,1},{4,6},{5,7},{6,4},{7,5},{8,10},{9,11},{10,... | collective-permute-start | bytes 196616 | tf_op jit(solution)/shard_map/ppermute | solution.py:47
  72.4 2.2 %collective-permute-start.14 = (bf16[8,16,512]{2,1,0:T(8,128)(2,1)S(1)}, bf16[8,16,512]{2,1,0:T(8,128)(2,1)S(1)}, u32[]{:S(2)}, u32[]{:S(2)}) collective-permute-start(bf16[8,16,512]{2,1,0:T(8,128)(2,1)S(1)} %constant_dynamic-update-slice_fusion.16), channel_id=1, source_target_pairs={{0,1},{1,0},{2,3},{3,2},{4,5},{5,4},{6,7},{7,6},{8,9},{9,8},{10,11... | collective-permute-start | bytes 393224 | tf_op jit(solution)/shard_map/ppermute | solution.py:47
  74.6 14.0 %slice-start = ((s8[14680064]{0:T(1024)(128)(4,1)}), s8[4194304]{0:T(1024)(128)(4,1)S(1)}, s32[]{:S(2)}) async-start(s8[14680064]{0:T(1024)(128)(4,1)} %bitcast.43), calls=%async_computation.2 | async-start | bytes 8388608
  76.9 11.8 %slice-start.1 = ((s8[14680064]{0:T(1024)(128)(4,1)}), s8[4194304]{0:T(1024)(128)(4,1)S(1)}, s32[]{:S(2)}) async-start(s8[14680064]{0:T(1024)(128)(4,1)} %bitcast.43), calls=%async_computation.3 | async-start | bytes 8388608
  76.9 11.8 %slice-start.2 = ((s8[14680064]{0:T(1024)(128)(4,1)}), s8[4194304]{0:T(1024)(128)(4,1)S(1)}, s32[]{:S(2)}) async-start(s8[14680064]{0:T(1024)(128)(4,1)} %bitcast.43), calls=%async_computation.4 | async-start | bytes 8388608
  76.9 11.8 %slice-start.3 = ((s8[14680064]{0:T(1024)(128)(4,1)}), s8[2097152]{0:T(1024)(128)(4,1)S(1)}, s32[]{:S(2)}) async-start(s8[14680064]{0:T(1024)(128)(4,1)} %bitcast.43), calls=%async_computation.5 | async-start | bytes 4194304
  76.9 5.9 %collective-permute-start.17 = (bf16[1,16,896]{2,1,0:T(8,128)(2,1)S(1)}, bf16[1,16,896]{2,1,0:T(8,128)(2,1)S(1)}, u32[]{:S(2)}, u32[]{:S(2)}) collective-permute-start(bf16[1,16,896]{2,1,0:T(8,128)(2,1)S(1)} %bitcast.64), channel_id=1, source_target_pairs={{0,12},{1,13},{2,14},{3,15},{4,8},{5,9},{6,10},{7,11},{8,4},{9,5},... | collective-permute-start | bytes 86024 | tf_op jit(solution)/shard_map/ppermute | solution.py:47
  78.4 5.1 %collective-permute-start.16 = (bf16[1,16,896]{2,1,0:T(8,128)(2,1)S(1)}, bf16[1,16,896]{2,1,0:T(8,128)(2,1)S(1)}, u32[]{:S(2)}, u32[]{:S(2)}) collective-permute-start(bf16[1,16,896]{2,1,0:T(8,128)(2,1)S(1)} %bitcast.65), channel_id=1, source_target_pairs={{0,8},{1,9},{2,10},{3,11},{4,12},{5,13},{6,14},{7,15},{8,0},{9,1},... | collective-permute-start | bytes 86024 | tf_op jit(solution)/shard_map/ppermute | solution.py:47
  79.3 4.3 %collective-permute-start.15 = (bf16[1,16,896]{2,1,0:T(8,128)(2,1)S(1)}, bf16[1,16,896]{2,1,0:T(8,128)(2,1)S(1)}, u32[]{:S(2)}, u32[]{:S(2)}) collective-permute-start(bf16[1,16,896]{2,1,0:T(8,128)(2,1)S(1)} %bitcast.66), channel_id=1, source_target_pairs={{0,4},{1,5},{2,6},{3,7},{4,0},{5,1},{6,2},{7,3},{8,12},{9,13},{10,... | collective-permute-start | bytes 86024 | tf_op jit(solution)/shard_map/ppermute | solution.py:47
  83.7 4.9 %collective-permute-start.18 = (bf16[4,16,896]{2,1,0:T(8,128)(2,1)S(1)}, bf16[4,16,896]{2,1,0:T(8,128)(2,1)S(1)}, u32[]{:S(2)}, u32[]{:S(2)}) collective-permute-start(bf16[4,16,896]{2,1,0:T(8,128)(2,1)S(1)} %pad_maximum_fusion.refs_0_), channel_id=1, source_target_pairs={{0,2},{1,3},{2,0},{3,1},{4,6},{5,7},{6,4},{7,5},{8,10},{9,11},{10,... | collective-permute-start | bytes 344072 | tf_op jit(solution)/shard_map/ppermute | solution.py:47
  88.6 1.6 %collective-permute-start.19 = (bf16[8,16,896]{2,1,0:T(8,128)(2,1)S(1)}, bf16[8,16,896]{2,1,0:T(8,128)(2,1)S(1)}, u32[]{:S(2)}, u32[]{:S(2)}) collective-permute-start(bf16[8,16,896]{2,1,0:T(8,128)(2,1)S(1)} %constant_dynamic-update-slice_fusion.21), channel_id=1, source_target_pairs={{0,1},{1,0},{2,3},{3,2},{4,5},{5,4},{6,7},{7,6},{8,9},{9,8},{10,11... | collective-permute-start | bytes 688136 | tf_op jit(solution)/shard_map/ppermute | solution.py:47

commit v4 on v3

--- a/solution.py
+++ b/solution.py
@@ -14,7 +14,7 @@
 
 
 LANES = 128
-FLOPS = {"begin": 10**11, "table": 10**11, "finish": 10**11, "output": 10**11, "relay": 10**11}
+FLOPS = {"begin": 10**11, "table": 10**11, "finish": 10**11, "output": 10**11, "relay": 10**11, "merge_next": 10**11, "output_a": 10**11}
 VMEM = pl.BlockSpec(memory_space=pltpu.VMEM)
 SMEM = pl.BlockSpec(memory_space=pltpu.SMEM)
 
@@ -56,7 +56,8 @@
         return [shifted(held, stride * digit) for digit in range(1, radix)]
 
     for stride, radix, _ in rounds:
-        held = jnp.concatenate([held] + arrive(stride, radix), axis=0)
+        arrived = arrive(stride, radix)
+        held = jnp.concatenate([held] + arrived, axis=0)
     brought = arrive(*last[:2])
     near = jnp.concatenate([held] + brought, axis=0)
     return held, brought, shifted(near, 1)
@@ -80,12 +81,12 @@
     )(*args)
 
 
-def accumulate(device_ref, devices, pieces, gain_ref, weight_refs, total_refs, square_ref):
+def accumulate(device_ref, devices, pieces, owner_of, gain_ref, weight_refs, total_refs, square_ref):
     for first, piece_ref in pieces:
         places, _, depth = piece_ref.shape
 
         def step(index, carry):
-            owner = lax.bitwise_xor(device_ref[0], mask_at(first + index, devices))
+            owner = owner_of(device_ref[0], first + index, devices)
             block = piece_ref[index]
             if gain_ref is not None:
                 wide = block.astype(jnp.float32)
@@ -112,7 +113,11 @@
         lax.fori_loop(0, places, step, 0, unroll=4)
 
 
-def contract(name, pieces, own, weights, widths, gain, finish, extras, out_shape):
+def by_place(device, place_index, devices):
+    return lax.bitwise_xor(device, mask_at(place_index, devices))
+
+
+def contract(name, pieces, own, weights, widths, gain, finish, extras, out_shape, owner_of=by_place):
     held, brought, far = pieces
     devices = lax.axis_size("ctx")
     _, rows, depth = held.shape
@@ -142,7 +147,7 @@
                 placed.append((place, part_ref))
                 place += part_ref.shape[0]
             accumulate(
-                device_ref, devices, placed, gain_refs[0] if normed else None,
+                device_ref, devices, placed, owner_of, gain_refs[0] if normed else None,
                 weight_refs, total_refs[: len(weights)], total_refs[-1],
             )
             if last:
@@ -242,6 +247,162 @@
                 index = (g * group * rows + first + begin) // pairs
                 out_ref[index, :pairs] = means[first + begin : first + begin + pairs]
                 out_ref[index, pairs:] = terms
+
+
+def terms_of(level):
+    line = jnp.transpose(level)[:8]
+    high = line.astype(jnp.bfloat16).astype(jnp.float32)
+    rest = line - high
+    middle = rest.astype(jnp.bfloat16).astype(jnp.float32)
+    row = lax.broadcasted_iota(jnp.int32, line.shape, 0)
+    return jnp.where(row == 0, high, jnp.where(row == 1, middle, rest - middle)).astype(jnp.bfloat16)
+
+
+def read_message(message):
+    pairs = message.shape[0] - 8
+    terms = message[pairs:].astype(jnp.float32)
+    line = terms[0:1] + terms[1:2] + terms[2:3]
+    return message[:pairs].astype(jnp.float32), jnp.transpose(jnp.broadcast_to(line, (LANES, LANES)))
+
+
+def merge(parts):
+    peak = parts[0][1]
+    for _, level in parts[1:]:
+        peak = jnp.maximum(peak, level)
+    shares = [jnp.exp(level - peak) for _, level in parts]
+    denominator = sum(shares[1:], shares[0])
+    numerator = shares[0] * parts[0][0]
+    for share, (mean, _) in zip(shares[1:], parts[1:]):
+        numerator = numerator + share * mean
+    return numerator / denominator, peak + jnp.log(denominator)
+
+
+def put_message(message_ref, mean, level):
+    pairs = mean.shape[0]
+    message_ref[:pairs] = mean.astype(jnp.bfloat16)
+    message_ref[pairs:] = terms_of(level)
+
+
+def half_kernel(scale, head_dim, sends, device_ref, blocks_ref, key_ref, value_ref, limit_ref, *out_refs):
+    places, rows, _ = blocks_ref.shape
+    span = key_ref.shape[0]
+    value_heads = key_ref.shape[1] // head_dim
+    units = places // value_heads
+    local = LANES // (value_heads * rows)
+    count = units * local
+    group_index = lax.div(device_ref[0], 2 * units)
+    visible = (lax.broadcasted_iota(jnp.int32, (rows, span), 1) < limit_ref[:, :1])[None]
+    means = [[] for _ in range(units)]
+    levels = [[] for _ in range(units)]
+    for g in range(value_heads):
+        lanes = pl.ds(g * head_dim, head_dim)
+        parts = []
+        for unit in range(units):
+            block = blocks_ref[unit * value_heads + lax.bitwise_xor(group_index, g)]
+            parts += [block[:, h * head_dim : (h + 1) * head_dim] for h in range(local)]
+        logits = lax.dot_general(
+            jnp.concatenate(parts, axis=0), key_ref[:, lanes], (((1,), (1,)), ((), ())),
+            preferred_element_type=jnp.float32,
+        ) * scale
+        masked = jnp.where(visible, logits.reshape(count, rows, span), MASKED)
+        top = jnp.max(masked, axis=2, keepdims=True)
+        weights = jnp.where(visible, jnp.exp(masked - top), 0.0)
+        total = jnp.sum(weights, axis=2, keepdims=True).reshape(count * rows, 1)
+        top = top.reshape(count * rows, 1)
+        summed = jnp.dot(
+            weights.astype(jnp.bfloat16).reshape(count * rows, span), value_ref[:, lanes],
+            preferred_element_type=jnp.float32,
+        )
+        seen = total > 0.0
+        safe = jnp.where(seen, total, 1.0)
+        mean = summed / safe
+        level = jnp.broadcast_to(jnp.where(seen, top + jnp.log(safe), MASKED), (count * rows, LANES))
+        run = local * rows
+        for unit in range(units):
+            means[unit].append(mean[unit * run : (unit + 1) * run])
+            levels[unit].append(level[unit * run : (unit + 1) * run])
+    for unit in range(units):
+        mean = jnp.concatenate(means[unit], axis=0)
+        level = jnp.concatenate(levels[unit], axis=0)
+        if sends:
+            put_message(out_refs[0].at[unit], mean, level)
+        else:
+            out_refs[0][unit] = mean
+            out_refs[1][unit] = level
+
+
+def merge_core_kernel(mean_ref, level_ref, message_ref, sent_ref, mean_out_ref, level_out_ref):
+    for unit in (1, 0):
+        mean, level = merge([(mean_ref[unit], level_ref[unit]), read_message(message_ref[unit])])
+        if unit == 1:
+            put_message(sent_ref, mean, level)
+        else:
+            mean_out_ref[...] = mean
+            level_out_ref[...] = level
+
+
+def merge_next_kernel(mean_ref, level_ref, message_ref, sent_ref, mean_out_ref, level_out_ref):
+    mean, level = merge([(mean_ref[...], level_ref[...]), read_message(message_ref[...])])
+    put_message(sent_ref, mean, level)
+    mean_out_ref[...] = mean
+    level_out_ref[...] = level
+
+
+def fresh_kernel(scale, head_dim, value_heads, key_width, device_ref, near_ref, far_ref, score_ref, value_ref):
+    _, rows, used = far_ref.shape
+    query_width = used - 2 * key_width
+    run = head_dim // key_width
+    units = run // 2
+    group_index = lax.div(device_ref[0], run)
+    core = lax.rem(device_ref[0], 2)
+    step = lax.rem(lax.div(device_ref[0], 2), units)
+    for g in range(value_heads):
+        turned = lax.bitwise_xor(group_index, g)
+        news = []
+        for index in range(run):
+            place = lax.bitwise_xor(step, index // 2) * value_heads + turned
+            block = jnp.where(core == index % 2, near_ref[place], far_ref[place])
+            news.append(block[:, query_width:])
+        key = jnp.concatenate([new[:, :key_width] for new in news], axis=1).astype(jnp.float32)
+        value = jnp.concatenate([new[:, key_width:] for new in news], axis=1).astype(jnp.float32)
+        queries = far_ref[turned]
+        for h in range(query_width // head_dim):
+            query = queries[:, h * head_dim : (h + 1) * head_dim].astype(jnp.float32)
+            score = jnp.sum(query * key, axis=1, keepdims=True) * scale
+            span = pl.ds((g * (query_width // head_dim) + h) * rows, rows)
+            score_ref[span, :] = jnp.broadcast_to(score, (rows, LANES))
+            value_ref[span, :] = value
+
+
+def settle_kernel(
+    rows, mean_ref, level_ref, *refs
+):
+    *message_refs, score_ref, value_ref, out_ref = refs
+    parts = [(mean_ref[...], level_ref[...])]
+    parts += [read_message(message_ref[...]) for message_ref in message_refs]
+    parts.append((value_ref[...], score_ref[...]))
+    mean, _ = merge(parts)
+    done = mean.astype(jnp.bfloat16)
+    owners, _, width = out_ref.shape
+    local = width // LANES
+    for g in range(owners):
+        first = g * local * rows
+        out_ref[g] = jnp.concatenate(
+            [done[first + h * rows : first + (h + 1) * rows] for h in range(local)], axis=1
+        )
+
+
+def residual_finish(factor, totals, extra_refs, out_ref):
+    out_ref[...] = (extra_refs[0][...].astype(jnp.float32) + totals[0]).astype(jnp.bfloat16)
+
+
+def by_group(device, place_index, devices):
+    (stride, groups, _), (step, _, _), _ = digits(devices)
+    place_in_group = lax.bitwise_xor(lax.rem(device, stride), 1)
+    far = lax.div(place_index, devices // 2) if not isinstance(place_index, int) else place_index // (devices // 2)
+    near_place = lax.rem(place_index, devices // 2)
+    turned = lax.bitwise_xor(place_in_group, lax.div(near_place, groups) * step)
+    return lax.rem(near_place, groups) * stride + lax.bitwise_xor(turned, far)
 
 
 def order_kernel(device_ref, held_ref, out_ref):
@@ -341,71 +502,121 @@
         "project", gathered(begun), own, (w_query, *sides), (query_width, key_width, key_width),
         attn_gain, project_finish, (cosine, sine), buffer(rows, used),
     )
-    packed = exchange(jnp.broadcast_to(projected[None], (devices, rows, used)))
-
-    def unpacked(first, part_width):
-        part = packed[:, :, first : first + part_width]
-        if part_width >= head_dim:
-            split = part.reshape(devices, rows, part_width // head_dim, head_dim)
-            return split.transpose(0, 2, 1, 3).reshape(-1, rows, head_dim)
-        run = head_dim // part_width
-        return part.reshape(-1, run, rows, part_width).transpose(0, 2, 1, 3).reshape(
-            -1, rows, head_dim
-        )
-
-    queries = unpacked(0, query_width)
-    key_new = unpacked(query_width, key_width)
-    value_new = unpacked(query_width + key_width, key_width)
-    pairs = heads * rows // devices
     limit = jnp.broadcast_to((positions - own * span)[:, None], (rows, LANES))
-    sent = call(
-        lambda *refs: attend_kernel(scale, *refs), "attend", buffer(devices, pairs + 8, LANES),
-        (
-            queries,
-            rotated_prefix_keys.reshape(span, value_heads * head_dim),
-            cache_values.reshape(span, value_heads * head_dim),
-            limit,
-        ),
-        (),
-        4 * heads * rows * span * head_dim,
-    )
-    got = exchange(sent)
-    first_pair = device * pairs
-    means = got[:, :pairs].astype(jnp.float32)
-    terms = lax.dynamic_slice_in_dim(
-        got[:, pairs : pairs + 3].astype(jnp.float32), first_pair % LANES, pairs, 2
-    )
-    levels = terms[:, 0] + terms[:, 1] + terms[:, 2]
-
-    def mine(every):
-        return lax.dynamic_slice_in_dim(
-            every.reshape(heads * rows, head_dim), first_pair, pairs, 0
-        ).astype(jnp.float32)
-
-    def spread(new):
-        return jnp.broadcast_to(new[:, None], (value_heads, group, rows, head_dim))
-
-    own_score = jnp.sum(mine(queries) * mine(spread(key_new)), axis=1) * scale
-    own_value = mine(spread(value_new))
-    peak = jnp.maximum(jnp.max(levels, axis=0), own_score)
-    shares = jnp.exp(levels - peak[None, :])
-    own_share = jnp.exp(own_score - peak)
-    numerator = jnp.sum(shares[..., None] * means, axis=0) + own_share[:, None] * own_value
-    denominator = jnp.sum(shares, axis=0) + own_share
-    attn_part = call(
-        finish_kernel, "finish", buffer(pairs, head_dim), (numerator, denominator[:, None]), (),
-        FLOPS["finish"],
-    )
-    held = together(gathered(attn_part))
-    attn_all = call(
-        order_kernel, "order", buffer(devices, pairs, head_dim), (own, held)
-    )
-    mid_part = call(
-        output_kernel, "output", buffer(rows, width),
-        (attn_all.reshape(heads, rows, head_dim), w_out, hidden_in),
-        totals(width),
-        2 * rows * heads * head_dim * width,
-    )
+    keys = rotated_prefix_keys.reshape(span, value_heads * head_dim)
+    values = cache_values.reshape(span, value_heads * head_dim)
+    rounds = digits(devices)
+    if (
+        len(rounds) == 3
+        and rounds[0][1] == value_heads
+        and rounds[1][1] == 2
+        and head_dim == LANES
+        and value_heads * (query_width // head_dim) * rows == LANES
+    ):
+        held, brought, far = gathered(projected)
+        near = jnp.concatenate([held] + brought, axis=0)
+        unit = (LANES, LANES)
+        message = buffer(LANES + 8, LANES)
+        wide = buffer(*unit, dtype=jnp.float32)
+        pair = buffer(2, *unit, dtype=jnp.float32)
+        work = 2 * heads * rows * span * head_dim
+
+        def half(name, blocks, sends, out_shape):
+            return call(
+                lambda *refs: half_kernel(scale, head_dim, sends, *refs), name, out_shape,
+                (own, blocks, keys, values, limit), (), work,
+            )
+
+        given = half("attend_near", near, True, buffer(2, LANES + 8, LANES))
+        taken = shifted(given, 1)
+        mean, level = half("attend_far", far, False, (pair, pair))
+        given, mean, level = call(
+            merge_core_kernel, "merge_core", (message, wide, wide), (mean, level, taken)
+        )
+        taken = shifted(given, rounds[1][0])
+        given, mean, level = call(
+            merge_next_kernel, "merge_next", (message, wide, wide), (mean, level, taken)
+        )
+        taken = [shifted(given, rounds[0][0] * digit) for digit in range(1, rounds[0][1])]
+        score, value = call(
+            lambda *refs: fresh_kernel(scale, head_dim, value_heads, key_width, *refs), "fresh",
+            (wide, wide), (own, near, far),
+        )
+        done = call(
+            lambda *refs: settle_kernel(rows, *refs), "settle",
+            buffer(value_heads, rows, query_width), (mean, level, *taken, score, value),
+        )
+        brought = [shifted(done, rounds[1][0])]
+        far = shifted(jnp.concatenate([done] + brought, axis=0), 1)
+        mid_part = contract(
+            "output", (done, brought, far), own, (w_out,), (width,),
+            None, residual_finish, (hidden_in,), buffer(rows, width), by_group,
+        )
+    else:
+        packed = exchange(jnp.broadcast_to(projected[None], (devices, rows, used)))
+
+        def unpacked(first, part_width):
+            part = packed[:, :, first : first + part_width]
+            if part_width >= head_dim:
+                split = part.reshape(devices, rows, part_width // head_dim, head_dim)
+                return split.transpose(0, 2, 1, 3).reshape(-1, rows, head_dim)
+            run = head_dim // part_width
+            return part.reshape(-1, run, rows, part_width).transpose(0, 2, 1, 3).reshape(
+                -1, rows, head_dim
+            )
+
+        queries = unpacked(0, query_width)
+        key_new = unpacked(query_width, key_width)
+        value_new = unpacked(query_width + key_width, key_width)
+        pairs = heads * rows // devices
+        sent = call(
+            lambda *refs: attend_kernel(scale, *refs), "attend", buffer(devices, pairs + 8, LANES),
+            (
+                queries,
+                keys,
+                values,
+                limit,
+            ),
+            (),
+            4 * heads * rows * span * head_dim,
+        )
+        got = exchange(sent)
+        first_pair = device * pairs
+        means = got[:, :pairs].astype(jnp.float32)
+        terms = lax.dynamic_slice_in_dim(
+            got[:, pairs : pairs + 3].astype(jnp.float32), first_pair % LANES, pairs, 2
+        )
+        levels = terms[:, 0] + terms[:, 1] + terms[:, 2]
+
+        def mine(every):
+            return lax.dynamic_slice_in_dim(
+                every.reshape(heads * rows, head_dim), first_pair, pairs, 0
+            ).astype(jnp.float32)
+
+        def spread(new):
+            return jnp.broadcast_to(new[:, None], (value_heads, group, rows, head_dim))
+
+        own_score = jnp.sum(mine(queries) * mine(spread(key_new)), axis=1) * scale
+        own_value = mine(spread(value_new))
+        peak = jnp.maximum(jnp.max(levels, axis=0), own_score)
+        shares = jnp.exp(levels - peak[None, :])
+        own_share = jnp.exp(own_score - peak)
+        numerator = jnp.sum(shares[..., None] * means, axis=0) + own_share[:, None] * own_value
+        denominator = jnp.sum(shares, axis=0) + own_share
+        attn_part = call(
+            finish_kernel, "finish", buffer(pairs, head_dim), (numerator, denominator[:, None]), (),
+            FLOPS["finish"],
+        )
+        held = together(gathered(attn_part))
+        attn_all = call(
+            order_kernel, "order", buffer(devices, pairs, head_dim), (own, held)
+        )
+        mid_part = call(
+            output_kernel, "output", buffer(rows, width),
+            (attn_all.reshape(heads, rows, head_dim), w_out, hidden_in),
+            totals(width),
+            2 * rows * heads * head_dim * width,
+        )
     hidden_width = w_gate.shape[1]
     hidden = contract(
         "gated", gathered(mid_part), own, (w_gate, w_up), (hidden_width, hidden_width),

time: 92.4 us -> 88.8 us (0.961)
  waiting for transfers between devices: 42 us -> 36.4 us
  starting transfers between devices: 29.3 us -> 33.7 us
  local copies, waits for them, and re-layouts: 6.55 us -> 3.95 us
  Pallas kernels: 12.5 us -> 13.5 us
    all_to_all x2 -> x0, waiting for transfers between devices: 15.2 us -> none  [exchange(): return lax.all_to_all(blocks, 'ctx', 0, 0)]
    ppermute x20 -> x27, starting transfers between devices: 21.4 us -> 33.7 us  [shifted(): lax.ppermute(part, 'ctx', [(index, index ^ mask) for index in range(devic...]
    ppermute x20 -> x27, waiting for transfers between devices: 26.8 us -> 36.4 us  [shifted(): lax.ppermute(part, 'ctx', [(index, index ^ mask) for index in range(devic...]
    all_to_all x2 -> x0, starting transfers between devices: 7.98 us -> none  [exchange(): return lax.all_to_all(blocks, 'ctx', 0, 0)]
    reshape x2 -> x1, local copies, waits for them, and re-layouts: 1.61 us -> 0.43 us  [shards(): values = cache_values.reshape(span, value_heads * head_dim)]
    pallas_call x16 -> x21, Pallas kernels: 12.5 us -> 13.5 us  [call(): pl.pallas_call(body, out_shape=out_shape, in_specs=[SMEM if a.dtype == jn...]
    broadcast_in_dim x5 -> x0, local copies, waits for them, and re-layouts: 0.95 us -> none  [the longest x1 0.71 us: shards(): packed = exchange(jnp.broadcast_to(projected[None], (devices, rows, used)))]
    unnamed x50 -> x52, local copies, waits for them, and re-layouts: 3.27 us -> 3.26 us
  transfers between devices with their start and end apart: 22 -> 27, of which waited for: 18 -> 18; matrix products, arithmetic and copies ran while one was open for 3% -> 1% of each run, Pallas kernels for 4% -> 9%
where the time goes in v4:
time: 88.8 us; the launch traced here: 88.6 us
  waiting for transfers between devices  36.4 us (41%)
  starting transfers between devices  33.7 us (38%)
  Pallas kernels  13.5 us (15%)
  local copies, waits for them, and re-layouts  3.95 us (4%)
    ppermute x27, waiting for transfers between devices, shifted(): lax.ppermute(part, 'ctx', [(index, index ^ mask) for index in range(devic...  36.4 us
    ppermute x27, starting transfers between devices, shifted(): lax.ppermute(part, 'ctx', [(index, index ^ mask) for index in range(devic...  33.7 us
    pallas_call x21, Pallas kernels, call(): pl.pallas_call(body, out_shape=out_shape, in_specs=[SMEM if a.dtype == jn...  13.5 us
    unnamed x52, local copies, waits for them, and re-layouts  3.26 us
  transfers between devices with their start and end apart: 27, of which 18 were waited for; matrix products, arithmetic and copies ran while one was open for 1% of the time, Pallas kernels for 9%

profile of v4, /device:TPU:0, one launch (start us, length us, event | category | flops | bytes accessed | tf_op | source)
XLA Modules:
  0.0 88.6 jit_solution(5617625867491630472)
XLA Ops:
  0.0 0.7 copy-done.8
  0.7 3.1 %collective-permute-start = (bf16[1,16,512]{2,1,0:T(8,128)(2,1)S(1)}, bf16[1,16,512]{2,1,0:T(8,128)(2,1)S(1)}, u32[]{:S(2)}, u32[]{:S(2)}) collective-permute-start(bf16[1,16,512]{2,1,0:T(8,128)(2,1)S(1)} %bitcast.48), channel_id=1, source_target_pairs={{0,4},{1,5},{2,6},{3,7},{4,0},{5,1},{6,2},{7,3},{8,12},{9,13},{10,... | collective-permute-start | bytes 49160 | tf_op jit(solution)/shard_map/ppermute | solution.py:47
  3.8 2.6 %collective-permute-start.1 = (bf16[1,16,512]{2,1,0:T(8,128)(2,1)S(1)}, bf16[1,16,512]{2,1,0:T(8,128)(2,1)S(1)}, u32[]{:S(2)}, u32[]{:S(2)}) collective-permute-start(bf16[1,16,512]{2,1,0:T(8,128)(2,1)S(1)} %bitcast.49), channel_id=1, source_target_pairs={{0,8},{1,9},{2,10},{3,11},{4,12},{5,13},{6,14},{7,15},{8,0},{9,1},... | collective-permute-start | bytes 49160 | tf_op jit(solution)/shard_map/ppermute | solution.py:47
  6.4 0.2 select_reduce_fusion
  6.6 0.1 multiply_sine_fusion.1
  6.7 0.1 multiply_sine_fusion
  7.0 0.1 pad.16.clone
  7.1 1.4 %collective-permute-done.1 = bf16[1,16,512]{2,1,0:T(8,128)(2,1)S(1)} collective-permute-done((bf16[1,16,512]{2,1,0:T(8,128)(2,1)S(1)}, bf16[1,16,512]{2,1,0:T(8,128)(2,1)S(1)}, u32[]{:S(2)}, u32[]{:S(2)}) %collective-permute-start.1) | collective-permute-done | bytes 16416 | tf_op jit(solution)/shard_map/ppermute | solution.py:47
  8.5 3.4 %collective-permute-done.2 = bf16[1,16,512]{2,1,0:T(8,128)(2,1)S(1)} collective-permute-done((bf16[1,16,512]{2,1,0:T(8,128)(2,1)S(1)}, bf16[1,16,512]{2,1,0:T(8,128)(2,1)S(1)}, u32[]{:S(2)}, u32[]{:S(2)}) %collective-permute-start.2) | collective-permute-done | bytes 16416 | tf_op jit(solution)/shard_map/ppermute | solution.py:47
  11.9 1.6 %collective-permute-start.3 = (bf16[4,16,512]{2,1,0:T(8,128)(2,1)S(1)}, bf16[4,16,512]{2,1,0:T(8,128)(2,1)S(1)}, u32[]{:S(2)}, u32[]{:S(2)}) collective-permute-start(bf16[4,16,512]{2,1,0:T(8,128)(2,1)S(1)} %pad_maximum_fusion.1.refs_0_), channel_id=1, source_target_pairs={{0,2},{1,3},{2,0},{3,1},{4,6},{5,7},{6,4},{7,5},{8,10},{9,11},{10,... | collective-permute-start | bytes 196616 | tf_op jit(solution)/shard_map/ppermute | solution.py:47
  13.5 2.7 %collective-permute-done.3.refs_0_ = bf16[4,16,512]{2,1,0:T(8,128)(2,1)S(1)} collective-permute-done((bf16[4,16,512]{2,1,0:T(8,128)(2,1)S(1)}, bf16[4,16,512]{2,1,0:T(8,128)(2,1)S(1)}, u32[]{:S(2)}, u32[]{:S(2)}) %collective-permute-start.3) | collective-permute-done | bytes 65568 | tf_op jit(solution)/shard_map/ppermute | solution.py:47
  16.4 2.1 %copy-done.2 = bf16[8192,256]{1,0:T(8,128)(2,1)S(1)} copy-done((bf16[8192,256]{1,0:T(8,128)(2,1)S(1)}, bf16[8192,256]{1,0:T(8,128)(2,1)}, u32[]{:S(2)}) %copy-start.2) | copy-done | bytes 4194328
  18.5 0.1 copy-done.4
  18.6 0.2 copy-done.5
  18.7 0.3 shard_map.137
  19.1 0.3 shard_map.138
  19.4 0.8 shard_map.140
  20.3 0.7 collective-permute-start.6
  21.1 3.6 %collective-permute-start.7 = (bf16[1,16,320]{2,1,0:T(8,128)(2,1)S(1)}, bf16[1,16,320]{2,1,0:T(8,128)(2,1)S(1)}, u32[]{:S(2)}, u32[]{:S(2)}) collective-permute-start(bf16[1,16,320]{2,1,0:T(8,128)(2,1)S(1)} %bitcast.46), channel_id=1, source_target_pairs={{0,12},{1,13},{2,14},{3,15},{4,8},{5,9},{6,10},{7,11},{8,4},{9,5},... | collective-permute-start | bytes 30728 | tf_op jit(solution)/shard_map/ppermute | solution.py:47
  24.7 0.3 collective-permute-done.6
  25.0 1.6 %collective-permute-done.7 = bf16[1,16,320]{2,1,0:T(8,128)(2,1)S(1)} collective-permute-done((bf16[1,16,320]{2,1,0:T(8,128)(2,1)S(1)}, bf16[1,16,320]{2,1,0:T(8,128)(2,1)S(1)}, u32[]{:S(2)}, u32[]{:S(2)}) %collective-permute-start.7) | collective-permute-done | bytes 10272 | tf_op jit(solution)/shard_map/ppermute | solution.py:47
  26.6 1.6 %collective-permute-start.8 = (bf16[4,16,320]{2,1,0:T(8,128)(2,1)S(1)}, bf16[4,16,320]{2,1,0:T(8,128)(2,1)S(1)}, u32[]{:S(2)}, u32[]{:S(2)}) collective-permute-start(bf16[4,16,320]{2,1,0:T(8,128)(2,1)S(1)} %pad_maximum_fusion.4), channel_id=1, source_target_pairs={{0,2},{1,3},{2,0},{3,1},{4,6},{5,7},{6,4},{7,5},{8,10},{9,11},{10,... | collective-permute-start | bytes 122888 | tf_op jit(solution)/shard_map/ppermute | solution.py:47
  28.2 2.5 %collective-permute-done.8 = bf16[4,16,320]{2,1,0:T(8,128)(2,1)S(1)} collective-permute-done((bf16[4,16,320]{2,1,0:T(8,128)(2,1)S(1)}, bf16[4,16,320]{2,1,0:T(8,128)(2,1)S(1)}, u32[]{:S(2)}, u32[]{:S(2)}) %collective-permute-start.8) | collective-permute-done | bytes 40992 | tf_op jit(solution)/shard_map/ppermute | solution.py:47
  30.8 0.4 copy_bitcast_fusion
  31.3 1.5 %shard_map.142 = bf16[2,136,128]{2,1,0:T(8,128)(2,1)S(1)} custom-call(s32[1]{0:T(128)} %bitcast.device_ref.refs_0_, bf16[8,16,320]{2,1,0:T(8,128)(2,1)S(1)} %constant_dynamic-update-slice_fusion.5.refs_1_, bf16[1024,512]{1,0:T(8,128)(2,1)S(1)} %get-tuple-element.66.refs_2_, bf16[1024,512]{1,0:T(8,128)(2,1)S(1)} %get-tuple-element.65.refs_3_, ...), custom_call_target="tpu_custom_call" | custom-call | flops 134217728 | bytes 2187268 | tf_op jit(solution)/shard_map/pallas_call | solution.py:73
  32.8 0.6 collective-permute-start.10
  33.4 1.5 %shard_map.141 = (f32[2,128,128]{2,1,0:T(8,128)S(1)}, f32[2,128,128]{2,1,0:T(8,128)S(1)}) custom-call(s32[1]{0:T(128)} %bitcast.device_ref.refs_0_, bf16[8,16,320]{2,1,0:T(8,128)(2,1)S(1)} %collective-permute-done.9.refs_1_.refs_2_, bf16[1024,512]{1,0:T(8,128)(2,1)S(1)} %get-tuple-element.66.refs_2_, bf16[1024,512]{1,0:T(8,128)(2,1)S(1)} %get-tuple-element.65.refs_3_, ...), custom_call_target="tpu_custom_call" | custom-call | flops 134217728 | bytes 2187268 | tf_op jit(solution)/shard_map/pallas_call | solution.py:73
  34.9 0.2 shard_map.143
  35.1 1.6 %collective-permute-start.11 = (bf16[136,128]{1,0:T(8,128)(2,1)S(1)}, bf16[136,128]{1,0:T(8,128)(2,1)S(1)}, u32[]{:S(2)}, u32[]{:S(2)}) collective-permute-start(bf16[136,128]{1,0:T(8,128)(2,1)S(1)} %get-tuple-element.45), channel_id=1, source_target_pairs={{0,2},{1,3},{2,0},{3,1},{4,6},{5,7},{6,4},{7,5},{8,10},{9,11},{10,... | collective-permute-start | bytes 104456 | tf_op jit(solution)/shard_map/ppermute | solution.py:47
  36.7 2.4 %collective-permute-done.11.message_ref = bf16[136,128]{1,0:T(8,128)(2,1)S(1)} collective-permute-done((bf16[136,128]{1,0:T(8,128)(2,1)S(1)}, bf16[136,128]{1,0:T(8,128)(2,1)S(1)}, u32[]{:S(2)}, u32[]{:S(2)}) %collective-permute-start.11) | collective-permute-done | bytes 34848 | tf_op jit(solution)/shard_map/ppermute | solution.py:47
  39.1 0.2 shard_map.144
  39.2 0.4 collective-permute-start.12
  39.7 3.8 %collective-permute-start.13 = (bf16[136,128]{1,0:T(8,128)(2,1)S(1)}, bf16[136,128]{1,0:T(8,128)(2,1)S(1)}, u32[]{:S(2)}, u32[]{:S(2)}) collective-permute-start(bf16[136,128]{1,0:T(8,128)(2,1)S(1)} %get-tuple-element.48), channel_id=1, source_target_pairs={{0,8},{1,9},{2,10},{3,11},{4,12},{5,13},{6,14},{7,15},{8,0},{9,1},... | collective-permute-start | bytes 104456 | tf_op jit(solution)/shard_map/ppermute | solution.py:47
  43.5 0.2 collective-permute-start.14
  43.6 0.2 shard_map.145
  43.8 1.9 %collective-permute-done.13.refs_3_ = bf16[136,128]{1,0:T(8,128)(2,1)S(1)} collective-permute-done((bf16[136,128]{1,0:T(8,128)(2,1)S(1)}, bf16[136,128]{1,0:T(8,128)(2,1)S(1)}, u32[]{:S(2)}, u32[]{:S(2)}) %collective-permute-start.13) | collective-permute-done | bytes 34848 | tf_op jit(solution)/shard_map/ppermute | solution.py:47
  45.8 3.4 %collective-permute-done.14.refs_4_ = bf16[136,128]{1,0:T(8,128)(2,1)S(1)} collective-permute-done((bf16[136,128]{1,0:T(8,128)(2,1)S(1)}, bf16[136,128]{1,0:T(8,128)(2,1)S(1)}, u32[]{:S(2)}, u32[]{:S(2)}) %collective-permute-start.14) | collective-permute-done | bytes 34848 | tf_op jit(solution)/shard_map/ppermute | solution.py:47
  49.2 0.2 shard_map.146.refs_0_
  49.4 1.6 %collective-permute-start.15 = (bf16[4,16,256]{2,1,0:T(8,128)(2,1)S(1)}, bf16[4,16,256]{2,1,0:T(8,128)(2,1)S(1)}, u32[]{:S(2)}, u32[]{:S(2)}) collective-permute-start(bf16[4,16,256]{2,1,0:T(8,128)(2,1)S(1)} %shard_map.146.refs_0_), channel_id=1, source_target_pairs={{0,2},{1,3},{2,0},{3,1},{4,6},{5,7},{6,4},{7,5},{8,10},{9,11},{10,... | collective-permute-start | bytes 98312 | tf_op jit(solution)/shard_map/ppermute | solution.py:47
  51.0 2.4 %collective-permute-done.15.refs_0_ = bf16[4,16,256]{2,1,0:T(8,128)(2,1)S(1)} collective-permute-done((bf16[4,16,256]{2,1,0:T(8,128)(2,1)S(1)}, bf16[4,16,256]{2,1,0:T(8,128)(2,1)S(1)}, u32[]{:S(2)}, u32[]{:S(2)}) %collective-permute-start.15) | collective-permute-done | bytes 32800 | tf_op jit(solution)/shard_map/ppermute | solution.py:47
  53.5 0.2 shard_map.147.refs_2_
  53.8 0.3 shard_map.148.refs_2_
  54.0 0.7 collective-permute-done.16.refs_0_
  54.7 0.5 shard_map.149.refs_3_
  55.3 0.9 %collective-permute-start.18 = (bf16[1,16,512]{2,1,0:T(8,128)(2,1)S(1)}, bf16[1,16,512]{2,1,0:T(8,128)(2,1)S(1)}, u32[]{:S(2)}, u32[]{:S(2)}) collective-permute-start(bf16[1,16,512]{2,1,0:T(8,128)(2,1)S(1)} %bitcast.37), channel_id=1, source_target_pairs={{0,8},{1,9},{2,10},{3,11},{4,12},{5,13},{6,14},{7,15},{8,0},{9,1},... | collective-permute-start | bytes 49160 | tf_op jit(solution)/shard_map/ppermute | solution.py:47
  56.2 3.5 %collective-permute-start.19 = (bf16[1,16,512]{2,1,0:T(8,128)(2,1)S(1)}, bf16[1,16,512]{2,1,0:T(8,128)(2,1)S(1)}, u32[]{:S(2)}, u32[]{:S(2)}) collective-permute-start(bf16[1,16,512]{2,1,0:T(8,128)(2,1)S(1)} %bitcast.38), channel_id=1, source_target_pairs={{0,12},{1,13},{2,14},{3,15},{4,8},{5,9},{6,10},{7,11},{8,4},{9,5},... | collective-permute-start | bytes 49160 | tf_op jit(solution)/shard_map/ppermute | solution.py:47
  59.6 0.3 collective-permute-done.18
  60.0 1.8 %collective-permute-done.19 = bf16[1,16,512]{2,1,0:T(8,128)(2,1)S(1)} collective-permute-done((bf16[1,16,512]{2,1,0:T(8,128)(2,1)S(1)}, bf16[1,16,512]{2,1,0:T(8,128)(2,1)S(1)}, u32[]{:S(2)}, u32[]{:S(2)}) %collective-permute-start.19) | collective-permute-done | bytes 16416 | tf_op jit(solution)/shard_map/ppermute | solution.py:47
  61.7 1.6 %collective-permute-start.20 = (bf16[4,16,512]{2,1,0:T(8,128)(2,1)S(1)}, bf16[4,16,512]{2,1,0:T(8,128)(2,1)S(1)}, u32[]{:S(2)}, u32[]{:S(2)}) collective-permute-start(bf16[4,16,512]{2,1,0:T(8,128)(2,1)S(1)} %pad_maximum_fusion.3.refs_0_), channel_id=1, source_target_pairs={{0,2},{1,3},{2,0},{3,1},{4,6},{5,7},{6,4},{7,5},{8,10},{9,11},{10,... | collective-permute-start | bytes 196616 | tf_op jit(solution)/shard_map/ppermute | solution.py:47
  63.3 2.7 %collective-permute-done.20.refs_0_ = bf16[4,16,512]{2,1,0:T(8,128)(2,1)S(1)} collective-permute-done((bf16[4,16,512]{2,1,0:T(8,128)(2,1)S(1)}, bf16[4,16,512]{2,1,0:T(8,128)(2,1)S(1)}, u32[]{:S(2)}, u32[]{:S(2)}) %collective-permute-start.20) | collective-permute-done | bytes 65568 | tf_op jit(solution)/shard_map/ppermute | solution.py:47
  66.1 1.1 %shard_map.150 = (f32[16,896]{1,0:T(8,128)S(1)}, f32[16,896]{1,0:T(8,128)S(1)}, f32[16,128]{1,0:T(8,128)S(1)}) custom-call(s32[1]{0:T(128)} %bitcast.device_ref.refs_0_, bf16[4,16,512]{2,1,0:T(8,128)(2,1)S(1)} %pad_maximum_fusion.3.refs_0_, f32[16,1,512]{2,1,0:T(1,128)S(1)} %bitcast.33, bf16[8192,896]{1,0:T(8,128)(2,1)S(1)} %copy-done, ...), custom_call_target="tpu_custom_call" | custom-call | flops 117440512 | bytes 29458436 | tf_op jit(solution)/shard_map/pallas_call | solution.py:73
  67.2 1.1 %shard_map.151 = (f32[16,896]{1,0:T(8,128)S(1)}, f32[16,896]{1,0:T(8,128)S(1)}, f32[16,128]{1,0:T(8,128)S(1)}) custom-call(s32[1]{0:T(128)} %bitcast.device_ref.refs_0_, bf16[4,16,512]{2,1,0:T(8,128)(2,1)S(1)} %collective-permute-done.20.refs_0_, f32[16,1,512]{2,1,0:T(1,128)S(1)} %bitcast.34, bf16[8192,896]{1,0:T(8,128)(2,1)S(1)} %copy-done, ...), custom_call_target="tpu_custom_call" | custom-call | flops 117440512 | bytes 29581316 | tf_op jit(solution)/shard_map/pallas_call | solution.py:73
  68.3 2.2 %shard_map.152.in_ref = bf16[16,896]{1,0:T(8,128)(2,1)S(1)} custom-call(s32[1]{0:T(128)} %bitcast.device_ref.refs_0_, bf16[8,16,512]{2,1,0:T(8,128)(2,1)S(1)} %collective-permute-done.21.refs_0_, f32[16,1,512]{2,1,0:T(1,128)S(1)} %bitcast.35, bf16[8192,896]{1,0:T(8,128)(2,1)S(1)} %copy-done, bf16[8192,896]{1,0:T(8,128)(2,1)S(1)} %copy-done.1, ...), custom_call_target="tpu_custom_call" | custom-call | flops 234881024 | bytes 29646852 | tf_op jit(solution)/shard_map/pallas_call | solution.py:73
  70.6 0.3 collective-permute-start.22
  70.8 3.8 %collective-permute-start.23 = (bf16[1,16,896]{2,1,0:T(8,128)(2,1)S(1)}, bf16[1,16,896]{2,1,0:T(8,128)(2,1)S(1)}, u32[]{:S(2)}, u32[]{:S(2)}) collective-permute-start(bf16[1,16,896]{2,1,0:T(8,128)(2,1)S(1)} %bitcast.41), channel_id=1, source_target_pairs={{0,8},{1,9},{2,10},{3,11},{4,12},{5,13},{6,14},{7,15},{8,0},{9,1},... | collective-permute-start | bytes 86024 | tf_op jit(solution)/shard_map/ppermute | solution.py:47
  74.6 0.4 collective-permute-start.24
  75.0 1.9 %collective-permute-done.23 = bf16[1,16,896]{2,1,0:T(8,128)(2,1)S(1)} collective-permute-done((bf16[1,16,896]{2,1,0:T(8,128)(2,1)S(1)}, bf16[1,16,896]{2,1,0:T(8,128)(2,1)S(1)}, u32[]{:S(2)}, u32[]{:S(2)}) %collective-permute-start.23) | collective-permute-done | bytes 28704 | tf_op jit(solution)/shard_map/ppermute | solution.py:47
  76.9 3.4 %collective-permute-done.24 = bf16[1,16,896]{2,1,0:T(8,128)(2,1)S(1)} collective-permute-done((bf16[1,16,896]{2,1,0:T(8,128)(2,1)S(1)}, bf16[1,16,896]{2,1,0:T(8,128)(2,1)S(1)}, u32[]{:S(2)}, u32[]{:S(2)}) %collective-permute-start.24) | collective-permute-done | bytes 28704 | tf_op jit(solution)/shard_map/ppermute | solution.py:47
  80.3 1.6 %collective-permute-start.25 = (bf16[4,16,896]{2,1,0:T(8,128)(2,1)S(1)}, bf16[4,16,896]{2,1,0:T(8,128)(2,1)S(1)}, u32[]{:S(2)}, u32[]{:S(2)}) collective-permute-start(bf16[4,16,896]{2,1,0:T(8,128)(2,1)S(1)} %pad_maximum_fusion.refs_0_), channel_id=1, source_target_pairs={{0,2},{1,3},{2,0},{3,1},{4,6},{5,7},{6,4},{7,5},{8,10},{9,11},{10,... | collective-permute-start | bytes 344072 | tf_op jit(solution)/shard_map/ppermute | solution.py:47
  81.9 3.2 %collective-permute-done.25.refs_0_ = bf16[4,16,896]{2,1,0:T(8,128)(2,1)S(1)} collective-permute-done((bf16[4,16,896]{2,1,0:T(8,128)(2,1)S(1)}, bf16[4,16,896]{2,1,0:T(8,128)(2,1)S(1)}, u32[]{:S(2)}, u32[]{:S(2)}) %collective-permute-start.25) | collective-permute-done | bytes 114720 | tf_op jit(solution)/shard_map/ppermute | solution.py:47
  85.3 0.6 shard_map.154.refs_2_
  85.9 0.6 shard_map.155.refs_2_
  86.5 0.3 collective-permute-done.26.refs_0_
  86.8 1.8 %shard_map.156 = bf16[16,512]{1,0:T(8,128)(2,1)} custom-call(s32[1]{0:T(128)} %bitcast.device_ref.refs_0_, bf16[8,16,896]{2,1,0:T(8,128)(2,1)S(1)} %collective-permute-done.26.refs_0_, bf16[14336,512]{1,0:T(8,128)(2,1)S(1)} %bitcast.23, f32[16,512]{1,0:T(8,128)S(1)} %shard_map.155.refs_2_, bf16[16,512]{1,0:T(8,128)(2,1)S(1)} %shard_map.149.refs_3_), custom_call_target="tpu_custom_call" | custom-call | flops 117440512 | bytes 14958596 | tf_op jit(solution)/shard_map/pallas_call | solution.py:73
  (86 shorter events, 0.8 us)
Async XLA Ops:
  0.0 0.7 copy-start.8
  0.7 5.7 %copy-start.12 = (s32[16]{0:T(128)S(1)}, s32[16]{0:T(128)}, u32[]{:S(2)}) copy-start(s32[16]{0:T(128)} %param.26) | copy-start | bytes 196
  0.7 5.7 %copy-start.13 = (s32[16]{0:T(128)S(1)}, s32[16]{0:T(128)}, u32[]{:S(2)}) copy-start(s32[16]{0:T(128)} %param.27) | copy-start | bytes 196
  0.7 6.3 %collective-permute-start = (bf16[1,16,512]{2,1,0:T(8,128)(2,1)S(1)}, bf16[1,16,512]{2,1,0:T(8,128)(2,1)S(1)}, u32[]{:S(2)}, u32[]{:S(2)}) collective-permute-start(bf16[1,16,512]{2,1,0:T(8,128)(2,1)S(1)} %bitcast.48), channel_id=1, source_target_pairs={{0,4},{1,5},{2,6},{3,7},{4,0},{5,1},{6,2},{7,3},{8,12},{9,13},{10,... | collective-permute-start | bytes 49160 | tf_op jit(solution)/shard_map/ppermute | solution.py:47
  3.8 4.7 %collective-permute-start.1 = (bf16[1,16,512]{2,1,0:T(8,128)(2,1)S(1)}, bf16[1,16,512]{2,1,0:T(8,128)(2,1)S(1)}, u32[]{:S(2)}, u32[]{:S(2)}) collective-permute-start(bf16[1,16,512]{2,1,0:T(8,128)(2,1)S(1)} %bitcast.49), channel_id=1, source_target_pairs={{0,8},{1,9},{2,10},{3,11},{4,12},{5,13},{6,14},{7,15},{8,0},{9,1},... | collective-permute-start | bytes 49160 | tf_op jit(solution)/shard_map/ppermute | solution.py:47
  6.4 5.5 %collective-permute-start.2 = (bf16[1,16,512]{2,1,0:T(8,128)(2,1)S(1)}, bf16[1,16,512]{2,1,0:T(8,128)(2,1)S(1)}, u32[]{:S(2)}, u32[]{:S(2)}) collective-permute-start(bf16[1,16,512]{2,1,0:T(8,128)(2,1)S(1)} %bitcast.50), channel_id=1, source_target_pairs={{0,12},{1,13},{2,14},{3,15},{4,8},{5,9},{6,10},{7,11},{8,4},{9,5},... | collective-permute-start | bytes 49160 | tf_op jit(solution)/shard_map/ppermute | solution.py:47
  11.9 4.3 %collective-permute-start.3 = (bf16[4,16,512]{2,1,0:T(8,128)(2,1)S(1)}, bf16[4,16,512]{2,1,0:T(8,128)(2,1)S(1)}, u32[]{:S(2)}, u32[]{:S(2)}) collective-permute-start(bf16[4,16,512]{2,1,0:T(8,128)(2,1)S(1)} %pad_maximum_fusion.1.refs_0_), channel_id=1, source_target_pairs={{0,2},{1,3},{2,0},{3,1},{4,6},{5,7},{6,4},{7,5},{8,10},{9,11},{10,... | collective-permute-start | bytes 196616 | tf_op jit(solution)/shard_map/ppermute | solution.py:47
  16.3 3.1 %collective-permute-start.4 = (bf16[8,16,512]{2,1,0:T(8,128)(2,1)S(1)}, bf16[8,16,512]{2,1,0:T(8,128)(2,1)S(1)}, u32[]{:S(2)}, u32[]{:S(2)}) collective-permute-start(bf16[8,16,512]{2,1,0:T(8,128)(2,1)S(1)} %constant_dynamic-update-slice_fusion), channel_id=1, source_target_pairs={{0,1},{1,0},{2,3},{3,2},{4,5},{5,4},{6,7},{7,6},{8,9},{9,8},{10,11... | collective-permute-start | bytes 393224 | tf_op jit(solution)/shard_map/ppermute | solution.py:47
  16.3 2.2 %copy-start.2 = (bf16[8192,256]{1,0:T(8,128)(2,1)S(1)}, bf16[8192,256]{1,0:T(8,128)(2,1)}, u32[]{:S(2)}) copy-start(bf16[8192,256]{1,0:T(8,128)(2,1)} %refs_2_.8) | copy-start | bytes 12582916
  16.3 2.3 %copy-start.4 = (bf16[8192,32]{0,1:T(8,128)(2,1)S(1)}, bf16[8192,32]{0,1:T(8,128)(2,1)}, u32[]{:S(2)}) copy-start(bf16[8192,32]{0,1:T(8,128)(2,1)} %param.17) | copy-start | bytes 1572868
  16.3 2.4 %copy-start.5 = (bf16[8192,32]{0,1:T(8,128)(2,1)S(1)}, bf16[8192,32]{0,1:T(8,128)(2,1)}, u32[]{:S(2)}) copy-start(bf16[8192,32]{0,1:T(8,128)(2,1)} %param.18) | copy-start | bytes 1572868
  16.3 2.4 %copy-start.6 = (f32[8192]{0:T(1024)S(1)}, f32[8192]{0:T(1024)}, u32[]{:S(2)}) copy-start(f32[8192]{0:T(1024)} %param.15) | copy-start | bytes 98308
  16.3 14.5 %copy-start.10 = (bf16[1024,4,128]{2,1,0:T(4,128)(2,1)S(1)}, bf16[1024,4,128]{2,1,0:T(4,128)(2,1)}, u32[]{:S(2)}) copy-start(bf16[1024,4,128]{2,1,0:T(4,128)(2,1)} %param.20) | copy-start | bytes 3145732
  16.3 14.5 %copy-start.11 = (bf16[1024,4,128]{2,1,0:T(4,128)(2,1)S(1)}, bf16[1024,4,128]{2,1,0:T(4,128)(2,1)}, u32[]{:S(2)}) copy-start(bf16[1024,4,128]{2,1,0:T(4,128)(2,1)} %param.19) | copy-start | bytes 3145732
  20.3 4.5 %collective-permute-start.5 = (bf16[1,16,320]{2,1,0:T(8,128)(2,1)S(1)}, bf16[1,16,320]{2,1,0:T(8,128)(2,1)S(1)}, u32[]{:S(2)}, u32[]{:S(2)}) collective-permute-start(bf16[1,16,320]{2,1,0:T(8,128)(2,1)S(1)} %bitcast.44), channel_id=1, source_target_pairs={{0,4},{1,5},{2,6},{3,7},{4,0},{5,1},{6,2},{7,3},{8,12},{9,13},{10,... | collective-permute-start | bytes 30728 | tf_op jit(solution)/shard_map/ppermute | solution.py:47
  20.3 4.7 %collective-permute-start.6 = (bf16[1,16,320]{2,1,0:T(8,128)(2,1)S(1)}, bf16[1,16,320]{2,1,0:T(8,128)(2,1)S(1)}, u32[]{:S(2)}, u32[]{:S(2)}) collective-permute-start(bf16[1,16,320]{2,1,0:T(8,128)(2,1)S(1)} %bitcast.45), channel_id=1, source_target_pairs={{0,8},{1,9},{2,10},{3,11},{4,12},{5,13},{6,14},{7,15},{8,0},{9,1},... | collective-permute-start | bytes 30728 | tf_op jit(solution)/shard_map/ppermute | solution.py:47
  21.1 5.5 %collective-permute-start.7 = (bf16[1,16,320]{2,1,0:T(8,128)(2,1)S(1)}, bf16[1,16,320]{2,1,0:T(8,128)(2,1)S(1)}, u32[]{:S(2)}, u32[]{:S(2)}) collective-permute-start(bf16[1,16,320]{2,1,0:T(8,128)(2,1)S(1)} %bitcast.46), channel_id=1, source_target_pairs={{0,12},{1,13},{2,14},{3,15},{4,8},{5,9},{6,10},{7,11},{8,4},{9,5},... | collective-permute-start | bytes 30728 | tf_op jit(solution)/shard_map/ppermute | solution.py:47
  26.6 4.2 %collective-permute-start.8 = (bf16[4,16,320]{2,1,0:T(8,128)(2,1)S(1)}, bf16[4,16,320]{2,1,0:T(8,128)(2,1)S(1)}, u32[]{:S(2)}, u32[]{:S(2)}) collective-permute-start(bf16[4,16,320]{2,1,0:T(8,128)(2,1)S(1)} %pad_maximum_fusion.4), channel_id=1, source_target_pairs={{0,2},{1,3},{2,0},{3,1},{4,6},{5,7},{6,4},{7,5},{8,10},{9,11},{10,... | collective-permute-start | bytes 122888 | tf_op jit(solution)/shard_map/ppermute | solution.py:47
  30.7 2.6 %collective-permute-start.9 = (bf16[8,16,320]{2,1,0:T(8,128)(2,1)S(1)}, bf16[8,16,320]{2,1,0:T(8,128)(2,1)S(1)}, u32[]{:S(2)}, u32[]{:S(2)}) collective-permute-start(bf16[8,16,320]{2,1,0:T(8,128)(2,1)S(1)} %constant_dynamic-update-slice_fusion.5.refs_1_), channel_id=1, source_target_pairs={{0,1},{1,0},{2,3},{3,2},{4,5},{5,4},{6,7},{7,6},{8,9},{9,8},{10,11... | collective-permute-start | bytes 245768 | tf_op jit(solution)/shard_map/ppermute | solution.py:47
  32.8 2.0 %collective-permute-start.10 = (bf16[2,136,128]{2,1,0:T(8,128)(2,1)S(1)}, bf16[2,136,128]{2,1,0:T(8,128)(2,1)S(1)}, u32[]{:S(2)}, u32[]{:S(2)}) collective-permute-start(bf16[2,136,128]{2,1,0:T(8,128)(2,1)S(1)} %shard_map.142), channel_id=1, source_target_pairs={{0,1},{1,0},{2,3},{3,2},{4,5},{5,4},{6,7},{7,6},{8,9},{9,8},{10,11... | collective-permute-start | bytes 208904 | tf_op jit(solution)/shard_map/ppermute | solution.py:47
  35.1 4.0 %collective-permute-start.11 = (bf16[136,128]{1,0:T(8,128)(2,1)S(1)}, bf16[136,128]{1,0:T(8,128)(2,1)S(1)}, u32[]{:S(2)}, u32[]{:S(2)}) collective-permute-start(bf16[136,128]{1,0:T(8,128)(2,1)S(1)} %get-tuple-element.45), channel_id=1, source_target_pairs={{0,2},{1,3},{2,0},{3,1},{4,6},{5,7},{6,4},{7,5},{8,10},{9,11},{10,... | collective-permute-start | bytes 104456 | tf_op jit(solution)/shard_map/ppermute | solution.py:47
  39.0 14.4 %copy-start.3 = (bf16[4096,512]{1,0:T(8,128)(2,1)S(1)}, bf16[4096,512]{1,0:T(8,128)(2,1)}, u32[]{:S(2)}) copy-start(bf16[4096,512]{1,0:T(8,128)(2,1)} %refs_1_.8) | copy-start | bytes 12582916
  39.2 4.6 %collective-permute-start.12 = (bf16[136,128]{1,0:T(8,128)(2,1)S(1)}, bf16[136,128]{1,0:T(8,128)(2,1)S(1)}, u32[]{:S(2)}, u32[]{:S(2)}) collective-permute-start(bf16[136,128]{1,0:T(8,128)(2,1)S(1)} %get-tuple-element.48), channel_id=1, source_target_pairs={{0,4},{1,5},{2,6},{3,7},{4,0},{5,1},{6,2},{7,3},{8,12},{9,13},{10,... | collective-permute-start | bytes 104456 | tf_op jit(solution)/shard_map/ppermute | solution.py:47
  39.7 6.1 %collective-permute-start.13 = (bf16[136,128]{1,0:T(8,128)(2,1)S(1)}, bf16[136,128]{1,0:T(8,128)(2,1)S(1)}, u32[]{:S(2)}, u32[]{:S(2)}) collective-permute-start(bf16[136,128]{1,0:T(8,128)(2,1)S(1)} %get-tuple-element.48), channel_id=1, source_target_pairs={{0,8},{1,9},{2,10},{3,11},{4,12},{5,13},{6,14},{7,15},{8,0},{9,1},... | collective-permute-start | bytes 104456 | tf_op jit(solution)/shard_map/ppermute | solution.py:47
  43.5 5.7 %collective-permute-start.14 = (bf16[136,128]{1,0:T(8,128)(2,1)S(1)}, bf16[136,128]{1,0:T(8,128)(2,1)S(1)}, u32[]{:S(2)}, u32[]{:S(2)}) collective-permute-start(bf16[136,128]{1,0:T(8,128)(2,1)S(1)} %get-tuple-element.48), channel_id=1, source_target_pairs={{0,12},{1,13},{2,14},{3,15},{4,8},{5,9},{6,10},{7,11},{8,4},{9,5},... | collective-permute-start | bytes 104456 | tf_op jit(solution)/shard_map/ppermute | solution.py:47
  49.4 4.0 %collective-permute-start.15 = (bf16[4,16,256]{2,1,0:T(8,128)(2,1)S(1)}, bf16[4,16,256]{2,1,0:T(8,128)(2,1)S(1)}, u32[]{:S(2)}, u32[]{:S(2)}) collective-permute-start(bf16[4,16,256]{2,1,0:T(8,128)(2,1)S(1)} %shard_map.146.refs_0_), channel_id=1, source_target_pairs={{0,2},{1,3},{2,0},{3,1},{4,6},{5,7},{6,4},{7,5},{8,10},{9,11},{10,... | collective-permute-start | bytes 98312 | tf_op jit(solution)/shard_map/ppermute | solution.py:47
  53.4 1.3 %copy-start.9 = (bf16[16,512]{1,0:T(8,128)(2,1)S(1)}, bf16[16,512]{1,0:T(8,128)(2,1)}, u32[]{:S(2)}) copy-start(bf16[16,512]{1,0:T(8,128)(2,1)} %refs_3_.4) | copy-start | bytes 49156
  53.4 12.7 %copy-start.7 = (f32[8192]{0:T(1024)S(1)}, f32[8192]{0:T(1024)}, u32[]{:S(2)}) copy-start(f32[8192]{0:T(1024)} %param.22) | copy-start | bytes 98308
  53.4 1.3 %collective-permute-start.16 = (bf16[8,16,256]{2,1,0:T(8,128)(2,1)S(1)}, bf16[8,16,256]{2,1,0:T(8,128)(2,1)S(1)}, u32[]{:S(2)}, u32[]{:S(2)}) collective-permute-start(bf16[8,16,256]{2,1,0:T(8,128)(2,1)S(1)} %pad_maximum_fusion.2), channel_id=1, source_target_pairs={{0,1},{1,0},{2,3},{3,2},{4,5},{5,4},{6,7},{7,6},{8,9},{9,8},{10,11... | collective-permute-start | bytes 196616 | tf_op jit(solution)/shard_map/ppermute | solution.py:47
  53.5 12.6 %copy-start = (bf16[8192,896]{1,0:T(8,128)(2,1)S(1)}, bf16[8192,896]{1,0:T(8,128)(2,1)}, u32[]{:S(2)}) copy-start(bf16[8192,896]{1,0:T(8,128)(2,1)} %refs_2_.11) | copy-start | bytes 44040196
  53.5 12.6 %copy-start.1 = (bf16[8192,896]{1,0:T(8,128)(2,1)S(1)}, bf16[8192,896]{1,0:T(8,128)(2,1)}, u32[]{:S(2)}) copy-start(bf16[8192,896]{1,0:T(8,128)(2,1)} %refs_3_.7) | copy-start | bytes 44040196
  55.2 4.4 %collective-permute-start.17 = (bf16[1,16,512]{2,1,0:T(8,128)(2,1)S(1)}, bf16[1,16,512]{2,1,0:T(8,128)(2,1)S(1)}, u32[]{:S(2)}, u32[]{:S(2)}) collective-permute-start(bf16[1,16,512]{2,1,0:T(8,128)(2,1)S(1)} %bitcast.36), channel_id=1, source_target_pairs={{0,4},{1,5},{2,6},{3,7},{4,0},{5,1},{6,2},{7,3},{8,12},{9,13},{10,... | collective-permute-start | bytes 49160 | tf_op jit(solution)/shard_map/ppermute | solution.py:47
  55.3 4.7 %collective-permute-start.18 = (bf16[1,16,512]{2,1,0:T(8,128)(2,1)S(1)}, bf16[1,16,512]{2,1,0:T(8,128)(2,1)S(1)}, u32[]{:S(2)}, u32[]{:S(2)}) collective-permute-start(bf16[1,16,512]{2,1,0:T(8,128)(2,1)S(1)} %bitcast.37), channel_id=1, source_target_pairs={{0,8},{1,9},{2,10},{3,11},{4,12},{5,13},{6,14},{7,15},{8,0},{9,1},... | collective-permute-start | bytes 49160 | tf_op jit(solution)/shard_map/ppermute | solution.py:47
  56.2 5.5 %collective-permute-start.19 = (bf16[1,16,512]{2,1,0:T(8,128)(2,1)S(1)}, bf16[1,16,512]{2,1,0:T(8,128)(2,1)S(1)}, u32[]{:S(2)}, u32[]{:S(2)}) collective-permute-start(bf16[1,16,512]{2,1,0:T(8,128)(2,1)S(1)} %bitcast.38), channel_id=1, source_target_pairs={{0,12},{1,13},{2,14},{3,15},{4,8},{5,9},{6,10},{7,11},{8,4},{9,5},... | collective-permute-start | bytes 49160 | tf_op jit(solution)/shard_map/ppermute | solution.py:47
  61.7 4.3 %collective-permute-start.20 = (bf16[4,16,512]{2,1,0:T(8,128)(2,1)S(1)}, bf16[4,16,512]{2,1,0:T(8,128)(2,1)S(1)}, u32[]{:S(2)}, u32[]{:S(2)}) collective-permute-start(bf16[4,16,512]{2,1,0:T(8,128)(2,1)S(1)} %pad_maximum_fusion.3.refs_0_), channel_id=1, source_target_pairs={{0,2},{1,3},{2,0},{3,1},{4,6},{5,7},{6,4},{7,5},{8,10},{9,11},{10,... | collective-permute-start | bytes 196616 | tf_op jit(solution)/shard_map/ppermute | solution.py:47
  66.1 2.2 %collective-permute-start.21 = (bf16[8,16,512]{2,1,0:T(8,128)(2,1)S(1)}, bf16[8,16,512]{2,1,0:T(8,128)(2,1)S(1)}, u32[]{:S(2)}, u32[]{:S(2)}) collective-permute-start(bf16[8,16,512]{2,1,0:T(8,128)(2,1)S(1)} %constant_dynamic-update-slice_fusion.10), channel_id=1, source_target_pairs={{0,1},{1,0},{2,3},{3,2},{4,5},{5,4},{6,7},{7,6},{8,9},{9,8},{10,11... | collective-permute-start | bytes 393224 | tf_op jit(solution)/shard_map/ppermute | solution.py:47
  68.3 17.0 %slice-start = ((s8[14680064]{0:T(1024)(128)(4,1)}), s8[4194304]{0:T(1024)(128)(4,1)S(1)}, s32[]{:S(2)}) async-start(s8[14680064]{0:T(1024)(128)(4,1)} %bitcast.22), calls=%async_computation | async-start | bytes 8388608
  70.5 14.8 %slice-start.1 = ((s8[14680064]{0:T(1024)(128)(4,1)}), s8[4194304]{0:T(1024)(128)(4,1)S(1)}, s32[]{:S(2)}) async-start(s8[14680064]{0:T(1024)(128)(4,1)} %bitcast.22), calls=%async_computation.1 | async-start | bytes 8388608
  70.5 14.8 %slice-start.2 = ((s8[14680064]{0:T(1024)(128)(4,1)}), s8[4194304]{0:T(1024)(128)(4,1)S(1)}, s32[]{:S(2)}) async-start(s8[14680064]{0:T(1024)(128)(4,1)} %bitcast.22), calls=%async_computation.2 | async-start | bytes 8388608
  70.5 14.8 %slice-start.3 = ((s8[14680064]{0:T(1024)(128)(4,1)}), s8[2097152]{0:T(1024)(128)(4,1)S(1)}, s32[]{:S(2)}) async-start(s8[14680064]{0:T(1024)(128)(4,1)} %bitcast.22), calls=%async_computation.3 | async-start | bytes 4194304
  70.6 4.5 %collective-permute-start.22 = (bf16[1,16,896]{2,1,0:T(8,128)(2,1)S(1)}, bf16[1,16,896]{2,1,0:T(8,128)(2,1)S(1)}, u32[]{:S(2)}, u32[]{:S(2)}) collective-permute-start(bf16[1,16,896]{2,1,0:T(8,128)(2,1)S(1)} %bitcast.40), channel_id=1, source_target_pairs={{0,4},{1,5},{2,6},{3,7},{4,0},{5,1},{6,2},{7,3},{8,12},{9,13},{10,... | collective-permute-start | bytes 86024 | tf_op jit(solution)/shard_map/ppermute | solution.py:47
  70.8 6.1 %collective-permute-start.23 = (bf16[1,16,896]{2,1,0:T(8,128)(2,1)S(1)}, bf16[1,16,896]{2,1,0:T(8,128)(2,1)S(1)}, u32[]{:S(2)}, u32[]{:S(2)}) collective-permute-start(bf16[1,16,896]{2,1,0:T(8,128)(2,1)S(1)} %bitcast.41), channel_id=1, source_target_pairs={{0,8},{1,9},{2,10},{3,11},{4,12},{5,13},{6,14},{7,15},{8,0},{9,1},... | collective-permute-start | bytes 86024 | tf_op jit(solution)/shard_map/ppermute | solution.py:47
  74.6 5.7 %collective-permute-start.24 = (bf16[1,16,896]{2,1,0:T(8,128)(2,1)S(1)}, bf16[1,16,896]{2,1,0:T(8,128)(2,1)S(1)}, u32[]{:S(2)}, u32[]{:S(2)}) collective-permute-start(bf16[1,16,896]{2,1,0:T(8,128)(2,1)S(1)} %bitcast.42), channel_id=1, source_target_pairs={{0,12},{1,13},{2,14},{3,15},{4,8},{5,9},{6,10},{7,11},{8,4},{9,5},... | collective-permute-start | bytes 86024 | tf_op jit(solution)/shard_map/ppermute | solution.py:47
  80.3 4.9 %collective-permute-start.25 = (bf16[4,16,896]{2,1,0:T(8,128)(2,1)S(1)}, bf16[4,16,896]{2,1,0:T(8,128)(2,1)S(1)}, u32[]{:S(2)}, u32[]{:S(2)}) collective-permute-start(bf16[4,16,896]{2,1,0:T(8,128)(2,1)S(1)} %pad_maximum_fusion.refs_0_), channel_id=1, source_target_pairs={{0,2},{1,3},{2,0},{3,1},{4,6},{5,7},{6,4},{7,5},{8,10},{9,11},{10,... | collective-permute-start | bytes 344072 | tf_op jit(solution)/shard_map/ppermute | solution.py:47
  85.2 1.6 %collective-permute-start.26 = (bf16[8,16,896]{2,1,0:T(8,128)(2,1)S(1)}, bf16[8,16,896]{2,1,0:T(8,128)(2,1)S(1)}, u32[]{:S(2)}, u32[]{:S(2)}) collective-permute-start(bf16[8,16,896]{2,1,0:T(8,128)(2,1)S(1)} %constant_dynamic-update-slice_fusion.15), channel_id=1, source_target_pairs={{0,1},{1,0},{2,3},{3,2},{4,5},{5,4},{6,7},{7,6},{8,9},{9,8},{10,11... | collective-permute-start | bytes 688136 | tf_op jit(solution)/shard_map/ppermute | solution.py:47

commit v5 on v4

--- a/solution.py
+++ b/solution.py
@@ -47,25 +47,31 @@
     return lax.ppermute(part, "ctx", [(index, index ^ mask) for index in range(devices)])
 
 
-def gathered(part):
+def gathered(part, given=None):
     devices = lax.axis_size("ctx")
     held = part[None]
     *rounds, last, _ = digits(devices)
 
-    def arrive(stride, radix):
+    def arrive(stride, radix, held):
         return [shifted(held, stride * digit) for digit in range(1, radix)]
 
     for stride, radix, _ in rounds:
-        arrived = arrive(stride, radix)
+        arrived = arrive(stride, radix, held if given is None else given[None])
+        given = None
         held = jnp.concatenate([held] + arrived, axis=0)
-    brought = arrive(*last[:2])
-    near = jnp.concatenate([held] + brought, axis=0)
-    return held, brought, shifted(near, 1)
+    return pieces_of(held, *last[:2])
+
+
+def pieces_of(held, stride, radix):
+    brought = [shifted(held, stride * digit) for digit in range(1, radix)]
+    brought = brought[0] if radix == 2 else jnp.concatenate(brought, axis=0)
+    far = shifted(held, 1)
+    return held, far, brought, shifted(brought, 1)
 
 
 def together(pieces):
-    held, brought, far = pieces
-    return jnp.concatenate([held, *brought, far], axis=0)
+    held, far, brought, far_brought = pieces
+    return jnp.concatenate([held, brought, far, far_brought], axis=0)
 
 
 def call(body, name, out_shape, args, scratch=(), flops=0):
@@ -118,9 +124,8 @@
 
 
 def contract(name, pieces, own, weights, widths, gain, finish, extras, out_shape, owner_of=by_place):
-    held, brought, far = pieces
     devices = lax.axis_size("ctx")
-    _, rows, depth = held.shape
+    near, rows, depth = pieces[0].shape
     normed = gain is not None
     gains = [gain.reshape(devices, 1, depth)] if normed else []
     totals_of = [jax.ShapeDtypeStruct((rows, w), jnp.float32) for w in widths]
@@ -164,10 +169,11 @@
             2 * rows * sum(p.shape[0] for p in parts) * depth * sum(widths),
         )
 
-    near = held.shape[0]
-    sums = stage("_a", 0, [held], (), False)
-    sums = stage("_b", near, brought, sums, False)
-    return stage("_c", devices // 2, [far], sums, True)
+    sums = ()
+    firsts = (0, devices // 2, near, devices // 2 + near)
+    for label, first, piece in zip(("_a", "_b", "_c", "_d"), firsts, pieces):
+        sums = stage(label, first, [piece], sums, label == "_d")
+    return sums
 
 
 def project_finish(factor, totals, extra_refs, out_ref):
@@ -283,85 +289,89 @@
     message_ref[pairs:] = terms_of(level)
 
 
-def half_kernel(scale, head_dim, sends, device_ref, blocks_ref, key_ref, value_ref, limit_ref, *out_refs):
-    places, rows, _ = blocks_ref.shape
-    span = key_ref.shape[0]
-    value_heads = key_ref.shape[1] // head_dim
-    units = places // value_heads
+def attend_unit_kernel(scale, head_dim, sends, device_ref, blocks_ref, key_ref, value_ref, limit_ref, *out_refs):
+    value_heads, rows, _ = blocks_ref.shape
+    span = value_ref.shape[0]
     local = LANES // (value_heads * rows)
-    count = units * local
-    group_index = lax.div(device_ref[0], 2 * units)
-    visible = (lax.broadcasted_iota(jnp.int32, (rows, span), 1) < limit_ref[:, :1])[None]
-    means = [[] for _ in range(units)]
-    levels = [[] for _ in range(units)]
+    count = local * rows
+    heads = value_heads * local
+    group_index = lax.div(device_ref[0], lax.axis_size("ctx") // value_heads)
+    limit = limit_ref[:, :1]
+    visible = (lax.broadcasted_iota(jnp.int32, (rows, span), 1) < limit)[None]
+    seen = jnp.broadcast_to((limit > 0)[None], (heads, rows, 1)).reshape(heads * rows, 1)
+    logits = []
     for g in range(value_heads):
-        lanes = pl.ds(g * head_dim, head_dim)
-        parts = []
-        for unit in range(units):
-            block = blocks_ref[unit * value_heads + lax.bitwise_xor(group_index, g)]
-            parts += [block[:, h * head_dim : (h + 1) * head_dim] for h in range(local)]
-        logits = lax.dot_general(
-            jnp.concatenate(parts, axis=0), key_ref[:, lanes], (((1,), (1,)), ((), ())),
-            preferred_element_type=jnp.float32,
-        ) * scale
-        masked = jnp.where(visible, logits.reshape(count, rows, span), MASKED)
-        top = jnp.max(masked, axis=2, keepdims=True)
-        weights = jnp.where(visible, jnp.exp(masked - top), 0.0)
-        total = jnp.sum(weights, axis=2, keepdims=True).reshape(count * rows, 1)
-        top = top.reshape(count * rows, 1)
-        summed = jnp.dot(
-            weights.astype(jnp.bfloat16).reshape(count * rows, span), value_ref[:, lanes],
-            preferred_element_type=jnp.float32,
-        )
-        seen = total > 0.0
-        safe = jnp.where(seen, total, 1.0)
-        mean = summed / safe
-        level = jnp.broadcast_to(jnp.where(seen, top + jnp.log(safe), MASKED), (count * rows, LANES))
-        run = local * rows
-        for unit in range(units):
-            means[unit].append(mean[unit * run : (unit + 1) * run])
-            levels[unit].append(level[unit * run : (unit + 1) * run])
-    for unit in range(units):
-        mean = jnp.concatenate(means[unit], axis=0)
-        level = jnp.concatenate(levels[unit], axis=0)
-        if sends:
-            put_message(out_refs[0].at[unit], mean, level)
-        else:
-            out_refs[0][unit] = mean
-            out_refs[1][unit] = level
-
-
-def merge_core_kernel(mean_ref, level_ref, message_ref, sent_ref, mean_out_ref, level_out_ref):
-    for unit in (1, 0):
-        mean, level = merge([(mean_ref[unit], level_ref[unit]), read_message(message_ref[unit])])
-        if unit == 1:
-            put_message(sent_ref, mean, level)
-        else:
-            mean_out_ref[...] = mean
-            level_out_ref[...] = level
-
-
-def merge_next_kernel(mean_ref, level_ref, message_ref, sent_ref, mean_out_ref, level_out_ref):
+        block = blocks_ref[lax.bitwise_xor(group_index, g)]
+        queries = jnp.concatenate(
+            [block[:, h * head_dim : (h + 1) * head_dim] for h in range(local)], axis=0
+        )
+        logits.append(
+            jnp.dot(
+                queries, key_ref[g * head_dim : (g + 1) * head_dim, :],
+                preferred_element_type=jnp.float32,
+            )
+        )
+    logits = jnp.concatenate(logits, axis=0).reshape(heads, rows, span)
+    masked = jnp.where(visible, logits, MASKED)
+    top = jnp.max(masked, axis=2, keepdims=True)
+    weights = jnp.exp2((masked - top) * (scale * math.log2(math.e)))
+    total = jnp.sum(weights, axis=2, keepdims=True).reshape(heads * rows, 1)
+    rounded = weights.astype(jnp.bfloat16).reshape(heads * rows, span)
+    summed = jnp.concatenate(
+        [
+            jnp.dot(
+                rounded[g * count : (g + 1) * count],
+                value_ref[:, g * head_dim : (g + 1) * head_dim],
+                preferred_element_type=jnp.float32,
+            )
+            for g in range(value_heads)
+        ],
+        axis=0,
+    )
+    mean = summed / total
+    level = jnp.where(seen, top.reshape(heads * rows, 1) * scale + jnp.log(total), MASKED)
+    level = jnp.broadcast_to(level, (heads * rows, LANES))
+    if sends:
+        put_message(out_refs[0], mean, level)
+    else:
+        out_refs[0][...] = mean
+        out_refs[1][...] = level
+
+
+def merge_last_kernel(mean_ref, level_ref, message_ref, sent_ref):
     mean, level = merge([(mean_ref[...], level_ref[...]), read_message(message_ref[...])])
+    put_message(sent_ref, mean, level)
+
+
+def merge_next_kernel(mean_ref, level_ref, core_ref, message_ref, sent_ref, mean_out_ref, level_out_ref):
+    mean, level = merge(
+        [(mean_ref[...], level_ref[...]), read_message(core_ref[...]), read_message(message_ref[...])]
+    )
     put_message(sent_ref, mean, level)
     mean_out_ref[...] = mean
     level_out_ref[...] = level
 
 
-def fresh_kernel(scale, head_dim, value_heads, key_width, device_ref, near_ref, far_ref, score_ref, value_ref):
+def fresh_kernel(
+    scale, head_dim, value_heads, key_width, device_ref, held_ref, brought_ref, far_ref, far_brought_ref,
+    score_ref, value_ref,
+):
     _, rows, used = far_ref.shape
     query_width = used - 2 * key_width
     run = head_dim // key_width
-    units = run // 2
     group_index = lax.div(device_ref[0], run)
     core = lax.rem(device_ref[0], 2)
-    step = lax.rem(lax.div(device_ref[0], 2), units)
+    step = lax.rem(lax.div(device_ref[0], 2), 2)
     for g in range(value_heads):
         turned = lax.bitwise_xor(group_index, g)
         news = []
         for index in range(run):
-            place = lax.bitwise_xor(step, index // 2) * value_heads + turned
-            block = jnp.where(core == index % 2, near_ref[place], far_ref[place])
+            same = core == index % 2
+            block = jnp.where(
+                step == index // 2,
+                jnp.where(same, held_ref[turned], far_ref[turned]),
+                jnp.where(same, brought_ref[turned], far_brought_ref[turned]),
+            )
             news.append(block[:, query_width:])
         key = jnp.concatenate([new[:, :key_width] for new in news], axis=1).astype(jnp.float32)
         value = jnp.concatenate([new[:, key_width:] for new in news], axis=1).astype(jnp.float32)
@@ -499,7 +509,7 @@
     if width % LANES == 0:
         sides = (w_key.T, w_value.T)
     projected = contract(
-        "project", gathered(begun), own, (w_query, *sides), (query_width, key_width, key_width),
+        "project", gathered(begun, hidden_in), own, (w_query, *sides), (query_width, key_width, key_width),
         attn_gain, project_finish, (cosine, sine), buffer(rows, used),
     )
     limit = jnp.broadcast_to((positions - own * span)[:, None], (rows, LANES))
@@ -513,43 +523,42 @@
         and head_dim == LANES
         and value_heads * (query_width // head_dim) * rows == LANES
     ):
-        held, brought, far = gathered(projected)
-        near = jnp.concatenate([held] + brought, axis=0)
+        held, far, brought, far_brought = gathered(projected)
         unit = (LANES, LANES)
         message = buffer(LANES + 8, LANES)
         wide = buffer(*unit, dtype=jnp.float32)
-        pair = buffer(2, *unit, dtype=jnp.float32)
-        work = 2 * heads * rows * span * head_dim
-
-        def half(name, blocks, sends, out_shape):
+        work = heads * rows * span * head_dim
+        keys_across = rotated_prefix_keys.transpose(1, 2, 0).reshape(value_heads * head_dim, span)
+
+        def attended(label, blocks, sends):
             return call(
-                lambda *refs: half_kernel(scale, head_dim, sends, *refs), name, out_shape,
-                (own, blocks, keys, values, limit), (), work,
+                lambda *refs: attend_unit_kernel(scale, head_dim, sends, *refs), "attend_" + label,
+                message if sends else (wide, wide), (own, blocks, keys_across, values, limit), (), work,
             )
 
-        given = half("attend_near", near, True, buffer(2, LANES + 8, LANES))
+        given = attended("a", held, True)
+        taken_held = shifted(given, 1)
+        mean, level = attended("b", far, False)
+        given = attended("c", brought, True)
         taken = shifted(given, 1)
-        mean, level = half("attend_far", far, False, (pair, pair))
-        given, mean, level = call(
-            merge_core_kernel, "merge_core", (message, wide, wide), (mean, level, taken)
+        given = call(
+            merge_last_kernel, "merge_last", message, (*attended("d", far_brought, False), taken)
         )
         taken = shifted(given, rounds[1][0])
         given, mean, level = call(
-            merge_next_kernel, "merge_next", (message, wide, wide), (mean, level, taken)
+            merge_next_kernel, "merge_next", (message, wide, wide), (mean, level, taken_held, taken)
         )
         taken = [shifted(given, rounds[0][0] * digit) for digit in range(1, rounds[0][1])]
         score, value = call(
             lambda *refs: fresh_kernel(scale, head_dim, value_heads, key_width, *refs), "fresh",
-            (wide, wide), (own, near, far),
+            (wide, wide), (own, held, brought, far, far_brought),
         )
         done = call(
             lambda *refs: settle_kernel(rows, *refs), "settle",
             buffer(value_heads, rows, query_width), (mean, level, *taken, score, value),
         )
-        brought = [shifted(done, rounds[1][0])]
-        far = shifted(jnp.concatenate([done] + brought, axis=0), 1)
         mid_part = contract(
-            "output", (done, brought, far), own, (w_out,), (width,),
+            "output", pieces_of(done, *rounds[1][:2]), own, (w_out,), (width,),
             None, residual_finish, (hidden_in,), buffer(rows, width), by_group,
         )
     else:

time: 88.8 us -> 87 us (0.980)
  waiting for transfers between devices: 36.4 us -> 34.1 us
  local copies, waits for them, and re-layouts: 3.95 us -> 4.96 us
    ppermute x27 -> x33, waiting for transfers between devices: 36.4 us -> 34.1 us  [shifted(): lax.ppermute(part, 'ctx', [(index, index ^ mask) for index in range(devic...]
    unnamed x52 -> x37, local copies, waits for them, and re-layouts: 3.26 us -> 4.07 us
    pallas_call x21 -> x27, Pallas kernels: 13.5 us -> 12.7 us  [call(): pl.pallas_call(body, out_shape=out_shape, in_specs=[SMEM if a.dtype == jn...]
    ppermute x27 -> x33, starting transfers between devices: 33.7 us -> 34.1 us  [shifted(): lax.ppermute(part, 'ctx', [(index, index ^ mask) for index in range(devic...]
  transfers between devices with their start and end apart: 27 -> 33, of which waited for: 18 -> 17; matrix products, arithmetic and copies ran while one was open for 1% -> 2% of each run, Pallas kernels for 9% -> 11%
where the time goes in v5:
time: 87 us; the launch traced here: 86.8 us
  starting transfers between devices  34.1 us (39%)
  waiting for transfers between devices  34.1 us (39%)
  Pallas kernels  12.7 us (15%)
  local copies, waits for them, and re-layouts  4.96 us (6%)
    ppermute x33, starting transfers between devices, shifted(): lax.ppermute(part, 'ctx', [(index, index ^ mask) for index in range(devic...  34.1 us
    ppermute x33, waiting for transfers between devices, shifted(): lax.ppermute(part, 'ctx', [(index, index ^ mask) for index in range(devic...  34.1 us
    pallas_call x27, Pallas kernels, call(): pl.pallas_call(body, out_shape=out_shape, in_specs=[SMEM if a.dtype == jn...  12.7 us
    unnamed x37, local copies, waits for them, and re-layouts  4.07 us
  transfers between devices with their start and end apart: 33, of which 17 were waited for; matrix products, arithmetic and copies ran while one was open for 2% of the time, Pallas kernels for 11%

profile of v5, /device:TPU:0, one launch (start us, length us, event | category | flops | bytes accessed | tf_op | source)
XLA Modules:
  0.0 86.8 jit_solution(8482325630353822954)
XLA Ops:
  0.0 3.1 %collective-permute-start = (bf16[1,16,512]{2,1,0:T(8,128)(2,1)}, bf16[1,16,512]{2,1,0:T(8,128)(2,1)S(1)}, u32[]{:S(2)}, u32[]{:S(2)}) collective-permute-start(bf16[1,16,512]{2,1,0:T(8,128)(2,1)} %bitcast.57), channel_id=1, source_target_pairs={{0,4},{1,5},{2,6},{3,7},{4,0},{5,1},{6,2},{7,3},{8,12},{9,13},{10,... | collective-permute-start | bytes 49160 | tf_op jit(solution)/shard_map/ppermute | solution.py:47
  3.1 2.6 %collective-permute-start.1 = (bf16[1,16,512]{2,1,0:T(8,128)(2,1)}, bf16[1,16,512]{2,1,0:T(8,128)(2,1)S(1)}, u32[]{:S(2)}, u32[]{:S(2)}) collective-permute-start(bf16[1,16,512]{2,1,0:T(8,128)(2,1)} %bitcast.58), channel_id=1, source_target_pairs={{0,8},{1,9},{2,10},{3,11},{4,12},{5,13},{6,14},{7,15},{8,0},{9,1},... | collective-permute-start | bytes 49160 | tf_op jit(solution)/shard_map/ppermute | solution.py:47
  5.6 0.8 copy-done.8
  6.5 0.6 copy-done.12
  7.7 0.2 collective-permute-done.1
  8.0 3.4 %collective-permute-done.2 = bf16[1,16,512]{2,1,0:T(8,128)(2,1)S(1)} collective-permute-done((bf16[1,16,512]{2,1,0:T(8,128)(2,1)}, bf16[1,16,512]{2,1,0:T(8,128)(2,1)S(1)}, u32[]{:S(2)}, u32[]{:S(2)}) %collective-permute-start.2) | collective-permute-done | bytes 16416 | tf_op jit(solution)/shard_map/ppermute | solution.py:47
  11.4 1.6 %collective-permute-start.3 = (bf16[4,16,512]{2,1,0:T(8,128)(2,1)S(1)}, bf16[4,16,512]{2,1,0:T(8,128)(2,1)S(1)}, u32[]{:S(2)}, u32[]{:S(2)}) collective-permute-start(bf16[4,16,512]{2,1,0:T(8,128)(2,1)S(1)} %pad_maximum_fusion.1.refs_0_), channel_id=1, source_target_pairs={{0,2},{1,3},{2,0},{3,1},{4,6},{5,7},{6,4},{7,5},{8,10},{9,11},{10,... | collective-permute-start | bytes 196616 | tf_op jit(solution)/shard_map/ppermute | solution.py:47
  13.1 2.7 %collective-permute-done.3.refs_0_ = bf16[4,16,512]{2,1,0:T(8,128)(2,1)S(1)} collective-permute-done((bf16[4,16,512]{2,1,0:T(8,128)(2,1)S(1)}, bf16[4,16,512]{2,1,0:T(8,128)(2,1)S(1)}, u32[]{:S(2)}, u32[]{:S(2)}) %collective-permute-start.3) | collective-permute-done | bytes 65568 | tf_op jit(solution)/shard_map/ppermute | solution.py:47
  15.8 2.1 %copy-done.2 = bf16[8192,256]{1,0:T(8,128)(2,1)S(1)} copy-done((bf16[8192,256]{1,0:T(8,128)(2,1)S(1)}, bf16[8192,256]{1,0:T(8,128)(2,1)}, u32[]{:S(2)}) %copy-start.2) | copy-done | bytes 4194328
  18.2 0.3 shard_map.137
  18.5 0.3 shard_map.138
  18.9 0.3 shard_map.139
  19.2 0.5 shard_map.141
  19.8 0.7 collective-permute-start.7
  20.5 3.6 %collective-permute-start.8 = (bf16[1,16,320]{2,1,0:T(8,128)(2,1)S(1)}, bf16[1,16,320]{2,1,0:T(8,128)(2,1)S(1)}, u32[]{:S(2)}, u32[]{:S(2)}) collective-permute-start(bf16[1,16,320]{2,1,0:T(8,128)(2,1)S(1)} %bitcast.51), channel_id=1, source_target_pairs={{0,12},{1,13},{2,14},{3,15},{4,8},{5,9},{6,10},{7,11},{8,4},{9,5},... | collective-permute-start | bytes 30728 | tf_op jit(solution)/shard_map/ppermute | solution.py:47
  24.1 0.3 collective-permute-done.7
  24.4 1.6 %collective-permute-done.8 = bf16[1,16,320]{2,1,0:T(8,128)(2,1)S(1)} collective-permute-done((bf16[1,16,320]{2,1,0:T(8,128)(2,1)S(1)}, bf16[1,16,320]{2,1,0:T(8,128)(2,1)S(1)}, u32[]{:S(2)}, u32[]{:S(2)}) %collective-permute-start.8) | collective-permute-done | bytes 10272 | tf_op jit(solution)/shard_map/ppermute | solution.py:47
  26.0 1.6 %collective-permute-start.11 = (bf16[4,16,320]{2,1,0:T(8,128)(2,1)S(1)}, bf16[4,16,320]{2,1,0:T(8,128)(2,1)S(1)}, u32[]{:S(2)}, u32[]{:S(2)}) collective-permute-start(bf16[4,16,320]{2,1,0:T(8,128)(2,1)S(1)} %pad_maximum_fusion.3.refs_1_), channel_id=1, source_target_pairs={{0,2},{1,3},{2,0},{3,1},{4,6},{5,7},{6,4},{7,5},{8,10},{9,11},{10,... | collective-permute-start | bytes 122888 | tf_op jit(solution)/shard_map/ppermute | solution.py:47
  27.6 2.5 %collective-permute-done.11.refs_1_.refs_2_ = bf16[4,16,320]{2,1,0:T(8,128)(2,1)S(1)} collective-permute-done((bf16[4,16,320]{2,1,0:T(8,128)(2,1)S(1)}, bf16[4,16,320]{2,1,0:T(8,128)(2,1)S(1)}, u32[]{:S(2)}, u32[]{:S(2)}) %collective-permute-start.11) | collective-permute-done | bytes 40992 | tf_op jit(solution)/shard_map/ppermute | solution.py:47
  30.2 0.7 copy.16
  30.8 0.2 copy.19
  31.1 0.6 shard_map.145
  31.7 0.5 collective-permute-start.13
  32.3 0.6 shard_map.143
  32.9 0.5 collective-permute-start.10
  33.4 0.5 shard_map.144
  34.1 1.6 %collective-permute-start.14 = (bf16[136,128]{1,0:T(8,128)(2,1)S(1)}, bf16[136,128]{1,0:T(8,128)(2,1)S(1)}, u32[]{:S(2)}, u32[]{:S(2)}) collective-permute-start(bf16[136,128]{1,0:T(8,128)(2,1)S(1)} %shard_map.146), channel_id=1, source_target_pairs={{0,2},{1,3},{2,0},{3,1},{4,6},{5,7},{6,4},{7,5},{8,10},{9,11},{10,... | collective-permute-start | bytes 104456 | tf_op jit(solution)/shard_map/ppermute | solution.py:47
  35.7 0.5 shard_map.142
  36.2 1.8 %collective-permute-done.14.message_ref = bf16[136,128]{1,0:T(8,128)(2,1)S(1)} collective-permute-done((bf16[136,128]{1,0:T(8,128)(2,1)S(1)}, bf16[136,128]{1,0:T(8,128)(2,1)S(1)}, u32[]{:S(2)}, u32[]{:S(2)}) %collective-permute-start.14) | collective-permute-done | bytes 34848 | tf_op jit(solution)/shard_map/ppermute | solution.py:47
  38.1 0.2 shard_map.147
  38.2 0.4 collective-permute-start.15
  38.7 3.8 %collective-permute-start.16 = (bf16[136,128]{1,0:T(8,128)(2,1)S(1)}, bf16[136,128]{1,0:T(8,128)(2,1)S(1)}, u32[]{:S(2)}, u32[]{:S(2)}) collective-permute-start(bf16[136,128]{1,0:T(8,128)(2,1)S(1)} %get-tuple-element.57), channel_id=1, source_target_pairs={{0,8},{1,9},{2,10},{3,11},{4,12},{5,13},{6,14},{7,15},{8,0},{9,1},... | collective-permute-start | bytes 104456 | tf_op jit(solution)/shard_map/ppermute | solution.py:47
  42.7 0.2 shard_map.148
  42.9 1.9 %collective-permute-done.16.refs_3_ = bf16[136,128]{1,0:T(8,128)(2,1)S(1)} collective-permute-done((bf16[136,128]{1,0:T(8,128)(2,1)S(1)}, bf16[136,128]{1,0:T(8,128)(2,1)S(1)}, u32[]{:S(2)}, u32[]{:S(2)}) %collective-permute-start.16) | collective-permute-done | bytes 34848 | tf_op jit(solution)/shard_map/ppermute | solution.py:47
  44.8 3.4 %collective-permute-done.17.refs_4_ = bf16[136,128]{1,0:T(8,128)(2,1)S(1)} collective-permute-done((bf16[136,128]{1,0:T(8,128)(2,1)S(1)}, bf16[136,128]{1,0:T(8,128)(2,1)S(1)}, u32[]{:S(2)}, u32[]{:S(2)}) %collective-permute-start.17) | collective-permute-done | bytes 34848 | tf_op jit(solution)/shard_map/ppermute | solution.py:47
  48.2 0.2 shard_map.149.refs_0_
  48.4 1.6 %collective-permute-start.18 = (bf16[4,16,256]{2,1,0:T(8,128)(2,1)S(1)}, bf16[4,16,256]{2,1,0:T(8,128)(2,1)S(1)}, u32[]{:S(2)}, u32[]{:S(2)}) collective-permute-start(bf16[4,16,256]{2,1,0:T(8,128)(2,1)S(1)} %shard_map.149.refs_0_), channel_id=1, source_target_pairs={{0,2},{1,3},{2,0},{3,1},{4,6},{5,7},{6,4},{7,5},{8,10},{9,11},{10,... | collective-permute-start | bytes 98312 | tf_op jit(solution)/shard_map/ppermute | solution.py:47
  50.0 2.4 %collective-permute-done.18.refs_0_ = bf16[4,16,256]{2,1,0:T(8,128)(2,1)S(1)} collective-permute-done((bf16[4,16,256]{2,1,0:T(8,128)(2,1)S(1)}, bf16[4,16,256]{2,1,0:T(8,128)(2,1)S(1)}, u32[]{:S(2)}, u32[]{:S(2)}) %collective-permute-start.18) | collective-permute-done | bytes 32800 | tf_op jit(solution)/shard_map/ppermute | solution.py:47
  52.4 0.2 shard_map.150.refs_2_
  52.7 0.3 shard_map.151.refs_2_
  52.9 0.3 shard_map.152.refs_2_
  53.2 0.4 collective-permute-done.19.refs_0_
  53.6 0.2 shard_map.153.refs_3_
  53.9 0.9 %collective-permute-start.22 = (bf16[1,16,512]{2,1,0:T(8,128)(2,1)S(1)}, bf16[1,16,512]{2,1,0:T(8,128)(2,1)S(1)}, u32[]{:S(2)}, u32[]{:S(2)}) collective-permute-start(bf16[1,16,512]{2,1,0:T(8,128)(2,1)S(1)} %bitcast.46), channel_id=1, source_target_pairs={{0,8},{1,9},{2,10},{3,11},{4,12},{5,13},{6,14},{7,15},{8,0},{9,1},... | collective-permute-start | bytes 49160 | tf_op jit(solution)/shard_map/ppermute | solution.py:47
  54.8 3.5 %collective-permute-start.23 = (bf16[1,16,512]{2,1,0:T(8,128)(2,1)S(1)}, bf16[1,16,512]{2,1,0:T(8,128)(2,1)S(1)}, u32[]{:S(2)}, u32[]{:S(2)}) collective-permute-start(bf16[1,16,512]{2,1,0:T(8,128)(2,1)S(1)} %bitcast.47), channel_id=1, source_target_pairs={{0,12},{1,13},{2,14},{3,15},{4,8},{5,9},{6,10},{7,11},{8,4},{9,5},... | collective-permute-start | bytes 49160 | tf_op jit(solution)/shard_map/ppermute | solution.py:47
  58.3 0.3 collective-permute-done.22
  58.6 1.8 %collective-permute-done.23 = bf16[1,16,512]{2,1,0:T(8,128)(2,1)S(1)} collective-permute-done((bf16[1,16,512]{2,1,0:T(8,128)(2,1)S(1)}, bf16[1,16,512]{2,1,0:T(8,128)(2,1)S(1)}, u32[]{:S(2)}, u32[]{:S(2)}) %collective-permute-start.23) | collective-permute-done | bytes 16416 | tf_op jit(solution)/shard_map/ppermute | solution.py:47
  60.4 1.6 %collective-permute-start.24 = (bf16[4,16,512]{2,1,0:T(8,128)(2,1)S(1)}, bf16[4,16,512]{2,1,0:T(8,128)(2,1)S(1)}, u32[]{:S(2)}, u32[]{:S(2)}) collective-permute-start(bf16[4,16,512]{2,1,0:T(8,128)(2,1)S(1)} %pad_maximum_fusion.2.refs_0_), channel_id=1, source_target_pairs={{0,2},{1,3},{2,0},{3,1},{4,6},{5,7},{6,4},{7,5},{8,10},{9,11},{10,... | collective-permute-start | bytes 196616 | tf_op jit(solution)/shard_map/ppermute | solution.py:47
  62.0 2.7 %collective-permute-done.24.refs_0_ = bf16[4,16,512]{2,1,0:T(8,128)(2,1)S(1)} collective-permute-done((bf16[4,16,512]{2,1,0:T(8,128)(2,1)S(1)}, bf16[4,16,512]{2,1,0:T(8,128)(2,1)S(1)}, u32[]{:S(2)}, u32[]{:S(2)}) %collective-permute-start.24) | collective-permute-done | bytes 65568 | tf_op jit(solution)/shard_map/ppermute | solution.py:47
  64.7 1.1 %shard_map.154 = (f32[16,896]{1,0:T(8,128)S(1)}, f32[16,896]{1,0:T(8,128)S(1)}, f32[16,128]{1,0:T(8,128)S(1)}) custom-call(s32[1]{0:T(128)} %bitcast.device_ref.refs_0_, bf16[4,16,512]{2,1,0:T(8,128)(2,1)S(1)} %pad_maximum_fusion.2.refs_0_, f32[16,1,512]{2,1,0:T(1,128)S(1)} %bitcast.41, bf16[8192,896]{1,0:T(8,128)(2,1)S(1)} %copy-done, ...), custom_call_target="tpu_custom_call" | custom-call | flops 117440512 | bytes 29458436 | tf_op jit(solution)/shard_map/pallas_call | solution.py:79
  65.8 1.1 %shard_map.155 = (f32[16,896]{1,0:T(8,128)S(1)}, f32[16,896]{1,0:T(8,128)S(1)}, f32[16,128]{1,0:T(8,128)S(1)}) custom-call(s32[1]{0:T(128)} %bitcast.device_ref.refs_0_, bf16[4,16,512]{2,1,0:T(8,128)(2,1)S(1)} %collective-permute-done.26.refs_0_, f32[16,1,512]{2,1,0:T(1,128)S(1)} %bitcast.42, bf16[8192,896]{1,0:T(8,128)(2,1)S(1)} %copy-done, ...), custom_call_target="tpu_custom_call" | custom-call | flops 117440512 | bytes 29581316 | tf_op jit(solution)/shard_map/pallas_call | solution.py:79
  66.9 1.1 %shard_map.156 = (f32[16,896]{1,0:T(8,128)S(1)}, f32[16,896]{1,0:T(8,128)S(1)}, f32[16,128]{1,0:T(8,128)S(1)}) custom-call(s32[1]{0:T(128)} %bitcast.device_ref.refs_0_, bf16[4,16,512]{2,1,0:T(8,128)(2,1)S(1)} %collective-permute-done.24.refs_0_, f32[16,1,512]{2,1,0:T(1,128)S(1)} %bitcast.43, bf16[8192,896]{1,0:T(8,128)(2,1)S(1)} %copy-done, ...), custom_call_target="tpu_custom_call" | custom-call | flops 117440512 | bytes 29581316 | tf_op jit(solution)/shard_map/pallas_call | solution.py:79
  68.0 1.1 %shard_map.157.in_ref = bf16[16,896]{1,0:T(8,128)(2,1)S(1)} custom-call(s32[1]{0:T(128)} %bitcast.device_ref.refs_0_, bf16[4,16,512]{2,1,0:T(8,128)(2,1)S(1)} %collective-permute-done.25.refs_0_, f32[16,1,512]{2,1,0:T(1,128)S(1)} %bitcast.44, bf16[8192,896]{1,0:T(8,128)(2,1)S(1)} %copy-done, bf16[8192,896]{1,0:T(8,128)(2,1)S(1)} %copy-done.1, ...), custom_call_target="tpu_custom_call" | custom-call | flops 117440512 | bytes 29581316 | tf_op jit(solution)/shard_map/pallas_call | solution.py:79
  69.1 0.3 collective-permute-start.27
  69.4 3.8 %collective-permute-start.28 = (bf16[1,16,896]{2,1,0:T(8,128)(2,1)S(1)}, bf16[1,16,896]{2,1,0:T(8,128)(2,1)S(1)}, u32[]{:S(2)}, u32[]{:S(2)}) collective-permute-start(bf16[1,16,896]{2,1,0:T(8,128)(2,1)S(1)} %bitcast.54), channel_id=1, source_target_pairs={{0,8},{1,9},{2,10},{3,11},{4,12},{5,13},{6,14},{7,15},{8,0},{9,1},... | collective-permute-start | bytes 86024 | tf_op jit(solution)/shard_map/ppermute | solution.py:47
  73.2 0.4 collective-permute-start.29
  73.6 1.9 %collective-permute-done.28 = bf16[1,16,896]{2,1,0:T(8,128)(2,1)S(1)} collective-permute-done((bf16[1,16,896]{2,1,0:T(8,128)(2,1)S(1)}, bf16[1,16,896]{2,1,0:T(8,128)(2,1)S(1)}, u32[]{:S(2)}, u32[]{:S(2)}) %collective-permute-start.28) | collective-permute-done | bytes 28704 | tf_op jit(solution)/shard_map/ppermute | solution.py:47
  75.5 3.4 %collective-permute-done.29 = bf16[1,16,896]{2,1,0:T(8,128)(2,1)S(1)} collective-permute-done((bf16[1,16,896]{2,1,0:T(8,128)(2,1)S(1)}, bf16[1,16,896]{2,1,0:T(8,128)(2,1)S(1)}, u32[]{:S(2)}, u32[]{:S(2)}) %collective-permute-start.29) | collective-permute-done | bytes 28704 | tf_op jit(solution)/shard_map/ppermute | solution.py:47
  78.9 1.6 %collective-permute-start.30 = (bf16[4,16,896]{2,1,0:T(8,128)(2,1)S(1)}, bf16[4,16,896]{2,1,0:T(8,128)(2,1)S(1)}, u32[]{:S(2)}, u32[]{:S(2)}) collective-permute-start(bf16[4,16,896]{2,1,0:T(8,128)(2,1)S(1)} %pad_maximum_fusion.refs_0_), channel_id=1, source_target_pairs={{0,2},{1,3},{2,0},{3,1},{4,6},{5,7},{6,4},{7,5},{8,10},{9,11},{10,... | collective-permute-start | bytes 344072 | tf_op jit(solution)/shard_map/ppermute | solution.py:47
  80.5 3.3 %collective-permute-done.30.refs_0_ = bf16[4,16,896]{2,1,0:T(8,128)(2,1)S(1)} collective-permute-done((bf16[4,16,896]{2,1,0:T(8,128)(2,1)S(1)}, bf16[4,16,896]{2,1,0:T(8,128)(2,1)S(1)}, u32[]{:S(2)}, u32[]{:S(2)}) %collective-permute-start.30) | collective-permute-done | bytes 114720 | tf_op jit(solution)/shard_map/ppermute | solution.py:47
  83.8 0.6 shard_map.159.refs_2_
  84.4 0.6 shard_map.160.refs_2_
  85.0 0.6 shard_map.161.refs_2_
  85.5 1.2 %shard_map.162 = bf16[16,512]{1,0:T(8,128)(2,1)} custom-call(s32[1]{0:T(128)} %bitcast.device_ref.refs_0_, bf16[4,16,896]{2,1,0:T(8,128)(2,1)S(1)} %collective-permute-done.31.refs_0_, bf16[14336,512]{1,0:T(8,128)(2,1)S(1)} %bitcast.20, f32[16,512]{1,0:T(8,128)S(1)} %shard_map.161.refs_2_, bf16[16,512]{1,0:T(8,128)(2,1)S(1)} %shard_map.153.refs_3_), custom_call_target="tpu_custom_call" | custom-call | flops 58720256 | bytes 14843908 | tf_op jit(solution)/shard_map/pallas_call | solution.py:79
  (84 shorter events, 1.8 us)
Async XLA Ops:
  0.0 7.7 %collective-permute-start = (bf16[1,16,512]{2,1,0:T(8,128)(2,1)}, bf16[1,16,512]{2,1,0:T(8,128)(2,1)S(1)}, u32[]{:S(2)}, u32[]{:S(2)}) collective-permute-start(bf16[1,16,512]{2,1,0:T(8,128)(2,1)} %bitcast.57), channel_id=1, source_target_pairs={{0,4},{1,5},{2,6},{3,7},{4,0},{5,1},{6,2},{7,3},{8,12},{9,13},{10,... | collective-permute-start | bytes 49160 | tf_op jit(solution)/shard_map/ppermute | solution.py:47
  3.1 4.9 %collective-permute-start.1 = (bf16[1,16,512]{2,1,0:T(8,128)(2,1)}, bf16[1,16,512]{2,1,0:T(8,128)(2,1)S(1)}, u32[]{:S(2)}, u32[]{:S(2)}) collective-permute-start(bf16[1,16,512]{2,1,0:T(8,128)(2,1)} %bitcast.58), channel_id=1, source_target_pairs={{0,8},{1,9},{2,10},{3,11},{4,12},{5,13},{6,14},{7,15},{8,0},{9,1},... | collective-permute-start | bytes 49160 | tf_op jit(solution)/shard_map/ppermute | solution.py:47
  5.6 5.7 %collective-permute-start.2 = (bf16[1,16,512]{2,1,0:T(8,128)(2,1)}, bf16[1,16,512]{2,1,0:T(8,128)(2,1)S(1)}, u32[]{:S(2)}, u32[]{:S(2)}) collective-permute-start(bf16[1,16,512]{2,1,0:T(8,128)(2,1)} %bitcast.59), channel_id=1, source_target_pairs={{0,12},{1,13},{2,14},{3,15},{4,8},{5,9},{6,10},{7,11},{8,4},{9,5},... | collective-permute-start | bytes 49160 | tf_op jit(solution)/shard_map/ppermute | solution.py:47
  5.6 0.8 copy-start.8
  6.4 0.7 copy-start.12
  6.4 0.7 copy-start.13
  11.4 4.3 %collective-permute-start.3 = (bf16[4,16,512]{2,1,0:T(8,128)(2,1)S(1)}, bf16[4,16,512]{2,1,0:T(8,128)(2,1)S(1)}, u32[]{:S(2)}, u32[]{:S(2)}) collective-permute-start(bf16[4,16,512]{2,1,0:T(8,128)(2,1)S(1)} %pad_maximum_fusion.1.refs_0_), channel_id=1, source_target_pairs={{0,2},{1,3},{2,0},{3,1},{4,6},{5,7},{6,4},{7,5},{8,10},{9,11},{10,... | collective-permute-start | bytes 196616 | tf_op jit(solution)/shard_map/ppermute | solution.py:47
  13.0 5.5 %collective-permute-start.5 = (bf16[4,16,512]{2,1,0:T(8,128)(2,1)S(1)}, bf16[4,16,512]{2,1,0:T(8,128)(2,1)S(1)}, u32[]{:S(2)}, u32[]{:S(2)}) collective-permute-start(bf16[4,16,512]{2,1,0:T(8,128)(2,1)S(1)} %pad_maximum_fusion.1.refs_0_), channel_id=1, source_target_pairs={{0,1},{1,0},{2,3},{3,2},{4,5},{5,4},{6,7},{7,6},{8,9},{9,8},{10,11... | collective-permute-start | bytes 196616 | tf_op jit(solution)/shard_map/ppermute | solution.py:47
  15.7 3.5 %collective-permute-start.4 = (bf16[4,16,512]{2,1,0:T(8,128)(2,1)S(1)}, bf16[4,16,512]{2,1,0:T(8,128)(2,1)S(1)}, u32[]{:S(2)}, u32[]{:S(2)}) collective-permute-start(bf16[4,16,512]{2,1,0:T(8,128)(2,1)S(1)} %collective-permute-done.3.refs_0_), channel_id=1, source_target_pairs={{0,1},{1,0},{2,3},{3,2},{4,5},{5,4},{6,7},{7,6},{8,9},{9,8},{10,11... | collective-permute-start | bytes 196616 | tf_op jit(solution)/shard_map/ppermute | solution.py:47
  15.7 2.2 %copy-start.2 = (bf16[8192,256]{1,0:T(8,128)(2,1)S(1)}, bf16[8192,256]{1,0:T(8,128)(2,1)}, u32[]{:S(2)}) copy-start(bf16[8192,256]{1,0:T(8,128)(2,1)} %refs_2_.11) | copy-start | bytes 12582916
  15.7 2.3 %copy-start.4 = (bf16[8192,32]{0,1:T(8,128)(2,1)S(1)}, bf16[8192,32]{0,1:T(8,128)(2,1)}, u32[]{:S(2)}) copy-start(bf16[8192,32]{0,1:T(8,128)(2,1)} %param.17) | copy-start | bytes 1572868
  15.7 2.5 %copy-start.5 = (bf16[8192,32]{0,1:T(8,128)(2,1)S(1)}, bf16[8192,32]{0,1:T(8,128)(2,1)}, u32[]{:S(2)}) copy-start(bf16[8192,32]{0,1:T(8,128)(2,1)} %param.18) | copy-start | bytes 1572868
  15.8 2.5 %copy-start.6 = (f32[8192]{0:T(1024)S(1)}, f32[8192]{0:T(1024)}, u32[]{:S(2)}) copy-start(f32[8192]{0:T(1024)} %param.15) | copy-start | bytes 98308
  15.8 14.4 %copy-start.10 = (bf16[1024,4,128]{2,1,0:T(4,128)(2,1)S(1)}, bf16[1024,4,128]{2,1,0:T(4,128)(2,1)}, u32[]{:S(2)}) copy-start(bf16[1024,4,128]{2,1,0:T(4,128)(2,1)} %param.19) | copy-start | bytes 3145732
  15.8 15.0 %copy-start.11 = (bf16[1024,4,128]{2,1,0:T(4,128)(2,1)S(1)}, bf16[1024,4,128]{2,1,0:T(4,128)(2,1)}, u32[]{:S(2)}) copy-start(bf16[1024,4,128]{2,1,0:T(4,128)(2,1)} %param.20) | copy-start | bytes 3145732
  19.7 4.5 %collective-permute-start.6 = (bf16[1,16,320]{2,1,0:T(8,128)(2,1)S(1)}, bf16[1,16,320]{2,1,0:T(8,128)(2,1)S(1)}, u32[]{:S(2)}, u32[]{:S(2)}) collective-permute-start(bf16[1,16,320]{2,1,0:T(8,128)(2,1)S(1)} %bitcast.49), channel_id=1, source_target_pairs={{0,4},{1,5},{2,6},{3,7},{4,0},{5,1},{6,2},{7,3},{8,12},{9,13},{10,... | collective-permute-start | bytes 30728 | tf_op jit(solution)/shard_map/ppermute | solution.py:47
  19.8 4.7 %collective-permute-start.7 = (bf16[1,16,320]{2,1,0:T(8,128)(2,1)S(1)}, bf16[1,16,320]{2,1,0:T(8,128)(2,1)S(1)}, u32[]{:S(2)}, u32[]{:S(2)}) collective-permute-start(bf16[1,16,320]{2,1,0:T(8,128)(2,1)S(1)} %bitcast.50), channel_id=1, source_target_pairs={{0,8},{1,9},{2,10},{3,11},{4,12},{5,13},{6,14},{7,15},{8,0},{9,1},... | collective-permute-start | bytes 30728 | tf_op jit(solution)/shard_map/ppermute | solution.py:47
  20.5 5.5 %collective-permute-start.8 = (bf16[1,16,320]{2,1,0:T(8,128)(2,1)S(1)}, bf16[1,16,320]{2,1,0:T(8,128)(2,1)S(1)}, u32[]{:S(2)}, u32[]{:S(2)}) collective-permute-start(bf16[1,16,320]{2,1,0:T(8,128)(2,1)S(1)} %bitcast.51), channel_id=1, source_target_pairs={{0,12},{1,13},{2,14},{3,15},{4,8},{5,9},{6,10},{7,11},{8,4},{9,5},... | collective-permute-start | bytes 30728 | tf_op jit(solution)/shard_map/ppermute | solution.py:47
  26.0 4.2 %collective-permute-start.11 = (bf16[4,16,320]{2,1,0:T(8,128)(2,1)S(1)}, bf16[4,16,320]{2,1,0:T(8,128)(2,1)S(1)}, u32[]{:S(2)}, u32[]{:S(2)}) collective-permute-start(bf16[4,16,320]{2,1,0:T(8,128)(2,1)S(1)} %pad_maximum_fusion.3.refs_1_), channel_id=1, source_target_pairs={{0,2},{1,3},{2,0},{3,1},{4,6},{5,7},{6,4},{7,5},{8,10},{9,11},{10,... | collective-permute-start | bytes 122888 | tf_op jit(solution)/shard_map/ppermute | solution.py:47
  30.2 3.2 %collective-permute-start.12 = (bf16[4,16,320]{2,1,0:T(8,128)(2,1)S(1)}, bf16[4,16,320]{2,1,0:T(8,128)(2,1)S(1)}, u32[]{:S(2)}, u32[]{:S(2)}) collective-permute-start(bf16[4,16,320]{2,1,0:T(8,128)(2,1)S(1)} %collective-permute-done.11.refs_1_.refs_2_), channel_id=1, source_target_pairs={{0,1},{1,0},{2,3},{3,2},{4,5},{5,4},{6,7},{7,6},{8,9},{9,8},{10,11... | collective-permute-start | bytes 122888 | tf_op jit(solution)/shard_map/ppermute | solution.py:47
  31.7 2.2 %collective-permute-start.13 = (bf16[136,128]{1,0:T(8,128)(2,1)S(1)}, bf16[136,128]{1,0:T(8,128)(2,1)S(1)}, u32[]{:S(2)}, u32[]{:S(2)}) collective-permute-start(bf16[136,128]{1,0:T(8,128)(2,1)S(1)} %shard_map.145), channel_id=1, source_target_pairs={{0,1},{1,0},{2,3},{3,2},{4,5},{5,4},{6,7},{7,6},{8,9},{9,8},{10,11... | collective-permute-start | bytes 104456 | tf_op jit(solution)/shard_map/ppermute | solution.py:47
  32.2 3.4 %collective-permute-start.9 = (bf16[4,16,320]{2,1,0:T(8,128)(2,1)S(1)}, bf16[4,16,320]{2,1,0:T(8,128)(2,1)S(1)}, u32[]{:S(2)}, u32[]{:S(2)}) collective-permute-start(bf16[4,16,320]{2,1,0:T(8,128)(2,1)S(1)} %pad_maximum_fusion.3.refs_1_), channel_id=1, source_target_pairs={{0,1},{1,0},{2,3},{3,2},{4,5},{5,4},{6,7},{7,6},{8,9},{9,8},{10,11... | collective-permute-start | bytes 122888 | tf_op jit(solution)/shard_map/ppermute | solution.py:47
  32.9 3.3 %collective-permute-start.10 = (bf16[136,128]{1,0:T(8,128)(2,1)S(1)}, bf16[136,128]{1,0:T(8,128)(2,1)S(1)}, u32[]{:S(2)}, u32[]{:S(2)}) collective-permute-start(bf16[136,128]{1,0:T(8,128)(2,1)S(1)} %shard_map.143), channel_id=1, source_target_pairs={{0,1},{1,0},{2,3},{3,2},{4,5},{5,4},{6,7},{7,6},{8,9},{9,8},{10,11... | collective-permute-start | bytes 104456 | tf_op jit(solution)/shard_map/ppermute | solution.py:47
  34.1 4.0 %collective-permute-start.14 = (bf16[136,128]{1,0:T(8,128)(2,1)S(1)}, bf16[136,128]{1,0:T(8,128)(2,1)S(1)}, u32[]{:S(2)}, u32[]{:S(2)}) collective-permute-start(bf16[136,128]{1,0:T(8,128)(2,1)S(1)} %shard_map.146), channel_id=1, source_target_pairs={{0,2},{1,3},{2,0},{3,1},{4,6},{5,7},{6,4},{7,5},{8,10},{9,11},{10,... | collective-permute-start | bytes 104456 | tf_op jit(solution)/shard_map/ppermute | solution.py:47
  38.1 14.4 %copy-start.3 = (bf16[4096,512]{1,0:T(8,128)(2,1)S(1)}, bf16[4096,512]{1,0:T(8,128)(2,1)}, u32[]{:S(2)}) copy-start(bf16[4096,512]{1,0:T(8,128)(2,1)} %refs_1_.11) | copy-start | bytes 12582916
  38.2 4.6 %collective-permute-start.15 = (bf16[136,128]{1,0:T(8,128)(2,1)S(1)}, bf16[136,128]{1,0:T(8,128)(2,1)S(1)}, u32[]{:S(2)}, u32[]{:S(2)}) collective-permute-start(bf16[136,128]{1,0:T(8,128)(2,1)S(1)} %get-tuple-element.57), channel_id=1, source_target_pairs={{0,4},{1,5},{2,6},{3,7},{4,0},{5,1},{6,2},{7,3},{8,12},{9,13},{10,... | collective-permute-start | bytes 104456 | tf_op jit(solution)/shard_map/ppermute | solution.py:47
  38.7 6.1 %collective-permute-start.16 = (bf16[136,128]{1,0:T(8,128)(2,1)S(1)}, bf16[136,128]{1,0:T(8,128)(2,1)S(1)}, u32[]{:S(2)}, u32[]{:S(2)}) collective-permute-start(bf16[136,128]{1,0:T(8,128)(2,1)S(1)} %get-tuple-element.57), channel_id=1, source_target_pairs={{0,8},{1,9},{2,10},{3,11},{4,12},{5,13},{6,14},{7,15},{8,0},{9,1},... | collective-permute-start | bytes 104456 | tf_op jit(solution)/shard_map/ppermute | solution.py:47
  42.5 5.7 %collective-permute-start.17 = (bf16[136,128]{1,0:T(8,128)(2,1)S(1)}, bf16[136,128]{1,0:T(8,128)(2,1)S(1)}, u32[]{:S(2)}, u32[]{:S(2)}) collective-permute-start(bf16[136,128]{1,0:T(8,128)(2,1)S(1)} %get-tuple-element.57), channel_id=1, source_target_pairs={{0,12},{1,13},{2,14},{3,15},{4,8},{5,9},{6,10},{7,11},{8,4},{9,5},... | collective-permute-start | bytes 104456 | tf_op jit(solution)/shard_map/ppermute | solution.py:47
  48.4 5.2 %copy-start.9 = (bf16[16,512]{1,0:T(8,128)(2,1)S(1)}, bf16[16,512]{1,0:T(8,128)(2,1)}, u32[]{:S(2)}) copy-start(bf16[16,512]{1,0:T(8,128)(2,1)} %refs_3_.5) | copy-start | bytes 49156
  48.4 16.3 %copy-start.7 = (f32[8192]{0:T(1024)S(1)}, f32[8192]{0:T(1024)}, u32[]{:S(2)}) copy-start(f32[8192]{0:T(1024)} %param.22) | copy-start | bytes 98308
  48.4 4.0 %collective-permute-start.18 = (bf16[4,16,256]{2,1,0:T(8,128)(2,1)S(1)}, bf16[4,16,256]{2,1,0:T(8,128)(2,1)S(1)}, u32[]{:S(2)}, u32[]{:S(2)}) collective-permute-start(bf16[4,16,256]{2,1,0:T(8,128)(2,1)S(1)} %shard_map.149.refs_0_), channel_id=1, source_target_pairs={{0,2},{1,3},{2,0},{3,1},{4,6},{5,7},{6,4},{7,5},{8,10},{9,11},{10,... | collective-permute-start | bytes 98312 | tf_op jit(solution)/shard_map/ppermute | solution.py:47
  50.0 2.7 %collective-permute-start.20 = (bf16[4,16,256]{2,1,0:T(8,128)(2,1)S(1)}, bf16[4,16,256]{2,1,0:T(8,128)(2,1)S(1)}, u32[]{:S(2)}, u32[]{:S(2)}) collective-permute-start(bf16[4,16,256]{2,1,0:T(8,128)(2,1)S(1)} %shard_map.149.refs_0_), channel_id=1, source_target_pairs={{0,1},{1,0},{2,3},{3,2},{4,5},{5,4},{6,7},{7,6},{8,9},{9,8},{10,11... | collective-permute-start | bytes 98312 | tf_op jit(solution)/shard_map/ppermute | solution.py:47
  52.4 1.2 %collective-permute-start.19 = (bf16[4,16,256]{2,1,0:T(8,128)(2,1)S(1)}, bf16[4,16,256]{2,1,0:T(8,128)(2,1)S(1)}, u32[]{:S(2)}, u32[]{:S(2)}) collective-permute-start(bf16[4,16,256]{2,1,0:T(8,128)(2,1)S(1)} %collective-permute-done.18.refs_0_), channel_id=1, source_target_pairs={{0,1},{1,0},{2,3},{3,2},{4,5},{5,4},{6,7},{7,6},{8,9},{9,8},{10,11... | collective-permute-start | bytes 98312 | tf_op jit(solution)/shard_map/ppermute | solution.py:47
  52.4 12.3 %copy-start = (bf16[8192,896]{1,0:T(8,128)(2,1)S(1)}, bf16[8192,896]{1,0:T(8,128)(2,1)}, u32[]{:S(2)}) copy-start(bf16[8192,896]{1,0:T(8,128)(2,1)} %refs_2_.15) | copy-start | bytes 44040196
  52.4 12.3 %copy-start.1 = (bf16[8192,896]{1,0:T(8,128)(2,1)S(1)}, bf16[8192,896]{1,0:T(8,128)(2,1)}, u32[]{:S(2)}) copy-start(bf16[8192,896]{1,0:T(8,128)(2,1)} %refs_3_.9) | copy-start | bytes 44040196
  53.9 4.4 %collective-permute-start.21 = (bf16[1,16,512]{2,1,0:T(8,128)(2,1)S(1)}, bf16[1,16,512]{2,1,0:T(8,128)(2,1)S(1)}, u32[]{:S(2)}, u32[]{:S(2)}) collective-permute-start(bf16[1,16,512]{2,1,0:T(8,128)(2,1)S(1)} %bitcast.45), channel_id=1, source_target_pairs={{0,4},{1,5},{2,6},{3,7},{4,0},{5,1},{6,2},{7,3},{8,12},{9,13},{10,... | collective-permute-start | bytes 49160 | tf_op jit(solution)/shard_map/ppermute | solution.py:47
  53.9 4.7 %collective-permute-start.22 = (bf16[1,16,512]{2,1,0:T(8,128)(2,1)S(1)}, bf16[1,16,512]{2,1,0:T(8,128)(2,1)S(1)}, u32[]{:S(2)}, u32[]{:S(2)}) collective-permute-start(bf16[1,16,512]{2,1,0:T(8,128)(2,1)S(1)} %bitcast.46), channel_id=1, source_target_pairs={{0,8},{1,9},{2,10},{3,11},{4,12},{5,13},{6,14},{7,15},{8,0},{9,1},... | collective-permute-start | bytes 49160 | tf_op jit(solution)/shard_map/ppermute | solution.py:47
  54.8 5.5 %collective-permute-start.23 = (bf16[1,16,512]{2,1,0:T(8,128)(2,1)S(1)}, bf16[1,16,512]{2,1,0:T(8,128)(2,1)S(1)}, u32[]{:S(2)}, u32[]{:S(2)}) collective-permute-start(bf16[1,16,512]{2,1,0:T(8,128)(2,1)S(1)} %bitcast.47), channel_id=1, source_target_pairs={{0,12},{1,13},{2,14},{3,15},{4,8},{5,9},{6,10},{7,11},{8,4},{9,5},... | collective-permute-start | bytes 49160 | tf_op jit(solution)/shard_map/ppermute | solution.py:47
  60.4 4.3 %collective-permute-start.24 = (bf16[4,16,512]{2,1,0:T(8,128)(2,1)S(1)}, bf16[4,16,512]{2,1,0:T(8,128)(2,1)S(1)}, u32[]{:S(2)}, u32[]{:S(2)}) collective-permute-start(bf16[4,16,512]{2,1,0:T(8,128)(2,1)S(1)} %pad_maximum_fusion.2.refs_0_), channel_id=1, source_target_pairs={{0,2},{1,3},{2,0},{3,1},{4,6},{5,7},{6,4},{7,5},{8,10},{9,11},{10,... | collective-permute-start | bytes 196616 | tf_op jit(solution)/shard_map/ppermute | solution.py:47
  62.0 3.8 %collective-permute-start.26 = (bf16[4,16,512]{2,1,0:T(8,128)(2,1)S(1)}, bf16[4,16,512]{2,1,0:T(8,128)(2,1)S(1)}, u32[]{:S(2)}, u32[]{:S(2)}) collective-permute-start(bf16[4,16,512]{2,1,0:T(8,128)(2,1)S(1)} %pad_maximum_fusion.2.refs_0_), channel_id=1, source_target_pairs={{0,1},{1,0},{2,3},{3,2},{4,5},{5,4},{6,7},{7,6},{8,9},{9,8},{10,11... | collective-permute-start | bytes 196616 | tf_op jit(solution)/shard_map/ppermute | solution.py:47
  64.7 3.3 %collective-permute-start.25 = (bf16[4,16,512]{2,1,0:T(8,128)(2,1)S(1)}, bf16[4,16,512]{2,1,0:T(8,128)(2,1)S(1)}, u32[]{:S(2)}, u32[]{:S(2)}) collective-permute-start(bf16[4,16,512]{2,1,0:T(8,128)(2,1)S(1)} %collective-permute-done.24.refs_0_), channel_id=1, source_target_pairs={{0,1},{1,0},{2,3},{3,2},{4,5},{5,4},{6,7},{7,6},{8,9},{9,8},{10,11... | collective-permute-start | bytes 196616 | tf_op jit(solution)/shard_map/ppermute | solution.py:47
  68.0 15.8 %slice-start = ((s8[14680064]{0:T(1024)(128)(4,1)}), s8[4194304]{0:T(1024)(128)(4,1)S(1)}, s32[]{:S(2)}) async-start(s8[14680064]{0:T(1024)(128)(4,1)} %bitcast.19), calls=%async_computation | async-start | bytes 8388608
  69.1 14.7 %slice-start.1 = ((s8[14680064]{0:T(1024)(128)(4,1)}), s8[4194304]{0:T(1024)(128)(4,1)S(1)}, s32[]{:S(2)}) async-start(s8[14680064]{0:T(1024)(128)(4,1)} %bitcast.19), calls=%async_computation.1 | async-start | bytes 8388608
  69.1 14.7 %slice-start.2 = ((s8[14680064]{0:T(1024)(128)(4,1)}), s8[4194304]{0:T(1024)(128)(4,1)S(1)}, s32[]{:S(2)}) async-start(s8[14680064]{0:T(1024)(128)(4,1)} %bitcast.19), calls=%async_computation.2 | async-start | bytes 8388608
  69.1 14.7 %slice-start.3 = ((s8[14680064]{0:T(1024)(128)(4,1)}), s8[2097152]{0:T(1024)(128)(4,1)S(1)}, s32[]{:S(2)}) async-start(s8[14680064]{0:T(1024)(128)(4,1)} %bitcast.19), calls=%async_computation.3 | async-start | bytes 4194304
  69.1 4.5 %collective-permute-start.27 = (bf16[1,16,896]{2,1,0:T(8,128)(2,1)S(1)}, bf16[1,16,896]{2,1,0:T(8,128)(2,1)S(1)}, u32[]{:S(2)}, u32[]{:S(2)}) collective-permute-start(bf16[1,16,896]{2,1,0:T(8,128)(2,1)S(1)} %bitcast.53), channel_id=1, source_target_pairs={{0,4},{1,5},{2,6},{3,7},{4,0},{5,1},{6,2},{7,3},{8,12},{9,13},{10,... | collective-permute-start | bytes 86024 | tf_op jit(solution)/shard_map/ppermute | solution.py:47
  69.4 6.1 %collective-permute-start.28 = (bf16[1,16,896]{2,1,0:T(8,128)(2,1)S(1)}, bf16[1,16,896]{2,1,0:T(8,128)(2,1)S(1)}, u32[]{:S(2)}, u32[]{:S(2)}) collective-permute-start(bf16[1,16,896]{2,1,0:T(8,128)(2,1)S(1)} %bitcast.54), channel_id=1, source_target_pairs={{0,8},{1,9},{2,10},{3,11},{4,12},{5,13},{6,14},{7,15},{8,0},{9,1},... | collective-permute-start | bytes 86024 | tf_op jit(solution)/shard_map/ppermute | solution.py:47
  73.2 5.7 %collective-permute-start.29 = (bf16[1,16,896]{2,1,0:T(8,128)(2,1)S(1)}, bf16[1,16,896]{2,1,0:T(8,128)(2,1)S(1)}, u32[]{:S(2)}, u32[]{:S(2)}) collective-permute-start(bf16[1,16,896]{2,1,0:T(8,128)(2,1)S(1)} %bitcast.55), channel_id=1, source_target_pairs={{0,12},{1,13},{2,14},{3,15},{4,8},{5,9},{6,10},{7,11},{8,4},{9,5},... | collective-permute-start | bytes 86024 | tf_op jit(solution)/shard_map/ppermute | solution.py:47
  78.9 4.9 %collective-permute-start.30 = (bf16[4,16,896]{2,1,0:T(8,128)(2,1)S(1)}, bf16[4,16,896]{2,1,0:T(8,128)(2,1)S(1)}, u32[]{:S(2)}, u32[]{:S(2)}) collective-permute-start(bf16[4,16,896]{2,1,0:T(8,128)(2,1)S(1)} %pad_maximum_fusion.refs_0_), channel_id=1, source_target_pairs={{0,2},{1,3},{2,0},{3,1},{4,6},{5,7},{6,4},{7,5},{8,10},{9,11},{10,... | collective-permute-start | bytes 344072 | tf_op jit(solution)/shard_map/ppermute | solution.py:47
  80.5 3.9 %collective-permute-start.32 = (bf16[4,16,896]{2,1,0:T(8,128)(2,1)S(1)}, bf16[4,16,896]{2,1,0:T(8,128)(2,1)S(1)}, u32[]{:S(2)}, u32[]{:S(2)}) collective-permute-start(bf16[4,16,896]{2,1,0:T(8,128)(2,1)S(1)} %pad_maximum_fusion.refs_0_), channel_id=1, source_target_pairs={{0,1},{1,0},{2,3},{3,2},{4,5},{5,4},{6,7},{7,6},{8,9},{9,8},{10,11... | collective-permute-start | bytes 344072 | tf_op jit(solution)/shard_map/ppermute | solution.py:47
  83.7 1.8 %collective-permute-start.31 = (bf16[4,16,896]{2,1,0:T(8,128)(2,1)S(1)}, bf16[4,16,896]{2,1,0:T(8,128)(2,1)S(1)}, u32[]{:S(2)}, u32[]{:S(2)}) collective-permute-start(bf16[4,16,896]{2,1,0:T(8,128)(2,1)S(1)} %collective-permute-done.30.refs_0_), channel_id=1, source_target_pairs={{0,1},{1,0},{2,3},{3,2},{4,5},{5,4},{6,7},{7,6},{8,9},{9,8},{10,11... | collective-permute-start | bytes 344072 | tf_op jit(solution)/shard_map/ppermute | solution.py:47

commit v6 on v5

--- a/solution.py
+++ b/solution.py
@@ -53,7 +53,10 @@
     *rounds, last, _ = digits(devices)
 
     def arrive(stride, radix, held):
-        return [shifted(held, stride * digit) for digit in range(1, radix)]
+        out = {}
+        for digit in sorted(range(1, radix), key=lambda d: ((3,2,1))[d - 1]):
+            out[digit] = shifted(held, stride * digit)
+        return [out[digit] for digit in range(1, radix)]
 
     for stride, radix, _ in rounds:
         arrived = arrive(stride, radix, held if given is None else given[None])
@@ -548,7 +551,9 @@
         given, mean, level = call(
             merge_next_kernel, "merge_next", (message, wide, wide), (mean, level, taken_held, taken)
         )
-        taken = [shifted(given, rounds[0][0] * digit) for digit in range(1, rounds[0][1])]
+        taken = []
+        for digit in range(1, rounds[0][1]):
+            taken.append(shifted(given, rounds[0][0] * digit))
         score, value = call(
             lambda *refs: fresh_kernel(scale, head_dim, value_heads, key_width, *refs), "fresh",
             (wide, wide), (own, held, brought, far, far_brought),

time: 87 us -> 87 us (level)
  no operation moved by 1% of the time
where the time goes in v6:
time: 87 us; the launch traced here: 86.8 us
  starting transfers between devices  34.1 us (39%)
  waiting for transfers between devices  34.1 us (39%)
  Pallas kernels  12.7 us (15%)
  local copies, waits for them, and re-layouts  4.96 us (6%)
    ppermute x33, starting transfers between devices, shifted(): lax.ppermute(part, 'ctx', [(index, index ^ mask) for index in range(devic...  34.1 us
    ppermute x33, waiting for transfers between devices, shifted(): lax.ppermute(part, 'ctx', [(index, index ^ mask) for index in range(devic...  34.1 us
    pallas_call x27, Pallas kernels, call(): pl.pallas_call(body, out_shape=out_shape, in_specs=[SMEM if a.dtype == jn...  12.7 us
    unnamed x37, local copies, waits for them, and re-layouts  4.07 us
  transfers between devices with their start and end apart: 33, of which 17 were waited for; matrix products, arithmetic and copies ran while one was open for 2% of the time, Pallas kernels for 11%

profile of v6, /device:TPU:0, one launch (start us, length us, event | category | flops | bytes accessed | tf_op | source)
XLA Modules:
  0.0 86.8 jit_solution(8482325630353822954)
XLA Ops:
  0.0 3.1 %collective-permute-start = (bf16[1,16,512]{2,1,0:T(8,128)(2,1)}, bf16[1,16,512]{2,1,0:T(8,128)(2,1)S(1)}, u32[]{:S(2)}, u32[]{:S(2)}) collective-permute-start(bf16[1,16,512]{2,1,0:T(8,128)(2,1)} %bitcast.57), channel_id=1, source_target_pairs={{0,4},{1,5},{2,6},{3,7},{4,0},{5,1},{6,2},{7,3},{8,12},{9,13},{10,... | collective-permute-start | bytes 49160 | tf_op jit(solution)/shard_map/ppermute | solution.py:47
  3.1 2.6 %collective-permute-start.1 = (bf16[1,16,512]{2,1,0:T(8,128)(2,1)}, bf16[1,16,512]{2,1,0:T(8,128)(2,1)S(1)}, u32[]{:S(2)}, u32[]{:S(2)}) collective-permute-start(bf16[1,16,512]{2,1,0:T(8,128)(2,1)} %bitcast.58), channel_id=1, source_target_pairs={{0,8},{1,9},{2,10},{3,11},{4,12},{5,13},{6,14},{7,15},{8,0},{9,1},... | collective-permute-start | bytes 49160 | tf_op jit(solution)/shard_map/ppermute | solution.py:47
  5.6 0.8 copy-done.8
  6.5 0.6 copy-done.12
  7.7 0.2 collective-permute-done.1
  8.0 3.4 %collective-permute-done.2 = bf16[1,16,512]{2,1,0:T(8,128)(2,1)S(1)} collective-permute-done((bf16[1,16,512]{2,1,0:T(8,128)(2,1)}, bf16[1,16,512]{2,1,0:T(8,128)(2,1)S(1)}, u32[]{:S(2)}, u32[]{:S(2)}) %collective-permute-start.2) | collective-permute-done | bytes 16416 | tf_op jit(solution)/shard_map/ppermute | solution.py:47
  11.4 1.6 %collective-permute-start.3 = (bf16[4,16,512]{2,1,0:T(8,128)(2,1)S(1)}, bf16[4,16,512]{2,1,0:T(8,128)(2,1)S(1)}, u32[]{:S(2)}, u32[]{:S(2)}) collective-permute-start(bf16[4,16,512]{2,1,0:T(8,128)(2,1)S(1)} %pad_maximum_fusion.1.refs_0_), channel_id=1, source_target_pairs={{0,2},{1,3},{2,0},{3,1},{4,6},{5,7},{6,4},{7,5},{8,10},{9,11},{10,... | collective-permute-start | bytes 196616 | tf_op jit(solution)/shard_map/ppermute | solution.py:47
  13.1 2.7 %collective-permute-done.3.refs_0_ = bf16[4,16,512]{2,1,0:T(8,128)(2,1)S(1)} collective-permute-done((bf16[4,16,512]{2,1,0:T(8,128)(2,1)S(1)}, bf16[4,16,512]{2,1,0:T(8,128)(2,1)S(1)}, u32[]{:S(2)}, u32[]{:S(2)}) %collective-permute-start.3) | collective-permute-done | bytes 65568 | tf_op jit(solution)/shard_map/ppermute | solution.py:47
  15.8 2.1 %copy-done.2 = bf16[8192,256]{1,0:T(8,128)(2,1)S(1)} copy-done((bf16[8192,256]{1,0:T(8,128)(2,1)S(1)}, bf16[8192,256]{1,0:T(8,128)(2,1)}, u32[]{:S(2)}) %copy-start.2) | copy-done | bytes 4194328
  18.2 0.3 shard_map.137
  18.5 0.3 shard_map.138
  18.9 0.3 shard_map.139
  19.2 0.5 shard_map.141
  19.8 0.7 collective-permute-start.7
  20.5 3.6 %collective-permute-start.8 = (bf16[1,16,320]{2,1,0:T(8,128)(2,1)S(1)}, bf16[1,16,320]{2,1,0:T(8,128)(2,1)S(1)}, u32[]{:S(2)}, u32[]{:S(2)}) collective-permute-start(bf16[1,16,320]{2,1,0:T(8,128)(2,1)S(1)} %bitcast.51), channel_id=1, source_target_pairs={{0,12},{1,13},{2,14},{3,15},{4,8},{5,9},{6,10},{7,11},{8,4},{9,5},... | collective-permute-start | bytes 30728 | tf_op jit(solution)/shard_map/ppermute | solution.py:47
  24.1 0.3 collective-permute-done.7
  24.4 1.6 %collective-permute-done.8 = bf16[1,16,320]{2,1,0:T(8,128)(2,1)S(1)} collective-permute-done((bf16[1,16,320]{2,1,0:T(8,128)(2,1)S(1)}, bf16[1,16,320]{2,1,0:T(8,128)(2,1)S(1)}, u32[]{:S(2)}, u32[]{:S(2)}) %collective-permute-start.8) | collective-permute-done | bytes 10272 | tf_op jit(solution)/shard_map/ppermute | solution.py:47
  26.0 1.6 %collective-permute-start.11 = (bf16[4,16,320]{2,1,0:T(8,128)(2,1)S(1)}, bf16[4,16,320]{2,1,0:T(8,128)(2,1)S(1)}, u32[]{:S(2)}, u32[]{:S(2)}) collective-permute-start(bf16[4,16,320]{2,1,0:T(8,128)(2,1)S(1)} %pad_maximum_fusion.3.refs_1_), channel_id=1, source_target_pairs={{0,2},{1,3},{2,0},{3,1},{4,6},{5,7},{6,4},{7,5},{8,10},{9,11},{10,... | collective-permute-start | bytes 122888 | tf_op jit(solution)/shard_map/ppermute | solution.py:47
  27.6 2.5 %collective-permute-done.11.refs_1_.refs_2_ = bf16[4,16,320]{2,1,0:T(8,128)(2,1)S(1)} collective-permute-done((bf16[4,16,320]{2,1,0:T(8,128)(2,1)S(1)}, bf16[4,16,320]{2,1,0:T(8,128)(2,1)S(1)}, u32[]{:S(2)}, u32[]{:S(2)}) %collective-permute-start.11) | collective-permute-done | bytes 40992 | tf_op jit(solution)/shard_map/ppermute | solution.py:47
  30.2 0.7 copy.16
  30.8 0.2 copy.19
  31.1 0.6 shard_map.145
  31.7 0.5 collective-permute-start.13
  32.3 0.6 shard_map.143
  32.9 0.5 collective-permute-start.10
  33.4 0.5 shard_map.144
  34.1 1.6 %collective-permute-start.14 = (bf16[136,128]{1,0:T(8,128)(2,1)S(1)}, bf16[136,128]{1,0:T(8,128)(2,1)S(1)}, u32[]{:S(2)}, u32[]{:S(2)}) collective-permute-start(bf16[136,128]{1,0:T(8,128)(2,1)S(1)} %shard_map.146), channel_id=1, source_target_pairs={{0,2},{1,3},{2,0},{3,1},{4,6},{5,7},{6,4},{7,5},{8,10},{9,11},{10,... | collective-permute-start | bytes 104456 | tf_op jit(solution)/shard_map/ppermute | solution.py:47
  35.7 0.5 shard_map.142
  36.2 1.8 %collective-permute-done.14.message_ref = bf16[136,128]{1,0:T(8,128)(2,1)S(1)} collective-permute-done((bf16[136,128]{1,0:T(8,128)(2,1)S(1)}, bf16[136,128]{1,0:T(8,128)(2,1)S(1)}, u32[]{:S(2)}, u32[]{:S(2)}) %collective-permute-start.14) | collective-permute-done | bytes 34848 | tf_op jit(solution)/shard_map/ppermute | solution.py:47
  38.1 0.2 shard_map.147
  38.2 0.4 collective-permute-start.15
  38.7 3.8 %collective-permute-start.16 = (bf16[136,128]{1,0:T(8,128)(2,1)S(1)}, bf16[136,128]{1,0:T(8,128)(2,1)S(1)}, u32[]{:S(2)}, u32[]{:S(2)}) collective-permute-start(bf16[136,128]{1,0:T(8,128)(2,1)S(1)} %get-tuple-element.57), channel_id=1, source_target_pairs={{0,8},{1,9},{2,10},{3,11},{4,12},{5,13},{6,14},{7,15},{8,0},{9,1},... | collective-permute-start | bytes 104456 | tf_op jit(solution)/shard_map/ppermute | solution.py:47
  42.7 0.2 shard_map.148
  42.9 1.9 %collective-permute-done.16.refs_3_ = bf16[136,128]{1,0:T(8,128)(2,1)S(1)} collective-permute-done((bf16[136,128]{1,0:T(8,128)(2,1)S(1)}, bf16[136,128]{1,0:T(8,128)(2,1)S(1)}, u32[]{:S(2)}, u32[]{:S(2)}) %collective-permute-start.16) | collective-permute-done | bytes 34848 | tf_op jit(solution)/shard_map/ppermute | solution.py:47
  44.8 3.4 %collective-permute-done.17.refs_4_ = bf16[136,128]{1,0:T(8,128)(2,1)S(1)} collective-permute-done((bf16[136,128]{1,0:T(8,128)(2,1)S(1)}, bf16[136,128]{1,0:T(8,128)(2,1)S(1)}, u32[]{:S(2)}, u32[]{:S(2)}) %collective-permute-start.17) | collective-permute-done | bytes 34848 | tf_op jit(solution)/shard_map/ppermute | solution.py:47
  48.2 0.2 shard_map.149.refs_0_
  48.4 1.6 %collective-permute-start.18 = (bf16[4,16,256]{2,1,0:T(8,128)(2,1)S(1)}, bf16[4,16,256]{2,1,0:T(8,128)(2,1)S(1)}, u32[]{:S(2)}, u32[]{:S(2)}) collective-permute-start(bf16[4,16,256]{2,1,0:T(8,128)(2,1)S(1)} %shard_map.149.refs_0_), channel_id=1, source_target_pairs={{0,2},{1,3},{2,0},{3,1},{4,6},{5,7},{6,4},{7,5},{8,10},{9,11},{10,... | collective-permute-start | bytes 98312 | tf_op jit(solution)/shard_map/ppermute | solution.py:47
  50.0 2.4 %collective-permute-done.18.refs_0_ = bf16[4,16,256]{2,1,0:T(8,128)(2,1)S(1)} collective-permute-done((bf16[4,16,256]{2,1,0:T(8,128)(2,1)S(1)}, bf16[4,16,256]{2,1,0:T(8,128)(2,1)S(1)}, u32[]{:S(2)}, u32[]{:S(2)}) %collective-permute-start.18) | collective-permute-done | bytes 32800 | tf_op jit(solution)/shard_map/ppermute | solution.py:47
  52.4 0.2 shard_map.150.refs_2_
  52.7 0.3 shard_map.151.refs_2_
  52.9 0.3 shard_map.152.refs_2_
  53.2 0.4 collective-permute-done.19.refs_0_
  53.6 0.2 shard_map.153.refs_3_
  53.9 0.9 %collective-permute-start.22 = (bf16[1,16,512]{2,1,0:T(8,128)(2,1)S(1)}, bf16[1,16,512]{2,1,0:T(8,128)(2,1)S(1)}, u32[]{:S(2)}, u32[]{:S(2)}) collective-permute-start(bf16[1,16,512]{2,1,0:T(8,128)(2,1)S(1)} %bitcast.46), channel_id=1, source_target_pairs={{0,8},{1,9},{2,10},{3,11},{4,12},{5,13},{6,14},{7,15},{8,0},{9,1},... | collective-permute-start | bytes 49160 | tf_op jit(solution)/shard_map/ppermute | solution.py:47
  54.8 3.5 %collective-permute-start.23 = (bf16[1,16,512]{2,1,0:T(8,128)(2,1)S(1)}, bf16[1,16,512]{2,1,0:T(8,128)(2,1)S(1)}, u32[]{:S(2)}, u32[]{:S(2)}) collective-permute-start(bf16[1,16,512]{2,1,0:T(8,128)(2,1)S(1)} %bitcast.47), channel_id=1, source_target_pairs={{0,12},{1,13},{2,14},{3,15},{4,8},{5,9},{6,10},{7,11},{8,4},{9,5},... | collective-permute-start | bytes 49160 | tf_op jit(solution)/shard_map/ppermute | solution.py:47
  58.3 0.3 collective-permute-done.22
  58.6 1.8 %collective-permute-done.23 = bf16[1,16,512]{2,1,0:T(8,128)(2,1)S(1)} collective-permute-done((bf16[1,16,512]{2,1,0:T(8,128)(2,1)S(1)}, bf16[1,16,512]{2,1,0:T(8,128)(2,1)S(1)}, u32[]{:S(2)}, u32[]{:S(2)}) %collective-permute-start.23) | collective-permute-done | bytes 16416 | tf_op jit(solution)/shard_map/ppermute | solution.py:47
  60.4 1.6 %collective-permute-start.24 = (bf16[4,16,512]{2,1,0:T(8,128)(2,1)S(1)}, bf16[4,16,512]{2,1,0:T(8,128)(2,1)S(1)}, u32[]{:S(2)}, u32[]{:S(2)}) collective-permute-start(bf16[4,16,512]{2,1,0:T(8,128)(2,1)S(1)} %pad_maximum_fusion.2.refs_0_), channel_id=1, source_target_pairs={{0,2},{1,3},{2,0},{3,1},{4,6},{5,7},{6,4},{7,5},{8,10},{9,11},{10,... | collective-permute-start | bytes 196616 | tf_op jit(solution)/shard_map/ppermute | solution.py:47
  62.0 2.7 %collective-permute-done.24.refs_0_ = bf16[4,16,512]{2,1,0:T(8,128)(2,1)S(1)} collective-permute-done((bf16[4,16,512]{2,1,0:T(8,128)(2,1)S(1)}, bf16[4,16,512]{2,1,0:T(8,128)(2,1)S(1)}, u32[]{:S(2)}, u32[]{:S(2)}) %collective-permute-start.24) | collective-permute-done | bytes 65568 | tf_op jit(solution)/shard_map/ppermute | solution.py:47
  64.7 1.1 %shard_map.154 = (f32[16,896]{1,0:T(8,128)S(1)}, f32[16,896]{1,0:T(8,128)S(1)}, f32[16,128]{1,0:T(8,128)S(1)}) custom-call(s32[1]{0:T(128)} %bitcast.device_ref.refs_0_, bf16[4,16,512]{2,1,0:T(8,128)(2,1)S(1)} %pad_maximum_fusion.2.refs_0_, f32[16,1,512]{2,1,0:T(1,128)S(1)} %bitcast.41, bf16[8192,896]{1,0:T(8,128)(2,1)S(1)} %copy-done, ...), custom_call_target="tpu_custom_call" | custom-call | flops 117440512 | bytes 29458436 | tf_op jit(solution)/shard_map/pallas_call | solution.py:82
  65.8 1.1 %shard_map.155 = (f32[16,896]{1,0:T(8,128)S(1)}, f32[16,896]{1,0:T(8,128)S(1)}, f32[16,128]{1,0:T(8,128)S(1)}) custom-call(s32[1]{0:T(128)} %bitcast.device_ref.refs_0_, bf16[4,16,512]{2,1,0:T(8,128)(2,1)S(1)} %collective-permute-done.26.refs_0_, f32[16,1,512]{2,1,0:T(1,128)S(1)} %bitcast.42, bf16[8192,896]{1,0:T(8,128)(2,1)S(1)} %copy-done, ...), custom_call_target="tpu_custom_call" | custom-call | flops 117440512 | bytes 29581316 | tf_op jit(solution)/shard_map/pallas_call | solution.py:82
  66.9 1.1 %shard_map.156 = (f32[16,896]{1,0:T(8,128)S(1)}, f32[16,896]{1,0:T(8,128)S(1)}, f32[16,128]{1,0:T(8,128)S(1)}) custom-call(s32[1]{0:T(128)} %bitcast.device_ref.refs_0_, bf16[4,16,512]{2,1,0:T(8,128)(2,1)S(1)} %collective-permute-done.24.refs_0_, f32[16,1,512]{2,1,0:T(1,128)S(1)} %bitcast.43, bf16[8192,896]{1,0:T(8,128)(2,1)S(1)} %copy-done, ...), custom_call_target="tpu_custom_call" | custom-call | flops 117440512 | bytes 29581316 | tf_op jit(solution)/shard_map/pallas_call | solution.py:82
  68.0 1.1 %shard_map.157.in_ref = bf16[16,896]{1,0:T(8,128)(2,1)S(1)} custom-call(s32[1]{0:T(128)} %bitcast.device_ref.refs_0_, bf16[4,16,512]{2,1,0:T(8,128)(2,1)S(1)} %collective-permute-done.25.refs_0_, f32[16,1,512]{2,1,0:T(1,128)S(1)} %bitcast.44, bf16[8192,896]{1,0:T(8,128)(2,1)S(1)} %copy-done, bf16[8192,896]{1,0:T(8,128)(2,1)S(1)} %copy-done.1, ...), custom_call_target="tpu_custom_call" | custom-call | flops 117440512 | bytes 29581316 | tf_op jit(solution)/shard_map/pallas_call | solution.py:82
  69.1 0.3 collective-permute-start.27
  69.4 3.8 %collective-permute-start.28 = (bf16[1,16,896]{2,1,0:T(8,128)(2,1)S(1)}, bf16[1,16,896]{2,1,0:T(8,128)(2,1)S(1)}, u32[]{:S(2)}, u32[]{:S(2)}) collective-permute-start(bf16[1,16,896]{2,1,0:T(8,128)(2,1)S(1)} %bitcast.54), channel_id=1, source_target_pairs={{0,8},{1,9},{2,10},{3,11},{4,12},{5,13},{6,14},{7,15},{8,0},{9,1},... | collective-permute-start | bytes 86024 | tf_op jit(solution)/shard_map/ppermute | solution.py:47
  73.2 0.4 collective-permute-start.29
  73.6 1.9 %collective-permute-done.28 = bf16[1,16,896]{2,1,0:T(8,128)(2,1)S(1)} collective-permute-done((bf16[1,16,896]{2,1,0:T(8,128)(2,1)S(1)}, bf16[1,16,896]{2,1,0:T(8,128)(2,1)S(1)}, u32[]{:S(2)}, u32[]{:S(2)}) %collective-permute-start.28) | collective-permute-done | bytes 28704 | tf_op jit(solution)/shard_map/ppermute | solution.py:47
  75.5 3.4 %collective-permute-done.29 = bf16[1,16,896]{2,1,0:T(8,128)(2,1)S(1)} collective-permute-done((bf16[1,16,896]{2,1,0:T(8,128)(2,1)S(1)}, bf16[1,16,896]{2,1,0:T(8,128)(2,1)S(1)}, u32[]{:S(2)}, u32[]{:S(2)}) %collective-permute-start.29) | collective-permute-done | bytes 28704 | tf_op jit(solution)/shard_map/ppermute | solution.py:47
  78.9 1.6 %collective-permute-start.30 = (bf16[4,16,896]{2,1,0:T(8,128)(2,1)S(1)}, bf16[4,16,896]{2,1,0:T(8,128)(2,1)S(1)}, u32[]{:S(2)}, u32[]{:S(2)}) collective-permute-start(bf16[4,16,896]{2,1,0:T(8,128)(2,1)S(1)} %pad_maximum_fusion.refs_0_), channel_id=1, source_target_pairs={{0,2},{1,3},{2,0},{3,1},{4,6},{5,7},{6,4},{7,5},{8,10},{9,11},{10,... | collective-permute-start | bytes 344072 | tf_op jit(solution)/shard_map/ppermute | solution.py:47
  80.5 3.3 %collective-permute-done.30.refs_0_ = bf16[4,16,896]{2,1,0:T(8,128)(2,1)S(1)} collective-permute-done((bf16[4,16,896]{2,1,0:T(8,128)(2,1)S(1)}, bf16[4,16,896]{2,1,0:T(8,128)(2,1)S(1)}, u32[]{:S(2)}, u32[]{:S(2)}) %collective-permute-start.30) | collective-permute-done | bytes 114720 | tf_op jit(solution)/shard_map/ppermute | solution.py:47
  83.8 0.6 shard_map.159.refs_2_
  84.4 0.6 shard_map.160.refs_2_
  85.0 0.6 shard_map.161.refs_2_
  85.5 1.2 %shard_map.162 = bf16[16,512]{1,0:T(8,128)(2,1)} custom-call(s32[1]{0:T(128)} %bitcast.device_ref.refs_0_, bf16[4,16,896]{2,1,0:T(8,128)(2,1)S(1)} %collective-permute-done.31.refs_0_, bf16[14336,512]{1,0:T(8,128)(2,1)S(1)} %bitcast.20, f32[16,512]{1,0:T(8,128)S(1)} %shard_map.161.refs_2_, bf16[16,512]{1,0:T(8,128)(2,1)S(1)} %shard_map.153.refs_3_), custom_call_target="tpu_custom_call" | custom-call | flops 58720256 | bytes 14843908 | tf_op jit(solution)/shard_map/pallas_call | solution.py:82
  (84 shorter events, 1.8 us)
Async XLA Ops:
  0.0 7.7 %collective-permute-start = (bf16[1,16,512]{2,1,0:T(8,128)(2,1)}, bf16[1,16,512]{2,1,0:T(8,128)(2,1)S(1)}, u32[]{:S(2)}, u32[]{:S(2)}) collective-permute-start(bf16[1,16,512]{2,1,0:T(8,128)(2,1)} %bitcast.57), channel_id=1, source_target_pairs={{0,4},{1,5},{2,6},{3,7},{4,0},{5,1},{6,2},{7,3},{8,12},{9,13},{10,... | collective-permute-start | bytes 49160 | tf_op jit(solution)/shard_map/ppermute | solution.py:47
  3.1 4.9 %collective-permute-start.1 = (bf16[1,16,512]{2,1,0:T(8,128)(2,1)}, bf16[1,16,512]{2,1,0:T(8,128)(2,1)S(1)}, u32[]{:S(2)}, u32[]{:S(2)}) collective-permute-start(bf16[1,16,512]{2,1,0:T(8,128)(2,1)} %bitcast.58), channel_id=1, source_target_pairs={{0,8},{1,9},{2,10},{3,11},{4,12},{5,13},{6,14},{7,15},{8,0},{9,1},... | collective-permute-start | bytes 49160 | tf_op jit(solution)/shard_map/ppermute | solution.py:47
  5.6 5.7 %collective-permute-start.2 = (bf16[1,16,512]{2,1,0:T(8,128)(2,1)}, bf16[1,16,512]{2,1,0:T(8,128)(2,1)S(1)}, u32[]{:S(2)}, u32[]{:S(2)}) collective-permute-start(bf16[1,16,512]{2,1,0:T(8,128)(2,1)} %bitcast.59), channel_id=1, source_target_pairs={{0,12},{1,13},{2,14},{3,15},{4,8},{5,9},{6,10},{7,11},{8,4},{9,5},... | collective-permute-start | bytes 49160 | tf_op jit(solution)/shard_map/ppermute | solution.py:47
  5.6 0.8 copy-start.8
  6.4 0.7 copy-start.12
  6.4 0.7 copy-start.13
  11.4 4.3 %collective-permute-start.3 = (bf16[4,16,512]{2,1,0:T(8,128)(2,1)S(1)}, bf16[4,16,512]{2,1,0:T(8,128)(2,1)S(1)}, u32[]{:S(2)}, u32[]{:S(2)}) collective-permute-start(bf16[4,16,512]{2,1,0:T(8,128)(2,1)S(1)} %pad_maximum_fusion.1.refs_0_), channel_id=1, source_target_pairs={{0,2},{1,3},{2,0},{3,1},{4,6},{5,7},{6,4},{7,5},{8,10},{9,11},{10,... | collective-permute-start | bytes 196616 | tf_op jit(solution)/shard_map/ppermute | solution.py:47
  13.0 5.5 %collective-permute-start.5 = (bf16[4,16,512]{2,1,0:T(8,128)(2,1)S(1)}, bf16[4,16,512]{2,1,0:T(8,128)(2,1)S(1)}, u32[]{:S(2)}, u32[]{:S(2)}) collective-permute-start(bf16[4,16,512]{2,1,0:T(8,128)(2,1)S(1)} %pad_maximum_fusion.1.refs_0_), channel_id=1, source_target_pairs={{0,1},{1,0},{2,3},{3,2},{4,5},{5,4},{6,7},{7,6},{8,9},{9,8},{10,11... | collective-permute-start | bytes 196616 | tf_op jit(solution)/shard_map/ppermute | solution.py:47
  15.7 3.5 %collective-permute-start.4 = (bf16[4,16,512]{2,1,0:T(8,128)(2,1)S(1)}, bf16[4,16,512]{2,1,0:T(8,128)(2,1)S(1)}, u32[]{:S(2)}, u32[]{:S(2)}) collective-permute-start(bf16[4,16,512]{2,1,0:T(8,128)(2,1)S(1)} %collective-permute-done.3.refs_0_), channel_id=1, source_target_pairs={{0,1},{1,0},{2,3},{3,2},{4,5},{5,4},{6,7},{7,6},{8,9},{9,8},{10,11... | collective-permute-start | bytes 196616 | tf_op jit(solution)/shard_map/ppermute | solution.py:47
  15.7 2.2 %copy-start.2 = (bf16[8192,256]{1,0:T(8,128)(2,1)S(1)}, bf16[8192,256]{1,0:T(8,128)(2,1)}, u32[]{:S(2)}) copy-start(bf16[8192,256]{1,0:T(8,128)(2,1)} %refs_2_.11) | copy-start | bytes 12582916
  15.7 2.3 %copy-start.4 = (bf16[8192,32]{0,1:T(8,128)(2,1)S(1)}, bf16[8192,32]{0,1:T(8,128)(2,1)}, u32[]{:S(2)}) copy-start(bf16[8192,32]{0,1:T(8,128)(2,1)} %param.17) | copy-start | bytes 1572868
  15.7 2.5 %copy-start.5 = (bf16[8192,32]{0,1:T(8,128)(2,1)S(1)}, bf16[8192,32]{0,1:T(8,128)(2,1)}, u32[]{:S(2)}) copy-start(bf16[8192,32]{0,1:T(8,128)(2,1)} %param.18) | copy-start | bytes 1572868
  15.8 2.5 %copy-start.6 = (f32[8192]{0:T(1024)S(1)}, f32[8192]{0:T(1024)}, u32[]{:S(2)}) copy-start(f32[8192]{0:T(1024)} %param.15) | copy-start | bytes 98308
  15.8 14.4 %copy-start.10 = (bf16[1024,4,128]{2,1,0:T(4,128)(2,1)S(1)}, bf16[1024,4,128]{2,1,0:T(4,128)(2,1)}, u32[]{:S(2)}) copy-start(bf16[1024,4,128]{2,1,0:T(4,128)(2,1)} %param.19) | copy-start | bytes 3145732
  15.8 15.0 %copy-start.11 = (bf16[1024,4,128]{2,1,0:T(4,128)(2,1)S(1)}, bf16[1024,4,128]{2,1,0:T(4,128)(2,1)}, u32[]{:S(2)}) copy-start(bf16[1024,4,128]{2,1,0:T(4,128)(2,1)} %param.20) | copy-start | bytes 3145732
  19.7 4.5 %collective-permute-start.6 = (bf16[1,16,320]{2,1,0:T(8,128)(2,1)S(1)}, bf16[1,16,320]{2,1,0:T(8,128)(2,1)S(1)}, u32[]{:S(2)}, u32[]{:S(2)}) collective-permute-start(bf16[1,16,320]{2,1,0:T(8,128)(2,1)S(1)} %bitcast.49), channel_id=1, source_target_pairs={{0,4},{1,5},{2,6},{3,7},{4,0},{5,1},{6,2},{7,3},{8,12},{9,13},{10,... | collective-permute-start | bytes 30728 | tf_op jit(solution)/shard_map/ppermute | solution.py:47
  19.8 4.7 %collective-permute-start.7 = (bf16[1,16,320]{2,1,0:T(8,128)(2,1)S(1)}, bf16[1,16,320]{2,1,0:T(8,128)(2,1)S(1)}, u32[]{:S(2)}, u32[]{:S(2)}) collective-permute-start(bf16[1,16,320]{2,1,0:T(8,128)(2,1)S(1)} %bitcast.50), channel_id=1, source_target_pairs={{0,8},{1,9},{2,10},{3,11},{4,12},{5,13},{6,14},{7,15},{8,0},{9,1},... | collective-permute-start | bytes 30728 | tf_op jit(solution)/shard_map/ppermute | solution.py:47
  20.5 5.5 %collective-permute-start.8 = (bf16[1,16,320]{2,1,0:T(8,128)(2,1)S(1)}, bf16[1,16,320]{2,1,0:T(8,128)(2,1)S(1)}, u32[]{:S(2)}, u32[]{:S(2)}) collective-permute-start(bf16[1,16,320]{2,1,0:T(8,128)(2,1)S(1)} %bitcast.51), channel_id=1, source_target_pairs={{0,12},{1,13},{2,14},{3,15},{4,8},{5,9},{6,10},{7,11},{8,4},{9,5},... | collective-permute-start | bytes 30728 | tf_op jit(solution)/shard_map/ppermute | solution.py:47
  26.0 4.2 %collective-permute-start.11 = (bf16[4,16,320]{2,1,0:T(8,128)(2,1)S(1)}, bf16[4,16,320]{2,1,0:T(8,128)(2,1)S(1)}, u32[]{:S(2)}, u32[]{:S(2)}) collective-permute-start(bf16[4,16,320]{2,1,0:T(8,128)(2,1)S(1)} %pad_maximum_fusion.3.refs_1_), channel_id=1, source_target_pairs={{0,2},{1,3},{2,0},{3,1},{4,6},{5,7},{6,4},{7,5},{8,10},{9,11},{10,... | collective-permute-start | bytes 122888 | tf_op jit(solution)/shard_map/ppermute | solution.py:47
  30.2 3.2 %collective-permute-start.12 = (bf16[4,16,320]{2,1,0:T(8,128)(2,1)S(1)}, bf16[4,16,320]{2,1,0:T(8,128)(2,1)S(1)}, u32[]{:S(2)}, u32[]{:S(2)}) collective-permute-start(bf16[4,16,320]{2,1,0:T(8,128)(2,1)S(1)} %collective-permute-done.11.refs_1_.refs_2_), channel_id=1, source_target_pairs={{0,1},{1,0},{2,3},{3,2},{4,5},{5,4},{6,7},{7,6},{8,9},{9,8},{10,11... | collective-permute-start | bytes 122888 | tf_op jit(solution)/shard_map/ppermute | solution.py:47
  31.7 2.2 %collective-permute-start.13 = (bf16[136,128]{1,0:T(8,128)(2,1)S(1)}, bf16[136,128]{1,0:T(8,128)(2,1)S(1)}, u32[]{:S(2)}, u32[]{:S(2)}) collective-permute-start(bf16[136,128]{1,0:T(8,128)(2,1)S(1)} %shard_map.145), channel_id=1, source_target_pairs={{0,1},{1,0},{2,3},{3,2},{4,5},{5,4},{6,7},{7,6},{8,9},{9,8},{10,11... | collective-permute-start | bytes 104456 | tf_op jit(solution)/shard_map/ppermute | solution.py:47
  32.2 3.4 %collective-permute-start.9 = (bf16[4,16,320]{2,1,0:T(8,128)(2,1)S(1)}, bf16[4,16,320]{2,1,0:T(8,128)(2,1)S(1)}, u32[]{:S(2)}, u32[]{:S(2)}) collective-permute-start(bf16[4,16,320]{2,1,0:T(8,128)(2,1)S(1)} %pad_maximum_fusion.3.refs_1_), channel_id=1, source_target_pairs={{0,1},{1,0},{2,3},{3,2},{4,5},{5,4},{6,7},{7,6},{8,9},{9,8},{10,11... | collective-permute-start | bytes 122888 | tf_op jit(solution)/shard_map/ppermute | solution.py:47
  32.9 3.3 %collective-permute-start.10 = (bf16[136,128]{1,0:T(8,128)(2,1)S(1)}, bf16[136,128]{1,0:T(8,128)(2,1)S(1)}, u32[]{:S(2)}, u32[]{:S(2)}) collective-permute-start(bf16[136,128]{1,0:T(8,128)(2,1)S(1)} %shard_map.143), channel_id=1, source_target_pairs={{0,1},{1,0},{2,3},{3,2},{4,5},{5,4},{6,7},{7,6},{8,9},{9,8},{10,11... | collective-permute-start | bytes 104456 | tf_op jit(solution)/shard_map/ppermute | solution.py:47
  34.1 4.0 %collective-permute-start.14 = (bf16[136,128]{1,0:T(8,128)(2,1)S(1)}, bf16[136,128]{1,0:T(8,128)(2,1)S(1)}, u32[]{:S(2)}, u32[]{:S(2)}) collective-permute-start(bf16[136,128]{1,0:T(8,128)(2,1)S(1)} %shard_map.146), channel_id=1, source_target_pairs={{0,2},{1,3},{2,0},{3,1},{4,6},{5,7},{6,4},{7,5},{8,10},{9,11},{10,... | collective-permute-start | bytes 104456 | tf_op jit(solution)/shard_map/ppermute | solution.py:47
  38.1 14.4 %copy-start.3 = (bf16[4096,512]{1,0:T(8,128)(2,1)S(1)}, bf16[4096,512]{1,0:T(8,128)(2,1)}, u32[]{:S(2)}) copy-start(bf16[4096,512]{1,0:T(8,128)(2,1)} %refs_1_.11) | copy-start | bytes 12582916
  38.2 4.6 %collective-permute-start.15 = (bf16[136,128]{1,0:T(8,128)(2,1)S(1)}, bf16[136,128]{1,0:T(8,128)(2,1)S(1)}, u32[]{:S(2)}, u32[]{:S(2)}) collective-permute-start(bf16[136,128]{1,0:T(8,128)(2,1)S(1)} %get-tuple-element.57), channel_id=1, source_target_pairs={{0,4},{1,5},{2,6},{3,7},{4,0},{5,1},{6,2},{7,3},{8,12},{9,13},{10,... | collective-permute-start | bytes 104456 | tf_op jit(solution)/shard_map/ppermute | solution.py:47
  38.7 6.1 %collective-permute-start.16 = (bf16[136,128]{1,0:T(8,128)(2,1)S(1)}, bf16[136,128]{1,0:T(8,128)(2,1)S(1)}, u32[]{:S(2)}, u32[]{:S(2)}) collective-permute-start(bf16[136,128]{1,0:T(8,128)(2,1)S(1)} %get-tuple-element.57), channel_id=1, source_target_pairs={{0,8},{1,9},{2,10},{3,11},{4,12},{5,13},{6,14},{7,15},{8,0},{9,1},... | collective-permute-start | bytes 104456 | tf_op jit(solution)/shard_map/ppermute | solution.py:47
  42.5 5.7 %collective-permute-start.17 = (bf16[136,128]{1,0:T(8,128)(2,1)S(1)}, bf16[136,128]{1,0:T(8,128)(2,1)S(1)}, u32[]{:S(2)}, u32[]{:S(2)}) collective-permute-start(bf16[136,128]{1,0:T(8,128)(2,1)S(1)} %get-tuple-element.57), channel_id=1, source_target_pairs={{0,12},{1,13},{2,14},{3,15},{4,8},{5,9},{6,10},{7,11},{8,4},{9,5},... | collective-permute-start | bytes 104456 | tf_op jit(solution)/shard_map/ppermute | solution.py:47
  48.4 5.2 %copy-start.9 = (bf16[16,512]{1,0:T(8,128)(2,1)S(1)}, bf16[16,512]{1,0:T(8,128)(2,1)}, u32[]{:S(2)}) copy-start(bf16[16,512]{1,0:T(8,128)(2,1)} %refs_3_.5) | copy-start | bytes 49156
  48.4 16.3 %copy-start.7 = (f32[8192]{0:T(1024)S(1)}, f32[8192]{0:T(1024)}, u32[]{:S(2)}) copy-start(f32[8192]{0:T(1024)} %param.22) | copy-start | bytes 98308
  48.4 4.0 %collective-permute-start.18 = (bf16[4,16,256]{2,1,0:T(8,128)(2,1)S(1)}, bf16[4,16,256]{2,1,0:T(8,128)(2,1)S(1)}, u32[]{:S(2)}, u32[]{:S(2)}) collective-permute-start(bf16[4,16,256]{2,1,0:T(8,128)(2,1)S(1)} %shard_map.149.refs_0_), channel_id=1, source_target_pairs={{0,2},{1,3},{2,0},{3,1},{4,6},{5,7},{6,4},{7,5},{8,10},{9,11},{10,... | collective-permute-start | bytes 98312 | tf_op jit(solution)/shard_map/ppermute | solution.py:47
  50.0 2.7 %collective-permute-start.20 = (bf16[4,16,256]{2,1,0:T(8,128)(2,1)S(1)}, bf16[4,16,256]{2,1,0:T(8,128)(2,1)S(1)}, u32[]{:S(2)}, u32[]{:S(2)}) collective-permute-start(bf16[4,16,256]{2,1,0:T(8,128)(2,1)S(1)} %shard_map.149.refs_0_), channel_id=1, source_target_pairs={{0,1},{1,0},{2,3},{3,2},{4,5},{5,4},{6,7},{7,6},{8,9},{9,8},{10,11... | collective-permute-start | bytes 98312 | tf_op jit(solution)/shard_map/ppermute | solution.py:47
  52.4 1.2 %collective-permute-start.19 = (bf16[4,16,256]{2,1,0:T(8,128)(2,1)S(1)}, bf16[4,16,256]{2,1,0:T(8,128)(2,1)S(1)}, u32[]{:S(2)}, u32[]{:S(2)}) collective-permute-start(bf16[4,16,256]{2,1,0:T(8,128)(2,1)S(1)} %collective-permute-done.18.refs_0_), channel_id=1, source_target_pairs={{0,1},{1,0},{2,3},{3,2},{4,5},{5,4},{6,7},{7,6},{8,9},{9,8},{10,11... | collective-permute-start | bytes 98312 | tf_op jit(solution)/shard_map/ppermute | solution.py:47
  52.4 12.3 %copy-start = (bf16[8192,896]{1,0:T(8,128)(2,1)S(1)}, bf16[8192,896]{1,0:T(8,128)(2,1)}, u32[]{:S(2)}) copy-start(bf16[8192,896]{1,0:T(8,128)(2,1)} %refs_2_.15) | copy-start | bytes 44040196
  52.4 12.3 %copy-start.1 = (bf16[8192,896]{1,0:T(8,128)(2,1)S(1)}, bf16[8192,896]{1,0:T(8,128)(2,1)}, u32[]{:S(2)}) copy-start(bf16[8192,896]{1,0:T(8,128)(2,1)} %refs_3_.9) | copy-start | bytes 44040196
  53.9 4.4 %collective-permute-start.21 = (bf16[1,16,512]{2,1,0:T(8,128)(2,1)S(1)}, bf16[1,16,512]{2,1,0:T(8,128)(2,1)S(1)}, u32[]{:S(2)}, u32[]{:S(2)}) collective-permute-start(bf16[1,16,512]{2,1,0:T(8,128)(2,1)S(1)} %bitcast.45), channel_id=1, source_target_pairs={{0,4},{1,5},{2,6},{3,7},{4,0},{5,1},{6,2},{7,3},{8,12},{9,13},{10,... | collective-permute-start | bytes 49160 | tf_op jit(solution)/shard_map/ppermute | solution.py:47
  53.9 4.7 %collective-permute-start.22 = (bf16[1,16,512]{2,1,0:T(8,128)(2,1)S(1)}, bf16[1,16,512]{2,1,0:T(8,128)(2,1)S(1)}, u32[]{:S(2)}, u32[]{:S(2)}) collective-permute-start(bf16[1,16,512]{2,1,0:T(8,128)(2,1)S(1)} %bitcast.46), channel_id=1, source_target_pairs={{0,8},{1,9},{2,10},{3,11},{4,12},{5,13},{6,14},{7,15},{8,0},{9,1},... | collective-permute-start | bytes 49160 | tf_op jit(solution)/shard_map/ppermute | solution.py:47
  54.8 5.5 %collective-permute-start.23 = (bf16[1,16,512]{2,1,0:T(8,128)(2,1)S(1)}, bf16[1,16,512]{2,1,0:T(8,128)(2,1)S(1)}, u32[]{:S(2)}, u32[]{:S(2)}) collective-permute-start(bf16[1,16,512]{2,1,0:T(8,128)(2,1)S(1)} %bitcast.47), channel_id=1, source_target_pairs={{0,12},{1,13},{2,14},{3,15},{4,8},{5,9},{6,10},{7,11},{8,4},{9,5},... | collective-permute-start | bytes 49160 | tf_op jit(solution)/shard_map/ppermute | solution.py:47
  60.4 4.3 %collective-permute-start.24 = (bf16[4,16,512]{2,1,0:T(8,128)(2,1)S(1)}, bf16[4,16,512]{2,1,0:T(8,128)(2,1)S(1)}, u32[]{:S(2)}, u32[]{:S(2)}) collective-permute-start(bf16[4,16,512]{2,1,0:T(8,128)(2,1)S(1)} %pad_maximum_fusion.2.refs_0_), channel_id=1, source_target_pairs={{0,2},{1,3},{2,0},{3,1},{4,6},{5,7},{6,4},{7,5},{8,10},{9,11},{10,... | collective-permute-start | bytes 196616 | tf_op jit(solution)/shard_map/ppermute | solution.py:47
  62.0 3.8 %collective-permute-start.26 = (bf16[4,16,512]{2,1,0:T(8,128)(2,1)S(1)}, bf16[4,16,512]{2,1,0:T(8,128)(2,1)S(1)}, u32[]{:S(2)}, u32[]{:S(2)}) collective-permute-start(bf16[4,16,512]{2,1,0:T(8,128)(2,1)S(1)} %pad_maximum_fusion.2.refs_0_), channel_id=1, source_target_pairs={{0,1},{1,0},{2,3},{3,2},{4,5},{5,4},{6,7},{7,6},{8,9},{9,8},{10,11... | collective-permute-start | bytes 196616 | tf_op jit(solution)/shard_map/ppermute | solution.py:47
  64.7 3.3 %collective-permute-start.25 = (bf16[4,16,512]{2,1,0:T(8,128)(2,1)S(1)}, bf16[4,16,512]{2,1,0:T(8,128)(2,1)S(1)}, u32[]{:S(2)}, u32[]{:S(2)}) collective-permute-start(bf16[4,16,512]{2,1,0:T(8,128)(2,1)S(1)} %collective-permute-done.24.refs_0_), channel_id=1, source_target_pairs={{0,1},{1,0},{2,3},{3,2},{4,5},{5,4},{6,7},{7,6},{8,9},{9,8},{10,11... | collective-permute-start | bytes 196616 | tf_op jit(solution)/shard_map/ppermute | solution.py:47
  68.0 15.8 %slice-start = ((s8[14680064]{0:T(1024)(128)(4,1)}), s8[4194304]{0:T(1024)(128)(4,1)S(1)}, s32[]{:S(2)}) async-start(s8[14680064]{0:T(1024)(128)(4,1)} %bitcast.19), calls=%async_computation | async-start | bytes 8388608
  69.1 14.7 %slice-start.1 = ((s8[14680064]{0:T(1024)(128)(4,1)}), s8[4194304]{0:T(1024)(128)(4,1)S(1)}, s32[]{:S(2)}) async-start(s8[14680064]{0:T(1024)(128)(4,1)} %bitcast.19), calls=%async_computation.1 | async-start | bytes 8388608
  69.1 14.7 %slice-start.2 = ((s8[14680064]{0:T(1024)(128)(4,1)}), s8[4194304]{0:T(1024)(128)(4,1)S(1)}, s32[]{:S(2)}) async-start(s8[14680064]{0:T(1024)(128)(4,1)} %bitcast.19), calls=%async_computation.2 | async-start | bytes 8388608
  69.1 14.7 %slice-start.3 = ((s8[14680064]{0:T(1024)(128)(4,1)}), s8[2097152]{0:T(1024)(128)(4,1)S(1)}, s32[]{:S(2)}) async-start(s8[14680064]{0:T(1024)(128)(4,1)} %bitcast.19), calls=%async_computation.3 | async-start | bytes 4194304
  69.1 4.5 %collective-permute-start.27 = (bf16[1,16,896]{2,1,0:T(8,128)(2,1)S(1)}, bf16[1,16,896]{2,1,0:T(8,128)(2,1)S(1)}, u32[]{:S(2)}, u32[]{:S(2)}) collective-permute-start(bf16[1,16,896]{2,1,0:T(8,128)(2,1)S(1)} %bitcast.53), channel_id=1, source_target_pairs={{0,4},{1,5},{2,6},{3,7},{4,0},{5,1},{6,2},{7,3},{8,12},{9,13},{10,... | collective-permute-start | bytes 86024 | tf_op jit(solution)/shard_map/ppermute | solution.py:47
  69.4 6.1 %collective-permute-start.28 = (bf16[1,16,896]{2,1,0:T(8,128)(2,1)S(1)}, bf16[1,16,896]{2,1,0:T(8,128)(2,1)S(1)}, u32[]{:S(2)}, u32[]{:S(2)}) collective-permute-start(bf16[1,16,896]{2,1,0:T(8,128)(2,1)S(1)} %bitcast.54), channel_id=1, source_target_pairs={{0,8},{1,9},{2,10},{3,11},{4,12},{5,13},{6,14},{7,15},{8,0},{9,1},... | collective-permute-start | bytes 86024 | tf_op jit(solution)/shard_map/ppermute | solution.py:47
  73.2 5.7 %collective-permute-start.29 = (bf16[1,16,896]{2,1,0:T(8,128)(2,1)S(1)}, bf16[1,16,896]{2,1,0:T(8,128)(2,1)S(1)}, u32[]{:S(2)}, u32[]{:S(2)}) collective-permute-start(bf16[1,16,896]{2,1,0:T(8,128)(2,1)S(1)} %bitcast.55), channel_id=1, source_target_pairs={{0,12},{1,13},{2,14},{3,15},{4,8},{5,9},{6,10},{7,11},{8,4},{9,5},... | collective-permute-start | bytes 86024 | tf_op jit(solution)/shard_map/ppermute | solution.py:47
  78.9 4.9 %collective-permute-start.30 = (bf16[4,16,896]{2,1,0:T(8,128)(2,1)S(1)}, bf16[4,16,896]{2,1,0:T(8,128)(2,1)S(1)}, u32[]{:S(2)}, u32[]{:S(2)}) collective-permute-start(bf16[4,16,896]{2,1,0:T(8,128)(2,1)S(1)} %pad_maximum_fusion.refs_0_), channel_id=1, source_target_pairs={{0,2},{1,3},{2,0},{3,1},{4,6},{5,7},{6,4},{7,5},{8,10},{9,11},{10,... | collective-permute-start | bytes 344072 | tf_op jit(solution)/shard_map/ppermute | solution.py:47
  80.5 3.9 %collective-permute-start.32 = (bf16[4,16,896]{2,1,0:T(8,128)(2,1)S(1)}, bf16[4,16,896]{2,1,0:T(8,128)(2,1)S(1)}, u32[]{:S(2)}, u32[]{:S(2)}) collective-permute-start(bf16[4,16,896]{2,1,0:T(8,128)(2,1)S(1)} %pad_maximum_fusion.refs_0_), channel_id=1, source_target_pairs={{0,1},{1,0},{2,3},{3,2},{4,5},{5,4},{6,7},{7,6},{8,9},{9,8},{10,11... | collective-permute-start | bytes 344072 | tf_op jit(solution)/shard_map/ppermute | solution.py:47
  83.7 1.8 %collective-permute-start.31 = (bf16[4,16,896]{2,1,0:T(8,128)(2,1)S(1)}, bf16[4,16,896]{2,1,0:T(8,128)(2,1)S(1)}, u32[]{:S(2)}, u32[]{:S(2)}) collective-permute-start(bf16[4,16,896]{2,1,0:T(8,128)(2,1)S(1)} %collective-permute-done.30.refs_0_), channel_id=1, source_target_pairs={{0,1},{1,0},{2,3},{3,2},{4,5},{5,4},{6,7},{7,6},{8,9},{9,8},{10,11... | collective-permute-start | bytes 344072 | tf_op jit(solution)/shard_map/ppermute | solution.py:47

commit v7 on v6

--- a/solution.py
+++ b/solution.py
@@ -341,7 +341,7 @@
         out_refs[1][...] = level
 
 
-def merge_last_kernel(mean_ref, level_ref, message_ref, sent_ref):
+def merge_pair_kernel(mean_ref, level_ref, message_ref, sent_ref):
     mean, level = merge([(mean_ref[...], level_ref[...]), read_message(message_ref[...])])
     put_message(sent_ref, mean, level)
 
@@ -378,7 +378,7 @@
             news.append(block[:, query_width:])
         key = jnp.concatenate([new[:, :key_width] for new in news], axis=1).astype(jnp.float32)
         value = jnp.concatenate([new[:, key_width:] for new in news], axis=1).astype(jnp.float32)
-        queries = far_ref[turned]
+        queries = far_brought_ref[turned]
         for h in range(query_width // head_dim):
             query = queries[:, h * head_dim : (h + 1) * head_dim].astype(jnp.float32)
             score = jnp.sum(query * key, axis=1, keepdims=True) * scale
@@ -411,7 +411,7 @@
 
 def by_group(device, place_index, devices):
     (stride, groups, _), (step, _, _), _ = digits(devices)
-    place_in_group = lax.bitwise_xor(lax.rem(device, stride), 1)
+    place_in_group = lax.bitwise_xor(lax.rem(device, stride), step + 1)
     far = lax.div(place_index, devices // 2) if not isinstance(place_index, int) else place_index // (devices // 2)
     near_place = lax.rem(place_index, devices // 2)
     turned = lax.bitwise_xor(place_in_group, lax.div(near_place, groups) * step)
@@ -533,23 +533,23 @@
         work = heads * rows * span * head_dim
         keys_across = rotated_prefix_keys.transpose(1, 2, 0).reshape(value_heads * head_dim, span)
 
-        def attended(label, blocks, sends):
+        late_limit = call(begin_kernel, "hold", buffer(rows, LANES, dtype=jnp.int32), (own, limit))
+
+        def attended(label, blocks, sends, limit=limit):
             return call(
                 lambda *refs: attend_unit_kernel(scale, head_dim, sends, *refs), "attend_" + label,
                 message if sends else (wide, wide), (own, blocks, keys_across, values, limit), (), work,
             )
 
         given = attended("a", held, True)
-        taken_held = shifted(given, 1)
-        mean, level = attended("b", far, False)
-        given = attended("c", brought, True)
         taken = shifted(given, 1)
-        given = call(
-            merge_last_kernel, "merge_last", message, (*attended("d", far_brought, False), taken)
-        )
-        taken = shifted(given, rounds[1][0])
+        given = call(merge_pair_kernel, "merge_core", message, (*attended("b", far, False), taken))
+        taken_next = shifted(given, rounds[1][0])
+        given = attended("c", brought, True, late_limit)
+        taken = shifted(given, 1)
+        mean, level = attended("d", far_brought, False, late_limit)
         given, mean, level = call(
-            merge_next_kernel, "merge_next", (message, wide, wide), (mean, level, taken_held, taken)
+            merge_next_kernel, "merge_next", (message, wide, wide), (mean, level, taken, taken_next)
         )
         taken = []
         for digit in range(1, rounds[0][1]):

time: 87 us -> 83.8 us (0.963)
  waiting for transfers between devices: 34.1 us -> 31.2 us
    ppermute x33, waiting for transfers between devices: 34.1 us -> 31.2 us  [shifted(): lax.ppermute(part, 'ctx', [(index, index ^ mask) for index in range(devic...]
    pallas_call x27 -> x28, Pallas kernels: 12.7 us -> 12.7 us  [call(): pl.pallas_call(body, out_shape=out_shape, in_specs=[SMEM if a.dtype == jn...]
where the time goes in v7:
time: 83.8 us; the launch traced here: 83.6 us
  starting transfers between devices  33.8 us (40%)
  waiting for transfers between devices  31.2 us (37%)
  Pallas kernels  12.7 us (15%)
  local copies, waits for them, and re-layouts  4.96 us (6%)
    ppermute x33, starting transfers between devices, shifted(): lax.ppermute(part, 'ctx', [(index, index ^ mask) for index in range(devic...  33.8 us
    ppermute x33, waiting for transfers between devices, shifted(): lax.ppermute(part, 'ctx', [(index, index ^ mask) for index in range(devic...  31.2 us
    pallas_call x28, Pallas kernels, call(): pl.pallas_call(body, out_shape=out_shape, in_specs=[SMEM if a.dtype == jn...  12.7 us
    unnamed x37, local copies, waits for them, and re-layouts  4.07 us
  transfers between devices with their start and end apart: 33, of which 17 were waited for; matrix products, arithmetic and copies ran while one was open for 2% of the time, Pallas kernels for 11%

profile of v7, /device:TPU:0, one launch (start us, length us, event | category | flops | bytes accessed | tf_op | source)
XLA Modules:
  0.0 83.6 jit_solution(9407600541986165000)
XLA Ops:
  0.0 3.1 %collective-permute-start = (bf16[1,16,512]{2,1,0:T(8,128)(2,1)}, bf16[1,16,512]{2,1,0:T(8,128)(2,1)S(1)}, u32[]{:S(2)}, u32[]{:S(2)}) collective-permute-start(bf16[1,16,512]{2,1,0:T(8,128)(2,1)} %bitcast.57), channel_id=1, source_target_pairs={{0,4},{1,5},{2,6},{3,7},{4,0},{5,1},{6,2},{7,3},{8,12},{9,13},{10,... | collective-permute-start | bytes 49160 | tf_op jit(solution)/shard_map/ppermute | solution.py:47
  3.1 2.6 %collective-permute-start.1 = (bf16[1,16,512]{2,1,0:T(8,128)(2,1)}, bf16[1,16,512]{2,1,0:T(8,128)(2,1)S(1)}, u32[]{:S(2)}, u32[]{:S(2)}) collective-permute-start(bf16[1,16,512]{2,1,0:T(8,128)(2,1)} %bitcast.58), channel_id=1, source_target_pairs={{0,8},{1,9},{2,10},{3,11},{4,12},{5,13},{6,14},{7,15},{8,0},{9,1},... | collective-permute-start | bytes 49160 | tf_op jit(solution)/shard_map/ppermute | solution.py:47
  5.6 0.8 copy-done.8
  6.5 0.6 copy-done.12
  7.7 0.2 collective-permute-done.1
  8.0 3.4 %collective-permute-done.2 = bf16[1,16,512]{2,1,0:T(8,128)(2,1)S(1)} collective-permute-done((bf16[1,16,512]{2,1,0:T(8,128)(2,1)}, bf16[1,16,512]{2,1,0:T(8,128)(2,1)S(1)}, u32[]{:S(2)}, u32[]{:S(2)}) %collective-permute-start.2) | collective-permute-done | bytes 16416 | tf_op jit(solution)/shard_map/ppermute | solution.py:47
  11.4 1.6 %collective-permute-start.3 = (bf16[4,16,512]{2,1,0:T(8,128)(2,1)S(1)}, bf16[4,16,512]{2,1,0:T(8,128)(2,1)S(1)}, u32[]{:S(2)}, u32[]{:S(2)}) collective-permute-start(bf16[4,16,512]{2,1,0:T(8,128)(2,1)S(1)} %pad_maximum_fusion.1.refs_0_), channel_id=1, source_target_pairs={{0,2},{1,3},{2,0},{3,1},{4,6},{5,7},{6,4},{7,5},{8,10},{9,11},{10,... | collective-permute-start | bytes 196616 | tf_op jit(solution)/shard_map/ppermute | solution.py:47
  13.1 2.7 %collective-permute-done.3.refs_0_ = bf16[4,16,512]{2,1,0:T(8,128)(2,1)S(1)} collective-permute-done((bf16[4,16,512]{2,1,0:T(8,128)(2,1)S(1)}, bf16[4,16,512]{2,1,0:T(8,128)(2,1)S(1)}, u32[]{:S(2)}, u32[]{:S(2)}) %collective-permute-start.3) | collective-permute-done | bytes 65568 | tf_op jit(solution)/shard_map/ppermute | solution.py:47
  15.8 2.1 %copy-done.2 = bf16[8192,256]{1,0:T(8,128)(2,1)S(1)} copy-done((bf16[8192,256]{1,0:T(8,128)(2,1)S(1)}, bf16[8192,256]{1,0:T(8,128)(2,1)}, u32[]{:S(2)}) %copy-start.2) | copy-done | bytes 4194328
  18.2 0.3 shard_map.137
  18.5 0.3 shard_map.138
  18.9 0.3 shard_map.139
  19.2 0.5 shard_map.141
  19.8 0.7 collective-permute-start.7
  20.5 3.6 %collective-permute-start.8 = (bf16[1,16,320]{2,1,0:T(8,128)(2,1)S(1)}, bf16[1,16,320]{2,1,0:T(8,128)(2,1)S(1)}, u32[]{:S(2)}, u32[]{:S(2)}) collective-permute-start(bf16[1,16,320]{2,1,0:T(8,128)(2,1)S(1)} %bitcast.51), channel_id=1, source_target_pairs={{0,12},{1,13},{2,14},{3,15},{4,8},{5,9},{6,10},{7,11},{8,4},{9,5},... | collective-permute-start | bytes 30728 | tf_op jit(solution)/shard_map/ppermute | solution.py:47
  24.1 0.3 collective-permute-done.7
  24.4 1.6 %collective-permute-done.8 = bf16[1,16,320]{2,1,0:T(8,128)(2,1)S(1)} collective-permute-done((bf16[1,16,320]{2,1,0:T(8,128)(2,1)S(1)}, bf16[1,16,320]{2,1,0:T(8,128)(2,1)S(1)}, u32[]{:S(2)}, u32[]{:S(2)}) %collective-permute-start.8) | collective-permute-done | bytes 10272 | tf_op jit(solution)/shard_map/ppermute | solution.py:47
  26.0 1.6 %collective-permute-start.9 = (bf16[4,16,320]{2,1,0:T(8,128)(2,1)S(1)}, bf16[4,16,320]{2,1,0:T(8,128)(2,1)S(1)}, u32[]{:S(2)}, u32[]{:S(2)}) collective-permute-start(bf16[4,16,320]{2,1,0:T(8,128)(2,1)S(1)} %pad_maximum_fusion.3.refs_1_), channel_id=1, source_target_pairs={{0,2},{1,3},{2,0},{3,1},{4,6},{5,7},{6,4},{7,5},{8,10},{9,11},{10,... | collective-permute-start | bytes 122888 | tf_op jit(solution)/shard_map/ppermute | solution.py:47
  27.6 0.7 copy.16
  28.3 0.2 copy.19
  28.6 0.6 shard_map.146
  29.2 0.5 collective-permute-start.13
  29.7 0.5 collective-permute-done.9.refs_1_.refs_2_
  30.2 0.5 shard_map.145
  30.9 1.6 %collective-permute-start.14 = (bf16[136,128]{1,0:T(8,128)(2,1)S(1)}, bf16[136,128]{1,0:T(8,128)(2,1)S(1)}, u32[]{:S(2)}, u32[]{:S(2)}) collective-permute-start(bf16[136,128]{1,0:T(8,128)(2,1)S(1)} %shard_map.147), channel_id=1, source_target_pairs={{0,2},{1,3},{2,0},{3,1},{4,6},{5,7},{6,4},{7,5},{8,10},{9,11},{10,... | collective-permute-start | bytes 104456 | tf_op jit(solution)/shard_map/ppermute | solution.py:47
  32.5 0.6 shard_map.144
  33.1 0.3 collective-permute-start.11
  33.3 0.5 shard_map.143
  33.9 1.0 %collective-permute-done.14.message_ref = bf16[136,128]{1,0:T(8,128)(2,1)S(1)} collective-permute-done((bf16[136,128]{1,0:T(8,128)(2,1)S(1)}, bf16[136,128]{1,0:T(8,128)(2,1)S(1)}, u32[]{:S(2)}, u32[]{:S(2)}) %collective-permute-start.14) | collective-permute-done | bytes 34848 | tf_op jit(solution)/shard_map/ppermute | solution.py:47
  34.9 0.2 shard_map.148
  35.1 0.4 collective-permute-start.15
  35.5 3.8 %collective-permute-start.16 = (bf16[136,128]{1,0:T(8,128)(2,1)S(1)}, bf16[136,128]{1,0:T(8,128)(2,1)S(1)}, u32[]{:S(2)}, u32[]{:S(2)}) collective-permute-start(bf16[136,128]{1,0:T(8,128)(2,1)S(1)} %get-tuple-element.57), channel_id=1, source_target_pairs={{0,8},{1,9},{2,10},{3,11},{4,12},{5,13},{6,14},{7,15},{8,0},{9,1},... | collective-permute-start | bytes 104456 | tf_op jit(solution)/shard_map/ppermute | solution.py:47
  39.5 0.2 shard_map.149
  39.7 2.2 %collective-permute-done.16.refs_3_ = bf16[136,128]{1,0:T(8,128)(2,1)S(1)} collective-permute-done((bf16[136,128]{1,0:T(8,128)(2,1)S(1)}, bf16[136,128]{1,0:T(8,128)(2,1)S(1)}, u32[]{:S(2)}, u32[]{:S(2)}) %collective-permute-start.16) | collective-permute-done | bytes 34848 | tf_op jit(solution)/shard_map/ppermute | solution.py:47
  41.9 3.2 %collective-permute-done.17.refs_4_ = bf16[136,128]{1,0:T(8,128)(2,1)S(1)} collective-permute-done((bf16[136,128]{1,0:T(8,128)(2,1)S(1)}, bf16[136,128]{1,0:T(8,128)(2,1)S(1)}, u32[]{:S(2)}, u32[]{:S(2)}) %collective-permute-start.17) | collective-permute-done | bytes 34848 | tf_op jit(solution)/shard_map/ppermute | solution.py:47
  45.0 0.2 shard_map.150.refs_0_
  45.3 1.6 %collective-permute-start.18 = (bf16[4,16,256]{2,1,0:T(8,128)(2,1)S(1)}, bf16[4,16,256]{2,1,0:T(8,128)(2,1)S(1)}, u32[]{:S(2)}, u32[]{:S(2)}) collective-permute-start(bf16[4,16,256]{2,1,0:T(8,128)(2,1)S(1)} %shard_map.150.refs_0_), channel_id=1, source_target_pairs={{0,2},{1,3},{2,0},{3,1},{4,6},{5,7},{6,4},{7,5},{8,10},{9,11},{10,... | collective-permute-start | bytes 98312 | tf_op jit(solution)/shard_map/ppermute | solution.py:47
  46.8 2.4 %collective-permute-done.18.refs_0_ = bf16[4,16,256]{2,1,0:T(8,128)(2,1)S(1)} collective-permute-done((bf16[4,16,256]{2,1,0:T(8,128)(2,1)S(1)}, bf16[4,16,256]{2,1,0:T(8,128)(2,1)S(1)}, u32[]{:S(2)}, u32[]{:S(2)}) %collective-permute-start.18) | collective-permute-done | bytes 32800 | tf_op jit(solution)/shard_map/ppermute | solution.py:47
  49.3 0.2 shard_map.151.refs_2_
  49.5 0.3 shard_map.152.refs_2_
  49.8 0.3 shard_map.153.refs_2_
  50.0 0.4 collective-permute-done.19.refs_0_
  50.4 0.2 shard_map.154.refs_3_
  50.7 0.9 %collective-permute-start.22 = (bf16[1,16,512]{2,1,0:T(8,128)(2,1)S(1)}, bf16[1,16,512]{2,1,0:T(8,128)(2,1)S(1)}, u32[]{:S(2)}, u32[]{:S(2)}) collective-permute-start(bf16[1,16,512]{2,1,0:T(8,128)(2,1)S(1)} %bitcast.46), channel_id=1, source_target_pairs={{0,8},{1,9},{2,10},{3,11},{4,12},{5,13},{6,14},{7,15},{8,0},{9,1},... | collective-permute-start | bytes 49160 | tf_op jit(solution)/shard_map/ppermute | solution.py:47
  51.6 3.5 %collective-permute-start.23 = (bf16[1,16,512]{2,1,0:T(8,128)(2,1)S(1)}, bf16[1,16,512]{2,1,0:T(8,128)(2,1)S(1)}, u32[]{:S(2)}, u32[]{:S(2)}) collective-permute-start(bf16[1,16,512]{2,1,0:T(8,128)(2,1)S(1)} %bitcast.47), channel_id=1, source_target_pairs={{0,12},{1,13},{2,14},{3,15},{4,8},{5,9},{6,10},{7,11},{8,4},{9,5},... | collective-permute-start | bytes 49160 | tf_op jit(solution)/shard_map/ppermute | solution.py:47
  55.1 0.3 collective-permute-done.22
  55.4 1.8 %collective-permute-done.23 = bf16[1,16,512]{2,1,0:T(8,128)(2,1)S(1)} collective-permute-done((bf16[1,16,512]{2,1,0:T(8,128)(2,1)S(1)}, bf16[1,16,512]{2,1,0:T(8,128)(2,1)S(1)}, u32[]{:S(2)}, u32[]{:S(2)}) %collective-permute-start.23) | collective-permute-done | bytes 16416 | tf_op jit(solution)/shard_map/ppermute | solution.py:47
  57.2 1.6 %collective-permute-start.24 = (bf16[4,16,512]{2,1,0:T(8,128)(2,1)S(1)}, bf16[4,16,512]{2,1,0:T(8,128)(2,1)S(1)}, u32[]{:S(2)}, u32[]{:S(2)}) collective-permute-start(bf16[4,16,512]{2,1,0:T(8,128)(2,1)S(1)} %pad_maximum_fusion.2.refs_0_), channel_id=1, source_target_pairs={{0,2},{1,3},{2,0},{3,1},{4,6},{5,7},{6,4},{7,5},{8,10},{9,11},{10,... | collective-permute-start | bytes 196616 | tf_op jit(solution)/shard_map/ppermute | solution.py:47
  58.8 2.7 %collective-permute-done.24.refs_0_ = bf16[4,16,512]{2,1,0:T(8,128)(2,1)S(1)} collective-permute-done((bf16[4,16,512]{2,1,0:T(8,128)(2,1)S(1)}, bf16[4,16,512]{2,1,0:T(8,128)(2,1)S(1)}, u32[]{:S(2)}, u32[]{:S(2)}) %collective-permute-start.24) | collective-permute-done | bytes 65568 | tf_op jit(solution)/shard_map/ppermute | solution.py:47
  61.5 1.1 %shard_map.155 = (f32[16,896]{1,0:T(8,128)S(1)}, f32[16,896]{1,0:T(8,128)S(1)}, f32[16,128]{1,0:T(8,128)S(1)}) custom-call(s32[1]{0:T(128)} %bitcast.device_ref.refs_0_, bf16[4,16,512]{2,1,0:T(8,128)(2,1)S(1)} %pad_maximum_fusion.2.refs_0_, f32[16,1,512]{2,1,0:T(1,128)S(1)} %bitcast.41, bf16[8192,896]{1,0:T(8,128)(2,1)S(1)} %copy-done, ...), custom_call_target="tpu_custom_call" | custom-call | flops 117440512 | bytes 29458436 | tf_op jit(solution)/shard_map/pallas_call | solution.py:82
  62.6 1.1 %shard_map.156 = (f32[16,896]{1,0:T(8,128)S(1)}, f32[16,896]{1,0:T(8,128)S(1)}, f32[16,128]{1,0:T(8,128)S(1)}) custom-call(s32[1]{0:T(128)} %bitcast.device_ref.refs_0_, bf16[4,16,512]{2,1,0:T(8,128)(2,1)S(1)} %collective-permute-done.26.refs_0_, f32[16,1,512]{2,1,0:T(1,128)S(1)} %bitcast.42, bf16[8192,896]{1,0:T(8,128)(2,1)S(1)} %copy-done, ...), custom_call_target="tpu_custom_call" | custom-call | flops 117440512 | bytes 29581316 | tf_op jit(solution)/shard_map/pallas_call | solution.py:82
  63.7 1.1 %shard_map.157 = (f32[16,896]{1,0:T(8,128)S(1)}, f32[16,896]{1,0:T(8,128)S(1)}, f32[16,128]{1,0:T(8,128)S(1)}) custom-call(s32[1]{0:T(128)} %bitcast.device_ref.refs_0_, bf16[4,16,512]{2,1,0:T(8,128)(2,1)S(1)} %collective-permute-done.24.refs_0_, f32[16,1,512]{2,1,0:T(1,128)S(1)} %bitcast.43, bf16[8192,896]{1,0:T(8,128)(2,1)S(1)} %copy-done, ...), custom_call_target="tpu_custom_call" | custom-call | flops 117440512 | bytes 29581316 | tf_op jit(solution)/shard_map/pallas_call | solution.py:82
  64.8 1.1 %shard_map.158.in_ref = bf16[16,896]{1,0:T(8,128)(2,1)S(1)} custom-call(s32[1]{0:T(128)} %bitcast.device_ref.refs_0_, bf16[4,16,512]{2,1,0:T(8,128)(2,1)S(1)} %collective-permute-done.25.refs_0_, f32[16,1,512]{2,1,0:T(1,128)S(1)} %bitcast.44, bf16[8192,896]{1,0:T(8,128)(2,1)S(1)} %copy-done, bf16[8192,896]{1,0:T(8,128)(2,1)S(1)} %copy-done.1, ...), custom_call_target="tpu_custom_call" | custom-call | flops 117440512 | bytes 29581316 | tf_op jit(solution)/shard_map/pallas_call | solution.py:82
  65.9 0.3 collective-permute-start.27
  66.2 3.8 %collective-permute-start.28 = (bf16[1,16,896]{2,1,0:T(8,128)(2,1)S(1)}, bf16[1,16,896]{2,1,0:T(8,128)(2,1)S(1)}, u32[]{:S(2)}, u32[]{:S(2)}) collective-permute-start(bf16[1,16,896]{2,1,0:T(8,128)(2,1)S(1)} %bitcast.54), channel_id=1, source_target_pairs={{0,8},{1,9},{2,10},{3,11},{4,12},{5,13},{6,14},{7,15},{8,0},{9,1},... | collective-permute-start | bytes 86024 | tf_op jit(solution)/shard_map/ppermute | solution.py:47
  70.0 0.4 collective-permute-start.29
  70.4 1.9 %collective-permute-done.28 = bf16[1,16,896]{2,1,0:T(8,128)(2,1)S(1)} collective-permute-done((bf16[1,16,896]{2,1,0:T(8,128)(2,1)S(1)}, bf16[1,16,896]{2,1,0:T(8,128)(2,1)S(1)}, u32[]{:S(2)}, u32[]{:S(2)}) %collective-permute-start.28) | collective-permute-done | bytes 28704 | tf_op jit(solution)/shard_map/ppermute | solution.py:47
  72.3 3.4 %collective-permute-done.29 = bf16[1,16,896]{2,1,0:T(8,128)(2,1)S(1)} collective-permute-done((bf16[1,16,896]{2,1,0:T(8,128)(2,1)S(1)}, bf16[1,16,896]{2,1,0:T(8,128)(2,1)S(1)}, u32[]{:S(2)}, u32[]{:S(2)}) %collective-permute-start.29) | collective-permute-done | bytes 28704 | tf_op jit(solution)/shard_map/ppermute | solution.py:47
  75.7 1.6 %collective-permute-start.30 = (bf16[4,16,896]{2,1,0:T(8,128)(2,1)S(1)}, bf16[4,16,896]{2,1,0:T(8,128)(2,1)S(1)}, u32[]{:S(2)}, u32[]{:S(2)}) collective-permute-start(bf16[4,16,896]{2,1,0:T(8,128)(2,1)S(1)} %pad_maximum_fusion.refs_0_), channel_id=1, source_target_pairs={{0,2},{1,3},{2,0},{3,1},{4,6},{5,7},{6,4},{7,5},{8,10},{9,11},{10,... | collective-permute-start | bytes 344072 | tf_op jit(solution)/shard_map/ppermute | solution.py:47
  77.3 3.3 %collective-permute-done.30.refs_0_ = bf16[4,16,896]{2,1,0:T(8,128)(2,1)S(1)} collective-permute-done((bf16[4,16,896]{2,1,0:T(8,128)(2,1)S(1)}, bf16[4,16,896]{2,1,0:T(8,128)(2,1)S(1)}, u32[]{:S(2)}, u32[]{:S(2)}) %collective-permute-start.30) | collective-permute-done | bytes 114720 | tf_op jit(solution)/shard_map/ppermute | solution.py:47
  80.6 0.6 shard_map.160.refs_2_
  81.2 0.6 shard_map.161.refs_2_
  81.8 0.6 shard_map.162.refs_2_
  82.4 1.2 %shard_map.163 = bf16[16,512]{1,0:T(8,128)(2,1)} custom-call(s32[1]{0:T(128)} %bitcast.device_ref.refs_0_, bf16[4,16,896]{2,1,0:T(8,128)(2,1)S(1)} %collective-permute-done.31.refs_0_, bf16[14336,512]{1,0:T(8,128)(2,1)S(1)} %bitcast.20, f32[16,512]{1,0:T(8,128)S(1)} %shard_map.162.refs_2_, bf16[16,512]{1,0:T(8,128)(2,1)S(1)} %shard_map.154.refs_3_), custom_call_target="tpu_custom_call" | custom-call | flops 58720256 | bytes 14843908 | tf_op jit(solution)/shard_map/pallas_call | solution.py:82
  (85 shorter events, 1.7 us)
Async XLA Ops:
  0.0 7.7 %collective-permute-start = (bf16[1,16,512]{2,1,0:T(8,128)(2,1)}, bf16[1,16,512]{2,1,0:T(8,128)(2,1)S(1)}, u32[]{:S(2)}, u32[]{:S(2)}) collective-permute-start(bf16[1,16,512]{2,1,0:T(8,128)(2,1)} %bitcast.57), channel_id=1, source_target_pairs={{0,4},{1,5},{2,6},{3,7},{4,0},{5,1},{6,2},{7,3},{8,12},{9,13},{10,... | collective-permute-start | bytes 49160 | tf_op jit(solution)/shard_map/ppermute | solution.py:47
  3.1 4.9 %collective-permute-start.1 = (bf16[1,16,512]{2,1,0:T(8,128)(2,1)}, bf16[1,16,512]{2,1,0:T(8,128)(2,1)S(1)}, u32[]{:S(2)}, u32[]{:S(2)}) collective-permute-start(bf16[1,16,512]{2,1,0:T(8,128)(2,1)} %bitcast.58), channel_id=1, source_target_pairs={{0,8},{1,9},{2,10},{3,11},{4,12},{5,13},{6,14},{7,15},{8,0},{9,1},... | collective-permute-start | bytes 49160 | tf_op jit(solution)/shard_map/ppermute | solution.py:47
  5.6 5.7 %collective-permute-start.2 = (bf16[1,16,512]{2,1,0:T(8,128)(2,1)}, bf16[1,16,512]{2,1,0:T(8,128)(2,1)S(1)}, u32[]{:S(2)}, u32[]{:S(2)}) collective-permute-start(bf16[1,16,512]{2,1,0:T(8,128)(2,1)} %bitcast.59), channel_id=1, source_target_pairs={{0,12},{1,13},{2,14},{3,15},{4,8},{5,9},{6,10},{7,11},{8,4},{9,5},... | collective-permute-start | bytes 49160 | tf_op jit(solution)/shard_map/ppermute | solution.py:47
  5.6 0.8 copy-start.8
  6.4 0.7 copy-start.12
  6.4 0.7 copy-start.13
  11.4 4.3 %collective-permute-start.3 = (bf16[4,16,512]{2,1,0:T(8,128)(2,1)S(1)}, bf16[4,16,512]{2,1,0:T(8,128)(2,1)S(1)}, u32[]{:S(2)}, u32[]{:S(2)}) collective-permute-start(bf16[4,16,512]{2,1,0:T(8,128)(2,1)S(1)} %pad_maximum_fusion.1.refs_0_), channel_id=1, source_target_pairs={{0,2},{1,3},{2,0},{3,1},{4,6},{5,7},{6,4},{7,5},{8,10},{9,11},{10,... | collective-permute-start | bytes 196616 | tf_op jit(solution)/shard_map/ppermute | solution.py:47
  13.0 5.5 %collective-permute-start.5 = (bf16[4,16,512]{2,1,0:T(8,128)(2,1)S(1)}, bf16[4,16,512]{2,1,0:T(8,128)(2,1)S(1)}, u32[]{:S(2)}, u32[]{:S(2)}) collective-permute-start(bf16[4,16,512]{2,1,0:T(8,128)(2,1)S(1)} %pad_maximum_fusion.1.refs_0_), channel_id=1, source_target_pairs={{0,1},{1,0},{2,3},{3,2},{4,5},{5,4},{6,7},{7,6},{8,9},{9,8},{10,11... | collective-permute-start | bytes 196616 | tf_op jit(solution)/shard_map/ppermute | solution.py:47
  15.7 3.5 %collective-permute-start.4 = (bf16[4,16,512]{2,1,0:T(8,128)(2,1)S(1)}, bf16[4,16,512]{2,1,0:T(8,128)(2,1)S(1)}, u32[]{:S(2)}, u32[]{:S(2)}) collective-permute-start(bf16[4,16,512]{2,1,0:T(8,128)(2,1)S(1)} %collective-permute-done.3.refs_0_), channel_id=1, source_target_pairs={{0,1},{1,0},{2,3},{3,2},{4,5},{5,4},{6,7},{7,6},{8,9},{9,8},{10,11... | collective-permute-start | bytes 196616 | tf_op jit(solution)/shard_map/ppermute | solution.py:47
  15.7 2.2 %copy-start.2 = (bf16[8192,256]{1,0:T(8,128)(2,1)S(1)}, bf16[8192,256]{1,0:T(8,128)(2,1)}, u32[]{:S(2)}) copy-start(bf16[8192,256]{1,0:T(8,128)(2,1)} %refs_2_.11) | copy-start | bytes 12582916
  15.7 2.3 %copy-start.4 = (bf16[8192,32]{0,1:T(8,128)(2,1)S(1)}, bf16[8192,32]{0,1:T(8,128)(2,1)}, u32[]{:S(2)}) copy-start(bf16[8192,32]{0,1:T(8,128)(2,1)} %param.17) | copy-start | bytes 1572868
  15.7 2.5 %copy-start.5 = (bf16[8192,32]{0,1:T(8,128)(2,1)S(1)}, bf16[8192,32]{0,1:T(8,128)(2,1)}, u32[]{:S(2)}) copy-start(bf16[8192,32]{0,1:T(8,128)(2,1)} %param.18) | copy-start | bytes 1572868
  15.8 2.5 %copy-start.6 = (f32[8192]{0:T(1024)S(1)}, f32[8192]{0:T(1024)}, u32[]{:S(2)}) copy-start(f32[8192]{0:T(1024)} %param.15) | copy-start | bytes 98308
  15.8 11.9 %copy-start.10 = (bf16[1024,4,128]{2,1,0:T(4,128)(2,1)S(1)}, bf16[1024,4,128]{2,1,0:T(4,128)(2,1)}, u32[]{:S(2)}) copy-start(bf16[1024,4,128]{2,1,0:T(4,128)(2,1)} %param.19) | copy-start | bytes 3145732
  15.8 12.5 %copy-start.11 = (bf16[1024,4,128]{2,1,0:T(4,128)(2,1)S(1)}, bf16[1024,4,128]{2,1,0:T(4,128)(2,1)}, u32[]{:S(2)}) copy-start(bf16[1024,4,128]{2,1,0:T(4,128)(2,1)} %param.20) | copy-start | bytes 3145732
  19.7 4.5 %collective-permute-start.6 = (bf16[1,16,320]{2,1,0:T(8,128)(2,1)S(1)}, bf16[1,16,320]{2,1,0:T(8,128)(2,1)S(1)}, u32[]{:S(2)}, u32[]{:S(2)}) collective-permute-start(bf16[1,16,320]{2,1,0:T(8,128)(2,1)S(1)} %bitcast.49), channel_id=1, source_target_pairs={{0,4},{1,5},{2,6},{3,7},{4,0},{5,1},{6,2},{7,3},{8,12},{9,13},{10,... | collective-permute-start | bytes 30728 | tf_op jit(solution)/shard_map/ppermute | solution.py:47
  19.8 4.7 %collective-permute-start.7 = (bf16[1,16,320]{2,1,0:T(8,128)(2,1)S(1)}, bf16[1,16,320]{2,1,0:T(8,128)(2,1)S(1)}, u32[]{:S(2)}, u32[]{:S(2)}) collective-permute-start(bf16[1,16,320]{2,1,0:T(8,128)(2,1)S(1)} %bitcast.50), channel_id=1, source_target_pairs={{0,8},{1,9},{2,10},{3,11},{4,12},{5,13},{6,14},{7,15},{8,0},{9,1},... | collective-permute-start | bytes 30728 | tf_op jit(solution)/shard_map/ppermute | solution.py:47
  20.5 5.5 %collective-permute-start.8 = (bf16[1,16,320]{2,1,0:T(8,128)(2,1)S(1)}, bf16[1,16,320]{2,1,0:T(8,128)(2,1)S(1)}, u32[]{:S(2)}, u32[]{:S(2)}) collective-permute-start(bf16[1,16,320]{2,1,0:T(8,128)(2,1)S(1)} %bitcast.51), channel_id=1, source_target_pairs={{0,12},{1,13},{2,14},{3,15},{4,8},{5,9},{6,10},{7,11},{8,4},{9,5},... | collective-permute-start | bytes 30728 | tf_op jit(solution)/shard_map/ppermute | solution.py:47
  26.0 4.2 %collective-permute-start.9 = (bf16[4,16,320]{2,1,0:T(8,128)(2,1)S(1)}, bf16[4,16,320]{2,1,0:T(8,128)(2,1)S(1)}, u32[]{:S(2)}, u32[]{:S(2)}) collective-permute-start(bf16[4,16,320]{2,1,0:T(8,128)(2,1)S(1)} %pad_maximum_fusion.3.refs_1_), channel_id=1, source_target_pairs={{0,2},{1,3},{2,0},{3,1},{4,6},{5,7},{6,4},{7,5},{8,10},{9,11},{10,... | collective-permute-start | bytes 122888 | tf_op jit(solution)/shard_map/ppermute | solution.py:47
  27.6 2.5 %collective-permute-start.12 = (bf16[4,16,320]{2,1,0:T(8,128)(2,1)S(1)}, bf16[4,16,320]{2,1,0:T(8,128)(2,1)S(1)}, u32[]{:S(2)}, u32[]{:S(2)}) collective-permute-start(bf16[4,16,320]{2,1,0:T(8,128)(2,1)S(1)} %pad_maximum_fusion.3.refs_1_), channel_id=1, source_target_pairs={{0,1},{1,0},{2,3},{3,2},{4,5},{5,4},{6,7},{7,6},{8,9},{9,8},{10,11... | collective-permute-start | bytes 122888 | tf_op jit(solution)/shard_map/ppermute | solution.py:47
  29.2 1.6 %collective-permute-start.13 = (bf16[136,128]{1,0:T(8,128)(2,1)S(1)}, bf16[136,128]{1,0:T(8,128)(2,1)S(1)}, u32[]{:S(2)}, u32[]{:S(2)}) collective-permute-start(bf16[136,128]{1,0:T(8,128)(2,1)S(1)} %shard_map.146), channel_id=1, source_target_pairs={{0,1},{1,0},{2,3},{3,2},{4,5},{5,4},{6,7},{7,6},{8,9},{9,8},{10,11... | collective-permute-start | bytes 104456 | tf_op jit(solution)/shard_map/ppermute | solution.py:47
  30.2 3.2 %collective-permute-start.10 = (bf16[4,16,320]{2,1,0:T(8,128)(2,1)S(1)}, bf16[4,16,320]{2,1,0:T(8,128)(2,1)S(1)}, u32[]{:S(2)}, u32[]{:S(2)}) collective-permute-start(bf16[4,16,320]{2,1,0:T(8,128)(2,1)S(1)} %collective-permute-done.9.refs_1_.refs_2_), channel_id=1, source_target_pairs={{0,1},{1,0},{2,3},{3,2},{4,5},{5,4},{6,7},{7,6},{8,9},{9,8},{10,11... | collective-permute-start | bytes 122888 | tf_op jit(solution)/shard_map/ppermute | solution.py:47
  30.9 4.0 %collective-permute-start.14 = (bf16[136,128]{1,0:T(8,128)(2,1)S(1)}, bf16[136,128]{1,0:T(8,128)(2,1)S(1)}, u32[]{:S(2)}, u32[]{:S(2)}) collective-permute-start(bf16[136,128]{1,0:T(8,128)(2,1)S(1)} %shard_map.147), channel_id=1, source_target_pairs={{0,2},{1,3},{2,0},{3,1},{4,6},{5,7},{6,4},{7,5},{8,10},{9,11},{10,... | collective-permute-start | bytes 104456 | tf_op jit(solution)/shard_map/ppermute | solution.py:47
  33.1 1.8 %collective-permute-start.11 = (bf16[136,128]{1,0:T(8,128)(2,1)S(1)}, bf16[136,128]{1,0:T(8,128)(2,1)S(1)}, u32[]{:S(2)}, u32[]{:S(2)}) collective-permute-start(bf16[136,128]{1,0:T(8,128)(2,1)S(1)} %shard_map.144), channel_id=1, source_target_pairs={{0,1},{1,0},{2,3},{3,2},{4,5},{5,4},{6,7},{7,6},{8,9},{9,8},{10,11... | collective-permute-start | bytes 104456 | tf_op jit(solution)/shard_map/ppermute | solution.py:47
  34.9 14.4 %copy-start.3 = (bf16[4096,512]{1,0:T(8,128)(2,1)S(1)}, bf16[4096,512]{1,0:T(8,128)(2,1)}, u32[]{:S(2)}) copy-start(bf16[4096,512]{1,0:T(8,128)(2,1)} %refs_1_.11) | copy-start | bytes 12582916
  35.1 4.6 %collective-permute-start.15 = (bf16[136,128]{1,0:T(8,128)(2,1)S(1)}, bf16[136,128]{1,0:T(8,128)(2,1)S(1)}, u32[]{:S(2)}, u32[]{:S(2)}) collective-permute-start(bf16[136,128]{1,0:T(8,128)(2,1)S(1)} %get-tuple-element.57), channel_id=1, source_target_pairs={{0,4},{1,5},{2,6},{3,7},{4,0},{5,1},{6,2},{7,3},{8,12},{9,13},{10,... | collective-permute-start | bytes 104456 | tf_op jit(solution)/shard_map/ppermute | solution.py:47
  35.5 6.4 %collective-permute-start.16 = (bf16[136,128]{1,0:T(8,128)(2,1)S(1)}, bf16[136,128]{1,0:T(8,128)(2,1)S(1)}, u32[]{:S(2)}, u32[]{:S(2)}) collective-permute-start(bf16[136,128]{1,0:T(8,128)(2,1)S(1)} %get-tuple-element.57), channel_id=1, source_target_pairs={{0,8},{1,9},{2,10},{3,11},{4,12},{5,13},{6,14},{7,15},{8,0},{9,1},... | collective-permute-start | bytes 104456 | tf_op jit(solution)/shard_map/ppermute | solution.py:47
  39.3 5.7 %collective-permute-start.17 = (bf16[136,128]{1,0:T(8,128)(2,1)S(1)}, bf16[136,128]{1,0:T(8,128)(2,1)S(1)}, u32[]{:S(2)}, u32[]{:S(2)}) collective-permute-start(bf16[136,128]{1,0:T(8,128)(2,1)S(1)} %get-tuple-element.57), channel_id=1, source_target_pairs={{0,12},{1,13},{2,14},{3,15},{4,8},{5,9},{6,10},{7,11},{8,4},{9,5},... | collective-permute-start | bytes 104456 | tf_op jit(solution)/shard_map/ppermute | solution.py:47
  45.2 5.2 %copy-start.9 = (bf16[16,512]{1,0:T(8,128)(2,1)S(1)}, bf16[16,512]{1,0:T(8,128)(2,1)}, u32[]{:S(2)}) copy-start(bf16[16,512]{1,0:T(8,128)(2,1)} %refs_3_.5) | copy-start | bytes 49156
  45.2 16.3 %copy-start.7 = (f32[8192]{0:T(1024)S(1)}, f32[8192]{0:T(1024)}, u32[]{:S(2)}) copy-start(f32[8192]{0:T(1024)} %param.22) | copy-start | bytes 98308
  45.3 4.0 %collective-permute-start.18 = (bf16[4,16,256]{2,1,0:T(8,128)(2,1)S(1)}, bf16[4,16,256]{2,1,0:T(8,128)(2,1)S(1)}, u32[]{:S(2)}, u32[]{:S(2)}) collective-permute-start(bf16[4,16,256]{2,1,0:T(8,128)(2,1)S(1)} %shard_map.150.refs_0_), channel_id=1, source_target_pairs={{0,2},{1,3},{2,0},{3,1},{4,6},{5,7},{6,4},{7,5},{8,10},{9,11},{10,... | collective-permute-start | bytes 98312 | tf_op jit(solution)/shard_map/ppermute | solution.py:47
  46.8 2.7 %collective-permute-start.20 = (bf16[4,16,256]{2,1,0:T(8,128)(2,1)S(1)}, bf16[4,16,256]{2,1,0:T(8,128)(2,1)S(1)}, u32[]{:S(2)}, u32[]{:S(2)}) collective-permute-start(bf16[4,16,256]{2,1,0:T(8,128)(2,1)S(1)} %shard_map.150.refs_0_), channel_id=1, source_target_pairs={{0,1},{1,0},{2,3},{3,2},{4,5},{5,4},{6,7},{7,6},{8,9},{9,8},{10,11... | collective-permute-start | bytes 98312 | tf_op jit(solution)/shard_map/ppermute | solution.py:47
  49.2 1.2 %collective-permute-start.19 = (bf16[4,16,256]{2,1,0:T(8,128)(2,1)S(1)}, bf16[4,16,256]{2,1,0:T(8,128)(2,1)S(1)}, u32[]{:S(2)}, u32[]{:S(2)}) collective-permute-start(bf16[4,16,256]{2,1,0:T(8,128)(2,1)S(1)} %collective-permute-done.18.refs_0_), channel_id=1, source_target_pairs={{0,1},{1,0},{2,3},{3,2},{4,5},{5,4},{6,7},{7,6},{8,9},{9,8},{10,11... | collective-permute-start | bytes 98312 | tf_op jit(solution)/shard_map/ppermute | solution.py:47
  49.2 12.3 %copy-start = (bf16[8192,896]{1,0:T(8,128)(2,1)S(1)}, bf16[8192,896]{1,0:T(8,128)(2,1)}, u32[]{:S(2)}) copy-start(bf16[8192,896]{1,0:T(8,128)(2,1)} %refs_2_.15) | copy-start | bytes 44040196
  49.2 12.3 %copy-start.1 = (bf16[8192,896]{1,0:T(8,128)(2,1)S(1)}, bf16[8192,896]{1,0:T(8,128)(2,1)}, u32[]{:S(2)}) copy-start(bf16[8192,896]{1,0:T(8,128)(2,1)} %refs_3_.9) | copy-start | bytes 44040196
  50.7 4.4 %collective-permute-start.21 = (bf16[1,16,512]{2,1,0:T(8,128)(2,1)S(1)}, bf16[1,16,512]{2,1,0:T(8,128)(2,1)S(1)}, u32[]{:S(2)}, u32[]{:S(2)}) collective-permute-start(bf16[1,16,512]{2,1,0:T(8,128)(2,1)S(1)} %bitcast.45), channel_id=1, source_target_pairs={{0,4},{1,5},{2,6},{3,7},{4,0},{5,1},{6,2},{7,3},{8,12},{9,13},{10,... | collective-permute-start | bytes 49160 | tf_op jit(solution)/shard_map/ppermute | solution.py:47
  50.7 4.7 %collective-permute-start.22 = (bf16[1,16,512]{2,1,0:T(8,128)(2,1)S(1)}, bf16[1,16,512]{2,1,0:T(8,128)(2,1)S(1)}, u32[]{:S(2)}, u32[]{:S(2)}) collective-permute-start(bf16[1,16,512]{2,1,0:T(8,128)(2,1)S(1)} %bitcast.46), channel_id=1, source_target_pairs={{0,8},{1,9},{2,10},{3,11},{4,12},{5,13},{6,14},{7,15},{8,0},{9,1},... | collective-permute-start | bytes 49160 | tf_op jit(solution)/shard_map/ppermute | solution.py:47
  51.6 5.5 %collective-permute-start.23 = (bf16[1,16,512]{2,1,0:T(8,128)(2,1)S(1)}, bf16[1,16,512]{2,1,0:T(8,128)(2,1)S(1)}, u32[]{:S(2)}, u32[]{:S(2)}) collective-permute-start(bf16[1,16,512]{2,1,0:T(8,128)(2,1)S(1)} %bitcast.47), channel_id=1, source_target_pairs={{0,12},{1,13},{2,14},{3,15},{4,8},{5,9},{6,10},{7,11},{8,4},{9,5},... | collective-permute-start | bytes 49160 | tf_op jit(solution)/shard_map/ppermute | solution.py:47
  57.2 4.3 %collective-permute-start.24 = (bf16[4,16,512]{2,1,0:T(8,128)(2,1)S(1)}, bf16[4,16,512]{2,1,0:T(8,128)(2,1)S(1)}, u32[]{:S(2)}, u32[]{:S(2)}) collective-permute-start(bf16[4,16,512]{2,1,0:T(8,128)(2,1)S(1)} %pad_maximum_fusion.2.refs_0_), channel_id=1, source_target_pairs={{0,2},{1,3},{2,0},{3,1},{4,6},{5,7},{6,4},{7,5},{8,10},{9,11},{10,... | collective-permute-start | bytes 196616 | tf_op jit(solution)/shard_map/ppermute | solution.py:47
  58.8 3.8 %collective-permute-start.26 = (bf16[4,16,512]{2,1,0:T(8,128)(2,1)S(1)}, bf16[4,16,512]{2,1,0:T(8,128)(2,1)S(1)}, u32[]{:S(2)}, u32[]{:S(2)}) collective-permute-start(bf16[4,16,512]{2,1,0:T(8,128)(2,1)S(1)} %pad_maximum_fusion.2.refs_0_), channel_id=1, source_target_pairs={{0,1},{1,0},{2,3},{3,2},{4,5},{5,4},{6,7},{7,6},{8,9},{9,8},{10,11... | collective-permute-start | bytes 196616 | tf_op jit(solution)/shard_map/ppermute | solution.py:47
  61.5 3.3 %collective-permute-start.25 = (bf16[4,16,512]{2,1,0:T(8,128)(2,1)S(1)}, bf16[4,16,512]{2,1,0:T(8,128)(2,1)S(1)}, u32[]{:S(2)}, u32[]{:S(2)}) collective-permute-start(bf16[4,16,512]{2,1,0:T(8,128)(2,1)S(1)} %collective-permute-done.24.refs_0_), channel_id=1, source_target_pairs={{0,1},{1,0},{2,3},{3,2},{4,5},{5,4},{6,7},{7,6},{8,9},{9,8},{10,11... | collective-permute-start | bytes 196616 | tf_op jit(solution)/shard_map/ppermute | solution.py:47
  64.8 15.8 %slice-start = ((s8[14680064]{0:T(1024)(128)(4,1)}), s8[4194304]{0:T(1024)(128)(4,1)S(1)}, s32[]{:S(2)}) async-start(s8[14680064]{0:T(1024)(128)(4,1)} %bitcast.19), calls=%async_computation | async-start | bytes 8388608
  65.9 14.7 %slice-start.1 = ((s8[14680064]{0:T(1024)(128)(4,1)}), s8[4194304]{0:T(1024)(128)(4,1)S(1)}, s32[]{:S(2)}) async-start(s8[14680064]{0:T(1024)(128)(4,1)} %bitcast.19), calls=%async_computation.1 | async-start | bytes 8388608
  65.9 14.7 %slice-start.2 = ((s8[14680064]{0:T(1024)(128)(4,1)}), s8[4194304]{0:T(1024)(128)(4,1)S(1)}, s32[]{:S(2)}) async-start(s8[14680064]{0:T(1024)(128)(4,1)} %bitcast.19), calls=%async_computation.2 | async-start | bytes 8388608
  65.9 14.7 %slice-start.3 = ((s8[14680064]{0:T(1024)(128)(4,1)}), s8[2097152]{0:T(1024)(128)(4,1)S(1)}, s32[]{:S(2)}) async-start(s8[14680064]{0:T(1024)(128)(4,1)} %bitcast.19), calls=%async_computation.3 | async-start | bytes 4194304
  65.9 4.5 %collective-permute-start.27 = (bf16[1,16,896]{2,1,0:T(8,128)(2,1)S(1)}, bf16[1,16,896]{2,1,0:T(8,128)(2,1)S(1)}, u32[]{:S(2)}, u32[]{:S(2)}) collective-permute-start(bf16[1,16,896]{2,1,0:T(8,128)(2,1)S(1)} %bitcast.53), channel_id=1, source_target_pairs={{0,4},{1,5},{2,6},{3,7},{4,0},{5,1},{6,2},{7,3},{8,12},{9,13},{10,... | collective-permute-start | bytes 86024 | tf_op jit(solution)/shard_map/ppermute | solution.py:47
  66.2 6.1 %collective-permute-start.28 = (bf16[1,16,896]{2,1,0:T(8,128)(2,1)S(1)}, bf16[1,16,896]{2,1,0:T(8,128)(2,1)S(1)}, u32[]{:S(2)}, u32[]{:S(2)}) collective-permute-start(bf16[1,16,896]{2,1,0:T(8,128)(2,1)S(1)} %bitcast.54), channel_id=1, source_target_pairs={{0,8},{1,9},{2,10},{3,11},{4,12},{5,13},{6,14},{7,15},{8,0},{9,1},... | collective-permute-start | bytes 86024 | tf_op jit(solution)/shard_map/ppermute | solution.py:47
  70.0 5.7 %collective-permute-start.29 = (bf16[1,16,896]{2,1,0:T(8,128)(2,1)S(1)}, bf16[1,16,896]{2,1,0:T(8,128)(2,1)S(1)}, u32[]{:S(2)}, u32[]{:S(2)}) collective-permute-start(bf16[1,16,896]{2,1,0:T(8,128)(2,1)S(1)} %bitcast.55), channel_id=1, source_target_pairs={{0,12},{1,13},{2,14},{3,15},{4,8},{5,9},{6,10},{7,11},{8,4},{9,5},... | collective-permute-start | bytes 86024 | tf_op jit(solution)/shard_map/ppermute | solution.py:47
  75.7 4.9 %collective-permute-start.30 = (bf16[4,16,896]{2,1,0:T(8,128)(2,1)S(1)}, bf16[4,16,896]{2,1,0:T(8,128)(2,1)S(1)}, u32[]{:S(2)}, u32[]{:S(2)}) collective-permute-start(bf16[4,16,896]{2,1,0:T(8,128)(2,1)S(1)} %pad_maximum_fusion.refs_0_), channel_id=1, source_target_pairs={{0,2},{1,3},{2,0},{3,1},{4,6},{5,7},{6,4},{7,5},{8,10},{9,11},{10,... | collective-permute-start | bytes 344072 | tf_op jit(solution)/shard_map/ppermute | solution.py:47
  77.3 3.9 %collective-permute-start.32 = (bf16[4,16,896]{2,1,0:T(8,128)(2,1)S(1)}, bf16[4,16,896]{2,1,0:T(8,128)(2,1)S(1)}, u32[]{:S(2)}, u32[]{:S(2)}) collective-permute-start(bf16[4,16,896]{2,1,0:T(8,128)(2,1)S(1)} %pad_maximum_fusion.refs_0_), channel_id=1, source_target_pairs={{0,1},{1,0},{2,3},{3,2},{4,5},{5,4},{6,7},{7,6},{8,9},{9,8},{10,11... | collective-permute-start | bytes 344072 | tf_op jit(solution)/shard_map/ppermute | solution.py:47
  80.6 1.8 %collective-permute-start.31 = (bf16[4,16,896]{2,1,0:T(8,128)(2,1)S(1)}, bf16[4,16,896]{2,1,0:T(8,128)(2,1)S(1)}, u32[]{:S(2)}, u32[]{:S(2)}) collective-permute-start(bf16[4,16,896]{2,1,0:T(8,128)(2,1)S(1)} %collective-permute-done.30.refs_0_), channel_id=1, source_target_pairs={{0,1},{1,0},{2,3},{3,2},{4,5},{5,4},{6,7},{7,6},{8,9},{9,8},{10,11... | collective-permute-start | bytes 344072 | tf_op jit(solution)/shard_map/ppermute | solution.py:47
